TPU v7x, 32 devices: a whole 2x2x4 slice. The times are simulated.
32 devices in a mesh: space: 8 (over z, y), path: 4 (over x, core).
Axes of the slice: x: 2, y: 2, z: 4, core: 2. Of those that a mesh axis runs over, the one named last changes fastest.
Arguments:
- path_field: float32 [32, 256, 1024], P('path', 'space'), may hold values from -2.5 to 2.5
- start_state: float32 [256, 1024], P('space'), may hold values from -2.5 to 2.5
- end_state: float32 [256, 1024], P('space'), may hold values from -2.5 to 2.5
Outputs:
- speed_ratio: float32 [32], P('path')
- residual: float32 [32, 256, 1024], P('path', 'space')
- gradient: float32 [32, 256, 1024], P('path', 'space')
All inputs are finite; a program needn't handle non-finite values.
Results may differ from a plain program's by a relative error of at most 0.00002.
Values sent between devices are 32-bit elements; how exact they have to be, the bound alone decides.
No kernel may reach another device: no remote copies, remote signals or barrier semaphores. Data moves between devices by JAX's collectives and lax.ppermute only.
A program may use at most 64 MiB of HBM per device.

v0:
```python
import jax
import jax.numpy as jnp
from jax import lax
from jax.sharding import PartitionSpec as P


def shifted(block, axis, distance):
    devices = range(lax.axis_size(axis))
    route = [(i - distance, i) for i in devices if i - distance in devices]
    return lax.ppermute(block, axis, route)


def extended_2(cells, sides, width):
    for axis, dim in sides:
        count = lax.axis_size(axis)
        head = lax.slice_in_dim(cells, 0, width, axis=dim)
        tail = lax.slice_in_dim(cells, cells.shape[dim] - width, cells.shape[dim], axis=dim)
        cells = jnp.concatenate(
            [
                lax.ppermute(tail, axis, [(i, (i + 1) % count) for i in range(count)]),
                cells,
                lax.ppermute(head, axis, [((i + 1) % count, i) for i in range(count)]),
            ],
            axis=dim,
        )
    return cells


def laplace_rows(padded):
    center = padded[:, 1:-1]
    return (
        padded[:, :-2]
        + padded[:, 2:]
        + jnp.roll(center, 1, 2)
        + jnp.roll(center, -1, 2)
        - 4.0 * center
    )


def slice_ratio(drift, tangent):
    drift_sq, tangent_sq = lax.psum(
        (jnp.sum(drift * drift, axis=(1, 2)), jnp.sum(tangent * tangent, axis=(1, 2))), "space"
    )
    return jnp.sqrt(drift_sq + 1e-06) / jnp.sqrt(tangent_sq + 1e-06)


def body(path_field, start_state, end_state):
    position = lax.axis_index("path")
    final = lax.axis_size("path") - 1
    from_below = shifted(path_field[-1:], "path", 1)
    from_above = shifted(path_field[:1], "path", -1)
    below = jnp.where(position == 0, start_state[None], from_below)
    above = jnp.where(position == final, end_state[None], from_above)
    extended = jnp.concatenate([below, path_field, above], axis=0)
    centers = extended[1:-1]
    padded = extended_2(centers, (("space", 1),), 1)
    drift_all = laplace_rows(padded) + centers - centers**3
    tangent_all = extended[2:] - extended[:-2]
    ratio_all = slice_ratio(drift_all, tangent_all)
    residual_all = ratio_all[:, None, None] * tangent_all - drift_all
    residual_pad = extended_2(residual_all, (("space", 1),), 1)
    laplace_res = laplace_rows(residual_pad)
    scaled_all = ratio_all[:, None, None] * residual_all
    lower = shifted(scaled_all[-1], "path", 1)
    upper = shifted(scaled_all[0], "path", -1)
    scaled_below = jnp.concatenate([lower[None], scaled_all[:-1]], axis=0)
    scaled_above = jnp.concatenate([scaled_all[1:], upper[None]], axis=0)
    gradient = (
        scaled_below - scaled_above - (laplace_res + (1.0 - 3.0 * path_field**2) * residual_all)
    )
    return (ratio_all, residual_all, gradient)


def solution(mesh):
    in_specs = (P("path", "space", None), P("space", None), P("space", None))
    out_specs = (P("path"), P("path", "space", None), P("path", "space", None))
    return jax.shard_map(body, mesh=mesh, in_specs=in_specs, out_specs=out_specs, check_vma=False)
```

profile of v0, /device:TPU:1, one launch (start us, length us, event | category | flops | bytes accessed | tf_op | source)
XLA Modules:
  0.0 52.4 jit_solution(4064909336589168774)
XLA Ops:
  0.6 1.1 %fusion.20 = (f32[8,1,1024]{2,1,0:T(1,128)S(1)}, f32[8,1,1024]{2,1,0:T(1,128)S(1)}) fusion(f32[8,32,1024]{2,1,0:T(8,128)} %param.3), kind=kLoop, calls=%fused_computation.37 | loop fusion | bytes 131072 | tf_op jit(solution)/shard_map/slice | solution.py:17
  1.7 2.1 %collective-permute-start = (f32[8,1,1024]{2,1,0:T(1,128)S(1)}, f32[8,1,1024]{2,1,0:T(1,128)S(1)}, u32[]{:S(2)}, u32[]{:S(2)}) collective-permute-start(f32[8,1,1024]{2,1,0:T(1,128)S(1)} %get-tuple-element.20), channel_id=1, source_target_pairs={{0,4},{4,8},{8,12},{12,16},{16,20},{20,24},{24,28},{28,0},{1,5},{5... | collective-permute-start | bytes 98312 | tf_op jit(solution)/shard_map/ppermute | solution.py:20
  3.8 3.1 %collective-permute-start.1 = (f32[8,1,1024]{2,1,0:T(1,128)S(1)}, f32[8,1,1024]{2,1,0:T(1,128)S(1)}, u32[]{:S(2)}, u32[]{:S(2)}) collective-permute-start(f32[8,1,1024]{2,1,0:T(1,128)S(1)} %get-tuple-element.21), channel_id=1, source_target_pairs={{4,0},{8,4},{12,8},{16,12},{20,16},{24,20},{28,24},{0,28},{5,1},{9... | collective-permute-start | bytes 98312 | tf_op jit(solution)/shard_map/ppermute | solution.py:22
  6.9 1.0 %fusion.23 = (f32[1,32,1024]{2,1,0:T(8,128)S(1)}, f32[1,32,1024]{2,1,0:T(8,128)S(1)}) fusion(f32[8,32,1024]{2,1,0:T(8,128)} %param.3), kind=kLoop, calls=%fused_computation.40 | loop fusion | bytes 524288 | tf_op jit(solution)/shard_map/slice | solution.py:51
  7.9 2.9 %collective-permute-start.2 = (f32[1,32,1024]{2,1,0:T(8,128)S(1)}, f32[1,32,1024]{2,1,0:T(8,128)S(1)}, u32[]{:S(2)}, u32[]{:S(2)}) collective-permute-start(f32[1,32,1024]{2,1,0:T(8,128)S(1)} %get-tuple-element.26), channel_id=1, source_target_pairs={{1,0},{2,1},{3,2},{5,4},{6,5},{7,6},{9,8},{10,9},{11,10},{13,12},{... | collective-permute-start | bytes 393224 | tf_op jit(solution)/shard_map/ppermute | solution.py:10
  10.8 3.1 %collective-permute-start.3 = (f32[1,32,1024]{2,1,0:T(8,128)S(1)}, f32[1,32,1024]{2,1,0:T(8,128)S(1)}, u32[]{:S(2)}, u32[]{:S(2)}) collective-permute-start(f32[1,32,1024]{2,1,0:T(8,128)S(1)} %get-tuple-element.27), channel_id=1, source_target_pairs={{0,1},{1,2},{2,3},{4,5},{5,6},{6,7},{8,9},{9,10},{10,11},{12,13},{... | collective-permute-start | bytes 393224 | tf_op jit(solution)/shard_map/ppermute | solution.py:10
  13.9 0.0 copy-start
  13.9 0.0 copy-start.3
  14.0 0.0 copy-start.4
  14.0 3.0 %fusion.22 = (f32[8,32,1023]{2,1,0:T(8,128)S(1)}, f32[8,32,1023]{2,1,0:T(8,128)}) fusion(f32[8,32,1024]{2,1,0:T(8,128)} %param.3), kind=kLoop, calls=%fused_computation.39 | loop fusion | bytes 4190208 | tf_op jit(solution)/shard_map/jit(_roll_static)/slice | solution.py:34
  17.0 0.0 copy-done
  17.0 0.0 copy-start.2
  17.0 0.1 fusion.21
  17.1 0.0 collective-permute-done.2
  17.1 0.0 copy-done.3
  17.1 0.0 collective-permute-done.3
  17.1 0.0 copy-done.4
  17.2 0.0 collective-permute-done
  17.2 0.0 collective-permute-done.1
  17.2 1.0 %copy-done.2 = f32[8,32,1023]{2,1,0:T(8,128)S(1)} copy-done((f32[8,32,1023]{2,1,0:T(8,128)S(1)}, f32[8,32,1023]{2,1,0:T(8,128)}, u32[]{:S(2)}) %copy-start.2) | copy-done | bytes 1047576
  18.2 0.9 %multiply_reduce_fusion.1 = (f32[8]{0:T(128)S(1)}, f32[8,32,1024]{2,1,0:T(8,128)S(1)}, f32[8]{0:T(128)S(1)}) fusion(f32[8,32,1024]{2,1,0:T(8,128)S(1)} %copy-done, f32[8,32,1]{2,1,0:T(8,128)S(1)} %get-tuple-element.23, f32[8,32,1023]{2,1,0:T(8,128)S(1)} %copy-done.2, f32[8,32,1023]{2,1,0:T(8,128)S(1)} %get-tuple-element.24, ...), kind=kLoop, calls=%fused_computation.26 | loop fusion | flops 5242864 | bytes 4522048 | tf_op jit(solution)/shard_map/reduce_sum | solution.py:42
  19.1 15.4 %all-reduce = (f32[8]{0:T(128)S(1)}, f32[8]{0:T(128)S(1)}) all-reduce(f32[8]{0:T(128)S(1)} %get-tuple-element.19, f32[8]{0:T(128)S(1)} %get-tuple-element.7), channel_id=1, replica_groups=mesh['space'=8,'path'=4] {'space'}, use_global_device_ids=true, to_apply=%region_3.4 | all-reduce | flops 16 | bytes 128 | tf_op jit(solution)/shard_map/psum | solution.py:41
  34.4 0.0 copy-start.5
  34.4 0.5 copy-done.5
  35.0 0.3 broadcast_multiply_fusion
  35.2 0.0 copy-start.1
  35.3 0.2 fusion.18
  35.5 0.1 fusion.19
  35.5 0.4 fusion.16
  35.9 0.1 collective-permute-start.6
  36.0 4.1 %collective-permute-start.7 = (f32[8,1,1024]{2,1,0:T(1,128)S(1)}, f32[8,1,1024]{2,1,0:T(1,128)S(1)}, u32[]{:S(2)}, u32[]{:S(2)}) collective-permute-start(f32[8,1,1024]{2,1,0:T(1,128)S(1)} %get-tuple-element.18), channel_id=1, source_target_pairs={{4,0},{8,4},{12,8},{16,12},{20,16},{24,20},{28,24},{0,28},{5,1},{9... | collective-permute-start | bytes 98312 | tf_op jit(solution)/shard_map/ppermute | solution.py:22
  40.2 5.5 %collective-permute-start.5 = (f32[32,1024]{1,0:T(8,128)S(1)}, f32[32,1024]{1,0:T(8,128)S(1)}, u32[]{:S(2)}, u32[]{:S(2)}) collective-permute-start(f32[32,1024]{1,0:T(8,128)S(1)} %get-tuple-element.15), channel_id=1, source_target_pairs={{1,0},{2,1},{3,2},{5,4},{6,5},{7,6},{9,8},{10,9},{11,10},{13,12},{... | collective-permute-start | bytes 393224 | tf_op jit(solution)/shard_map/ppermute | solution.py:10
  45.6 3.0 %collective-permute-start.4 = (f32[32,1024]{1,0:T(8,128)S(1)}, f32[32,1024]{1,0:T(8,128)S(1)}, u32[]{:S(2)}, u32[]{:S(2)}) collective-permute-start(f32[32,1024]{1,0:T(8,128)S(1)} %get-tuple-element.16), channel_id=1, source_target_pairs={{0,1},{1,2},{2,3},{4,5},{5,6},{6,7},{8,9},{9,10},{10,11},{12,13},{... | collective-permute-start | bytes 393224 | tf_op jit(solution)/shard_map/ppermute | solution.py:10
  48.6 0.1 fusion.17
  48.7 0.0 collective-permute-done.6
  48.8 0.0 collective-permute-done.7
  48.8 0.6 %collective-permute-done.5 = f32[32,1024]{1,0:T(8,128)S(1)} collective-permute-done((f32[32,1024]{1,0:T(8,128)S(1)}, f32[32,1024]{1,0:T(8,128)S(1)}, u32[]{:S(2)}, u32[]{:S(2)}) %collective-permute-start.5) | collective-permute-done | bytes 131104 | tf_op jit(solution)/shard_map/ppermute | solution.py:10
  49.4 1.2 %collective-permute-done.4 = f32[32,1024]{1,0:T(8,128)S(1)} collective-permute-done((f32[32,1024]{1,0:T(8,128)S(1)}, f32[32,1024]{1,0:T(8,128)S(1)}, u32[]{:S(2)}, u32[]{:S(2)}) %collective-permute-start.4) | collective-permute-done | bytes 131104 | tf_op jit(solution)/shard_map/ppermute | solution.py:10
  50.6 0.0 copy-done.1
  50.6 1.8 %fusion.4 = f32[8,32,1024]{2,1,0:T(8,128)} fusion(f32[8,32,1024]{2,1,0:T(8,128)S(1)} %get-tuple-element.6, f32[8,32,1024]{2,1,0:T(8,128)S(1)} %copy-done, f32[8,1,1024]{2,1,0:T(1,128)S(1)} %collective-permute-done.7, f32[8,1,1024]{2,1,0:T(1,128)S(1)} %collective-permute-done.6, f32[7,32,1024]{2,1,0:T(8,128)S(1)} %get-tuple-element.14, ...), kind=kLoop, calls=%fused_computation.6 | loop fusion | flops 4718592 | bytes 7405568 | tf_op jit(solution)/shard_map/sub | solution.py:69
  (4 shorter events, 0.1 us)
Async XLA Ops:
  1.7 15.4 %collective-permute-start = (f32[8,1,1024]{2,1,0:T(1,128)S(1)}, f32[8,1,1024]{2,1,0:T(1,128)S(1)}, u32[]{:S(2)}, u32[]{:S(2)}) collective-permute-start(f32[8,1,1024]{2,1,0:T(1,128)S(1)} %get-tuple-element.20), channel_id=1, source_target_pairs={{0,4},{4,8},{8,12},{12,16},{16,20},{20,24},{24,28},{28,0},{1,5},{5... | collective-permute-start | bytes 98312 | tf_op jit(solution)/shard_map/ppermute | solution.py:20
  3.8 13.3 %collective-permute-start.1 = (f32[8,1,1024]{2,1,0:T(1,128)S(1)}, f32[8,1,1024]{2,1,0:T(1,128)S(1)}, u32[]{:S(2)}, u32[]{:S(2)}) collective-permute-start(f32[8,1,1024]{2,1,0:T(1,128)S(1)} %get-tuple-element.21), channel_id=1, source_target_pairs={{4,0},{8,4},{12,8},{16,12},{20,16},{24,20},{28,24},{0,28},{5,1},{9... | collective-permute-start | bytes 98312 | tf_op jit(solution)/shard_map/ppermute | solution.py:22
  7.9 9.1 %collective-permute-start.2 = (f32[1,32,1024]{2,1,0:T(8,128)S(1)}, f32[1,32,1024]{2,1,0:T(8,128)S(1)}, u32[]{:S(2)}, u32[]{:S(2)}) collective-permute-start(f32[1,32,1024]{2,1,0:T(8,128)S(1)} %get-tuple-element.26), channel_id=1, source_target_pairs={{1,0},{2,1},{3,2},{5,4},{6,5},{7,6},{9,8},{10,9},{11,10},{13,12},{... | collective-permute-start | bytes 393224 | tf_op jit(solution)/shard_map/ppermute | solution.py:10
  10.8 6.3 %collective-permute-start.3 = (f32[1,32,1024]{2,1,0:T(8,128)S(1)}, f32[1,32,1024]{2,1,0:T(8,128)S(1)}, u32[]{:S(2)}, u32[]{:S(2)}) collective-permute-start(f32[1,32,1024]{2,1,0:T(8,128)S(1)} %get-tuple-element.27), channel_id=1, source_target_pairs={{0,1},{1,2},{2,3},{4,5},{5,6},{6,7},{8,9},{9,10},{10,11},{12,13},{... | collective-permute-start | bytes 393224 | tf_op jit(solution)/shard_map/ppermute | solution.py:10
  13.9 3.0 %copy-start = (f32[8,32,1024]{2,1,0:T(8,128)S(1)}, f32[8,32,1024]{2,1,0:T(8,128)}, u32[]{:S(2)}) copy-start(f32[8,32,1024]{2,1,0:T(8,128)} %param.3) | copy-start | bytes 3145732
  13.9 3.1 %copy-start.3 = (f32[32,1024]{1,0:T(8,128)S(1)}, f32[32,1024]{1,0:T(8,128)}, u32[]{:S(2)}) copy-start(f32[32,1024]{1,0:T(8,128)} %param.5) | copy-start | bytes 393220
  14.0 3.2 %copy-start.4 = (f32[32,1024]{1,0:T(8,128)S(1)}, f32[32,1024]{1,0:T(8,128)}, u32[]{:S(2)}) copy-start(f32[32,1024]{1,0:T(8,128)} %param.4) | copy-start | bytes 393220
  17.0 1.2 %copy-start.2 = (f32[8,32,1023]{2,1,0:T(8,128)S(1)}, f32[8,32,1023]{2,1,0:T(8,128)}, u32[]{:S(2)}) copy-start(f32[8,32,1023]{2,1,0:T(8,128)} %get-tuple-element.25) | copy-start | bytes 3142660
  34.4 0.5 copy-start.5
  35.2 15.3 %copy-start.1 = (f32[8,32,1024]{2,1,0:T(8,128)}, f32[8,32,1024]{2,1,0:T(8,128)S(1)}, u32[]{:S(2)}) copy-start(f32[8,32,1024]{2,1,0:T(8,128)S(1)} %get-tuple-element.6) | copy-start | bytes 3145732
  35.9 12.8 %collective-permute-start.6 = (f32[8,1,1024]{2,1,0:T(1,128)S(1)}, f32[8,1,1024]{2,1,0:T(1,128)S(1)}, u32[]{:S(2)}, u32[]{:S(2)}) collective-permute-start(f32[8,1,1024]{2,1,0:T(1,128)S(1)} %get-tuple-element.17), channel_id=1, source_target_pairs={{0,4},{4,8},{8,12},{12,16},{16,20},{20,24},{24,28},{28,0},{1,5},{5... | collective-permute-start | bytes 98312 | tf_op jit(solution)/shard_map/ppermute | solution.py:20
  36.0 12.8 %collective-permute-start.7 = (f32[8,1,1024]{2,1,0:T(1,128)S(1)}, f32[8,1,1024]{2,1,0:T(1,128)S(1)}, u32[]{:S(2)}, u32[]{:S(2)}) collective-permute-start(f32[8,1,1024]{2,1,0:T(1,128)S(1)} %get-tuple-element.18), channel_id=1, source_target_pairs={{4,0},{8,4},{12,8},{16,12},{20,16},{24,20},{28,24},{0,28},{5,1},{9... | collective-permute-start | bytes 98312 | tf_op jit(solution)/shard_map/ppermute | solution.py:22
  40.2 9.2 %collective-permute-start.5 = (f32[32,1024]{1,0:T(8,128)S(1)}, f32[32,1024]{1,0:T(8,128)S(1)}, u32[]{:S(2)}, u32[]{:S(2)}) collective-permute-start(f32[32,1024]{1,0:T(8,128)S(1)} %get-tuple-element.15), channel_id=1, source_target_pairs={{1,0},{2,1},{3,2},{5,4},{6,5},{7,6},{9,8},{10,9},{11,10},{13,12},{... | collective-permute-start | bytes 393224 | tf_op jit(solution)/shard_map/ppermute | solution.py:10
  45.6 5.0 %collective-permute-start.4 = (f32[32,1024]{1,0:T(8,128)S(1)}, f32[32,1024]{1,0:T(8,128)S(1)}, u32[]{:S(2)}, u32[]{:S(2)}) collective-permute-start(f32[32,1024]{1,0:T(8,128)S(1)} %get-tuple-element.16), channel_id=1, source_target_pairs={{0,1},{1,2},{2,3},{4,5},{5,6},{6,7},{8,9},{9,10},{10,11},{12,13},{... | collective-permute-start | bytes 393224 | tf_op jit(solution)/shard_map/ppermute | solution.py:10
where the time goes:
time: 52.7 us; the launch traced here: 52.4 us
  starting transfers between devices  23.9 us (45%)
  blocking collectives  15.4 us (29%)
  local copies, waits for them, and re-layouts  7.45 us (14%)
  other arithmetic  3.01 us (6%)
  waiting for transfers between devices  1.82 us (3%)
  between operations  0.85 us (2%)
    psum x1, blocking collectives, slice_ratio(): lax.psum((jnp.sum(drift * drift, axis=(1, 2)), jnp.sum(tangent * tangent,...  15.4 us
    ppermute x4, starting transfers between devices, shifted(): return lax.ppermute(block, axis, route)  14.5 us
    ppermute x2, starting transfers between devices, extended_2(): lax.ppermute(head, axis, [((i + 1) % count, i) for i in range(count)])  7.25 us
    slice x2, local copies, waits for them, and re-layouts, laplace_rows(): jnp.roll(center, 1, 2)  3.08 us
    ppermute x2, starting transfers between devices, extended_2(): lax.ppermute(tail, axis, [(i, (i + 1) % count) for i in range(count)])  2.18 us
    ppermute x4, waiting for transfers between devices, shifted(): return lax.ppermute(block, axis, route)  1.81 us
    sub x1, other arithmetic, body(): scaled_below - scaled_above  1.8 us
    unnamed x12, local copies, waits for them, and re-layouts  1.54 us
  transfers between devices with their start and end apart: 8, of which 2 were waited for; matrix products, arithmetic and copies ran while one was open for 8% of the time, Pallas kernels for 0%

commit v1 on v0

v1 whole, which is shorter than its diff:
```python
import functools

import jax
import jax.numpy as jnp
from jax import lax
from jax.experimental import pallas as pl
from jax.experimental.pallas import tpu as pltpu
from jax.sharding import PartitionSpec as P

F32 = jnp.float32
LANES = 128
TILE = 8
EPS = 1e-06
VMEM = pl.BlockSpec(memory_space=pltpu.VMEM)
ANY = pl.BlockSpec(memory_space=pl.ANY)
SUMS = 1


def lanes_sum(x):
    parts = [x[:, i : i + LANES] for i in range(0, x.shape[1], LANES)]
    while len(parts) > 1:
        parts = [a + b for a, b in zip(parts[::2], parts[1::2])] + parts[len(parts) & ~1 :]
    return parts[0]


def sides(x):
    cols = x.shape[1]
    return pltpu.roll(x, 1, 1) + pltpu.roll(x, cols - 1, 1)


def iota(shape, dim):
    return lax.broadcasted_iota(jnp.int32, shape, dim)


def edge_kernel(f_ref, up_ref, tail_ref, head_ref, buf, sem):
    count, rows, _ = f_ref.shape
    copies = [
        pltpu.make_async_copy(f_ref.at[pl.ds(count - 2, 2)], up_ref, sem.at[0]),
        pltpu.make_async_copy(f_ref.at[:, pl.ds(rows - TILE, TILE)], buf.at[0], sem.at[1]),
        pltpu.make_async_copy(f_ref.at[:, pl.ds(0, TILE)], buf.at[1], sem.at[2]),
    ]
    for copy in copies:
        copy.start()
    copies[1].wait()
    for s in range(count):
        for r in range(2):
            tail_ref[r, s : s + 1, :] = buf[0, s, TILE - 2 + r : TILE - 1 + r, :]
    copies[2].wait()
    for s in range(count):
        for r in range(2):
            head_ref[r, s : s + 1, :] = buf[1, s, r : r + 1, :]
    copies[0].wait()


def edges(f):
    count, rows, cols = f.shape
    pair = jax.ShapeDtypeStruct((2, rows, cols), F32)
    strip = jax.ShapeDtypeStruct((2, count, cols), F32)
    return pl.pallas_call(
        edge_kernel,
        out_shape=(pair, strip, strip),
        in_specs=[ANY],
        out_specs=(VMEM, VMEM, VMEM),
        scratch_shapes=[pltpu.VMEM((2, count, TILE, cols), F32), pltpu.SemaphoreType.DMA((3,))],
        name="edges",
    )(f)


def interior_kernel(f_ref, part_ref):
    count, rows, cols = f_ref.shape
    tiles = rows // TILE
    row = iota((TILE, cols), 0)
    part_ref[...] = jnp.zeros_like(part_ref)

    def drift_sum(s, _):
        total = jnp.zeros((TILE, LANES), F32)
        for k in range(tiles):
            c = f_ref[s, pl.ds(TILE * k, TILE), :]
            up = f_ref[s, pl.ds(TILE * k - 1, TILE), :] if k > 0 else pltpu.roll(c, 1, 0)
            dn = f_ref[s, pl.ds(TILE * k + 1, TILE), :] if k < tiles - 1 else pltpu.roll(c, TILE - 1, 0)
            drift = up + dn + sides(c) - 3.0 * c - c * c * c
            if k == 0:
                drift = jnp.where(row == 0, 0.0, drift)
            if k == tiles - 1:
                drift = jnp.where(row == TILE - 1, 0.0, drift)
            total += lanes_sum(drift * drift)
        part_ref[pl.ds(s, 1), :] = jnp.sum(total, axis=0, keepdims=True)
        return 0

    def tangent_sum(s, _):
        total = jnp.zeros((TILE, LANES), F32)
        for k in range(tiles):
            tangent = f_ref[s + 1, pl.ds(TILE * k, TILE), :] - f_ref[s - 1, pl.ds(TILE * k, TILE), :]
            total += lanes_sum(tangent * tangent)
        part_ref[pl.ds(count + s + 1, 1), :] = jnp.sum(total, axis=0, keepdims=True)
        return 0

    lax.fori_loop(0, count, drift_sum, 0)
    lax.fori_loop(1, count - 1, tangent_sum, 0)


def interior(f):
    count, rows, cols = f.shape
    return pl.pallas_call(
        interior_kernel,
        out_shape=jax.ShapeDtypeStruct((2 * count + TILE, LANES), F32),
        in_specs=[VMEM],
        out_specs=VMEM,
        cost_estimate=pl.CostEstimate(flops=20 * count * rows * cols, transcendentals=0, bytes_accessed=4 * count * rows * cols),
        name="interior",
    )(f)


def chunk_kernel(m, n, chunk, f_ref, below_ref, above_ref, tail_ref, head_ref, start_ref, end_ref, part_ref, out_ref):
    count, rows, cols = f_ref.shape
    tiles = rows // TILE
    path = lax.axis_index("path")
    space = lax.axis_index("space")
    first = path == 0
    last = path == m - 1

    r0, r1 = tail_ref[0], tail_ref[1]
    r2, r3 = head_ref[0], head_ref[1]
    drift_a = r0 + r2 + sides(r1) - 3.0 * r1 - r1 * r1 * r1
    drift_b = r1 + r3 + sides(r2) - 3.0 * r2 - r2 * r2 * r2
    drift = part_ref[0:count, :] + lanes_sum(drift_a * drift_a) + lanes_sum(drift_b * drift_b)

    totals = [jnp.zeros((TILE, LANES), F32) for _ in range(3)]
    for k in range(tiles):
        at = pl.ds(TILE * k, TILE)
        prior = jnp.where(first, start_ref[at, :], below_ref[1, at, :])
        tangents = (
            f_ref[0, at, :] - below_ref[0, at, :],
            f_ref[1, at, :] - prior,
            jnp.where(last, end_ref[at, :] - f_ref[count - 2, at, :], 0.0),
        )
        totals = [a + lanes_sum(t * t) for a, t in zip(totals, tangents)]
    sums = [jnp.sum(a, axis=0, keepdims=True) for a in totals]
    sub = iota((TILE, LANES), 0)
    tan_a = part_ref[count : count + TILE, :]
    tan_a = jnp.where(sub == 0, sums[0], jnp.where(sub == 1, sums[1], tan_a))

    lane = iota((TILE, LANES), 1)
    spread = jnp.where(lane == sub, jnp.sum(drift, axis=1, keepdims=True), 0.0)
    spread += jnp.where(lane == sub + count, jnp.sum(tan_a, axis=1, keepdims=True), 0.0)
    line = jnp.sum(spread, axis=0, keepdims=True)
    tan_last = jnp.sum(sums[2], axis=1, keepdims=True)
    line += jnp.where(lane[0:1] == 2 * count, tan_last, 0.0)

    for j in range(m * n):
        out_ref[chunk * j : chunk * j + SUMS, :] = line
    right = lax.rem(space + 1, n) * m
    left = lax.rem(space + n - 1, n) * m

    def put(base, source):
        for i in range(cols // LANES):
            out_ref[pl.ds(base * chunk + SUMS + i, 1), :] = source[:, i * LANES : (i + 1) * LANES]

    @pl.when(jnp.logical_not(first))
    def _():
        put(right + path - 1, f_ref[0, rows - 1 : rows, :])
        put(left + path - 1, f_ref[0, 0:1, :])

    @pl.when(jnp.logical_not(last))
    def _():
        put(right + path + 1, f_ref[count - 1, rows - 1 : rows, :])
        put(left + path + 1, f_ref[count - 1, 0:1, :])

    @pl.when(first)
    def _():
        put(right + path, start_ref[rows - 1 : rows, :])
        put(left + path, start_ref[0:1, :])

    @pl.when(last)
    def _():
        put(right + path, end_ref[rows - 1 : rows, :])
        put(left + path, end_ref[0:1, :])


def chunks(m, n, f, below, tail_in, head, start, end, part):
    chunk = SUMS + f.shape[2] // LANES
    return pl.pallas_call(
        functools.partial(chunk_kernel, m, n, chunk),
        out_shape=jax.ShapeDtypeStruct((m * n * chunk, LANES), F32),
        in_specs=[VMEM] * 8,
        out_specs=VMEM,
        name="chunks",
    )(f, below, below, tail_in, head, start, end, part)


def final_kernel(
    m, n, chunk, got_ref, f_ref, below_ref, above_ref, tail_ref, head_ref, start_ref, end_ref,
    ratio_ref, res_out, grad_out, field, resid, scale, rowbuf, sem,
):
    count, rows, cols = f_ref.shape
    tiles = rows // TILE
    path = lax.axis_index("path")
    space = lax.axis_index("space")
    first = path == 0
    last = path == m - 1
    path_lo = jnp.where(first, path, path - 1)
    path_hi = jnp.where(last, path, path + 1)

    def gathered(p):
        total = got_ref[pl.ds(p * chunk, 1), :]
        for i in range(1, n):
            total += got_ref[pl.ds((i * m + p) * chunk, 1), :]
        return jnp.broadcast_to(total, (TILE, LANES))

    mine = gathered(path)
    lower = gathered(path_lo)
    upper = gathered(path_hi)
    lane = iota((TILE, LANES), 1)
    sub = iota((TILE, LANES), 0)

    def shift(x, k):
        return pltpu.roll(x, k % LANES, 1)

    drift_sq = jnp.where(lane == 0, shift(lower, 1 - count), jnp.where(lane <= count, shift(mine, 1), shift(upper, count + 1)))
    at_end = shift(mine, -count) + jnp.where(last, 0.0, upper)
    tangent_sq = jnp.where(lane < count, shift(mine, -count), jnp.where(lane == count, at_end, upper))
    ratio = jnp.sqrt(drift_sq + EPS) / jnp.sqrt(tangent_sq + EPS)
    ratio = jnp.where((lane == 0) & first, 0.0, ratio)
    ratio = jnp.where((lane == count + 1) & last, 0.0, ratio)
    ratio_ref[...] = shift(ratio, -1)[0, 0:count]
    for s in range(count + 2):
        splat = jnp.sum(jnp.where(lane == s, ratio, 0.0), axis=1, keepdims=True)
        scale[s] = jnp.broadcast_to(splat, (TILE, LANES))
    column = jnp.sum(jnp.where(lane == sub + 1, ratio, 0.0), axis=1, keepdims=True)

    for k in range(tiles):
        src = pl.ds(TILE * k, TILE)
        dst = pl.ds(TILE * (k + 1), TILE)
        field[0, dst, :] = below_ref[0, src, :]
        field[1, dst, :] = jnp.where(first, start_ref[src, :], below_ref[1, src, :])
        field[count + 2, dst, :] = jnp.where(last, end_ref[src, :], above_ref[0, src, :])
        field[count + 3, dst, :] = above_ref[1, src, :]

    def copy_in(s, _):
        for k in range(tiles):
            field[s + 2, pl.ds(TILE * (k + 1), TILE), :] = f_ref[s, pl.ds(TILE * k, TILE), :]
        field[s + 2, pl.ds(TILE - 1, 1), :] = tail_ref[1, pl.ds(s, 1), :]
        field[s + 2, pl.ds(TILE + rows, 1), :] = head_ref[0, pl.ds(s, 1), :]
        return 0

    lax.fori_loop(0, count, copy_in, 0)

    def corner(slot, at, source):
        for i in range(cols // LANES):
            value = got_ref[pl.ds(source * chunk + SUMS + i, 1), :]
            field[slot, pl.ds(at, 1), i * LANES : (i + 1) * LANES] = value

    prev = lax.rem(space + n - 1, n) * m
    nxt = lax.rem(space + 1, n) * m
    corner(1, TILE - 1, prev + path_lo)
    corner(1, TILE + rows, nxt + path_lo)
    corner(count + 2, TILE - 1, prev + path_hi)
    corner(count + 2, TILE + rows, nxt + path_hi)

    def edge_residual(outer, mid, inner, at):
        below = field[1, at : at + 1, :]
        above = field[count + 2, at : at + 1, :]
        subs = iota(mid.shape, 0)
        ahead = jnp.where(subs == count - 1, above, pltpu.roll(mid, count - 1, 0))
        behind = jnp.where(subs == 0, below, pltpu.roll(mid, 1, 0))
        drift = outer + inner + sides(mid) - 3.0 * mid - mid * mid * mid
        return column * (ahead - behind) - drift

    for s in range(count):
        rowbuf[0, s : s + 1, :] = f_ref[s, 0:1, :]
        rowbuf[1, s : s + 1, :] = f_ref[s, rows - 1 : rows, :]
    top = edge_residual(tail_ref[0], tail_ref[1], rowbuf[0], TILE - 1)
    bottom = edge_residual(head_ref[1], head_ref[0], rowbuf[1], TILE + rows)
    for s in range(count):
        resid[s + 1, TILE - 1 : TILE, :] = top[s : s + 1, :]
        resid[s + 1, TILE + rows : TILE + rows + 1, :] = bottom[s : s + 1, :]

    def widen(x):
        return jnp.concatenate([x] * (cols // LANES), axis=1)

    def residual_of(t, _):
        r = widen(scale[t])
        for k in range(tiles):
            base = TILE * (k + 1)
            c = field[t + 1, pl.ds(base, TILE), :]
            drift = field[t + 1, pl.ds(base - 1, TILE), :] + field[t + 1, pl.ds(base + 1, TILE), :] + sides(c) - 3.0 * c - c * c * c
            tangent = field[t + 2, pl.ds(base, TILE), :] - field[t, pl.ds(base, TILE), :]
            resid[t, pl.ds(base, TILE), :] = r * tangent - drift
        return 0

    lax.fori_loop(0, count + 2, residual_of, 0)
    res_copy = pltpu.make_async_copy(resid.at[pl.ds(1, count), pl.ds(TILE, rows)], res_out, sem.at[0])
    res_copy.start()

    def gradient_of(s, _):
        lo = widen(scale[s])
        hi = widen(scale[s + 2])
        for k in range(tiles):
            base = TILE * (k + 1)
            c = field[s + 2, pl.ds(base, TILE), :]
            r = resid[s + 1, pl.ds(base, TILE), :]
            lap = resid[s + 1, pl.ds(base - 1, TILE), :] + resid[s + 1, pl.ds(base + 1, TILE), :] + sides(r)
            out = lo * resid[s, pl.ds(base, TILE), :] - hi * resid[s + 2, pl.ds(base, TILE), :]
            field[s, pl.ds(base, TILE), :] = out - (lap - (3.0 + 3.0 * c * c) * r)
        return 0

    lax.fori_loop(0, count, gradient_of, 0)
    grad_copy = pltpu.make_async_copy(field.at[pl.ds(0, count), pl.ds(TILE, rows)], grad_out, sem.at[1])
    grad_copy.start()
    res_copy.wait()
    grad_copy.wait()


def final(m, n, got, f, below, above, tail_in, head_in, start, end):
    count, rows, cols = f.shape
    chunk = SUMS + cols // LANES
    big = jax.ShapeDtypeStruct(f.shape, F32)
    return pl.pallas_call(
        functools.partial(final_kernel, m, n, chunk),
        out_shape=(jax.ShapeDtypeStruct((count,), F32), big, big),
        in_specs=[VMEM] * 8,
        out_specs=(VMEM, ANY, ANY),
        scratch_shapes=[
            pltpu.VMEM((count + 4, rows + 2 * TILE, cols), F32),
            pltpu.VMEM((count + 2, rows + 2 * TILE, cols), F32),
            pltpu.VMEM((count + 2, TILE, LANES), F32),
            pltpu.VMEM((2, count, cols), F32),
            pltpu.SemaphoreType.DMA((2,)),
        ],
        name="final",
    )(got, f, below, above, tail_in, head_in, start, end)


def body(m, n, f, start, end):
    count = f.shape[0]
    up, tail, head = edges(f)
    tail_in = lax.ppermute(tail, "space", [(i, (i + 1) % n) for i in range(n)])
    below = lax.ppermute(up, "path", [(i, i + 1) for i in range(m - 1)])
    part = interior(f)
    send = chunks(m, n, f, below, tail_in, head, start, end, part)
    got = lax.all_to_all(send, ("space", "path"), 0, 0, tiled=True)
    down, head_out, send = lax.optimization_barrier((f[0:2], head, send))
    above = lax.ppermute(down, "path", [(i + 1, i) for i in range(m - 1)])
    head_in = lax.ppermute(head_out, "space", [((i + 1) % n, i) for i in range(n)])
    return final(m, n, got, f, below, above, tail_in, head_in, start, end)


def solution(mesh):
    m, n = mesh.shape["path"], mesh.shape["space"]
    in_specs = (P("path", "space", None), P("space", None), P("space", None))
    out_specs = (P("path"), P("path", "space", None), P("path", "space", None))
    return jax.shard_map(
        functools.partial(body, m, n), mesh=mesh, in_specs=in_specs, out_specs=out_specs, check_vma=False
    )
```

time: 52.7 us -> 41.7 us (0.79)
  the two profiles are of different devices: /device:TPU:1 before, /device:TPU:0 now
where the time goes in v1:
time: 41.7 us; the launch traced here: 41.3 us
  starting transfers between devices  15.6 us (37%)
  Pallas kernels  13.9 us (33%)
  waiting for transfers between devices  5.83 us (14%)
  local copies, waits for them, and re-layouts  5.36 us (13%)
  between operations  0.69 us (2%)
    pallas_call x1, Pallas kernels, final(): pl.pallas_call(functools.partial(final_kernel, m, n, chunk), out_shape=(j...  6.25 us
    all_to_all x1, starting transfers between devices, body(): got = lax.all_to_all(send, ('space', 'path'), 0, 0, tiled=True)  4.89 us
    ppermute x1, starting transfers between devices, body(): lax.ppermute(head_out, 'space', [((i + 1) % n, i) for i in range(n)])  4.6 us
    all_to_all x1, waiting for transfers between devices, body(): got = lax.all_to_all(send, ('space', 'path'), 0, 0, tiled=True)  3.67 us
    pallas_call x1, Pallas kernels, interior(): pl.pallas_call(interior_kernel, out_shape=jax.ShapeDtypeStruct((2 * count...  3.34 us
    ppermute x1, starting transfers between devices, body(): tail_in = lax.ppermute(tail, 'space', [(i, (i + 1) % n) for i in range(n)])  2.4 us
    pallas_call x1, Pallas kernels, chunks(): pl.pallas_call(functools.partial(chunk_kernel, m, n, chunk), out_shape=ja...  2.38 us
    ppermute x1, starting transfers between devices, body(): below = lax.ppermute(up, 'path', [(i, i + 1) for i in range(m - 1)])  2.37 us
  transfers between devices with their start and end apart: 5, of which 2 were waited for; matrix products, arithmetic and copies ran while one was open for 2% of the time, Pallas kernels for 8%

profile of v1, /device:TPU:0, one launch (start us, length us, event | category | flops | bytes accessed | tf_op | source)
XLA Modules:
  0.0 41.3 jit_solution(15464580585818884718)
XLA Ops:
  0.6 1.9 %edges.1 = (f32[2,32,1024]{2,1,0:T(8,128)}, f32[2,8,1024]{2,1,0:T(8,128)}, f32[2,8,1024]{2,1,0:T(8,128)}) custom-call(f32[8,32,1024]{2,1,0:T(8,128)} %f_ref.7), custom_call_target="tpu_custom_call" | custom-call | tf_op jit(solution)/shard_map/edges/pallas_call | solution.py:59
  2.5 2.4 %collective-permute-start = (f32[2,32,1024]{2,1,0:T(8,128)}, f32[2,32,1024]{2,1,0:T(8,128)S(1)}, u32[]{:S(2)}, u32[]{:S(2)}) collective-permute-start(f32[2,32,1024]{2,1,0:T(8,128)} %get-tuple-element.8), channel_id=1, source_target_pairs={{0,1},{1,2},{2,3},{4,5},{5,6},{6,7},{8,9},{9,10},{10,11},{12,13},{... | collective-permute-start | bytes 786440 | tf_op jit(solution)/shard_map/ppermute | solution.py:338
  4.9 2.4 %collective-permute-start.1 = (f32[2,8,1024]{2,1,0:T(8,128)}, f32[2,8,1024]{2,1,0:T(8,128)S(1)}, u32[]{:S(2)}, u32[]{:S(2)}) collective-permute-start(f32[2,8,1024]{2,1,0:T(8,128)} %get-tuple-element.9), channel_id=1, source_target_pairs={{0,4},{4,8},{8,12},{12,16},{16,20},{20,24},{24,28},{28,0},{1,5},{5... | collective-permute-start | bytes 196616 | tf_op jit(solution)/shard_map/ppermute | solution.py:337
  7.3 3.3 %interior.1.part_ref = f32[24,128]{1,0:T(8,128)} custom-call(f32[8,32,1024]{2,1,0:T(8,128)} %f_ref.7), custom_call_target="tpu_custom_call" | custom-call | flops 5242880 | bytes 1048576 | tf_op jit(solution)/shard_map/interior/pallas_call | solution.py:104
  10.6 2.1 %collective-permute-done.1.tail_ref = f32[2,8,1024]{2,1,0:T(8,128)S(1)} collective-permute-done((f32[2,8,1024]{2,1,0:T(8,128)}, f32[2,8,1024]{2,1,0:T(8,128)S(1)}, u32[]{:S(2)}, u32[]{:S(2)}) %collective-permute-start.1) | collective-permute-done | bytes 65568 | tf_op jit(solution)/shard_map/ppermute | solution.py:337
  12.8 0.0 copy-start.1
  12.8 0.0 collective-permute-done.below_ref.above_ref
  12.8 0.0 copy-start
  12.8 0.6 %copy-done.1 = f32[2,8,1024]{2,1,0:T(8,128)} copy-done((f32[2,8,1024]{2,1,0:T(8,128)}, f32[2,8,1024]{2,1,0:T(8,128)S(1)}, u32[]{:S(2)}) %copy-start.1) | copy-done | bytes 65560
  13.4 0.1 copy-done
  13.5 2.4 %chunks.1 = f32[288,128]{1,0:T(8,128)} custom-call(f32[8,32,1024]{2,1,0:T(8,128)} %f_ref.7, f32[2,32,1024]{2,1,0:T(8,128)} %copy-done, f32[2,32,1024]{2,1,0:T(8,128)} %copy-done, f32[2,8,1024]{2,1,0:T(8,128)} %copy-done.1, f32[2,8,1024]{2,1,0:T(8,128)} %get-tuple-element.12.head_ref, f32[32,1024]{1,0:T(8,128)} %start_ref.3, f32[32,1024]{1,0:T(8,128)} %end_ref.3, ...), custom_call_target="tpu_custom_call" | custom-call | tf_op jit(solution)/shard_map/chunks/pallas_call | solution.py:182
  15.9 1.6 %all_to_all.7 = f32[32,9,128]{2,1,0:T(8,128)} reshape(f32[288,128]{1,0:T(8,128)} %chunks.1) | data formatting | bytes 294912 | tf_op jit(solution)/shard_map/all_to_all | solution.py:341
  17.5 4.9 %all-to-all-start = ((f32[32,9,128]{2,1,0:T(8,128)}), f32[32,9,128]{2,1,0:T(8,128)S(1)}, u32[]{:S(2)}, u32[]{:S(2)}) async-start(f32[32,9,128]{2,1,0:T(8,128)} %all_to_all.7), calls=%async_computation | async-start | bytes 524288 | tf_op jit(solution)/shard_map/all_to_all | solution.py:341
  22.4 0.0 copy-start.3
  22.4 1.0 %slice.3 = f32[2,32,1024]{2,1,0:T(8,128)S(1)} slice(f32[8,32,1024]{2,1,0:T(8,128)} %f_ref.7), slice={[0:2], [0:32], [0:1024]} | slice | bytes 524288 | tf_op jit(solution)/shard_map/slice | solution.py:342
  23.5 1.3 %collective-permute-start.2 = (f32[2,32,1024]{2,1,0:T(8,128)S(1)}, f32[2,32,1024]{2,1,0:T(8,128)S(1)}, u32[]{:S(2)}, u32[]{:S(2)}) collective-permute-start(f32[2,32,1024]{2,1,0:T(8,128)S(1)} %slice.3), channel_id=1, source_target_pairs={{1,0},{2,1},{3,2},{5,4},{6,5},{7,6},{9,8},{10,9},{11,10},{13,12},{... | collective-permute-start | bytes 786440 | tf_op jit(solution)/shard_map/ppermute | solution.py:343
  24.8 0.0 copy-done.3
  24.8 4.6 %collective-permute-start.3 = (f32[2,8,1024]{2,1,0:T(8,128)S(1)}, f32[2,8,1024]{2,1,0:T(8,128)S(1)}, u32[]{:S(2)}, u32[]{:S(2)}) collective-permute-start(f32[2,8,1024]{2,1,0:T(8,128)S(1)} %copy-done.3), channel_id=1, source_target_pairs={{4,0},{8,4},{12,8},{16,12},{20,16},{24,20},{28,24},{0,28},{5,1},{9... | collective-permute-start | bytes 196616 | tf_op jit(solution)/shard_map/ppermute | solution.py:344
  29.4 3.7 %all-to-all-done = f32[32,9,128]{2,1,0:T(8,128)S(1)} async-done(((f32[32,9,128]{2,1,0:T(8,128)}), f32[32,9,128]{2,1,0:T(8,128)S(1)}, u32[]{:S(2)}, u32[]{:S(2)}) %all-to-all-start) | async-done | bytes 147488 | tf_op jit(solution)/shard_map/all_to_all | solution.py:341
  33.0 0.7 %all_to_all.9.got_ref = f32[288,128]{1,0:T(8,128)} reshape(f32[32,9,128]{2,1,0:T(8,128)S(1)} %all-to-all-done) | data formatting | bytes 294912 | tf_op jit(solution)/shard_map/all_to_all | solution.py:341
  33.7 0.0 collective-permute-done.3.head_ref
  33.7 0.0 copy-start.4
  33.7 0.0 collective-permute-done.2.above_ref
  33.7 0.6 %copy-done.4 = f32[2,8,1024]{2,1,0:T(8,128)} copy-done((f32[2,8,1024]{2,1,0:T(8,128)}, f32[2,8,1024]{2,1,0:T(8,128)S(1)}, u32[]{:S(2)}) %copy-start.4) | copy-done | bytes 65560
  34.3 0.0 copy-start.2
  34.3 0.7 %copy-done.2 = f32[2,32,1024]{2,1,0:T(8,128)} copy-done((f32[2,32,1024]{2,1,0:T(8,128)}, f32[2,32,1024]{2,1,0:T(8,128)S(1)}, u32[]{:S(2)}) %copy-start.2) | copy-done | bytes 262168
  35.0 6.3 %final.1 = (f32[8]{0:T(128)}, f32[8,32,1024]{2,1,0:T(8,128)}, f32[8,32,1024]{2,1,0:T(8,128)}) custom-call(f32[288,128]{1,0:T(8,128)} %all_to_all.9.got_ref, f32[8,32,1024]{2,1,0:T(8,128)} %f_ref.7, f32[2,32,1024]{2,1,0:T(8,128)} %copy-done, f32[2,32,1024]{2,1,0:T(8,128)} %copy-done.2, f32[2,8,1024]{2,1,0:T(8,128)} %copy-done.1, f32[2,8,1024]{2,1,0:T(8,128)} %copy-done.4, ...), custom_call_target="tpu_custom_call" | custom-call | tf_op jit(solution)/shard_map/final/pallas_call | solution.py:318
Async XLA Ops:
  2.5 10.3 %collective-permute-start = (f32[2,32,1024]{2,1,0:T(8,128)}, f32[2,32,1024]{2,1,0:T(8,128)S(1)}, u32[]{:S(2)}, u32[]{:S(2)}) collective-permute-start(f32[2,32,1024]{2,1,0:T(8,128)} %get-tuple-element.8), channel_id=1, source_target_pairs={{0,1},{1,2},{2,3},{4,5},{5,6},{6,7},{8,9},{9,10},{10,11},{12,13},{... | collective-permute-start | bytes 786440 | tf_op jit(solution)/shard_map/ppermute | solution.py:338
  4.9 7.9 %collective-permute-start.1 = (f32[2,8,1024]{2,1,0:T(8,128)}, f32[2,8,1024]{2,1,0:T(8,128)S(1)}, u32[]{:S(2)}, u32[]{:S(2)}) collective-permute-start(f32[2,8,1024]{2,1,0:T(8,128)} %get-tuple-element.9), channel_id=1, source_target_pairs={{0,4},{4,8},{8,12},{12,16},{16,20},{20,24},{24,28},{28,0},{1,5},{5... | collective-permute-start | bytes 196616 | tf_op jit(solution)/shard_map/ppermute | solution.py:337
  12.8 0.6 %copy-start.1 = (f32[2,8,1024]{2,1,0:T(8,128)}, f32[2,8,1024]{2,1,0:T(8,128)S(1)}, u32[]{:S(2)}) copy-start(f32[2,8,1024]{2,1,0:T(8,128)S(1)} %collective-permute-done.1.tail_ref) | copy-start | bytes 196612
  12.8 0.7 %copy-start = (f32[2,32,1024]{2,1,0:T(8,128)}, f32[2,32,1024]{2,1,0:T(8,128)S(1)}, u32[]{:S(2)}) copy-start(f32[2,32,1024]{2,1,0:T(8,128)S(1)} %collective-permute-done.below_ref.above_ref) | copy-start | bytes 786436
  17.5 15.5 %all-to-all-start = ((f32[32,9,128]{2,1,0:T(8,128)}), f32[32,9,128]{2,1,0:T(8,128)S(1)}, u32[]{:S(2)}, u32[]{:S(2)}) async-start(f32[32,9,128]{2,1,0:T(8,128)} %all_to_all.7), calls=%async_computation | async-start | bytes 524288 | tf_op jit(solution)/shard_map/all_to_all | solution.py:341
  22.4 2.3 %copy-start.3 = (f32[2,8,1024]{2,1,0:T(8,128)S(1)}, f32[2,8,1024]{2,1,0:T(8,128)}, u32[]{:S(2)}) copy-start(f32[2,8,1024]{2,1,0:T(8,128)} %get-tuple-element.12.head_ref) | copy-start | bytes 196612
  23.5 10.3 %collective-permute-start.2 = (f32[2,32,1024]{2,1,0:T(8,128)S(1)}, f32[2,32,1024]{2,1,0:T(8,128)S(1)}, u32[]{:S(2)}, u32[]{:S(2)}) collective-permute-start(f32[2,32,1024]{2,1,0:T(8,128)S(1)} %slice.3), channel_id=1, source_target_pairs={{1,0},{2,1},{3,2},{5,4},{6,5},{7,6},{9,8},{10,9},{11,10},{13,12},{... | collective-permute-start | bytes 786440 | tf_op jit(solution)/shard_map/ppermute | solution.py:343
  24.8 8.9 %collective-permute-start.3 = (f32[2,8,1024]{2,1,0:T(8,128)S(1)}, f32[2,8,1024]{2,1,0:T(8,128)S(1)}, u32[]{:S(2)}, u32[]{:S(2)}) collective-permute-start(f32[2,8,1024]{2,1,0:T(8,128)S(1)} %copy-done.3), channel_id=1, source_target_pairs={{4,0},{8,4},{12,8},{16,12},{20,16},{24,20},{28,24},{0,28},{5,1},{9... | collective-permute-start | bytes 196616 | tf_op jit(solution)/shard_map/ppermute | solution.py:344
  33.7 0.6 %copy-start.4 = (f32[2,8,1024]{2,1,0:T(8,128)}, f32[2,8,1024]{2,1,0:T(8,128)S(1)}, u32[]{:S(2)}) copy-start(f32[2,8,1024]{2,1,0:T(8,128)S(1)} %collective-permute-done.3.head_ref) | copy-start | bytes 196612
  34.3 0.7 %copy-start.2 = (f32[2,32,1024]{2,1,0:T(8,128)}, f32[2,32,1024]{2,1,0:T(8,128)S(1)}, u32[]{:S(2)}) copy-start(f32[2,32,1024]{2,1,0:T(8,128)S(1)} %collective-permute-done.2.above_ref) | copy-start | bytes 786436

commit v2 on v1

--- a/solution.py
+++ b/solution.py
@@ -13,7 +13,7 @@
 EPS = 1e-06
 VMEM = pl.BlockSpec(memory_space=pltpu.VMEM)
 ANY = pl.BlockSpec(memory_space=pl.ANY)
-SUMS = 1
+PARAMS = pltpu.CompilerParams(vmem_limit_bytes=16 * 2**20)
 
 
 def lanes_sum(x):
@@ -32,24 +32,15 @@
     return lax.broadcasted_iota(jnp.int32, shape, dim)
 
 
-def edge_kernel(f_ref, up_ref, tail_ref, head_ref, buf, sem):
+def edge_kernel(f_ref, up_ref, down_ref, tail_ref, head_ref):
     count, rows, _ = f_ref.shape
-    copies = [
-        pltpu.make_async_copy(f_ref.at[pl.ds(count - 2, 2)], up_ref, sem.at[0]),
-        pltpu.make_async_copy(f_ref.at[:, pl.ds(rows - TILE, TILE)], buf.at[0], sem.at[1]),
-        pltpu.make_async_copy(f_ref.at[:, pl.ds(0, TILE)], buf.at[1], sem.at[2]),
-    ]
-    for copy in copies:
-        copy.start()
-    copies[1].wait()
     for s in range(count):
         for r in range(2):
-            tail_ref[r, s : s + 1, :] = buf[0, s, TILE - 2 + r : TILE - 1 + r, :]
-    copies[2].wait()
-    for s in range(count):
-        for r in range(2):
-            head_ref[r, s : s + 1, :] = buf[1, s, r : r + 1, :]
-    copies[0].wait()
+            tail_ref[r, s : s + 1, :] = f_ref[s, rows - 2 + r : rows - 1 + r, :]
+            head_ref[r, s : s + 1, :] = f_ref[s, r : r + 1, :]
+    for s in range(2):
+        up_ref[s] = f_ref[count - 2 + s]
+        down_ref[s] = f_ref[s]
 
 
 def edges(f):
@@ -58,10 +49,10 @@
     strip = jax.ShapeDtypeStruct((2, count, cols), F32)
     return pl.pallas_call(
         edge_kernel,
-        out_shape=(pair, strip, strip),
-        in_specs=[ANY],
-        out_specs=(VMEM, VMEM, VMEM),
-        scratch_shapes=[pltpu.VMEM((2, count, TILE, cols), F32), pltpu.SemaphoreType.DMA((3,))],
+        out_shape=(pair, pair, strip, strip),
+        in_specs=[VMEM],
+        out_specs=(VMEM, VMEM, VMEM, VMEM),
+        compiler_params=PARAMS,
         name="edges",
     )(f)
 
@@ -107,11 +98,12 @@
         in_specs=[VMEM],
         out_specs=VMEM,
         cost_estimate=pl.CostEstimate(flops=20 * count * rows * cols, transcendentals=0, bytes_accessed=4 * count * rows * cols),
+        compiler_params=PARAMS,
         name="interior",
     )(f)
 
 
-def chunk_kernel(m, n, chunk, f_ref, below_ref, above_ref, tail_ref, head_ref, start_ref, end_ref, part_ref, out_ref):
+def chunk_kernel(m, n, f_ref, below_ref, above_ref, tail_ref, head_ref, start_ref, end_ref, part_ref, out_ref):
     count, rows, cols = f_ref.shape
     tiles = rows // TILE
     path = lax.axis_index("path")
@@ -148,13 +140,12 @@
     line += jnp.where(lane[0:1] == 2 * count, tan_last, 0.0)
 
     for j in range(m * n):
-        out_ref[chunk * j : chunk * j + SUMS, :] = line
+        out_ref[j, :, 0:LANES] = line
     right = lax.rem(space + 1, n) * m
     left = lax.rem(space + n - 1, n) * m
 
     def put(base, source):
-        for i in range(cols // LANES):
-            out_ref[pl.ds(base * chunk + SUMS + i, 1), :] = source[:, i * LANES : (i + 1) * LANES]
+        out_ref[base, :, LANES:] = source
 
     @pl.when(jnp.logical_not(first))
     def _():
@@ -178,18 +169,18 @@
 
 
 def chunks(m, n, f, below, tail_in, head, start, end, part):
-    chunk = SUMS + f.shape[2] // LANES
     return pl.pallas_call(
-        functools.partial(chunk_kernel, m, n, chunk),
-        out_shape=jax.ShapeDtypeStruct((m * n * chunk, LANES), F32),
+        functools.partial(chunk_kernel, m, n),
+        out_shape=jax.ShapeDtypeStruct((m * n, 1, LANES + f.shape[2]), F32),
         in_specs=[VMEM] * 8,
         out_specs=VMEM,
+        compiler_params=PARAMS,
         name="chunks",
     )(f, below, below, tail_in, head, start, end, part)
 
 
 def final_kernel(
-    m, n, chunk, got_ref, f_ref, below_ref, above_ref, tail_ref, head_ref, start_ref, end_ref,
+    m, n, got_ref, f_ref, below_ref, above_ref, tail_ref, head_ref, start_ref, end_ref,
     ratio_ref, res_out, grad_out, field, resid, scale, rowbuf, sem,
 ):
     count, rows, cols = f_ref.shape
@@ -202,9 +193,9 @@
     path_hi = jnp.where(last, path, path + 1)
 
     def gathered(p):
-        total = got_ref[pl.ds(p * chunk, 1), :]
+        total = got_ref[p, :, 0:LANES]
         for i in range(1, n):
-            total += got_ref[pl.ds((i * m + p) * chunk, 1), :]
+            total += got_ref[i * m + p, :, 0:LANES]
         return jnp.broadcast_to(total, (TILE, LANES))
 
     mine = gathered(path)
@@ -246,9 +237,7 @@
     lax.fori_loop(0, count, copy_in, 0)
 
     def corner(slot, at, source):
-        for i in range(cols // LANES):
-            value = got_ref[pl.ds(source * chunk + SUMS + i, 1), :]
-            field[slot, pl.ds(at, 1), i * LANES : (i + 1) * LANES] = value
+        field[slot, pl.ds(at, 1), :] = got_ref[source, :, LANES:]
 
     prev = lax.rem(space + n - 1, n) * m
     nxt = lax.rem(space + 1, n) * m
@@ -313,10 +302,9 @@
 
 def final(m, n, got, f, below, above, tail_in, head_in, start, end):
     count, rows, cols = f.shape
-    chunk = SUMS + cols // LANES
     big = jax.ShapeDtypeStruct(f.shape, F32)
     return pl.pallas_call(
-        functools.partial(final_kernel, m, n, chunk),
+        functools.partial(final_kernel, m, n),
         out_shape=(jax.ShapeDtypeStruct((count,), F32), big, big),
         in_specs=[VMEM] * 8,
         out_specs=(VMEM, ANY, ANY),
@@ -327,19 +315,20 @@
             pltpu.VMEM((2, count, cols), F32),
             pltpu.SemaphoreType.DMA((2,)),
         ],
+        compiler_params=PARAMS,
         name="final",
     )(got, f, below, above, tail_in, head_in, start, end)
 
 
 def body(m, n, f, start, end):
     count = f.shape[0]
-    up, tail, head = edges(f)
+    up, down, tail, head = edges(f)
     tail_in = lax.ppermute(tail, "space", [(i, (i + 1) % n) for i in range(n)])
     below = lax.ppermute(up, "path", [(i, i + 1) for i in range(m - 1)])
     part = interior(f)
     send = chunks(m, n, f, below, tail_in, head, start, end, part)
     got = lax.all_to_all(send, ("space", "path"), 0, 0, tiled=True)
-    down, head_out, send = lax.optimization_barrier((f[0:2], head, send))
+    down, head_out, send = lax.optimization_barrier((down, head, send))
     above = lax.ppermute(down, "path", [(i + 1, i) for i in range(m - 1)])
     head_in = lax.ppermute(head_out, "space", [((i + 1) % n, i) for i in range(n)])
     return final(m, n, got, f, below, above, tail_in, head_in, start, end)

time: 41.7 us -> 31.2 us (0.75)
  Pallas kernels: 13.9 us -> 7.2 us
  local copies, waits for them, and re-layouts: 5.36 us -> 1.24 us
  waiting for transfers between devices: 5.83 us -> 6.28 us
    pallas_call x3, Pallas kernels: 10.5 us -> 5.68 us  [the longest x1 4.74 us: final(): pl.pallas_call(functools.partial(final_kernel, m, n), out_shape=(jax.Shap...]
    all_to_all x1, waiting for transfers between devices: 3.67 us -> 0.18 us  [body(): got = lax.all_to_all(send, ('space', 'path'), 0, 0, tiled=True)]
    ppermute x1, waiting for transfers between devices: 0.01 us -> 2.33 us  [body(): lax.ppermute(head_out, 'space', [((i + 1) % n, i) for i in range(n)])]
    all_to_all x2 -> x0, local copies, waits for them, and re-layouts: 2.3 us -> none  [body(): got = lax.all_to_all(send, ('space', 'path'), 0, 0, tiled=True)]
    pallas_call x1, Pallas kernels: 3.34 us -> 1.52 us  [interior(): pl.pallas_call(interior_kernel, out_shape=jax.ShapeDtypeStruct((2 * count...]
    ppermute x1, waiting for transfers between devices: 2.15 us -> 3.76 us  [body(): tail_in = lax.ppermute(tail, 'space', [(i, (i + 1) % n) for i in range(n)])]
    slice x1 -> x0, local copies, waits for them, and re-layouts: 1 us -> none  [body(): down, head_out, send = lax.optimization_barrier((f[0:2], head, send))]
    unnamed x10 -> x8, local copies, waits for them, and re-layouts: 2.06 us -> 1.24 us
  transfers between devices with their start and end apart: 5 -> 5, of which waited for: 2 -> 3; matrix products, arithmetic and copies ran while one was open for 2% -> 0% of each run, Pallas kernels for 8% -> 5%
where the time goes in v2:
time: 31.2 us; the launch traced here: 31 us
  starting transfers between devices  15.6 us (50%)
  Pallas kernels  7.2 us (23%)
  waiting for transfers between devices  6.28 us (20%)
  local copies, waits for them, and re-layouts  1.24 us (4%)
  between operations  0.7 us (2%)
    all_to_all x1, starting transfers between devices, body(): got = lax.all_to_all(send, ('space', 'path'), 0, 0, tiled=True)  4.88 us
    pallas_call x1, Pallas kernels, final(): pl.pallas_call(functools.partial(final_kernel, m, n), out_shape=(jax.Shap...  4.74 us
    ppermute x1, starting transfers between devices, body(): lax.ppermute(head_out, 'space', [((i + 1) % n, i) for i in range(n)])  4.6 us
    ppermute x1, waiting for transfers between devices, body(): tail_in = lax.ppermute(tail, 'space', [(i, (i + 1) % n) for i in range(n)])  3.76 us
    ppermute x1, starting transfers between devices, body(): tail_in = lax.ppermute(tail, 'space', [(i, (i + 1) % n) for i in range(n)])  2.4 us
    ppermute x1, starting transfers between devices, body(): below = lax.ppermute(up, 'path', [(i, i + 1) for i in range(m - 1)])  2.37 us
    ppermute x1, waiting for transfers between devices, body(): lax.ppermute(head_out, 'space', [((i + 1) % n, i) for i in range(n)])  2.33 us
    pallas_call x1, Pallas kernels, interior(): pl.pallas_call(interior_kernel, out_shape=jax.ShapeDtypeStruct((2 * count...  1.52 us
  transfers between devices with their start and end apart: 5, of which 3 were waited for; matrix products, arithmetic and copies ran while one was open for 0% of the time, Pallas kernels for 5%

profile of v2, /device:TPU:0, one launch (start us, length us, event | category | flops | bytes accessed | tf_op | source)
XLA Modules:
  0.0 31.0 jit_solution(6054062717218989820)
XLA Ops:
  0.6 0.0 copy-start
  0.6 1.2 %copy-done = f32[8,32,1024]{2,1,0:T(8,128)S(1)} copy-done((f32[8,32,1024]{2,1,0:T(8,128)S(1)}, f32[8,32,1024]{2,1,0:T(8,128)}, u32[]{:S(2)}) %copy-start) | copy-done | bytes 1048600
  1.9 0.1 edges.1
  1.9 2.4 %collective-permute-start = (f32[2,32,1024]{2,1,0:T(8,128)S(1)}, f32[2,32,1024]{2,1,0:T(8,128)S(1)}, u32[]{:S(2)}, u32[]{:S(2)}) collective-permute-start(f32[2,32,1024]{2,1,0:T(8,128)S(1)} %get-tuple-element.9), channel_id=1, source_target_pairs={{0,1},{1,2},{2,3},{4,5},{5,6},{6,7},{8,9},{9,10},{10,11},{12,13},{... | collective-permute-start | bytes 786440 | tf_op jit(solution)/shard_map/ppermute | solution.py:327
  4.3 0.0 copy-start.2
  4.3 0.0 copy-start.3
  4.3 2.4 %collective-permute-start.1 = (f32[2,8,1024]{2,1,0:T(8,128)S(1)}, f32[2,8,1024]{2,1,0:T(8,128)S(1)}, u32[]{:S(2)}, u32[]{:S(2)}) collective-permute-start(f32[2,8,1024]{2,1,0:T(8,128)S(1)} %get-tuple-element.10), channel_id=1, source_target_pairs={{0,4},{4,8},{8,12},{12,16},{16,20},{20,24},{24,28},{28,0},{1,5},{5... | collective-permute-start | bytes 196616 | tf_op jit(solution)/shard_map/ppermute | solution.py:326
  6.7 1.5 %interior.1.part_ref = f32[24,128]{1,0:T(8,128)S(1)} custom-call(f32[8,32,1024]{2,1,0:T(8,128)S(1)} %copy-done), custom_call_target="tpu_custom_call" | custom-call | flops 5242880 | bytes 1048576 | tf_op jit(solution)/shard_map/interior/pallas_call | solution.py:95
  8.3 3.8 %collective-permute-done.1.tail_ref = f32[2,8,1024]{2,1,0:T(8,128)S(1)} collective-permute-done((f32[2,8,1024]{2,1,0:T(8,128)S(1)}, f32[2,8,1024]{2,1,0:T(8,128)S(1)}, u32[]{:S(2)}, u32[]{:S(2)}) %collective-permute-start.1) | collective-permute-done | bytes 65568 | tf_op jit(solution)/shard_map/ppermute | solution.py:326
  12.0 0.0 collective-permute-done.below_ref.above_ref
  12.0 0.0 copy-done.2
  12.0 0.0 copy-done.3
  12.0 0.0 copy-start.1
  12.0 0.9 %chunks.1 = f32[32,1,1152]{2,1,0:T(1,128)} custom-call(f32[8,32,1024]{2,1,0:T(8,128)S(1)} %copy-done, f32[2,32,1024]{2,1,0:T(8,128)S(1)} %collective-permute-done.below_ref.above_ref, f32[2,32,1024]{2,1,0:T(8,128)S(1)} %collective-permute-done.below_ref.above_ref, f32[2,8,1024]{2,1,0:T(8,128)S(1)} %collective-permute-done.1.tail_ref, ...), custom_call_target="tpu_custom_call" | custom-call | tf_op jit(solution)/shard_map/chunks/pallas_call | solution.py:172
  12.9 4.9 %all-to-all-start = ((f32[32,1,1152]{2,1,0:T(1,128)}), f32[32,1,1152]{2,1,0:T(1,128)S(1)}, u32[]{:S(2)}, u32[]{:S(2)}) async-start(f32[32,1,1152]{2,1,0:T(1,128)} %chunks.1), calls=%async_computation | async-start | bytes 294912 | tf_op jit(solution)/shard_map/all_to_all | solution.py:330
  17.8 1.3 %collective-permute-start.2 = (f32[2,32,1024]{2,1,0:T(8,128)S(1)}, f32[2,32,1024]{2,1,0:T(8,128)S(1)}, u32[]{:S(2)}, u32[]{:S(2)}) collective-permute-start(f32[2,32,1024]{2,1,0:T(8,128)S(1)} %get-tuple-element.13), channel_id=1, source_target_pairs={{1,0},{2,1},{3,2},{5,4},{6,5},{7,6},{9,8},{10,9},{11,10},{13,12},{... | collective-permute-start | bytes 786440 | tf_op jit(solution)/shard_map/ppermute | solution.py:332
  19.1 4.6 %collective-permute-start.3 = (f32[2,8,1024]{2,1,0:T(8,128)S(1)}, f32[2,8,1024]{2,1,0:T(8,128)S(1)}, u32[]{:S(2)}, u32[]{:S(2)}) collective-permute-start(f32[2,8,1024]{2,1,0:T(8,128)S(1)} %get-tuple-element.14.head_ref), channel_id=1, source_target_pairs={{4,0},{8,4},{12,8},{16,12},{20,16},{24,20},{28,24},{0,28},{5,1},{9... | collective-permute-start | bytes 196616 | tf_op jit(solution)/shard_map/ppermute | solution.py:333
  23.7 2.3 %collective-permute-done.3.head_ref = f32[2,8,1024]{2,1,0:T(8,128)S(1)} collective-permute-done((f32[2,8,1024]{2,1,0:T(8,128)S(1)}, f32[2,8,1024]{2,1,0:T(8,128)S(1)}, u32[]{:S(2)}, u32[]{:S(2)}) %collective-permute-start.3) | collective-permute-done | bytes 65568 | tf_op jit(solution)/shard_map/ppermute | solution.py:333
  26.0 0.0 collective-permute-done.2.above_ref
  26.0 0.2 all-to-all-done.got_ref
  26.2 0.0 copy-done.1
  26.2 4.7 %final.1 = (f32[8]{0:T(128)}, f32[8,32,1024]{2,1,0:T(8,128)}, f32[8,32,1024]{2,1,0:T(8,128)}) custom-call(f32[32,1,1152]{2,1,0:T(1,128)S(1)} %all-to-all-done.got_ref, f32[8,32,1024]{2,1,0:T(8,128)S(1)} %copy-done.1, f32[2,32,1024]{2,1,0:T(8,128)S(1)} %collective-permute-done.below_ref.above_ref, f32[2,32,1024]{2,1,0:T(8,128)S(1)} %collective-permute-done.2.above_ref, ...), custom_call_target="tpu_custom_call" | custom-call | tf_op jit(solution)/shard_map/final/pallas_call | solution.py:306
Async XLA Ops:
  0.6 1.2 %copy-start = (f32[8,32,1024]{2,1,0:T(8,128)S(1)}, f32[8,32,1024]{2,1,0:T(8,128)}, u32[]{:S(2)}) copy-start(f32[8,32,1024]{2,1,0:T(8,128)} %f_ref.7) | copy-start | bytes 3145732
  1.9 10.1 %collective-permute-start = (f32[2,32,1024]{2,1,0:T(8,128)S(1)}, f32[2,32,1024]{2,1,0:T(8,128)S(1)}, u32[]{:S(2)}, u32[]{:S(2)}) collective-permute-start(f32[2,32,1024]{2,1,0:T(8,128)S(1)} %get-tuple-element.9), channel_id=1, source_target_pairs={{0,1},{1,2},{2,3},{4,5},{5,6},{6,7},{8,9},{9,10},{10,11},{12,13},{... | collective-permute-start | bytes 786440 | tf_op jit(solution)/shard_map/ppermute | solution.py:327
  4.3 7.7 %copy-start.2 = (f32[32,1024]{1,0:T(8,128)S(1)}, f32[32,1024]{1,0:T(8,128)}, u32[]{:S(2)}) copy-start(f32[32,1024]{1,0:T(8,128)} %start_ref.3) | copy-start | bytes 393220
  4.3 7.7 %copy-start.3 = (f32[32,1024]{1,0:T(8,128)S(1)}, f32[32,1024]{1,0:T(8,128)}, u32[]{:S(2)}) copy-start(f32[32,1024]{1,0:T(8,128)} %end_ref.3) | copy-start | bytes 393220
  4.3 7.7 %collective-permute-start.1 = (f32[2,8,1024]{2,1,0:T(8,128)S(1)}, f32[2,8,1024]{2,1,0:T(8,128)S(1)}, u32[]{:S(2)}, u32[]{:S(2)}) collective-permute-start(f32[2,8,1024]{2,1,0:T(8,128)S(1)} %get-tuple-element.10), channel_id=1, source_target_pairs={{0,4},{4,8},{8,12},{12,16},{16,20},{20,24},{24,28},{28,0},{1,5},{5... | collective-permute-start | bytes 196616 | tf_op jit(solution)/shard_map/ppermute | solution.py:326
  12.0 14.2 %copy-start.1 = (f32[8,32,1024]{2,1,0:T(8,128)S(1)}, f32[8,32,1024]{2,1,0:T(8,128)}, u32[]{:S(2)}) copy-start(f32[8,32,1024]{2,1,0:T(8,128)} %f_ref.7) | copy-start | bytes 3145732
  12.9 13.3 %all-to-all-start = ((f32[32,1,1152]{2,1,0:T(1,128)}), f32[32,1,1152]{2,1,0:T(1,128)S(1)}, u32[]{:S(2)}, u32[]{:S(2)}) async-start(f32[32,1,1152]{2,1,0:T(1,128)} %chunks.1), calls=%async_computation | async-start | bytes 294912 | tf_op jit(solution)/shard_map/all_to_all | solution.py:330
  17.8 8.2 %collective-permute-start.2 = (f32[2,32,1024]{2,1,0:T(8,128)S(1)}, f32[2,32,1024]{2,1,0:T(8,128)S(1)}, u32[]{:S(2)}, u32[]{:S(2)}) collective-permute-start(f32[2,32,1024]{2,1,0:T(8,128)S(1)} %get-tuple-element.13), channel_id=1, source_target_pairs={{1,0},{2,1},{3,2},{5,4},{6,5},{7,6},{9,8},{10,9},{11,10},{13,12},{... | collective-permute-start | bytes 786440 | tf_op jit(solution)/shard_map/ppermute | solution.py:332
  19.1 6.9 %collective-permute-start.3 = (f32[2,8,1024]{2,1,0:T(8,128)S(1)}, f32[2,8,1024]{2,1,0:T(8,128)S(1)}, u32[]{:S(2)}, u32[]{:S(2)}) collective-permute-start(f32[2,8,1024]{2,1,0:T(8,128)S(1)} %get-tuple-element.14.head_ref), channel_id=1, source_target_pairs={{4,0},{8,4},{12,8},{16,12},{20,16},{24,20},{28,24},{0,28},{5,1},{9... | collective-permute-start | bytes 196616 | tf_op jit(solution)/shard_map/ppermute | solution.py:333

commit v3 on v2

v3 whole, which is shorter than its diff:
```python
import functools

import jax
import jax.numpy as jnp
from jax import lax
from jax.experimental import pallas as pl
from jax.experimental.pallas import tpu as pltpu
from jax.sharding import PartitionSpec as P

F32 = jnp.float32
LANES = 128
TILE = 8
EPS = 1e-06
VMEM = pl.BlockSpec(memory_space=pltpu.VMEM)
ANY = pl.BlockSpec(memory_space=pl.ANY)
PARAMS = pltpu.CompilerParams(vmem_limit_bytes=16 * 2**20)


def lanes_sum(x):
    parts = [x[:, i : i + LANES] for i in range(0, x.shape[1], LANES)]
    while len(parts) > 1:
        parts = [a + b for a, b in zip(parts[::2], parts[1::2])] + parts[len(parts) & ~1 :]
    return parts[0]


def sides(x):
    cols = x.shape[1]
    return pltpu.roll(x, 1, 1) + pltpu.roll(x, cols - 1, 1)


def iota(shape, dim):
    return lax.broadcasted_iota(jnp.int32, shape, dim)


def edge_kernel(f_ref, up_ref, down_ref, tail_ref, head_ref):
    count, rows, _ = f_ref.shape
    for s in range(count):
        for r in range(2):
            tail_ref[r, s : s + 1, :] = f_ref[s, rows - 2 + r : rows - 1 + r, :]
            head_ref[r, s : s + 1, :] = f_ref[s, r : r + 1, :]
    for s in range(2):
        up_ref[s] = f_ref[count - 2 + s]
        down_ref[s] = f_ref[s]


def edges(f):
    count, rows, cols = f.shape
    pair = jax.ShapeDtypeStruct((2, rows, cols), F32)
    strip = jax.ShapeDtypeStruct((2, count, cols), F32)
    return pl.pallas_call(
        edge_kernel,
        out_shape=(pair, pair, strip, strip),
        in_specs=[VMEM],
        out_specs=(VMEM, VMEM, VMEM, VMEM),
        compiler_params=PARAMS,
        name="edges",
    )(f)


def interior_kernel(f_ref, part_ref, drift_ref, rim_ref):
    count, rows, cols = f_ref.shape
    tiles = rows // TILE
    row = iota((TILE, cols), 0)
    part_ref[...] = jnp.zeros_like(part_ref)

    def drift_sum(s, _):
        total = jnp.zeros((TILE, LANES), F32)
        for k in range(tiles):
            c = f_ref[s, pl.ds(TILE * k, TILE), :]
            above = f_ref[s, pl.ds(TILE * k - 1, 1), :] if k > 0 else 0.0
            under = f_ref[s, pl.ds(TILE * (k + 1), 1), :] if k < tiles - 1 else 0.0
            up = jnp.where(row == 0, above, pltpu.roll(c, 1, 0))
            dn = jnp.where(row == TILE - 1, under, pltpu.roll(c, TILE - 1, 0))
            drift = up + dn + sides(c) - 3.0 * c - c * c * c
            drift_ref[s, pl.ds(TILE * k, TILE), :] = drift
            if k == 0:
                rim_ref[0, pl.ds(s, 1), :] = drift[0:1]
                drift = jnp.where(row == 0, 0.0, drift)
            if k == tiles - 1:
                rim_ref[1, pl.ds(s, 1), :] = drift[TILE - 1 : TILE]
                drift = jnp.where(row == TILE - 1, 0.0, drift)
            total += lanes_sum(drift * drift)
        part_ref[pl.ds(s, 1), :] = jnp.sum(total, axis=0, keepdims=True)
        return 0

    def tangent_sum(s, _):
        total = jnp.zeros((TILE, LANES), F32)
        for k in range(tiles):
            tangent = f_ref[s + 1, pl.ds(TILE * k, TILE), :] - f_ref[s - 1, pl.ds(TILE * k, TILE), :]
            total += lanes_sum(tangent * tangent)
        part_ref[pl.ds(count + s + 1, 1), :] = jnp.sum(total, axis=0, keepdims=True)
        return 0

    lax.fori_loop(0, count, drift_sum, 0)
    lax.fori_loop(1, count - 1, tangent_sum, 0)


def interior(f):
    count, rows, cols = f.shape
    return pl.pallas_call(
        interior_kernel,
        out_shape=(
            jax.ShapeDtypeStruct((2 * count + TILE, LANES), F32),
            jax.ShapeDtypeStruct(f.shape, F32),
            jax.ShapeDtypeStruct((2, count, cols), F32),
        ),
        in_specs=[VMEM],
        out_specs=[VMEM] * 3,
        cost_estimate=pl.CostEstimate(flops=20 * count * rows * cols, transcendentals=0, bytes_accessed=8 * count * rows * cols),
        compiler_params=PARAMS,
        name="interior",
    )(f)


def chunk_kernel(m, n, f_ref, below_ref, tail_ref, head_ref, start_ref, end_ref, part_ref, rim_ref, out_ref):
    count, rows, cols = f_ref.shape
    tiles = rows // TILE
    path = lax.axis_index("path")
    space = lax.axis_index("space")
    first = path == 0
    last = path == m - 1

    drift_a = rim_ref[0] + tail_ref[1]
    drift_b = rim_ref[1] + head_ref[0]
    drift = part_ref[0:count, :] + lanes_sum(drift_a * drift_a) + lanes_sum(drift_b * drift_b)

    totals = [jnp.zeros((TILE, LANES), F32) for _ in range(3)]
    for k in range(tiles):
        at = pl.ds(TILE * k, TILE)
        prior = jnp.where(first, start_ref[at, :], below_ref[1, at, :])
        tangents = (
            f_ref[0, at, :] - below_ref[0, at, :],
            f_ref[1, at, :] - prior,
            jnp.where(last, end_ref[at, :] - f_ref[count - 2, at, :], 0.0),
        )
        totals = [a + lanes_sum(t * t) for a, t in zip(totals, tangents)]
    sums = [jnp.sum(a, axis=0, keepdims=True) for a in totals]
    sub = iota((TILE, LANES), 0)
    tan_a = part_ref[count : count + TILE, :]
    tan_a = jnp.where(sub == 0, sums[0], jnp.where(sub == 1, sums[1], tan_a))

    lane = iota((TILE, LANES), 1)
    spread = jnp.where(lane == sub, jnp.sum(drift, axis=1, keepdims=True), 0.0)
    spread += jnp.where(lane == sub + count, jnp.sum(tan_a, axis=1, keepdims=True), 0.0)
    line = jnp.sum(spread, axis=0, keepdims=True)
    tan_last = jnp.sum(sums[2], axis=1, keepdims=True)
    line += jnp.where(lane[0:1] == 2 * count, tan_last, 0.0)

    for j in range(m * n):
        out_ref[j, :, 0:LANES] = line
    right = lax.rem(space + 1, n) * m
    left = lax.rem(space + n - 1, n) * m

    def put(base, source):
        out_ref[base, :, LANES:] = source

    @pl.when(jnp.logical_not(first))
    def _():
        put(right + path - 1, f_ref[0, rows - 1 : rows, :])
        put(left + path - 1, f_ref[0, 0:1, :])

    @pl.when(jnp.logical_not(last))
    def _():
        put(right + path + 1, f_ref[count - 1, rows - 1 : rows, :])
        put(left + path + 1, f_ref[count - 1, 0:1, :])

    @pl.when(first)
    def _():
        put(right + path, start_ref[rows - 1 : rows, :])
        put(left + path, start_ref[0:1, :])

    @pl.when(last)
    def _():
        put(right + path, end_ref[rows - 1 : rows, :])
        put(left + path, end_ref[0:1, :])


def chunks(m, n, f, below, tail_in, head_in, start, end, part, rim):
    return pl.pallas_call(
        functools.partial(chunk_kernel, m, n),
        out_shape=jax.ShapeDtypeStruct((m * n, 1, LANES + f.shape[2]), F32),
        in_specs=[VMEM] * 8,
        out_specs=VMEM,
        compiler_params=PARAMS,
        name="chunks",
    )(f, below, tail_in, head_in, start, end, part, rim)


def final_kernel(
    m, n, got_ref, f_ref, drift_ref, below_ref, above_ref, tail_ref, head_ref, start_ref, end_ref,
    ratio_ref, res_out, grad_out, resid, grad, outer, rim, sem,
):
    count, rows, cols = f_ref.shape
    tiles = rows // TILE
    path = lax.axis_index("path")
    space = lax.axis_index("space")
    first = path == 0
    last = path == m - 1
    path_lo = jnp.where(first, path, path - 1)
    path_hi = jnp.where(last, path, path + 1)

    def gathered(p):
        total = got_ref[p, :, 0:LANES]
        for i in range(1, n):
            total += got_ref[i * m + p, :, 0:LANES]
        return jnp.broadcast_to(total, (TILE, LANES))

    mine = gathered(path)
    lower = gathered(path_lo)
    upper = gathered(path_hi)
    lane = iota((TILE, LANES), 1)
    sub = iota((TILE, LANES), 0)

    def shift(x, k):
        return pltpu.roll(x, k % LANES, 1)

    drift_sq = jnp.where(lane == 0, shift(lower, 1 - count), jnp.where(lane <= count, shift(mine, 1), shift(upper, count + 1)))
    at_end = shift(mine, -count) + jnp.where(last, 0.0, upper)
    tangent_sq = jnp.where(lane < count, shift(mine, -count), jnp.where(lane == count, at_end, upper))
    ratio = jnp.sqrt(drift_sq + EPS) / jnp.sqrt(tangent_sq + EPS)
    ratio = jnp.where((lane == 0) & first, 0.0, ratio)
    ratio = jnp.where((lane == count + 1) & last, 0.0, ratio)
    ratio_ref[...] = shift(ratio, -1)[0, 0:count]

    def splat(t):
        return jnp.broadcast_to(jnp.sum(jnp.where(lane == t, ratio, 0.0), axis=1, keepdims=True), (TILE, LANES))

    def widen(x):
        return jnp.concatenate([x] * (cols // LANES), axis=1)

    scale = [widen(splat(t)) for t in range(count + 2)]
    column = jnp.sum(jnp.where(lane == sub + 1, ratio, 0.0), axis=1, keepdims=True)
    row = iota((TILE, cols), 0)
    prev = lax.rem(space + n - 1, n) * m
    nxt = lax.rem(space + 1, n) * m

    def at(k):
        return pl.ds(TILE * k, TILE)

    for k in range(tiles):
        outer[0, at(k), :] = jnp.where(first, start_ref[at(k), :], below_ref[1, at(k), :])
        outer[1, at(k), :] = jnp.where(last, end_ref[at(k), :], above_ref[0, at(k), :])

    def value(s, k):
        where = {-2: (below_ref, 0), -1: (outer, 0), count: (outer, 1), count + 1: (above_ref, 1)}
        ref, slot = where.get(s, (f_ref, s))
        return ref[slot, at(k), :]

    for s in range(count):
        rim[0, s : s + 1, :] = f_ref[s, 0:1, :]
        rim[1, s : s + 1, :] = f_ref[s, rows - 1 : rows, :]
    for far, mid, near, base, place in (
        (tail_ref[0], tail_ref[1], rim[0], prev, TILE - 1),
        (head_ref[1], head_ref[0], rim[1], nxt, TILE + rows),
    ):
        low = got_ref[base + path_lo, :, LANES:]
        high = got_ref[base + path_hi, :, LANES:]
        ahead = jnp.where(row == count - 1, high, pltpu.roll(mid, count - 1, 0))
        behind = jnp.where(row == 0, low, pltpu.roll(mid, 1, 0))
        edge = column * (ahead - behind) - (far + near + sides(mid) - 3.0 * mid - mid * mid * mid)
        for s in range(count):
            resid[s + 1, place : place + 1, :] = edge[s : s + 1, :]

    def residual_of(s):
        if s in (-1, count):
            slot, q = (0, path_lo) if s < 0 else (1, path_hi)
            top, bottom = got_ref[prev + q, :, LANES:], got_ref[nxt + q, :, LANES:]
        else:
            top, bottom = tail_ref[1, s : s + 1, :], head_ref[0, s : s + 1, :]
        for k in range(tiles):
            if s in (-1, count):
                c = outer[slot, at(k), :]
                above = outer[slot, TILE * k - 1 : TILE * k, :] if k > 0 else top
                under = outer[slot, TILE * (k + 1) : TILE * (k + 1) + 1, :] if k < tiles - 1 else bottom
                up = jnp.where(row == 0, above, pltpu.roll(c, 1, 0))
                dn = jnp.where(row == TILE - 1, under, pltpu.roll(c, TILE - 1, 0))
                drift = up + dn + sides(c) - 3.0 * c - c * c * c
            else:
                drift = drift_ref[s, at(k), :]
                if k == 0:
                    drift += jnp.where(row == 0, top, 0.0)
                if k == tiles - 1:
                    drift += jnp.where(row == TILE - 1, bottom, 0.0)
            resid[s + 1, at(k + 1), :] = scale[s + 1] * (value(s + 1, k) - value(s - 1, k)) - drift

    def gradient_of(s):
        for k in range(tiles):
            base = TILE * (k + 1)
            c = f_ref[s, pl.ds(TILE * k, TILE), :]
            r = resid[s + 1, pl.ds(base, TILE), :]
            around = resid[s + 1, pl.ds(base - 1, TILE), :] + resid[s + 1, pl.ds(base + 1, TILE), :] + sides(r)
            out = scale[s] * resid[s, pl.ds(base, TILE), :] - scale[s + 2] * resid[s + 2, pl.ds(base, TILE), :]
            grad[s, pl.ds(TILE * k, TILE), :] = out - (around - (3.0 + 3.0 * c * c) * r)

    copies = []

    def send(src, dst, slot):
        copy = pltpu.make_async_copy(src, dst, slot)
        copy.start()
        copies.append(copy)

    residual_of(-1)
    residual_of(0)
    for s in range(count):
        residual_of(s + 1)
        send(resid.at[s + 1, pl.ds(TILE, rows)], res_out.at[s], sem.at[0, s])
        gradient_of(s)
        send(grad.at[s], grad_out.at[s], sem.at[1, s])
    for copy in copies:
        copy.wait()


def final(m, n, got, f, drift, below, above, tail_in, head_in, start, end):
    count, rows, cols = f.shape
    big = jax.ShapeDtypeStruct(f.shape, F32)
    return pl.pallas_call(
        functools.partial(final_kernel, m, n),
        out_shape=(jax.ShapeDtypeStruct((count,), F32), big, big),
        in_specs=[VMEM] * 9,
        out_specs=(VMEM, ANY, ANY),
        scratch_shapes=[
            pltpu.VMEM((count + 2, rows + 2 * TILE, cols), F32),
            pltpu.VMEM(f.shape, F32),
            pltpu.VMEM((2, rows, cols), F32),
            pltpu.VMEM((2, count, cols), F32),
            pltpu.SemaphoreType.DMA((2, count)),
        ],
        compiler_params=PARAMS,
        name="final",
    )(got, f, drift, below, above, tail_in, head_in, start, end)


def ring(x, n, step):
    return lax.ppermute(x, "space", [(i, (i + step) % n) for i in range(n)])


def body(m, n, f, start, end):
    up, down, tail, head = edges(f)
    tail_in = ring(tail, n, 1)
    below = lax.ppermute(up, "path", [(i, i + 1) for i in range(m - 1)])
    head_in = ring(head, n, -1)
    above = lax.ppermute(down, "path", [(i + 1, i) for i in range(m - 1)])
    part, drift, rim = interior(f)
    send = chunks(m, n, f, below, tail_in, head_in, start, end, part, rim)
    got = lax.all_to_all(send, ("space", "path"), 0, 0, tiled=True)
    return final(m, n, got, f, drift, below, above, tail_in, head_in, start, end)


def solution(mesh):
    m, n = mesh.shape["path"], mesh.shape["space"]
    in_specs = (P("path", "space", None), P("space", None), P("space", None))
    out_specs = (P("path"), P("path", "space", None), P("path", "space", None))
    return jax.shard_map(
        functools.partial(body, m, n), mesh=mesh, in_specs=in_specs, out_specs=out_specs, check_vma=False
    )
```

time: 31.2 us -> 30.6 us (0.981)
  Pallas kernels: 7.2 us -> 5.05 us
  waiting for transfers between devices: 6.28 us -> 8 us
    ppermute x2, waiting for transfers between devices: 6.09 us -> 0.88 us  [ring(): return lax.ppermute(x, 'space', [(i, (i + step) % n) for i in range(n)])]
    all_to_all x1, waiting for transfers between devices: 0.18 us -> 4.99 us  [body(): got = lax.all_to_all(send, ('space', 'path'), 0, 0, tiled=True)]
    ppermute x1, waiting for transfers between devices: 0.01 us -> 2.13 us  [body(): above = lax.ppermute(down, 'path', [(i + 1, i) for i in range(m - 1)])]
    pallas_call x1, Pallas kernels: 4.74 us -> 2.77 us  [final(): pl.pallas_call(functools.partial(final_kernel, m, n), out_shape=(jax.Shap...]
    ppermute x2, starting transfers between devices: 7.01 us -> 5.53 us  [ring(): return lax.ppermute(x, 'space', [(i, (i + step) % n) for i in range(n)])]
    all_to_all x1, starting transfers between devices: 4.88 us -> 6.23 us  [body(): got = lax.all_to_all(send, ('space', 'path'), 0, 0, tiled=True)]
where the time goes in v3:
time: 30.6 us; the launch traced here: 30.4 us
  starting transfers between devices  15.4 us (50%)
  waiting for transfers between devices  8 us (26%)
  Pallas kernels  5.05 us (17%)
  local copies, waits for them, and re-layouts  1.23 us (4%)
  between operations  0.7 us (2%)
    all_to_all x1, starting transfers between devices, body(): got = lax.all_to_all(send, ('space', 'path'), 0, 0, tiled=True)  6.23 us
    ppermute x2, starting transfers between devices, ring(): return lax.ppermute(x, 'space', [(i, (i + step) % n) for i in range(n)])  5.53 us
    all_to_all x1, waiting for transfers between devices, body(): got = lax.all_to_all(send, ('space', 'path'), 0, 0, tiled=True)  4.99 us
    pallas_call x1, Pallas kernels, final(): pl.pallas_call(functools.partial(final_kernel, m, n), out_shape=(jax.Shap...  2.77 us
    ppermute x1, starting transfers between devices, body(): below = lax.ppermute(up, 'path', [(i, i + 1) for i in range(m - 1)])  2.37 us
    ppermute x1, waiting for transfers between devices, body(): above = lax.ppermute(down, 'path', [(i + 1, i) for i in range(m - 1)])  2.13 us
    pallas_call x1, Pallas kernels, interior(): pl.pallas_call(interior_kernel, out_shape=(jax.ShapeDtypeStruct((2 * coun...  1.38 us
    ppermute x1, starting transfers between devices, body(): above = lax.ppermute(down, 'path', [(i + 1, i) for i in range(m - 1)])  1.29 us
  transfers between devices with their start and end apart: 5, of which 3 were waited for; matrix products, arithmetic and copies ran while one was open for 0% of the time, Pallas kernels for 5%

profile of v3, /device:TPU:0, one launch (start us, length us, event | category | flops | bytes accessed | tf_op | source)
XLA Modules:
  0.0 30.4 jit_solution(8660464324384337728)
XLA Ops:
  0.6 0.0 copy-start
  0.6 1.2 %copy-done = f32[8,32,1024]{2,1,0:T(8,128)S(1)} copy-done((f32[8,32,1024]{2,1,0:T(8,128)S(1)}, f32[8,32,1024]{2,1,0:T(8,128)}, u32[]{:S(2)}) %copy-start) | copy-done | bytes 1048600
  1.9 0.1 edges.1
  1.9 2.4 %collective-permute-start = (f32[2,32,1024]{2,1,0:T(8,128)S(1)}, f32[2,32,1024]{2,1,0:T(8,128)S(1)}, u32[]{:S(2)}, u32[]{:S(2)}) collective-permute-start(f32[2,32,1024]{2,1,0:T(8,128)S(1)} %get-tuple-element.10), channel_id=1, source_target_pairs={{0,1},{1,2},{2,3},{4,5},{5,6},{6,7},{8,9},{9,10},{10,11},{12,13},{... | collective-permute-start | bytes 786440 | tf_op jit(solution)/shard_map/ppermute | solution.py:340
  4.3 2.4 %collective-permute-start.1 = (f32[2,8,1024]{2,1,0:T(8,128)S(1)}, f32[2,8,1024]{2,1,0:T(8,128)S(1)}, u32[]{:S(2)}, u32[]{:S(2)}) collective-permute-start(f32[2,8,1024]{2,1,0:T(8,128)S(1)} %get-tuple-element.11), channel_id=1, source_target_pairs={{0,4},{4,8},{8,12},{12,16},{16,20},{20,24},{24,28},{28,0},{1,5},{5... | collective-permute-start | bytes 196616 | tf_op jit(solution)/shard_map/ppermute | solution.py:334
  6.7 0.0 copy-start.2
  6.7 0.0 copy-start.3
  6.7 3.1 %collective-permute-start.2 = (f32[2,8,1024]{2,1,0:T(8,128)S(1)}, f32[2,8,1024]{2,1,0:T(8,128)S(1)}, u32[]{:S(2)}, u32[]{:S(2)}) collective-permute-start(f32[2,8,1024]{2,1,0:T(8,128)S(1)} %get-tuple-element.12), channel_id=1, source_target_pairs={{0,28},{4,0},{8,4},{12,8},{16,12},{20,16},{24,20},{28,24},{1,29},{... | collective-permute-start | bytes 196616 | tf_op jit(solution)/shard_map/ppermute | solution.py:334
  9.8 1.4 %interior.1 = (f32[24,128]{1,0:T(8,128)S(1)}, f32[8,32,1024]{2,1,0:T(8,128)S(1)}, f32[2,8,1024]{2,1,0:T(8,128)S(1)}) custom-call(f32[8,32,1024]{2,1,0:T(8,128)S(1)} %copy-done), custom_call_target="tpu_custom_call" | custom-call | flops 5242880 | bytes 2097152 | tf_op jit(solution)/shard_map/interior/pallas_call | solution.py:100
  11.2 0.9 %collective-permute-done.1.tail_ref = f32[2,8,1024]{2,1,0:T(8,128)S(1)} collective-permute-done((f32[2,8,1024]{2,1,0:T(8,128)S(1)}, f32[2,8,1024]{2,1,0:T(8,128)S(1)}, u32[]{:S(2)}, u32[]{:S(2)}) %collective-permute-start.1) | collective-permute-done | bytes 65568 | tf_op jit(solution)/shard_map/ppermute | solution.py:334
  12.1 0.0 collective-permute-done.2.head_ref
  12.1 0.0 collective-permute-done.below_ref
  12.1 0.0 copy-done.2
  12.1 0.0 copy-done.3
  12.1 0.0 copy-start.1
  12.1 0.8 %chunks.1 = f32[32,1,1152]{2,1,0:T(1,128)} custom-call(f32[8,32,1024]{2,1,0:T(8,128)S(1)} %copy-done, f32[2,32,1024]{2,1,0:T(8,128)S(1)} %collective-permute-done.below_ref, f32[2,8,1024]{2,1,0:T(8,128)S(1)} %collective-permute-done.1.tail_ref, f32[2,8,1024]{2,1,0:T(8,128)S(1)} %collective-permute-done.2.head_ref, f32[32,1024]{1,0:T(8,128)S(1)} %copy-done.2, ...), custom_call_target="tpu_custom_call" | custom-call | tf_op jit(solution)/shard_map/chunks/pallas_call | solution.py:179
  13.0 6.2 %all-to-all-start = ((f32[32,1,1152]{2,1,0:T(1,128)}), f32[32,1,1152]{2,1,0:T(1,128)S(1)}, u32[]{:S(2)}, u32[]{:S(2)}) async-start(f32[32,1,1152]{2,1,0:T(1,128)} %chunks.1), calls=%async_computation | async-start | bytes 294912 | tf_op jit(solution)/shard_map/all_to_all | solution.py:345
  19.2 1.3 %collective-permute-start.3 = (f32[2,32,1024]{2,1,0:T(8,128)S(1)}, f32[2,32,1024]{2,1,0:T(8,128)S(1)}, u32[]{:S(2)}, u32[]{:S(2)}) collective-permute-start(f32[2,32,1024]{2,1,0:T(8,128)S(1)} %get-tuple-element.16), channel_id=1, source_target_pairs={{1,0},{2,1},{3,2},{5,4},{6,5},{7,6},{9,8},{10,9},{11,10},{13,12},{... | collective-permute-start | bytes 786440 | tf_op jit(solution)/shard_map/ppermute | solution.py:342
  20.5 2.1 %collective-permute-done.3.above_ref = f32[2,32,1024]{2,1,0:T(8,128)S(1)} collective-permute-done((f32[2,32,1024]{2,1,0:T(8,128)S(1)}, f32[2,32,1024]{2,1,0:T(8,128)S(1)}, u32[]{:S(2)}, u32[]{:S(2)}) %collective-permute-start.3) | collective-permute-done | bytes 262176 | tf_op jit(solution)/shard_map/ppermute | solution.py:342
  22.6 5.0 %all-to-all-done.got_ref = f32[32,1,1152]{2,1,0:T(1,128)S(1)} async-done(((f32[32,1,1152]{2,1,0:T(1,128)}), f32[32,1,1152]{2,1,0:T(1,128)S(1)}, u32[]{:S(2)}, u32[]{:S(2)}) %all-to-all-start) | async-done | bytes 147488 | tf_op jit(solution)/shard_map/all_to_all | solution.py:345
  27.6 0.0 copy-done.1
  27.6 2.8 %final.1 = (f32[8]{0:T(128)}, f32[8,32,1024]{2,1,0:T(8,128)}, f32[8,32,1024]{2,1,0:T(8,128)}) custom-call(f32[32,1,1152]{2,1,0:T(1,128)S(1)} %all-to-all-done.got_ref, f32[8,32,1024]{2,1,0:T(8,128)S(1)} %copy-done.1, f32[8,32,1024]{2,1,0:T(8,128)S(1)} %get-tuple-element.15.drift_ref, f32[2,32,1024]{2,1,0:T(8,128)S(1)} %collective-permute-done.below_ref, ...), custom_call_target="tpu_custom_call" | custom-call | tf_op jit(solution)/shard_map/final/pallas_call | solution.py:316
Async XLA Ops:
  0.6 1.2 %copy-start = (f32[8,32,1024]{2,1,0:T(8,128)S(1)}, f32[8,32,1024]{2,1,0:T(8,128)}, u32[]{:S(2)}) copy-start(f32[8,32,1024]{2,1,0:T(8,128)} %f_ref.7) | copy-start | bytes 3145732
  1.9 10.2 %collective-permute-start = (f32[2,32,1024]{2,1,0:T(8,128)S(1)}, f32[2,32,1024]{2,1,0:T(8,128)S(1)}, u32[]{:S(2)}, u32[]{:S(2)}) collective-permute-start(f32[2,32,1024]{2,1,0:T(8,128)S(1)} %get-tuple-element.10), channel_id=1, source_target_pairs={{0,1},{1,2},{2,3},{4,5},{5,6},{6,7},{8,9},{9,10},{10,11},{12,13},{... | collective-permute-start | bytes 786440 | tf_op jit(solution)/shard_map/ppermute | solution.py:340
  4.3 7.8 %collective-permute-start.1 = (f32[2,8,1024]{2,1,0:T(8,128)S(1)}, f32[2,8,1024]{2,1,0:T(8,128)S(1)}, u32[]{:S(2)}, u32[]{:S(2)}) collective-permute-start(f32[2,8,1024]{2,1,0:T(8,128)S(1)} %get-tuple-element.11), channel_id=1, source_target_pairs={{0,4},{4,8},{8,12},{12,16},{16,20},{20,24},{24,28},{28,0},{1,5},{5... | collective-permute-start | bytes 196616 | tf_op jit(solution)/shard_map/ppermute | solution.py:334
  6.7 5.4 %copy-start.2 = (f32[32,1024]{1,0:T(8,128)S(1)}, f32[32,1024]{1,0:T(8,128)}, u32[]{:S(2)}) copy-start(f32[32,1024]{1,0:T(8,128)} %start_ref.3) | copy-start | bytes 393220
  6.7 5.4 %copy-start.3 = (f32[32,1024]{1,0:T(8,128)S(1)}, f32[32,1024]{1,0:T(8,128)}, u32[]{:S(2)}) copy-start(f32[32,1024]{1,0:T(8,128)} %end_ref.3) | copy-start | bytes 393220
  6.7 5.4 %collective-permute-start.2 = (f32[2,8,1024]{2,1,0:T(8,128)S(1)}, f32[2,8,1024]{2,1,0:T(8,128)S(1)}, u32[]{:S(2)}, u32[]{:S(2)}) collective-permute-start(f32[2,8,1024]{2,1,0:T(8,128)S(1)} %get-tuple-element.12), channel_id=1, source_target_pairs={{0,28},{4,0},{8,4},{12,8},{16,12},{20,16},{24,20},{28,24},{1,29},{... | collective-permute-start | bytes 196616 | tf_op jit(solution)/shard_map/ppermute | solution.py:334
  12.1 15.5 %copy-start.1 = (f32[8,32,1024]{2,1,0:T(8,128)S(1)}, f32[8,32,1024]{2,1,0:T(8,128)}, u32[]{:S(2)}) copy-start(f32[8,32,1024]{2,1,0:T(8,128)} %f_ref.7) | copy-start | bytes 3145732
  13.0 14.7 %all-to-all-start = ((f32[32,1,1152]{2,1,0:T(1,128)}), f32[32,1,1152]{2,1,0:T(1,128)S(1)}, u32[]{:S(2)}, u32[]{:S(2)}) async-start(f32[32,1,1152]{2,1,0:T(1,128)} %chunks.1), calls=%async_computation | async-start | bytes 294912 | tf_op jit(solution)/shard_map/all_to_all | solution.py:345
  19.2 3.4 %collective-permute-start.3 = (f32[2,32,1024]{2,1,0:T(8,128)S(1)}, f32[2,32,1024]{2,1,0:T(8,128)S(1)}, u32[]{:S(2)}, u32[]{:S(2)}) collective-permute-start(f32[2,32,1024]{2,1,0:T(8,128)S(1)} %get-tuple-element.16), channel_id=1, source_target_pairs={{1,0},{2,1},{3,2},{5,4},{6,5},{7,6},{9,8},{10,9},{11,10},{13,12},{... | collective-permute-start | bytes 786440 | tf_op jit(solution)/shard_map/ppermute | solution.py:342

commit v4 on v3

--- a/solution.py
+++ b/solution.py
@@ -88,7 +88,7 @@
         for k in range(tiles):
             tangent = f_ref[s + 1, pl.ds(TILE * k, TILE), :] - f_ref[s - 1, pl.ds(TILE * k, TILE), :]
             total += lanes_sum(tangent * tangent)
-        part_ref[pl.ds(count + s + 1, 1), :] = jnp.sum(total, axis=0, keepdims=True)
+        part_ref[pl.ds(count + s, 1), :] = jnp.sum(total, axis=0, keepdims=True)
         return 0
 
     lax.fori_loop(0, count, drift_sum, 0)
@@ -100,7 +100,7 @@
     return pl.pallas_call(
         interior_kernel,
         out_shape=(
-            jax.ShapeDtypeStruct((2 * count + TILE, LANES), F32),
+            jax.ShapeDtypeStruct((2 * count, LANES), F32),
             jax.ShapeDtypeStruct(f.shape, F32),
             jax.ShapeDtypeStruct((2, count, cols), F32),
         ),
@@ -112,7 +112,7 @@
     )(f)
 
 
-def chunk_kernel(m, n, f_ref, below_ref, tail_ref, head_ref, start_ref, end_ref, part_ref, rim_ref, out_ref):
+def chunk_kernel(m, n, f_ref, below_ref, above_ref, tail_ref, head_ref, start_ref, end_ref, part_ref, rim_ref, out_ref):
     count, rows, cols = f_ref.shape
     tiles = rows // TILE
     path = lax.axis_index("path")
@@ -124,27 +124,22 @@
     drift_b = rim_ref[1] + head_ref[0]
     drift = part_ref[0:count, :] + lanes_sum(drift_a * drift_a) + lanes_sum(drift_b * drift_b)
 
-    totals = [jnp.zeros((TILE, LANES), F32) for _ in range(3)]
+    totals = [jnp.zeros((TILE, LANES), F32) for _ in range(2)]
     for k in range(tiles):
         at = pl.ds(TILE * k, TILE)
         prior = jnp.where(first, start_ref[at, :], below_ref[1, at, :])
-        tangents = (
-            f_ref[0, at, :] - below_ref[0, at, :],
-            f_ref[1, at, :] - prior,
-            jnp.where(last, end_ref[at, :] - f_ref[count - 2, at, :], 0.0),
-        )
+        after = jnp.where(last, end_ref[at, :], above_ref[0, at, :])
+        tangents = (f_ref[1, at, :] - prior, after - f_ref[count - 2, at, :])
         totals = [a + lanes_sum(t * t) for a, t in zip(totals, tangents)]
-    sums = [jnp.sum(a, axis=0, keepdims=True) for a in totals]
+    head_sum, tail_sum = [jnp.sum(a, axis=0, keepdims=True) for a in totals]
     sub = iota((TILE, LANES), 0)
-    tan_a = part_ref[count : count + TILE, :]
-    tan_a = jnp.where(sub == 0, sums[0], jnp.where(sub == 1, sums[1], tan_a))
+    tangent = part_ref[count : 2 * count, :]
+    tangent = jnp.where(sub == 0, head_sum, jnp.where(sub == count - 1, tail_sum, tangent))
 
     lane = iota((TILE, LANES), 1)
     spread = jnp.where(lane == sub, jnp.sum(drift, axis=1, keepdims=True), 0.0)
-    spread += jnp.where(lane == sub + count, jnp.sum(tan_a, axis=1, keepdims=True), 0.0)
+    spread += jnp.where(lane == sub + count, jnp.sum(tangent, axis=1, keepdims=True), 0.0)
     line = jnp.sum(spread, axis=0, keepdims=True)
-    tan_last = jnp.sum(sums[2], axis=1, keepdims=True)
-    line += jnp.where(lane[0:1] == 2 * count, tan_last, 0.0)
 
     for j in range(m * n):
         out_ref[j, :, 0:LANES] = line
@@ -175,15 +170,15 @@
         put(left + path, end_ref[0:1, :])
 
 
-def chunks(m, n, f, below, tail_in, head_in, start, end, part, rim):
+def chunks(m, n, f, below, above, tail_in, head_in, start, end, part, rim):
     return pl.pallas_call(
         functools.partial(chunk_kernel, m, n),
         out_shape=jax.ShapeDtypeStruct((m * n, 1, LANES + f.shape[2]), F32),
-        in_specs=[VMEM] * 8,
+        in_specs=[VMEM] * 9,
         out_specs=VMEM,
         compiler_params=PARAMS,
         name="chunks",
-    )(f, below, tail_in, head_in, start, end, part, rim)
+    )(f, below, above, tail_in, head_in, start, end, part, rim)
 
 
 def final_kernel(
@@ -214,13 +209,14 @@
     def shift(x, k):
         return pltpu.roll(x, k % LANES, 1)
 
-    drift_sq = jnp.where(lane == 0, shift(lower, 1 - count), jnp.where(lane <= count, shift(mine, 1), shift(upper, count + 1)))
-    at_end = shift(mine, -count) + jnp.where(last, 0.0, upper)
-    tangent_sq = jnp.where(lane < count, shift(mine, -count), jnp.where(lane == count, at_end, upper))
-    ratio = jnp.sqrt(drift_sq + EPS) / jnp.sqrt(tangent_sq + EPS)
-    ratio = jnp.where((lane == 0) & first, 0.0, ratio)
-    ratio = jnp.where((lane == count + 1) & last, 0.0, ratio)
-    ratio_ref[...] = shift(ratio, -1)[0, 0:count]
+    def ratios(x):
+        return jnp.sqrt(x + EPS) / jnp.sqrt(shift(x, -count) + EPS)
+
+    low = jnp.where(first, 0.0, shift(ratios(lower), 1 - count))
+    high = jnp.where(last, 0.0, shift(ratios(upper), count + 1))
+    own = ratios(mine)
+    ratio_ref[...] = own[0, 0:count]
+    ratio = jnp.where(lane == 0, low, jnp.where(lane == count + 1, high, shift(own, 1)))
 
     def splat(t):
         return jnp.broadcast_to(jnp.sum(jnp.where(lane == t, ratio, 0.0), axis=1, keepdims=True), (TILE, LANES))
@@ -341,7 +337,7 @@
     head_in = ring(head, n, -1)
     above = lax.ppermute(down, "path", [(i + 1, i) for i in range(m - 1)])
     part, drift, rim = interior(f)
-    send = chunks(m, n, f, below, tail_in, head_in, start, end, part, rim)
+    send = chunks(m, n, f, below, above, tail_in, head_in, start, end, part, rim)
     got = lax.all_to_all(send, ("space", "path"), 0, 0, tiled=True)
     return final(m, n, got, f, drift, below, above, tail_in, head_in, start, end)
 

time: 30.6 us -> 33.5 us (1.095)
  blocking collectives: 0 us -> 16.8 us
  waiting for transfers between devices: 8 us -> 0.83 us
  starting transfers between devices: 15.4 us -> 9.19 us
  Pallas kernels: 5.05 us -> 4.47 us
    all_to_all x0 -> x1, blocking collectives: none -> 16.8 us  [body(): got = lax.all_to_all(send, ('space', 'path'), 0, 0, tiled=True)]
    all_to_all x1 -> x0, starting transfers between devices: 6.23 us -> none  [body(): got = lax.all_to_all(send, ('space', 'path'), 0, 0, tiled=True)]
    all_to_all x1 -> x0, waiting for transfers between devices: 4.99 us -> none  [body(): got = lax.all_to_all(send, ('space', 'path'), 0, 0, tiled=True)]
    ppermute x1, waiting for transfers between devices: 2.13 us -> 0.01 us  [body(): above = lax.ppermute(down, 'path', [(i + 1, i) for i in range(m - 1)])]
    pallas_call x1, Pallas kernels: 0.83 us -> 0.17 us  [chunks(): pl.pallas_call(functools.partial(chunk_kernel, m, n), out_shape=jax.Shape...]
    unnamed x8 -> x6, local copies, waits for them, and re-layouts: 1.23 us -> 1.23 us
  transfers between devices with their start and end apart: 5 -> 4, of which waited for: 3 -> 1; matrix products, arithmetic and copies ran while one was open for 0% -> 0% of each run, Pallas kernels for 5% -> 4%
where the time goes in v4:
time: 33.5 us; the launch traced here: 33.3 us
  blocking collectives  16.8 us (50%)
  starting transfers between devices  9.19 us (27%)
  Pallas kernels  4.47 us (13%)
  local copies, waits for them, and re-layouts  1.23 us (4%)
  waiting for transfers between devices  0.83 us (2%)
  between operations  0.69 us (2%)
    all_to_all x1, blocking collectives, body(): got = lax.all_to_all(send, ('space', 'path'), 0, 0, tiled=True)  16.8 us
    ppermute x2, starting transfers between devices, ring(): return lax.ppermute(x, 'space', [(i, (i + step) % n) for i in range(n)])  5.53 us
    pallas_call x1, Pallas kernels, final(): pl.pallas_call(functools.partial(final_kernel, m, n), out_shape=(jax.Shap...  2.85 us
    ppermute x1, starting transfers between devices, body(): below = lax.ppermute(up, 'path', [(i, i + 1) for i in range(m - 1)])  2.37 us
    pallas_call x1, Pallas kernels, interior(): pl.pallas_call(interior_kernel, out_shape=(jax.ShapeDtypeStruct((2 * coun...  1.38 us
    ppermute x1, starting transfers between devices, body(): above = lax.ppermute(down, 'path', [(i + 1, i) for i in range(m - 1)])  1.29 us
    unnamed x6, local copies, waits for them, and re-layouts  1.23 us
    ppermute x2, waiting for transfers between devices, ring(): return lax.ppermute(x, 'space', [(i, (i + step) % n) for i in range(n)])  0.83 us
  transfers between devices with their start and end apart: 4, of which 1 were waited for; matrix products, arithmetic and copies ran while one was open for 0% of the time, Pallas kernels for 4%

profile of v4, /device:TPU:0, one launch (start us, length us, event | category | flops | bytes accessed | tf_op | source)
XLA Modules:
  0.0 33.3 jit_solution(6243133083900690870)
XLA Ops:
  0.6 0.0 copy-start
  0.6 1.2 %copy-done = f32[8,32,1024]{2,1,0:T(8,128)S(1)} copy-done((f32[8,32,1024]{2,1,0:T(8,128)S(1)}, f32[8,32,1024]{2,1,0:T(8,128)}, u32[]{:S(2)}) %copy-start) | copy-done | bytes 1048600
  1.9 0.1 edges.1
  1.9 2.4 %collective-permute-start = (f32[2,32,1024]{2,1,0:T(8,128)S(1)}, f32[2,32,1024]{2,1,0:T(8,128)S(1)}, u32[]{:S(2)}, u32[]{:S(2)}) collective-permute-start(f32[2,32,1024]{2,1,0:T(8,128)S(1)} %get-tuple-element.10), channel_id=1, source_target_pairs={{0,1},{1,2},{2,3},{4,5},{5,6},{6,7},{8,9},{9,10},{10,11},{12,13},{... | collective-permute-start | bytes 786440 | tf_op jit(solution)/shard_map/ppermute | solution.py:336
  4.3 1.3 %collective-permute-start.1 = (f32[2,32,1024]{2,1,0:T(8,128)S(1)}, f32[2,32,1024]{2,1,0:T(8,128)S(1)}, u32[]{:S(2)}, u32[]{:S(2)}) collective-permute-start(f32[2,32,1024]{2,1,0:T(8,128)S(1)} %get-tuple-element.11), channel_id=1, source_target_pairs={{1,0},{2,1},{3,2},{5,4},{6,5},{7,6},{9,8},{10,9},{11,10},{13,12},{... | collective-permute-start | bytes 786440 | tf_op jit(solution)/shard_map/ppermute | solution.py:338
  5.6 2.4 %collective-permute-start.2 = (f32[2,8,1024]{2,1,0:T(8,128)S(1)}, f32[2,8,1024]{2,1,0:T(8,128)S(1)}, u32[]{:S(2)}, u32[]{:S(2)}) collective-permute-start(f32[2,8,1024]{2,1,0:T(8,128)S(1)} %get-tuple-element.12), channel_id=1, source_target_pairs={{0,4},{4,8},{8,12},{12,16},{16,20},{20,24},{24,28},{28,0},{1,5},{5... | collective-permute-start | bytes 196616 | tf_op jit(solution)/shard_map/ppermute | solution.py:330
  8.0 0.0 copy-start.1
  8.0 0.0 copy-start.2
  8.0 3.1 %collective-permute-start.3 = (f32[2,8,1024]{2,1,0:T(8,128)S(1)}, f32[2,8,1024]{2,1,0:T(8,128)S(1)}, u32[]{:S(2)}, u32[]{:S(2)}) collective-permute-start(f32[2,8,1024]{2,1,0:T(8,128)S(1)} %get-tuple-element.13), channel_id=1, source_target_pairs={{0,28},{4,0},{8,4},{12,8},{16,12},{20,16},{24,20},{28,24},{1,29},{... | collective-permute-start | bytes 196616 | tf_op jit(solution)/shard_map/ppermute | solution.py:330
  11.1 1.4 %interior.1 = (f32[16,128]{1,0:T(8,128)S(1)}, f32[8,32,1024]{2,1,0:T(8,128)S(1)}, f32[2,8,1024]{2,1,0:T(8,128)S(1)}) custom-call(f32[8,32,1024]{2,1,0:T(8,128)S(1)} %copy-done), custom_call_target="tpu_custom_call" | custom-call | flops 5242880 | bytes 2097152 | tf_op jit(solution)/shard_map/interior/pallas_call | solution.py:100
  12.5 0.8 %collective-permute-done.2.tail_ref = f32[2,8,1024]{2,1,0:T(8,128)S(1)} collective-permute-done((f32[2,8,1024]{2,1,0:T(8,128)S(1)}, f32[2,8,1024]{2,1,0:T(8,128)S(1)}, u32[]{:S(2)}, u32[]{:S(2)}) %collective-permute-start.2) | collective-permute-done | bytes 65568 | tf_op jit(solution)/shard_map/ppermute | solution.py:330
  13.4 0.0 collective-permute-done.3.head_ref
  13.4 0.0 collective-permute-done.below_ref
  13.4 0.0 collective-permute-done.1.above_ref
  13.4 0.0 copy-done.1
  13.4 0.0 copy-done.2
  13.4 0.2 chunks.1
  13.6 16.8 %all_to_all.5.got_ref = f32[32,1,1152]{2,1,0:T(1,128)S(1)} all-to-all(f32[32,1,1152]{2,1,0:T(1,128)S(1)} %chunks.1), channel_id=1, replica_groups=mesh['space'=8,'path'=4] {'space','path'}, dimensions={0} | all-to-all | bytes 294912 | tf_op jit(solution)/shard_map/all_to_all | solution.py:341
  30.4 2.9 %final.1 = (f32[8]{0:T(128)}, f32[8,32,1024]{2,1,0:T(8,128)}, f32[8,32,1024]{2,1,0:T(8,128)}) custom-call(f32[32,1,1152]{2,1,0:T(1,128)S(1)} %all_to_all.5.got_ref, f32[8,32,1024]{2,1,0:T(8,128)S(1)} %copy-done, f32[8,32,1024]{2,1,0:T(8,128)S(1)} %get-tuple-element.16.drift_ref, f32[2,32,1024]{2,1,0:T(8,128)S(1)} %collective-permute-done.below_ref, ...), custom_call_target="tpu_custom_call" | custom-call | tf_op jit(solution)/shard_map/final/pallas_call | solution.py:312
Async XLA Ops:
  0.6 1.2 %copy-start = (f32[8,32,1024]{2,1,0:T(8,128)S(1)}, f32[8,32,1024]{2,1,0:T(8,128)}, u32[]{:S(2)}) copy-start(f32[8,32,1024]{2,1,0:T(8,128)} %f_ref.7) | copy-start | bytes 3145732
  1.9 11.4 %collective-permute-start = (f32[2,32,1024]{2,1,0:T(8,128)S(1)}, f32[2,32,1024]{2,1,0:T(8,128)S(1)}, u32[]{:S(2)}, u32[]{:S(2)}) collective-permute-start(f32[2,32,1024]{2,1,0:T(8,128)S(1)} %get-tuple-element.10), channel_id=1, source_target_pairs={{0,1},{1,2},{2,3},{4,5},{5,6},{6,7},{8,9},{9,10},{10,11},{12,13},{... | collective-permute-start | bytes 786440 | tf_op jit(solution)/shard_map/ppermute | solution.py:336
  4.3 9.1 %collective-permute-start.1 = (f32[2,32,1024]{2,1,0:T(8,128)S(1)}, f32[2,32,1024]{2,1,0:T(8,128)S(1)}, u32[]{:S(2)}, u32[]{:S(2)}) collective-permute-start(f32[2,32,1024]{2,1,0:T(8,128)S(1)} %get-tuple-element.11), channel_id=1, source_target_pairs={{1,0},{2,1},{3,2},{5,4},{6,5},{7,6},{9,8},{10,9},{11,10},{13,12},{... | collective-permute-start | bytes 786440 | tf_op jit(solution)/shard_map/ppermute | solution.py:338
  5.6 7.7 %collective-permute-start.2 = (f32[2,8,1024]{2,1,0:T(8,128)S(1)}, f32[2,8,1024]{2,1,0:T(8,128)S(1)}, u32[]{:S(2)}, u32[]{:S(2)}) collective-permute-start(f32[2,8,1024]{2,1,0:T(8,128)S(1)} %get-tuple-element.12), channel_id=1, source_target_pairs={{0,4},{4,8},{8,12},{12,16},{16,20},{20,24},{24,28},{28,0},{1,5},{5... | collective-permute-start | bytes 196616 | tf_op jit(solution)/shard_map/ppermute | solution.py:330
  8.0 5.4 %copy-start.1 = (f32[32,1024]{1,0:T(8,128)S(1)}, f32[32,1024]{1,0:T(8,128)}, u32[]{:S(2)}) copy-start(f32[32,1024]{1,0:T(8,128)} %start_ref.3) | copy-start | bytes 393220
  8.0 5.4 %copy-start.2 = (f32[32,1024]{1,0:T(8,128)S(1)}, f32[32,1024]{1,0:T(8,128)}, u32[]{:S(2)}) copy-start(f32[32,1024]{1,0:T(8,128)} %end_ref.3) | copy-start | bytes 393220
  8.0 5.3 %collective-permute-start.3 = (f32[2,8,1024]{2,1,0:T(8,128)S(1)}, f32[2,8,1024]{2,1,0:T(8,128)S(1)}, u32[]{:S(2)}, u32[]{:S(2)}) collective-permute-start(f32[2,8,1024]{2,1,0:T(8,128)S(1)} %get-tuple-element.13), channel_id=1, source_target_pairs={{0,28},{4,0},{8,4},{12,8},{16,12},{20,16},{24,20},{28,24},{1,29},{... | collective-permute-start | bytes 196616 | tf_op jit(solution)/shard_map/ppermute | solution.py:330

commit v5 on v4

--- a/solution.py
+++ b/solution.py
@@ -32,36 +32,87 @@
     return lax.broadcasted_iota(jnp.int32, shape, dim)
 
 
-def edge_kernel(f_ref, up_ref, down_ref, tail_ref, head_ref):
+def odd(axis):
+    return lax.rem(lax.axis_index(axis), 2) == 1
+
+
+def pick(flag, x, y):
+    return jnp.where(flag, x, y)
+
+
+def edge_kernel(f_ref, start_ref, end_ref, far_ref, near_strip_ref, far_strip_ref, tiles, sem):
     count, rows, _ = f_ref.shape
-    for s in range(count):
-        for r in range(2):
-            tail_ref[r, s : s + 1, :] = f_ref[s, rows - 2 + r : rows - 1 + r, :]
-            head_ref[r, s : s + 1, :] = f_ref[s, r : r + 1, :]
-    for s in range(2):
-        up_ref[s] = f_ref[count - 2 + s]
-        down_ref[s] = f_ref[s]
-
-
-def edges(f):
+    flag = odd("space")
+    copies = []
+    for i, at in enumerate((pl.ds(0, TILE), pl.ds(rows - TILE, TILE))):
+        copies.append(pltpu.make_async_copy(f_ref.at[:, at], tiles.at[i, pl.ds(0, count)], sem.at[3 * i]))
+        copies.append(pltpu.make_async_copy(start_ref.at[at], tiles.at[i, count], sem.at[3 * i + 1]))
+        copies.append(pltpu.make_async_copy(end_ref.at[at], tiles.at[i, count + 1], sem.at[3 * i + 2]))
+    base = pick(odd("path"), count - 2, 0)
+    copies.append(pltpu.make_async_copy(f_ref.at[pl.ds(base, 2)], far_ref, sem.at[6]))
+    for copy in copies:
+        copy.start()
+    for copy in copies[:-1]:
+        copy.wait()
+    for ref, low in ((near_strip_ref, flag), (far_strip_ref, jnp.logical_not(flag))):
+        side = pick(low, 0, 1)
+        at = pick(low, 0, TILE - 2)
+        face = pick(low, 0, TILE - 1)
+        ref[2] = jnp.zeros_like(ref[2])
+        for i in range(2):
+            ref[2, i : i + 1, :] = tiles[side, count + i, pl.ds(face, 1), :]
+        for s in range(count):
+            for r in range(2):
+                ref[r, s : s + 1, :] = tiles[side, s, pl.ds(at + r, 1), :]
+    copies[-1].wait()
+
+
+def edges(f, start, end):
     count, rows, cols = f.shape
-    pair = jax.ShapeDtypeStruct((2, rows, cols), F32)
-    strip = jax.ShapeDtypeStruct((2, count, cols), F32)
+    strip = jax.ShapeDtypeStruct((3, count, cols), F32)
     return pl.pallas_call(
         edge_kernel,
-        out_shape=(pair, pair, strip, strip),
-        in_specs=[VMEM],
-        out_specs=(VMEM, VMEM, VMEM, VMEM),
+        out_shape=(jax.ShapeDtypeStruct((2, rows, cols), F32), strip, strip),
+        in_specs=[pl.BlockSpec(memory_space=pltpu.MemorySpace.HBM)] * 3,
+        out_specs=[VMEM] * 3,
+        scratch_shapes=[pltpu.VMEM((2, count + 2, TILE, cols), F32), pltpu.SemaphoreType.DMA((7,))],
         compiler_params=PARAMS,
         name="edges",
-    )(f)
-
-
-def interior_kernel(f_ref, part_ref, drift_ref, rim_ref):
+    )(f, start, end)
+
+
+class Halo:
+    def __init__(self, m, near_ref, far_ref, near_strip_ref, far_strip_ref, start_ref, end_ref):
+        self.path, self.space = odd("path"), odd("space")
+        self.first = lax.axis_index("path") == 0
+        self.last = lax.axis_index("path") == m - 1
+        self.near, self.far = near_ref, far_ref
+        self.strips = near_strip_ref, far_strip_ref
+        self.start, self.end = start_ref, end_ref
+
+    def below(self, i, at):
+        got = pick(self.path, self.near[i, at, :], self.far[i, at, :])
+        return pick(self.first, self.start[at, :], got) if i else got
+
+    def above(self, i, at):
+        got = pick(self.path, self.far[i, at, :], self.near[i, at, :])
+        return got if i else pick(self.last, self.end[at, :], got)
+
+    def tail(self, *at):
+        return pick(self.space, self.strips[0][at], self.strips[1][at])
+
+    def head(self, *at):
+        return pick(self.space, self.strips[1][at], self.strips[0][at])
+
+
+def interior_kernel(f_ref, part_ref, drift_ref, rim_ref, near_ref):
     count, rows, cols = f_ref.shape
     tiles = rows // TILE
     row = iota((TILE, cols), 0)
     part_ref[...] = jnp.zeros_like(part_ref)
+    base = pick(odd("path"), 0, count - 2)
+    for s in range(2):
+        near_ref[s] = f_ref[base + s]
 
     def drift_sum(s, _):
         total = jnp.zeros((TILE, LANES), F32)
@@ -103,33 +154,35 @@
             jax.ShapeDtypeStruct((2 * count, LANES), F32),
             jax.ShapeDtypeStruct(f.shape, F32),
             jax.ShapeDtypeStruct((2, count, cols), F32),
+            jax.ShapeDtypeStruct((2, rows, cols), F32),
         ),
         in_specs=[VMEM],
-        out_specs=[VMEM] * 3,
+        out_specs=[VMEM] * 4,
         cost_estimate=pl.CostEstimate(flops=20 * count * rows * cols, transcendentals=0, bytes_accessed=8 * count * rows * cols),
         compiler_params=PARAMS,
         name="interior",
     )(f)
 
 
-def chunk_kernel(m, n, f_ref, below_ref, above_ref, tail_ref, head_ref, start_ref, end_ref, part_ref, rim_ref, out_ref):
+def chunk_kernel(m, n, f_ref, part_ref, rim_ref, *refs):
+    halo_refs, (out_ref, near_corner_ref, far_corner_ref) = refs[:6], refs[6:]
+    halo = Halo(m, *halo_refs)
     count, rows, cols = f_ref.shape
     tiles = rows // TILE
-    path = lax.axis_index("path")
-    space = lax.axis_index("space")
-    first = path == 0
-    last = path == m - 1
-
-    drift_a = rim_ref[0] + tail_ref[1]
-    drift_b = rim_ref[1] + head_ref[0]
+
+    for ref, low in ((near_corner_ref, halo.path), (far_corner_ref, jnp.logical_not(halo.path))):
+        s = pl.ds(pick(low, 0, count - 1), 1)
+        ref[0:1, :] = halo.tail(1, s)
+        ref[1:2, :] = halo.head(0, s)
+
+    drift_a = rim_ref[0] + halo.tail(1)
+    drift_b = rim_ref[1] + halo.head(0)
     drift = part_ref[0:count, :] + lanes_sum(drift_a * drift_a) + lanes_sum(drift_b * drift_b)
 
     totals = [jnp.zeros((TILE, LANES), F32) for _ in range(2)]
     for k in range(tiles):
         at = pl.ds(TILE * k, TILE)
-        prior = jnp.where(first, start_ref[at, :], below_ref[1, at, :])
-        after = jnp.where(last, end_ref[at, :], above_ref[0, at, :])
-        tangents = (f_ref[1, at, :] - prior, after - f_ref[count - 2, at, :])
+        tangents = (f_ref[1, at, :] - halo.below(1, at), halo.above(0, at) - f_ref[count - 2, at, :])
         totals = [a + lanes_sum(t * t) for a, t in zip(totals, tangents)]
     head_sum, tail_sum = [jnp.sum(a, axis=0, keepdims=True) for a in totals]
     sub = iota((TILE, LANES), 0)
@@ -142,62 +195,36 @@
     line = jnp.sum(spread, axis=0, keepdims=True)
 
     for j in range(m * n):
-        out_ref[j, :, 0:LANES] = line
-    right = lax.rem(space + 1, n) * m
-    left = lax.rem(space + n - 1, n) * m
-
-    def put(base, source):
-        out_ref[base, :, LANES:] = source
-
-    @pl.when(jnp.logical_not(first))
-    def _():
-        put(right + path - 1, f_ref[0, rows - 1 : rows, :])
-        put(left + path - 1, f_ref[0, 0:1, :])
-
-    @pl.when(jnp.logical_not(last))
-    def _():
-        put(right + path + 1, f_ref[count - 1, rows - 1 : rows, :])
-        put(left + path + 1, f_ref[count - 1, 0:1, :])
-
-    @pl.when(first)
-    def _():
-        put(right + path, start_ref[rows - 1 : rows, :])
-        put(left + path, start_ref[0:1, :])
-
-    @pl.when(last)
-    def _():
-        put(right + path, end_ref[rows - 1 : rows, :])
-        put(left + path, end_ref[0:1, :])
-
-
-def chunks(m, n, f, below, above, tail_in, head_in, start, end, part, rim):
+        out_ref[j] = line
+
+
+def chunks(m, n, f, part, rim, halo):
+    cols = f.shape[2]
+    corner = jax.ShapeDtypeStruct((2, cols), F32)
     return pl.pallas_call(
         functools.partial(chunk_kernel, m, n),
-        out_shape=jax.ShapeDtypeStruct((m * n, 1, LANES + f.shape[2]), F32),
+        out_shape=(jax.ShapeDtypeStruct((m * n, 1, LANES), F32), corner, corner),
         in_specs=[VMEM] * 9,
-        out_specs=VMEM,
+        out_specs=[VMEM] * 3,
         compiler_params=PARAMS,
         name="chunks",
-    )(f, below, above, tail_in, head_in, start, end, part, rim)
-
-
-def final_kernel(
-    m, n, got_ref, f_ref, drift_ref, below_ref, above_ref, tail_ref, head_ref, start_ref, end_ref,
-    ratio_ref, res_out, grad_out, resid, grad, outer, rim, sem,
-):
+    )(f, part, rim, *halo)
+
+
+def final_kernel(m, n, got_ref, near_corner_ref, far_corner_ref, f_ref, drift_ref, *refs):
+    halo_refs, (ratio_ref, res_out, grad_out, resid, grad, outer, rim, sem) = refs[:6], refs[6:]
+    halo = Halo(m, *halo_refs)
     count, rows, cols = f_ref.shape
     tiles = rows // TILE
     path = lax.axis_index("path")
-    space = lax.axis_index("space")
-    first = path == 0
-    last = path == m - 1
+    first, last = halo.first, halo.last
     path_lo = jnp.where(first, path, path - 1)
     path_hi = jnp.where(last, path, path + 1)
 
     def gathered(p):
-        total = got_ref[p, :, 0:LANES]
+        total = got_ref[p]
         for i in range(1, n):
-            total += got_ref[i * m + p, :, 0:LANES]
+            total += got_ref[i * m + p]
         return jnp.broadcast_to(total, (TILE, LANES))
 
     mine = gathered(path)
@@ -227,30 +254,36 @@
     scale = [widen(splat(t)) for t in range(count + 2)]
     column = jnp.sum(jnp.where(lane == sub + 1, ratio, 0.0), axis=1, keepdims=True)
     row = iota((TILE, cols), 0)
-    prev = lax.rem(space + n - 1, n) * m
-    nxt = lax.rem(space + 1, n) * m
+    fixed = halo.tail(2), halo.head(2)
+    corners = []
+    for i in range(2):
+        near, far = near_corner_ref[i : i + 1, :], far_corner_ref[i : i + 1, :]
+        low = pick(first, fixed[i][0:1], pick(halo.path, near, far))
+        high = pick(last, fixed[i][1:2], pick(halo.path, far, near))
+        corners.append((low, high))
 
     def at(k):
         return pl.ds(TILE * k, TILE)
 
     for k in range(tiles):
-        outer[0, at(k), :] = jnp.where(first, start_ref[at(k), :], below_ref[1, at(k), :])
-        outer[1, at(k), :] = jnp.where(last, end_ref[at(k), :], above_ref[0, at(k), :])
+        outer[0, at(k), :] = halo.below(1, at(k))
+        outer[1, at(k), :] = halo.above(0, at(k))
 
     def value(s, k):
-        where = {-2: (below_ref, 0), -1: (outer, 0), count: (outer, 1), count + 1: (above_ref, 1)}
-        ref, slot = where.get(s, (f_ref, s))
+        if s == -2:
+            return halo.below(0, at(k))
+        if s == count + 1:
+            return halo.above(1, at(k))
+        ref, slot = {-1: (outer, 0), count: (outer, 1)}.get(s, (f_ref, s))
         return ref[slot, at(k), :]
 
     for s in range(count):
         rim[0, s : s + 1, :] = f_ref[s, 0:1, :]
         rim[1, s : s + 1, :] = f_ref[s, rows - 1 : rows, :]
-    for far, mid, near, base, place in (
-        (tail_ref[0], tail_ref[1], rim[0], prev, TILE - 1),
-        (head_ref[1], head_ref[0], rim[1], nxt, TILE + rows),
+    for far, mid, near, (low, high), place in (
+        (halo.tail(0), halo.tail(1), rim[0], corners[0], TILE - 1),
+        (halo.head(1), halo.head(0), rim[1], corners[1], TILE + rows),
     ):
-        low = got_ref[base + path_lo, :, LANES:]
-        high = got_ref[base + path_hi, :, LANES:]
         ahead = jnp.where(row == count - 1, high, pltpu.roll(mid, count - 1, 0))
         behind = jnp.where(row == 0, low, pltpu.roll(mid, 1, 0))
         edge = column * (ahead - behind) - (far + near + sides(mid) - 3.0 * mid - mid * mid * mid)
@@ -259,10 +292,10 @@
 
     def residual_of(s):
         if s in (-1, count):
-            slot, q = (0, path_lo) if s < 0 else (1, path_hi)
-            top, bottom = got_ref[prev + q, :, LANES:], got_ref[nxt + q, :, LANES:]
+            slot = 0 if s < 0 else 1
+            top, bottom = corners[0][slot], corners[1][slot]
         else:
-            top, bottom = tail_ref[1, s : s + 1, :], head_ref[0, s : s + 1, :]
+            top, bottom = halo.tail(1, pl.ds(s, 1)), halo.head(0, pl.ds(s, 1))
         for k in range(tiles):
             if s in (-1, count):
                 c = outer[slot, at(k), :]
@@ -306,13 +339,13 @@
         copy.wait()
 
 
-def final(m, n, got, f, drift, below, above, tail_in, head_in, start, end):
+def final(m, n, got, corners, f, drift, halo):
     count, rows, cols = f.shape
     big = jax.ShapeDtypeStruct(f.shape, F32)
     return pl.pallas_call(
         functools.partial(final_kernel, m, n),
         out_shape=(jax.ShapeDtypeStruct((count,), F32), big, big),
-        in_specs=[VMEM] * 9,
+        in_specs=[VMEM] * 11,
         out_specs=(VMEM, ANY, ANY),
         scratch_shapes=[
             pltpu.VMEM((count + 2, rows + 2 * TILE, cols), F32),
@@ -323,23 +356,30 @@
         ],
         compiler_params=PARAMS,
         name="final",
-    )(got, f, drift, below, above, tail_in, head_in, start, end)
-
-
-def ring(x, n, step):
-    return lax.ppermute(x, "space", [(i, (i + step) % n) for i in range(n)])
+    )(got, *corners, f, drift, *halo)
+
+
+def swap(x, axis, kind, wrap):
+    size = lax.axis_size(axis)
+    pairs = [(i, i ^ 1) for i in range(size)]
+    if kind == 1:
+        pairs = [((i + 1) % size, (j + 1) % size) for i, j in pairs]
+        pairs = [(i, j) for i, j in pairs if wrap or abs(i - j) == 1]
+    return lax.ppermute(x, axis, pairs)
 
 
 def body(m, n, f, start, end):
-    up, down, tail, head = edges(f)
-    tail_in = ring(tail, n, 1)
-    below = lax.ppermute(up, "path", [(i, i + 1) for i in range(m - 1)])
-    head_in = ring(head, n, -1)
-    above = lax.ppermute(down, "path", [(i + 1, i) for i in range(m - 1)])
-    part, drift, rim = interior(f)
-    send = chunks(m, n, f, below, above, tail_in, head_in, start, end, part, rim)
+    far, near_strip, far_strip = edges(f, start, end)
+    far = swap(far, "path", 1, False)
+    far_strip = swap(far_strip, "space", 1, True)
+    near_strip = swap(near_strip, "space", 0, True)
+    part, drift, rim, near = interior(f)
+    near = swap(near, "path", 0, False)
+    halo = near, far, near_strip, far_strip, start, end
+    send, near_corner, far_corner = chunks(m, n, f, part, rim, halo)
     got = lax.all_to_all(send, ("space", "path"), 0, 0, tiled=True)
-    return final(m, n, got, f, drift, below, above, tail_in, head_in, start, end)
+    corners = swap(near_corner, "path", 0, False), swap(far_corner, "path", 1, False)
+    return final(m, n, got, corners, f, drift, halo)
 
 
 def solution(mesh):

time: 33.5 us -> 34.4 us (1.027)
  blocking collectives: 16.8 us -> 0 us
  waiting for transfers between devices: 0.83 us -> 9.87 us
  starting transfers between devices: 9.19 us -> 15.1 us
  local copies, waits for them, and re-layouts: 1.23 us -> 3.05 us
  Pallas kernels: 4.47 us -> 5.39 us
    all_to_all x1 -> x0, blocking collectives: 16.8 us -> none  [body(): got = lax.all_to_all(send, ('space', 'path'), 0, 0, tiled=True)]
    all_to_all x0 -> x1, waiting for transfers between devices: none -> 5.83 us  [body(): got = lax.all_to_all(send, ('space', 'path'), 0, 0, tiled=True)]
    all_to_all x0 -> x1, starting transfers between devices: none -> 3.91 us  [body(): got = lax.all_to_all(send, ('space', 'path'), 0, 0, tiled=True)]
    ppermute x4 -> x6, waiting for transfers between devices: 0.83 us -> 4.04 us  [swap(): return lax.ppermute(x, axis, pairs)]
    ppermute x4 -> x6, starting transfers between devices: 9.19 us -> 11.2 us  [swap(): return lax.ppermute(x, axis, pairs)]
    unnamed x6 -> x12, local copies, waits for them, and re-layouts: 1.23 us -> 3.05 us
    pallas_call x2, Pallas kernels: 0.24 us -> 1.12 us  [the longest x1 0.78 us: chunks(): pl.pallas_call(functools.partial(chunk_kernel, m, n), out_shape=(jax.Shap...]
  transfers between devices with their start and end apart: 4 -> 7, of which waited for: 1 -> 4; matrix products, arithmetic and copies ran while one was open for 0% -> 0% of each run, Pallas kernels for 4% -> 4%
where the time goes in v5:
time: 34.4 us; the launch traced here: 34.1 us
  starting transfers between devices  15.1 us (44%)
  waiting for transfers between devices  9.87 us (29%)
  Pallas kernels  5.39 us (16%)
  local copies, waits for them, and re-layouts  3.05 us (9%)
  between operations  0.72 us (2%)
    ppermute x6, starting transfers between devices, swap(): return lax.ppermute(x, axis, pairs)  11.2 us
    all_to_all x1, waiting for transfers between devices, body(): got = lax.all_to_all(send, ('space', 'path'), 0, 0, tiled=True)  5.83 us
    ppermute x6, waiting for transfers between devices, swap(): return lax.ppermute(x, axis, pairs)  4.04 us
    all_to_all x1, starting transfers between devices, body(): got = lax.all_to_all(send, ('space', 'path'), 0, 0, tiled=True)  3.91 us
    unnamed x12, local copies, waits for them, and re-layouts  3.05 us
    pallas_call x1, Pallas kernels, final(): pl.pallas_call(functools.partial(final_kernel, m, n), out_shape=(jax.Shap...  2.86 us
    pallas_call x1, Pallas kernels, interior(): pl.pallas_call(interior_kernel, out_shape=(jax.ShapeDtypeStruct((2 * coun...  1.41 us
    pallas_call x1, Pallas kernels, chunks(): pl.pallas_call(functools.partial(chunk_kernel, m, n), out_shape=(jax.Shap...  0.78 us
  transfers between devices with their start and end apart: 7, of which 4 were waited for; matrix products, arithmetic and copies ran while one was open for 0% of the time, Pallas kernels for 4%

profile of v5, /device:TPU:0, one launch (start us, length us, event | category | flops | bytes accessed | tf_op | source)
XLA Modules:
  0.0 34.1 jit_solution(14679822186223733809)
XLA Ops:
  0.6 0.0 copy-start
  0.6 1.2 %copy-done = f32[8,32,1024]{2,1,0:T(8,128)S(1)} copy-done((f32[8,32,1024]{2,1,0:T(8,128)S(1)}, f32[8,32,1024]{2,1,0:T(8,128)}, u32[]{:S(2)}) %copy-start) | copy-done | bytes 1048600
  1.9 0.0 copy-start.2
  1.9 0.9 %copy-done.2 = f32[32,1024]{1,0:T(8,128)S(1)} copy-done((f32[32,1024]{1,0:T(8,128)S(1)}, f32[32,1024]{1,0:T(8,128)}, u32[]{:S(2)}) %copy-start.2) | copy-done | bytes 131096
  2.8 0.0 copy-start.4
  2.8 0.9 %copy-done.4 = f32[32,1024]{1,0:T(8,128)S(1)} copy-done((f32[32,1024]{1,0:T(8,128)S(1)}, f32[32,1024]{1,0:T(8,128)}, u32[]{:S(2)}) %copy-start.4) | copy-done | bytes 131096
  3.7 0.3 edges.1
  4.0 0.0 copy-start.3
  4.0 0.0 copy-start.5
  4.0 0.8 %collective-permute-start.1 = (f32[2,32,1024]{2,1,0:T(8,128)S(1)}, f32[2,32,1024]{2,1,0:T(8,128)S(1)}, u32[]{:S(2)}, u32[]{:S(2)}) collective-permute-start(f32[2,32,1024]{2,1,0:T(8,128)S(1)} %get-tuple-element.16), channel_id=1, source_target_pairs={{1,2},{2,1},{5,6},{6,5},{9,10},{10,9},{13,14},{14,13},{17,18},{18,... | collective-permute-start | bytes 786440 | tf_op jit(solution)/shard_map/ppermute | solution.py:368
  4.9 1.4 %interior.1 = (f32[16,128]{1,0:T(8,128)S(1)}, f32[8,32,1024]{2,1,0:T(8,128)S(1)}, f32[2,8,1024]{2,1,0:T(8,128)S(1)}, f32[2,32,1024]{2,1,0:T(8,128)S(1)}) custom-call(f32[8,32,1024]{2,1,0:T(8,128)S(1)} %copy-done), custom_call_target="tpu_custom_call" | custom-call | flops 5242880 | bytes 2097152 | tf_op jit(solution)/shard_map/interior/pallas_call | solution.py:151
  6.3 4.3 %collective-permute-start = (f32[2,32,1024]{2,1,0:T(8,128)S(1)}, f32[2,32,1024]{2,1,0:T(8,128)S(1)}, u32[]{:S(2)}, u32[]{:S(2)}) collective-permute-start(f32[2,32,1024]{2,1,0:T(8,128)S(1)} %get-tuple-element.15), channel_id=1, source_target_pairs={{0,1},{1,0},{2,3},{3,2},{4,5},{5,4},{6,7},{7,6},{8,9},{9,8},{10,11... | collective-permute-start | bytes 786440 | tf_op jit(solution)/shard_map/ppermute | solution.py:368
  10.6 1.5 %collective-permute-start.2 = (f32[3,8,1024]{2,1,0:T(8,128)S(1)}, f32[3,8,1024]{2,1,0:T(8,128)S(1)}, u32[]{:S(2)}, u32[]{:S(2)}) collective-permute-start(f32[3,8,1024]{2,1,0:T(8,128)S(1)} %get-tuple-element.17), channel_id=1, source_target_pairs={{0,4},{4,0},{8,12},{12,8},{16,20},{20,16},{24,28},{28,24},{1,5},{5... | collective-permute-start | bytes 294920 | tf_op jit(solution)/shard_map/ppermute | solution.py:368
  12.1 3.5 %collective-permute-start.3 = (f32[3,8,1024]{2,1,0:T(8,128)S(1)}, f32[3,8,1024]{2,1,0:T(8,128)S(1)}, u32[]{:S(2)}, u32[]{:S(2)}) collective-permute-start(f32[3,8,1024]{2,1,0:T(8,128)S(1)} %get-tuple-element.18), channel_id=1, source_target_pairs={{4,8},{8,4},{12,16},{16,12},{20,24},{24,20},{28,0},{0,28},{5,9},{9... | collective-permute-start | bytes 294920 | tf_op jit(solution)/shard_map/ppermute | solution.py:368
  15.7 0.9 %collective-permute-done.2.refs_2_ = f32[3,8,1024]{2,1,0:T(8,128)S(1)} collective-permute-done((f32[3,8,1024]{2,1,0:T(8,128)S(1)}, f32[3,8,1024]{2,1,0:T(8,128)S(1)}, u32[]{:S(2)}, u32[]{:S(2)}) %collective-permute-start.2) | collective-permute-done | bytes 98336 | tf_op jit(solution)/shard_map/ppermute | solution.py:368
  16.5 2.9 %collective-permute-done.3.refs_3_ = f32[3,8,1024]{2,1,0:T(8,128)S(1)} collective-permute-done((f32[3,8,1024]{2,1,0:T(8,128)S(1)}, f32[3,8,1024]{2,1,0:T(8,128)S(1)}, u32[]{:S(2)}, u32[]{:S(2)}) %collective-permute-start.3) | collective-permute-done | bytes 98336 | tf_op jit(solution)/shard_map/ppermute | solution.py:368
  19.5 0.0 collective-permute-done.1.refs_1_
  19.5 0.0 collective-permute-done.refs_0_
  19.5 0.0 copy-done.3
  19.5 0.0 copy-done.5
  19.5 0.0 copy-start.1
  19.5 0.8 %chunks.1 = (f32[32,1,128]{2,1,0:T(1,128)}, f32[2,1024]{1,0:T(2,128)S(1)}, f32[2,1024]{1,0:T(2,128)S(1)}) custom-call(f32[8,32,1024]{2,1,0:T(8,128)S(1)} %copy-done, f32[16,128]{1,0:T(8,128)S(1)} %get-tuple-element.13.part_ref, f32[2,8,1024]{2,1,0:T(8,128)S(1)} %get-tuple-element.14.rim_ref, f32[2,32,1024]{2,1,0:T(8,128)S(1)} %collective-permute-done.refs_0_, ...), custom_call_target="tpu_custom_call" | custom-call | tf_op jit(solution)/shard_map/chunks/pallas_call | solution.py:204
  20.3 3.9 %all-to-all-start = ((f32[32,1,128]{2,1,0:T(1,128)}), f32[32,1,128]{2,1,0:T(1,128)S(1)}, u32[]{:S(2)}, u32[]{:S(2)}) async-start(f32[32,1,128]{2,1,0:T(1,128)} %get-tuple-element.19), calls=%async_computation | async-start | bytes 32768 | tf_op jit(solution)/shard_map/all_to_all | solution.py:380
  24.2 0.3 collective-permute-start.4
  24.5 0.6 %collective-permute-start.5 = (f32[2,1024]{1,0:T(2,128)S(1)}, f32[2,1024]{1,0:T(2,128)S(1)}, u32[]{:S(2)}, u32[]{:S(2)}) collective-permute-start(f32[2,1024]{1,0:T(2,128)S(1)} %get-tuple-element.21), channel_id=1, source_target_pairs={{1,2},{2,1},{5,6},{6,5},{9,10},{10,9},{13,14},{14,13},{17,18},{18,... | collective-permute-start | bytes 24584 | tf_op jit(solution)/shard_map/ppermute | solution.py:368
  25.2 0.3 collective-permute-done.4.near_corner_ref
  25.4 0.0 collective-permute-done.5.far_corner_ref
  25.4 5.8 %all-to-all-done.got_ref = f32[32,1,128]{2,1,0:T(1,128)S(1)} async-done(((f32[32,1,128]{2,1,0:T(1,128)}), f32[32,1,128]{2,1,0:T(1,128)S(1)}, u32[]{:S(2)}, u32[]{:S(2)}) %all-to-all-start) | async-done | bytes 16416 | tf_op jit(solution)/shard_map/all_to_all | solution.py:380
  31.3 0.0 copy-done.1
  31.3 2.9 %final.1 = (f32[8]{0:T(128)}, f32[8,32,1024]{2,1,0:T(8,128)}, f32[8,32,1024]{2,1,0:T(8,128)}) custom-call(f32[32,1,128]{2,1,0:T(1,128)S(1)} %all-to-all-done.got_ref, f32[2,1024]{1,0:T(2,128)S(1)} %collective-permute-done.4.near_corner_ref, f32[2,1024]{1,0:T(2,128)S(1)} %collective-permute-done.5.far_corner_ref, f32[8,32,1024]{2,1,0:T(8,128)S(1)} %copy-done.1, ...), custom_call_target="tpu_custom_call" | custom-call | tf_op jit(solution)/shard_map/final/pallas_call | solution.py:345
Async XLA Ops:
  0.6 1.2 %copy-start = (f32[8,32,1024]{2,1,0:T(8,128)S(1)}, f32[8,32,1024]{2,1,0:T(8,128)}, u32[]{:S(2)}) copy-start(f32[8,32,1024]{2,1,0:T(8,128)} %f_ref.7) | copy-start | bytes 3145732
  1.9 0.9 %copy-start.2 = (f32[32,1024]{1,0:T(8,128)S(1)}, f32[32,1024]{1,0:T(8,128)}, u32[]{:S(2)}) copy-start(f32[32,1024]{1,0:T(8,128)} %refs_4_.3) | copy-start | bytes 393220
  2.8 0.9 %copy-start.4 = (f32[32,1024]{1,0:T(8,128)S(1)}, f32[32,1024]{1,0:T(8,128)}, u32[]{:S(2)}) copy-start(f32[32,1024]{1,0:T(8,128)} %refs_5_.3) | copy-start | bytes 393220
  4.0 15.5 %copy-start.3 = (f32[32,1024]{1,0:T(8,128)S(1)}, f32[32,1024]{1,0:T(8,128)}, u32[]{:S(2)}) copy-start(f32[32,1024]{1,0:T(8,128)} %refs_4_.3) | copy-start | bytes 393220
  4.0 15.4 %copy-start.5 = (f32[32,1024]{1,0:T(8,128)S(1)}, f32[32,1024]{1,0:T(8,128)}, u32[]{:S(2)}) copy-start(f32[32,1024]{1,0:T(8,128)} %refs_5_.3) | copy-start | bytes 393220
  4.0 15.4 %collective-permute-start.1 = (f32[2,32,1024]{2,1,0:T(8,128)S(1)}, f32[2,32,1024]{2,1,0:T(8,128)S(1)}, u32[]{:S(2)}, u32[]{:S(2)}) collective-permute-start(f32[2,32,1024]{2,1,0:T(8,128)S(1)} %get-tuple-element.16), channel_id=1, source_target_pairs={{1,2},{2,1},{5,6},{6,5},{9,10},{10,9},{13,14},{14,13},{17,18},{18,... | collective-permute-start | bytes 786440 | tf_op jit(solution)/shard_map/ppermute | solution.py:368
  6.3 13.2 %collective-permute-start = (f32[2,32,1024]{2,1,0:T(8,128)S(1)}, f32[2,32,1024]{2,1,0:T(8,128)S(1)}, u32[]{:S(2)}, u32[]{:S(2)}) collective-permute-start(f32[2,32,1024]{2,1,0:T(8,128)S(1)} %get-tuple-element.15), channel_id=1, source_target_pairs={{0,1},{1,0},{2,3},{3,2},{4,5},{5,4},{6,7},{7,6},{8,9},{9,8},{10,11... | collective-permute-start | bytes 786440 | tf_op jit(solution)/shard_map/ppermute | solution.py:368
  10.6 5.9 %collective-permute-start.2 = (f32[3,8,1024]{2,1,0:T(8,128)S(1)}, f32[3,8,1024]{2,1,0:T(8,128)S(1)}, u32[]{:S(2)}, u32[]{:S(2)}) collective-permute-start(f32[3,8,1024]{2,1,0:T(8,128)S(1)} %get-tuple-element.17), channel_id=1, source_target_pairs={{0,4},{4,0},{8,12},{12,8},{16,20},{20,16},{24,28},{28,24},{1,5},{5... | collective-permute-start | bytes 294920 | tf_op jit(solution)/shard_map/ppermute | solution.py:368
  12.1 7.3 %collective-permute-start.3 = (f32[3,8,1024]{2,1,0:T(8,128)S(1)}, f32[3,8,1024]{2,1,0:T(8,128)S(1)}, u32[]{:S(2)}, u32[]{:S(2)}) collective-permute-start(f32[3,8,1024]{2,1,0:T(8,128)S(1)} %get-tuple-element.18), channel_id=1, source_target_pairs={{4,8},{8,4},{12,16},{16,12},{20,24},{24,20},{28,0},{0,28},{5,9},{9... | collective-permute-start | bytes 294920 | tf_op jit(solution)/shard_map/ppermute | solution.py:368
  19.5 11.8 %copy-start.1 = (f32[8,32,1024]{2,1,0:T(8,128)S(1)}, f32[8,32,1024]{2,1,0:T(8,128)}, u32[]{:S(2)}) copy-start(f32[8,32,1024]{2,1,0:T(8,128)} %f_ref.7) | copy-start | bytes 3145732
  20.3 11.0 %all-to-all-start = ((f32[32,1,128]{2,1,0:T(1,128)}), f32[32,1,128]{2,1,0:T(1,128)S(1)}, u32[]{:S(2)}, u32[]{:S(2)}) async-start(f32[32,1,128]{2,1,0:T(1,128)} %get-tuple-element.19), calls=%async_computation | async-start | bytes 32768 | tf_op jit(solution)/shard_map/all_to_all | solution.py:380
  24.2 1.2 %collective-permute-start.4 = (f32[2,1024]{1,0:T(2,128)S(1)}, f32[2,1024]{1,0:T(2,128)S(1)}, u32[]{:S(2)}, u32[]{:S(2)}) collective-permute-start(f32[2,1024]{1,0:T(2,128)S(1)} %get-tuple-element.20), channel_id=1, source_target_pairs={{0,1},{1,0},{2,3},{3,2},{4,5},{5,4},{6,7},{7,6},{8,9},{9,8},{10,11... | collective-permute-start | bytes 24584 | tf_op jit(solution)/shard_map/ppermute | solution.py:368
  24.5 0.9 %collective-permute-start.5 = (f32[2,1024]{1,0:T(2,128)S(1)}, f32[2,1024]{1,0:T(2,128)S(1)}, u32[]{:S(2)}, u32[]{:S(2)}) collective-permute-start(f32[2,1024]{1,0:T(2,128)S(1)} %get-tuple-element.21), channel_id=1, source_target_pairs={{1,2},{2,1},{5,6},{6,5},{9,10},{10,9},{13,14},{14,13},{17,18},{18,... | collective-permute-start | bytes 24584 | tf_op jit(solution)/shard_map/ppermute | solution.py:368

commit v6 on v3

--- a/solution.py
+++ b/solution.py
@@ -13,6 +13,7 @@
 EPS = 1e-06
 VMEM = pl.BlockSpec(memory_space=pltpu.VMEM)
 ANY = pl.BlockSpec(memory_space=pl.ANY)
+EDGE_VMEM = 66_200_000
 PARAMS = pltpu.CompilerParams(vmem_limit_bytes=16 * 2**20)
 
 
@@ -32,29 +33,47 @@
     return lax.broadcasted_iota(jnp.int32, shape, dim)
 
 
-def edge_kernel(f_ref, up_ref, down_ref, tail_ref, head_ref):
+def odd(axis):
+    return lax.rem(lax.axis_index(axis), 2) == 1
+
+
+def edge_kernel(f_ref, start_ref, end_ref, up_ref, down_ref, tail_ref, head_ref, tiles, sem):
     count, rows, _ = f_ref.shape
-    for s in range(count):
-        for r in range(2):
-            tail_ref[r, s : s + 1, :] = f_ref[s, rows - 2 + r : rows - 1 + r, :]
-            head_ref[r, s : s + 1, :] = f_ref[s, r : r + 1, :]
-    for s in range(2):
-        up_ref[s] = f_ref[count - 2 + s]
-        down_ref[s] = f_ref[s]
-
-
-def edges(f):
+    sides_at = pl.ds(rows - TILE, TILE), pl.ds(0, TILE)
+    copies = [pltpu.make_async_copy(f_ref.at[pl.ds(count - 2, 2)], up_ref, sem.at[0])]
+    for i, at in enumerate(sides_at):
+        copies.append(pltpu.make_async_copy(f_ref.at[:, at], tiles.at[i, pl.ds(0, count)], sem.at[3 * i + 1]))
+        copies.append(pltpu.make_async_copy(start_ref.at[at], tiles.at[i, count], sem.at[3 * i + 2]))
+        copies.append(pltpu.make_async_copy(end_ref.at[at], tiles.at[i, count + 1], sem.at[3 * i + 3]))
+    copies.append(pltpu.make_async_copy(f_ref.at[pl.ds(0, 2)], down_ref, sem.at[7]))
+    for copy in copies:
+        copy.start()
+    for copy in copies[1:7]:
+        copy.wait()
+    for i, (ref, at, face) in enumerate(((tail_ref, TILE - 2, TILE - 1), (head_ref, 0, 0))):
+        ref[2] = jnp.zeros_like(ref[2])
+        for j in range(2):
+            ref[2, j : j + 1, :] = tiles[i, count + j, face : face + 1, :]
+        for s in range(count):
+            for r in range(2):
+                ref[r, s : s + 1, :] = tiles[i, s, at + r : at + r + 1, :]
+    copies[0].wait()
+    copies[7].wait()
+
+
+def edges(f, start, end):
     count, rows, cols = f.shape
     pair = jax.ShapeDtypeStruct((2, rows, cols), F32)
-    strip = jax.ShapeDtypeStruct((2, count, cols), F32)
+    strip = jax.ShapeDtypeStruct((3, count, cols), F32)
     return pl.pallas_call(
         edge_kernel,
         out_shape=(pair, pair, strip, strip),
-        in_specs=[VMEM],
-        out_specs=(VMEM, VMEM, VMEM, VMEM),
-        compiler_params=PARAMS,
+        in_specs=[ANY] * 3,
+        out_specs=[VMEM] * 4,
+        scratch_shapes=[pltpu.VMEM((2, count + 2, TILE, cols), F32), pltpu.SemaphoreType.DMA((8,))],
+        compiler_params=pltpu.CompilerParams(vmem_limit_bytes=EDGE_VMEM),
         name="edges",
-    )(f)
+    )(f, start, end)
 
 
 def interior_kernel(f_ref, part_ref, drift_ref, rim_ref):
@@ -112,13 +131,21 @@
     )(f)
 
 
-def chunk_kernel(m, n, f_ref, below_ref, tail_ref, head_ref, start_ref, end_ref, part_ref, rim_ref, out_ref):
+def chunk_kernel(
+    m, n, f_ref, below_ref, tail_ref, head_ref, start_ref, end_ref, part_ref, rim_ref,
+    out_ref, near_corner_ref, far_corner_ref,
+):
     count, rows, cols = f_ref.shape
     tiles = rows // TILE
     path = lax.axis_index("path")
-    space = lax.axis_index("space")
     first = path == 0
     last = path == m - 1
+
+    flag = odd("path")
+    for ref, low in ((near_corner_ref, flag), (far_corner_ref, jnp.logical_not(flag))):
+        s = pl.ds(jnp.where(low, 0, count - 1), 1)
+        ref[0:1, :] = tail_ref[1, s, :]
+        ref[1:2, :] = head_ref[0, s, :]
 
     drift_a = rim_ref[0] + tail_ref[1]
     drift_b = rim_ref[1] + head_ref[0]
@@ -147,62 +174,37 @@
     line += jnp.where(lane[0:1] == 2 * count, tan_last, 0.0)
 
     for j in range(m * n):
-        out_ref[j, :, 0:LANES] = line
-    right = lax.rem(space + 1, n) * m
-    left = lax.rem(space + n - 1, n) * m
-
-    def put(base, source):
-        out_ref[base, :, LANES:] = source
-
-    @pl.when(jnp.logical_not(first))
-    def _():
-        put(right + path - 1, f_ref[0, rows - 1 : rows, :])
-        put(left + path - 1, f_ref[0, 0:1, :])
-
-    @pl.when(jnp.logical_not(last))
-    def _():
-        put(right + path + 1, f_ref[count - 1, rows - 1 : rows, :])
-        put(left + path + 1, f_ref[count - 1, 0:1, :])
-
-    @pl.when(first)
-    def _():
-        put(right + path, start_ref[rows - 1 : rows, :])
-        put(left + path, start_ref[0:1, :])
-
-    @pl.when(last)
-    def _():
-        put(right + path, end_ref[rows - 1 : rows, :])
-        put(left + path, end_ref[0:1, :])
+        out_ref[j] = line
 
 
 def chunks(m, n, f, below, tail_in, head_in, start, end, part, rim):
+    corner = jax.ShapeDtypeStruct((2, f.shape[2]), F32)
     return pl.pallas_call(
         functools.partial(chunk_kernel, m, n),
-        out_shape=jax.ShapeDtypeStruct((m * n, 1, LANES + f.shape[2]), F32),
+        out_shape=(jax.ShapeDtypeStruct((m * n, 1, LANES), F32), corner, corner),
         in_specs=[VMEM] * 8,
-        out_specs=VMEM,
+        out_specs=[VMEM] * 3,
         compiler_params=PARAMS,
         name="chunks",
     )(f, below, tail_in, head_in, start, end, part, rim)
 
 
 def final_kernel(
-    m, n, got_ref, f_ref, drift_ref, below_ref, above_ref, tail_ref, head_ref, start_ref, end_ref,
+    m, n, got_ref, near_corner_ref, far_corner_ref, f_ref, drift_ref, below_ref, above_ref, tail_ref, head_ref, start_ref, end_ref,
     ratio_ref, res_out, grad_out, resid, grad, outer, rim, sem,
 ):
     count, rows, cols = f_ref.shape
     tiles = rows // TILE
     path = lax.axis_index("path")
-    space = lax.axis_index("space")
     first = path == 0
     last = path == m - 1
     path_lo = jnp.where(first, path, path - 1)
     path_hi = jnp.where(last, path, path + 1)
 
     def gathered(p):
-        total = got_ref[p, :, 0:LANES]
+        total = got_ref[p]
         for i in range(1, n):
-            total += got_ref[i * m + p, :, 0:LANES]
+            total += got_ref[i * m + p]
         return jnp.broadcast_to(total, (TILE, LANES))
 
     mine = gathered(path)
@@ -231,8 +233,13 @@
     scale = [widen(splat(t)) for t in range(count + 2)]
     column = jnp.sum(jnp.where(lane == sub + 1, ratio, 0.0), axis=1, keepdims=True)
     row = iota((TILE, cols), 0)
-    prev = lax.rem(space + n - 1, n) * m
-    nxt = lax.rem(space + 1, n) * m
+    flag = odd("path")
+    corners = []
+    for i, fixed in enumerate((tail_ref, head_ref)):
+        near, far = near_corner_ref[i : i + 1, :], far_corner_ref[i : i + 1, :]
+        low = jnp.where(first, fixed[2, 0:1, :], jnp.where(flag, near, far))
+        high = jnp.where(last, fixed[2, 1:2, :], jnp.where(flag, far, near))
+        corners.append((low, high))
 
     def at(k):
         return pl.ds(TILE * k, TILE)
@@ -249,12 +256,10 @@
     for s in range(count):
         rim[0, s : s + 1, :] = f_ref[s, 0:1, :]
         rim[1, s : s + 1, :] = f_ref[s, rows - 1 : rows, :]
-    for far, mid, near, base, place in (
-        (tail_ref[0], tail_ref[1], rim[0], prev, TILE - 1),
-        (head_ref[1], head_ref[0], rim[1], nxt, TILE + rows),
+    for far, mid, near, (low, high), place in (
+        (tail_ref[0], tail_ref[1], rim[0], corners[0], TILE - 1),
+        (head_ref[1], head_ref[0], rim[1], corners[1], TILE + rows),
     ):
-        low = got_ref[base + path_lo, :, LANES:]
-        high = got_ref[base + path_hi, :, LANES:]
         ahead = jnp.where(row == count - 1, high, pltpu.roll(mid, count - 1, 0))
         behind = jnp.where(row == 0, low, pltpu.roll(mid, 1, 0))
         edge = column * (ahead - behind) - (far + near + sides(mid) - 3.0 * mid - mid * mid * mid)
@@ -263,8 +268,8 @@
 
     def residual_of(s):
         if s in (-1, count):
-            slot, q = (0, path_lo) if s < 0 else (1, path_hi)
-            top, bottom = got_ref[prev + q, :, LANES:], got_ref[nxt + q, :, LANES:]
+            slot = 0 if s < 0 else 1
+            top, bottom = corners[0][slot], corners[1][slot]
         else:
             top, bottom = tail_ref[1, s : s + 1, :], head_ref[0, s : s + 1, :]
         for k in range(tiles):
@@ -310,13 +315,13 @@
         copy.wait()
 
 
-def final(m, n, got, f, drift, below, above, tail_in, head_in, start, end):
+def final(m, n, got, corners, f, drift, below, above, tail_in, head_in, start, end):
     count, rows, cols = f.shape
     big = jax.ShapeDtypeStruct(f.shape, F32)
     return pl.pallas_call(
         functools.partial(final_kernel, m, n),
         out_shape=(jax.ShapeDtypeStruct((count,), F32), big, big),
-        in_specs=[VMEM] * 9,
+        in_specs=[VMEM] * 11,
         out_specs=(VMEM, ANY, ANY),
         scratch_shapes=[
             pltpu.VMEM((count + 2, rows + 2 * TILE, cols), F32),
@@ -327,23 +332,30 @@
         ],
         compiler_params=PARAMS,
         name="final",
-    )(got, f, drift, below, above, tail_in, head_in, start, end)
-
-
-def ring(x, n, step):
-    return lax.ppermute(x, "space", [(i, (i + step) % n) for i in range(n)])
+    )(got, *corners, f, drift, below, above, tail_in, head_in, start, end)
+
+
+def ring(x, axis, step):
+    size = lax.axis_size(axis)
+    return lax.ppermute(x, axis, [(i, (i + step) % size) for i in range(size)])
+
+
+def swap(x, axis, kind):
+    size = lax.axis_size(axis)
+    return lax.ppermute(x, axis, [((i + kind) % size, ((i ^ 1) + kind) % size) for i in range(size)])
 
 
 def body(m, n, f, start, end):
-    up, down, tail, head = edges(f)
-    tail_in = ring(tail, n, 1)
-    below = lax.ppermute(up, "path", [(i, i + 1) for i in range(m - 1)])
-    head_in = ring(head, n, -1)
-    above = lax.ppermute(down, "path", [(i + 1, i) for i in range(m - 1)])
+    up, down, tail, head = edges(f, start, end)
+    tail_in = ring(tail, "space", 1)
+    below = ring(up, "path", 1)
+    head_in = ring(head, "space", -1)
+    above = ring(down, "path", -1)
     part, drift, rim = interior(f)
-    send = chunks(m, n, f, below, tail_in, head_in, start, end, part, rim)
+    send, near_corner, far_corner = chunks(m, n, f, below, tail_in, head_in, start, end, part, rim)
     got = lax.all_to_all(send, ("space", "path"), 0, 0, tiled=True)
-    return final(m, n, got, f, drift, below, above, tail_in, head_in, start, end)
+    corners = swap(near_corner, "path", 0), swap(far_corner, "path", 1)
+    return final(m, n, got, corners, f, drift, below, above, tail_in, head_in, start, end)
 
 
 def solution(mesh):

time: 30.6 us -> 30.4 us (level)
  Pallas kernels: 5.05 us -> 7.1 us
  waiting for transfers between devices: 8 us -> 6.39 us
  starting transfers between devices: 15.4 us -> 14.8 us
    pallas_call x1, Pallas kernels: 0.07 us -> 2.17 us  [edges(): pl.pallas_call(edge_kernel, out_shape=(pair, pair, strip, strip), in_spec...]
    all_to_all x1, waiting for transfers between devices: 4.99 us -> 3.66 us  [body(): got = lax.all_to_all(send, ('space', 'path'), 0, 0, tiled=True)]
    all_to_all x1, starting transfers between devices: 6.23 us -> 5.09 us  [body(): got = lax.all_to_all(send, ('space', 'path'), 0, 0, tiled=True)]
    ppermute x4 -> x6, starting transfers between devices: 9.19 us -> 9.75 us  [the longest x4 7.81 us: ring(): return lax.ppermute(x, axis, [(i, (i + step) % size) for i in range(size)])]
    ppermute x4 -> x6, waiting for transfers between devices: 3.01 us -> 2.72 us  [the longest x2 1.46 us: swap(): lax.ppermute(x, axis, [((i + kind) % size, ((i ^ 1) + kind) % size) for i...]
  transfers between devices with their start and end apart: 5 -> 7, of which waited for: 3 -> 4; matrix products, arithmetic and copies ran while one was open for 0% -> 0% of each run, Pallas kernels for 5% -> 7%
where the time goes in v6:
time: 30.4 us; the launch traced here: 30.2 us
  starting transfers between devices  14.8 us (49%)
  Pallas kernels  7.1 us (23%)
  waiting for transfers between devices  6.39 us (21%)
  local copies, waits for them, and re-layouts  1.24 us (4%)
  between operations  0.67 us (2%)
    ppermute x4, starting transfers between devices, ring(): return lax.ppermute(x, axis, [(i, (i + step) % size) for i in range(size)])  7.81 us
    all_to_all x1, starting transfers between devices, body(): got = lax.all_to_all(send, ('space', 'path'), 0, 0, tiled=True)  5.09 us
    all_to_all x1, waiting for transfers between devices, body(): got = lax.all_to_all(send, ('space', 'path'), 0, 0, tiled=True)  3.66 us
    pallas_call x1, Pallas kernels, final(): pl.pallas_call(functools.partial(final_kernel, m, n), out_shape=(jax.Shap...  2.78 us
    pallas_call x1, Pallas kernels, edges(): pl.pallas_call(edge_kernel, out_shape=(pair, pair, strip, strip), in_spec...  2.17 us
    ppermute x2, starting transfers between devices, swap(): lax.ppermute(x, axis, [((i + kind) % size, ((i ^ 1) + kind) % size) for i...  1.95 us
    ppermute x2, waiting for transfers between devices, swap(): lax.ppermute(x, axis, [((i + kind) % size, ((i ^ 1) + kind) % size) for i...  1.46 us
    pallas_call x1, Pallas kernels, interior(): pl.pallas_call(interior_kernel, out_shape=(jax.ShapeDtypeStruct((2 * coun...  1.38 us
  transfers between devices with their start and end apart: 7, of which 4 were waited for; matrix products, arithmetic and copies ran while one was open for 0% of the time, Pallas kernels for 7%

profile of v6, /device:TPU:0, one launch (start us, length us, event | category | flops | bytes accessed | tf_op | source)
XLA Modules:
  0.0 30.2 jit_solution(3072680077440317113)
XLA Ops:
  0.6 2.2 %edges.1 = (f32[2,32,1024]{2,1,0:T(8,128)}, f32[2,32,1024]{2,1,0:T(8,128)}, f32[3,8,1024]{2,1,0:T(8,128)}, f32[3,8,1024]{2,1,0:T(8,128)}) custom-call(f32[8,32,1024]{2,1,0:T(8,128)} %f_ref.7, f32[32,1024]{1,0:T(8,128)} %start_ref.5, f32[32,1024]{1,0:T(8,128)} %end_ref.5), custom_call_target="tpu_custom_call" | custom-call | tf_op jit(solution)/shard_map/edges/pallas_call | solution.py:68
  2.8 0.5 %collective-permute-start = (f32[2,32,1024]{2,1,0:T(8,128)}, f32[2,32,1024]{2,1,0:T(8,128)S(1)}, u32[]{:S(2)}, u32[]{:S(2)}) collective-permute-start(f32[2,32,1024]{2,1,0:T(8,128)} %get-tuple-element.13), channel_id=1, source_target_pairs={{0,1},{1,2},{2,3},{3,0},{4,5},{5,6},{6,7},{7,4},{8,9},{9,10},{10,1... | collective-permute-start | bytes 786440 | tf_op jit(solution)/shard_map/ppermute | solution.py:340
  3.3 2.0 %collective-permute-start.5 = (f32[2,32,1024]{2,1,0:T(8,128)}, f32[2,32,1024]{2,1,0:T(8,128)S(1)}, u32[]{:S(2)}, u32[]{:S(2)}) collective-permute-start(f32[2,32,1024]{2,1,0:T(8,128)} %get-tuple-element.22), channel_id=1, source_target_pairs={{0,3},{1,0},{2,1},{3,2},{4,7},{5,4},{6,5},{7,6},{8,11},{9,8},{10,9... | collective-permute-start | bytes 786440 | tf_op jit(solution)/shard_map/ppermute | solution.py:340
  5.3 2.3 %collective-permute-start.1 = (f32[3,8,1024]{2,1,0:T(8,128)}, f32[3,8,1024]{2,1,0:T(8,128)S(1)}, u32[]{:S(2)}, u32[]{:S(2)}) collective-permute-start(f32[3,8,1024]{2,1,0:T(8,128)} %get-tuple-element.14), channel_id=1, source_target_pairs={{0,4},{4,8},{8,12},{12,16},{16,20},{20,24},{24,28},{28,0},{1,5},{5... | collective-permute-start | bytes 294920 | tf_op jit(solution)/shard_map/ppermute | solution.py:340
  7.6 3.0 %collective-permute-start.2 = (f32[3,8,1024]{2,1,0:T(8,128)}, f32[3,8,1024]{2,1,0:T(8,128)S(1)}, u32[]{:S(2)}, u32[]{:S(2)}) collective-permute-start(f32[3,8,1024]{2,1,0:T(8,128)} %get-tuple-element.15), channel_id=1, source_target_pairs={{0,28},{4,0},{8,4},{12,8},{16,12},{20,16},{24,20},{28,24},{1,29},{... | collective-permute-start | bytes 294920 | tf_op jit(solution)/shard_map/ppermute | solution.py:340
  10.6 0.0 copy-start
  10.6 1.2 %copy-done = f32[8,32,1024]{2,1,0:T(8,128)S(1)} copy-done((f32[8,32,1024]{2,1,0:T(8,128)S(1)}, f32[8,32,1024]{2,1,0:T(8,128)}, u32[]{:S(2)}) %copy-start) | copy-done | bytes 1048600
  11.8 0.0 copy-start.2
  11.8 0.0 copy-start.3
  11.8 1.4 %interior.1 = (f32[24,128]{1,0:T(8,128)S(1)}, f32[8,32,1024]{2,1,0:T(8,128)S(1)}, f32[2,8,1024]{2,1,0:T(8,128)S(1)}) custom-call(f32[8,32,1024]{2,1,0:T(8,128)S(1)} %copy-done), custom_call_target="tpu_custom_call" | custom-call | flops 5242880 | bytes 2097152 | tf_op jit(solution)/shard_map/interior/pallas_call | solution.py:119
  13.2 0.0 copy-start.1
  13.2 0.5 %collective-permute-done.1.tail_ref = f32[3,8,1024]{2,1,0:T(8,128)S(1)} collective-permute-done((f32[3,8,1024]{2,1,0:T(8,128)}, f32[3,8,1024]{2,1,0:T(8,128)S(1)}, u32[]{:S(2)}, u32[]{:S(2)}) %collective-permute-start.1) | collective-permute-done | bytes 98336 | tf_op jit(solution)/shard_map/ppermute | solution.py:340
  13.8 0.8 %collective-permute-done.2.head_ref = f32[3,8,1024]{2,1,0:T(8,128)S(1)} collective-permute-done((f32[3,8,1024]{2,1,0:T(8,128)}, f32[3,8,1024]{2,1,0:T(8,128)S(1)}, u32[]{:S(2)}, u32[]{:S(2)}) %collective-permute-start.2) | collective-permute-done | bytes 98336 | tf_op jit(solution)/shard_map/ppermute | solution.py:340
  14.5 0.0 collective-permute-done.below_ref
  14.5 0.0 copy-done.2
  14.5 0.0 copy-done.3
  14.5 0.8 %chunks.1 = (f32[32,1,128]{2,1,0:T(1,128)}, f32[2,1024]{1,0:T(2,128)S(1)}, f32[2,1024]{1,0:T(2,128)S(1)}) custom-call(f32[8,32,1024]{2,1,0:T(8,128)S(1)} %copy-done, f32[2,32,1024]{2,1,0:T(8,128)S(1)} %collective-permute-done.below_ref, f32[3,8,1024]{2,1,0:T(8,128)S(1)} %collective-permute-done.1.tail_ref, ...), custom_call_target="tpu_custom_call" | custom-call | tf_op jit(solution)/shard_map/chunks/pallas_call | solution.py:182
  15.3 5.1 %all-to-all-start = ((f32[32,1,128]{2,1,0:T(1,128)}), f32[32,1,128]{2,1,0:T(1,128)S(1)}, u32[]{:S(2)}, u32[]{:S(2)}) async-start(f32[32,1,128]{2,1,0:T(1,128)} %get-tuple-element.18), calls=%async_computation | async-start | bytes 32768 | tf_op jit(solution)/shard_map/all_to_all | solution.py:356
  20.4 0.3 %collective-permute-start.3 = (f32[2,1024]{1,0:T(2,128)S(1)}, f32[2,1024]{1,0:T(2,128)S(1)}, u32[]{:S(2)}, u32[]{:S(2)}) collective-permute-start(f32[2,1024]{1,0:T(2,128)S(1)} %get-tuple-element.19), channel_id=1, source_target_pairs={{0,1},{1,0},{2,3},{3,2},{4,5},{5,4},{6,7},{7,6},{8,9},{9,8},{10,11... | collective-permute-start | bytes 24584 | tf_op jit(solution)/shard_map/ppermute | solution.py:345
  20.7 1.6 %collective-permute-start.4 = (f32[2,1024]{1,0:T(2,128)S(1)}, f32[2,1024]{1,0:T(2,128)S(1)}, u32[]{:S(2)}, u32[]{:S(2)}) collective-permute-start(f32[2,1024]{1,0:T(2,128)S(1)} %get-tuple-element.20), channel_id=1, source_target_pairs={{1,2},{2,1},{3,0},{0,3},{5,6},{6,5},{7,4},{4,7},{9,10},{10,9},{11,... | collective-permute-start | bytes 24584 | tf_op jit(solution)/shard_map/ppermute | solution.py:345
  22.3 0.0 collective-permute-done.5.above_ref
  22.3 0.0 collective-permute-done.3.near_corner_ref
  22.3 1.5 %collective-permute-done.4.far_corner_ref = f32[2,1024]{1,0:T(2,128)S(1)} collective-permute-done((f32[2,1024]{1,0:T(2,128)S(1)}, f32[2,1024]{1,0:T(2,128)S(1)}, u32[]{:S(2)}, u32[]{:S(2)}) %collective-permute-start.4) | collective-permute-done | bytes 8224 | tf_op jit(solution)/shard_map/ppermute | solution.py:345
  23.8 3.7 %all-to-all-done.got_ref = f32[32,1,128]{2,1,0:T(1,128)S(1)} async-done(((f32[32,1,128]{2,1,0:T(1,128)}), f32[32,1,128]{2,1,0:T(1,128)S(1)}, u32[]{:S(2)}, u32[]{:S(2)}) %all-to-all-start) | async-done | bytes 16416 | tf_op jit(solution)/shard_map/all_to_all | solution.py:356
  27.5 0.0 copy-done.1
  27.5 2.8 %final.1 = (f32[8]{0:T(128)}, f32[8,32,1024]{2,1,0:T(8,128)}, f32[8,32,1024]{2,1,0:T(8,128)}) custom-call(f32[32,1,128]{2,1,0:T(1,128)S(1)} %all-to-all-done.got_ref, f32[2,1024]{1,0:T(2,128)S(1)} %collective-permute-done.3.near_corner_ref, f32[2,1024]{1,0:T(2,128)S(1)} %collective-permute-done.4.far_corner_ref, f32[8,32,1024]{2,1,0:T(8,128)S(1)} %copy-done.1, ...), custom_call_target="tpu_custom_call" | custom-call | tf_op jit(solution)/shard_map/final/pallas_call | solution.py:321
Async XLA Ops:
  2.8 11.7 %collective-permute-start = (f32[2,32,1024]{2,1,0:T(8,128)}, f32[2,32,1024]{2,1,0:T(8,128)S(1)}, u32[]{:S(2)}, u32[]{:S(2)}) collective-permute-start(f32[2,32,1024]{2,1,0:T(8,128)} %get-tuple-element.13), channel_id=1, source_target_pairs={{0,1},{1,2},{2,3},{3,0},{4,5},{5,6},{6,7},{7,4},{8,9},{9,10},{10,1... | collective-permute-start | bytes 786440 | tf_op jit(solution)/shard_map/ppermute | solution.py:340
  3.3 19.0 %collective-permute-start.5 = (f32[2,32,1024]{2,1,0:T(8,128)}, f32[2,32,1024]{2,1,0:T(8,128)S(1)}, u32[]{:S(2)}, u32[]{:S(2)}) collective-permute-start(f32[2,32,1024]{2,1,0:T(8,128)} %get-tuple-element.22), channel_id=1, source_target_pairs={{0,3},{1,0},{2,1},{3,2},{4,7},{5,4},{6,5},{7,6},{8,11},{9,8},{10,9... | collective-permute-start | bytes 786440 | tf_op jit(solution)/shard_map/ppermute | solution.py:340
  5.3 8.4 %collective-permute-start.1 = (f32[3,8,1024]{2,1,0:T(8,128)}, f32[3,8,1024]{2,1,0:T(8,128)S(1)}, u32[]{:S(2)}, u32[]{:S(2)}) collective-permute-start(f32[3,8,1024]{2,1,0:T(8,128)} %get-tuple-element.14), channel_id=1, source_target_pairs={{0,4},{4,8},{8,12},{12,16},{16,20},{20,24},{24,28},{28,0},{1,5},{5... | collective-permute-start | bytes 294920 | tf_op jit(solution)/shard_map/ppermute | solution.py:340
  7.6 6.9 %collective-permute-start.2 = (f32[3,8,1024]{2,1,0:T(8,128)}, f32[3,8,1024]{2,1,0:T(8,128)S(1)}, u32[]{:S(2)}, u32[]{:S(2)}) collective-permute-start(f32[3,8,1024]{2,1,0:T(8,128)} %get-tuple-element.15), channel_id=1, source_target_pairs={{0,28},{4,0},{8,4},{12,8},{16,12},{20,16},{24,20},{28,24},{1,29},{... | collective-permute-start | bytes 294920 | tf_op jit(solution)/shard_map/ppermute | solution.py:340
  10.6 1.2 %copy-start = (f32[8,32,1024]{2,1,0:T(8,128)S(1)}, f32[8,32,1024]{2,1,0:T(8,128)}, u32[]{:S(2)}) copy-start(f32[8,32,1024]{2,1,0:T(8,128)} %f_ref.7) | copy-start | bytes 3145732
  11.8 2.7 %copy-start.2 = (f32[32,1024]{1,0:T(8,128)S(1)}, f32[32,1024]{1,0:T(8,128)}, u32[]{:S(2)}) copy-start(f32[32,1024]{1,0:T(8,128)} %start_ref.5) | copy-start | bytes 393220
  11.8 2.7 %copy-start.3 = (f32[32,1024]{1,0:T(8,128)S(1)}, f32[32,1024]{1,0:T(8,128)}, u32[]{:S(2)}) copy-start(f32[32,1024]{1,0:T(8,128)} %end_ref.5) | copy-start | bytes 393220
  13.2 14.2 %copy-start.1 = (f32[8,32,1024]{2,1,0:T(8,128)S(1)}, f32[8,32,1024]{2,1,0:T(8,128)}, u32[]{:S(2)}) copy-start(f32[8,32,1024]{2,1,0:T(8,128)} %f_ref.7) | copy-start | bytes 3145732
  15.3 12.2 %all-to-all-start = ((f32[32,1,128]{2,1,0:T(1,128)}), f32[32,1,128]{2,1,0:T(1,128)S(1)}, u32[]{:S(2)}, u32[]{:S(2)}) async-start(f32[32,1,128]{2,1,0:T(1,128)} %get-tuple-element.18), calls=%async_computation | async-start | bytes 32768 | tf_op jit(solution)/shard_map/all_to_all | solution.py:356
  20.4 2.0 %collective-permute-start.3 = (f32[2,1024]{1,0:T(2,128)S(1)}, f32[2,1024]{1,0:T(2,128)S(1)}, u32[]{:S(2)}, u32[]{:S(2)}) collective-permute-start(f32[2,1024]{1,0:T(2,128)S(1)} %get-tuple-element.19), channel_id=1, source_target_pairs={{0,1},{1,0},{2,3},{3,2},{4,5},{5,4},{6,7},{7,6},{8,9},{9,8},{10,11... | collective-permute-start | bytes 24584 | tf_op jit(solution)/shard_map/ppermute | solution.py:345
  20.7 3.1 %collective-permute-start.4 = (f32[2,1024]{1,0:T(2,128)S(1)}, f32[2,1024]{1,0:T(2,128)S(1)}, u32[]{:S(2)}, u32[]{:S(2)}) collective-permute-start(f32[2,1024]{1,0:T(2,128)S(1)} %get-tuple-element.20), channel_id=1, source_target_pairs={{1,2},{2,1},{3,0},{0,3},{5,6},{6,5},{7,4},{4,7},{9,10},{10,9},{11,... | collective-permute-start | bytes 24584 | tf_op jit(solution)/shard_map/ppermute | solution.py:345

commit v7 on v5

--- a/solution.py
+++ b/solution.py
@@ -13,6 +13,7 @@
 EPS = 1e-06
 VMEM = pl.BlockSpec(memory_space=pltpu.VMEM)
 ANY = pl.BlockSpec(memory_space=pl.ANY)
+FAR_TILES = 4
 PARAMS = pltpu.CompilerParams(vmem_limit_bytes=16 * 2**20)
 
 
@@ -40,63 +41,73 @@
     return jnp.where(flag, x, y)
 
 
-def edge_kernel(f_ref, start_ref, end_ref, far_ref, near_strip_ref, far_strip_ref, tiles, sem):
+def slices_kernel(f_ref, near_ref, far_ref):
+    count = f_ref.shape[0]
+    flag = odd("path")
+    base = pick(flag, 0, count - 2)
+    for s in range(2):
+        near_ref[s] = f_ref[base + s]
+    far_ref[...] = f_ref[pick(flag, count - 1, 0)]
+
+
+def strips_kernel(f_ref, start_ref, end_ref, near_ref, far_ref):
     count, rows, _ = f_ref.shape
     flag = odd("space")
-    copies = []
-    for i, at in enumerate((pl.ds(0, TILE), pl.ds(rows - TILE, TILE))):
-        copies.append(pltpu.make_async_copy(f_ref.at[:, at], tiles.at[i, pl.ds(0, count)], sem.at[3 * i]))
-        copies.append(pltpu.make_async_copy(start_ref.at[at], tiles.at[i, count], sem.at[3 * i + 1]))
-        copies.append(pltpu.make_async_copy(end_ref.at[at], tiles.at[i, count + 1], sem.at[3 * i + 2]))
-    base = pick(odd("path"), count - 2, 0)
-    copies.append(pltpu.make_async_copy(f_ref.at[pl.ds(base, 2)], far_ref, sem.at[6]))
-    for copy in copies:
-        copy.start()
-    for copy in copies[:-1]:
-        copy.wait()
-    for ref, low in ((near_strip_ref, flag), (far_strip_ref, jnp.logical_not(flag))):
-        side = pick(low, 0, 1)
-        at = pick(low, 0, TILE - 2)
-        face = pick(low, 0, TILE - 1)
-        ref[2] = jnp.zeros_like(ref[2])
-        for i in range(2):
-            ref[2, i : i + 1, :] = tiles[side, count + i, pl.ds(face, 1), :]
+    for ref, low in ((near_ref, flag), (far_ref, jnp.logical_not(flag))):
+        at = pick(low, 0, rows - 2)
+        face = pl.ds(pick(low, 0, rows - 1), 1)
+        ref[2:] = jnp.zeros_like(ref[2:])
+        ref[2, 0:1, :] = start_ref[face, :]
+        ref[2, 1:2, :] = end_ref[face, :]
         for s in range(count):
             for r in range(2):
-                ref[r, s : s + 1, :] = tiles[side, s, pl.ds(at + r, 1), :]
-    copies[-1].wait()
-
-
-def edges(f, start, end):
+                ref[r, s : s + 1, :] = f_ref[s, pl.ds(at + r, 1), :]
+
+
+def slices(f):
     count, rows, cols = f.shape
-    strip = jax.ShapeDtypeStruct((3, count, cols), F32)
     return pl.pallas_call(
-        edge_kernel,
-        out_shape=(jax.ShapeDtypeStruct((2, rows, cols), F32), strip, strip),
-        in_specs=[pl.BlockSpec(memory_space=pltpu.MemorySpace.HBM)] * 3,
-        out_specs=[VMEM] * 3,
-        scratch_shapes=[pltpu.VMEM((2, count + 2, TILE, cols), F32), pltpu.SemaphoreType.DMA((7,))],
+        slices_kernel,
+        out_shape=(jax.ShapeDtypeStruct((2, rows, cols), F32), jax.ShapeDtypeStruct((rows, cols), F32)),
+        in_specs=[VMEM],
+        out_specs=[VMEM] * 2,
         compiler_params=PARAMS,
-        name="edges",
+        name="slices",
+    )(f)
+
+
+def strips(f, start, end):
+    count, rows, cols = f.shape
+    return pl.pallas_call(
+        strips_kernel,
+        out_shape=tuple(jax.ShapeDtypeStruct((k, count, cols), F32) for k in (3, FAR_TILES)),
+        in_specs=[VMEM] * 3,
+        out_specs=[VMEM] * 2,
+        compiler_params=PARAMS,
+        name="strips",
     )(f, start, end)
 
 
 class Halo:
-    def __init__(self, m, near_ref, far_ref, near_strip_ref, far_strip_ref, start_ref, end_ref):
+    def __init__(self, m, near_ref, far_ref, near_strip_ref, far_strip_ref, start_ref, end_ref, far_b_ref=None):
         self.path, self.space = odd("path"), odd("space")
         self.first = lax.axis_index("path") == 0
         self.last = lax.axis_index("path") == m - 1
-        self.near, self.far = near_ref, far_ref
+        self.near, self.far, self.far_b = near_ref, far_ref, far_b_ref
         self.strips = near_strip_ref, far_strip_ref
         self.start, self.end = start_ref, end_ref
 
-    def below(self, i, at):
-        got = pick(self.path, self.near[i, at, :], self.far[i, at, :])
-        return pick(self.first, self.start[at, :], got) if i else got
-
-    def above(self, i, at):
-        got = pick(self.path, self.far[i, at, :], self.near[i, at, :])
-        return got if i else pick(self.last, self.end[at, :], got)
+    def below(self, at):
+        return pick(self.first, self.start[at, :], pick(self.path, self.near[1, at, :], self.far[at, :]))
+
+    def above(self, at):
+        return pick(self.last, self.end[at, :], pick(self.path, self.far[at, :], self.near[0, at, :]))
+
+    def below_2(self, at):
+        return pick(self.path, self.near[0, at, :], self.far_b[at, :])
+
+    def above_2(self, at):
+        return pick(self.path, self.far_b[at, :], self.near[1, at, :])
 
     def tail(self, *at):
         return pick(self.space, self.strips[0][at], self.strips[1][at])
@@ -105,14 +116,11 @@
         return pick(self.space, self.strips[1][at], self.strips[0][at])
 
 
-def interior_kernel(f_ref, part_ref, drift_ref, rim_ref, near_ref):
+def interior_kernel(f_ref, part_ref, drift_ref, rim_ref):
     count, rows, cols = f_ref.shape
     tiles = rows // TILE
     row = iota((TILE, cols), 0)
     part_ref[...] = jnp.zeros_like(part_ref)
-    base = pick(odd("path"), 0, count - 2)
-    for s in range(2):
-        near_ref[s] = f_ref[base + s]
 
     def drift_sum(s, _):
         total = jnp.zeros((TILE, LANES), F32)
@@ -154,10 +162,9 @@
             jax.ShapeDtypeStruct((2 * count, LANES), F32),
             jax.ShapeDtypeStruct(f.shape, F32),
             jax.ShapeDtypeStruct((2, count, cols), F32),
-            jax.ShapeDtypeStruct((2, rows, cols), F32),
         ),
         in_specs=[VMEM],
-        out_specs=[VMEM] * 4,
+        out_specs=[VMEM] * 3,
         cost_estimate=pl.CostEstimate(flops=20 * count * rows * cols, transcendentals=0, bytes_accessed=8 * count * rows * cols),
         compiler_params=PARAMS,
         name="interior",
@@ -165,15 +172,17 @@
 
 
 def chunk_kernel(m, n, f_ref, part_ref, rim_ref, *refs):
-    halo_refs, (out_ref, near_corner_ref, far_corner_ref) = refs[:6], refs[6:]
+    halo_refs, (out_ref, near_corner_ref, far_b_ref) = refs[:6], refs[6:]
     halo = Halo(m, *halo_refs)
     count, rows, cols = f_ref.shape
     tiles = rows // TILE
 
-    for ref, low in ((near_corner_ref, halo.path), (far_corner_ref, jnp.logical_not(halo.path))):
+    for ref, low, at in ((near_corner_ref, halo.path, 0), (far_b_ref, jnp.logical_not(halo.path), rows)):
         s = pl.ds(pick(low, 0, count - 1), 1)
-        ref[0:1, :] = halo.tail(1, s)
-        ref[1:2, :] = halo.head(0, s)
+        ref[at : at + 1, :] = halo.tail(1, s)
+        ref[at + 1 : at + 2, :] = halo.head(0, s)
+    far_b_ref[0:rows, :] = f_ref[pick(halo.path, count - 2, 1)]
+    far_b_ref[rows + 2 :, :] = jnp.zeros((TILE - 2, cols), F32)
 
     drift_a = rim_ref[0] + halo.tail(1)
     drift_b = rim_ref[1] + halo.head(0)
@@ -182,7 +191,7 @@
     totals = [jnp.zeros((TILE, LANES), F32) for _ in range(2)]
     for k in range(tiles):
         at = pl.ds(TILE * k, TILE)
-        tangents = (f_ref[1, at, :] - halo.below(1, at), halo.above(0, at) - f_ref[count - 2, at, :])
+        tangents = (f_ref[1, at, :] - halo.below(at), halo.above(at) - f_ref[count - 2, at, :])
         totals = [a + lanes_sum(t * t) for a, t in zip(totals, tangents)]
     head_sum, tail_sum = [jnp.sum(a, axis=0, keepdims=True) for a in totals]
     sub = iota((TILE, LANES), 0)
@@ -199,11 +208,14 @@
 
 
 def chunks(m, n, f, part, rim, halo):
-    cols = f.shape[2]
-    corner = jax.ShapeDtypeStruct((2, cols), F32)
+    _, rows, cols = f.shape
     return pl.pallas_call(
         functools.partial(chunk_kernel, m, n),
-        out_shape=(jax.ShapeDtypeStruct((m * n, 1, LANES), F32), corner, corner),
+        out_shape=(
+            jax.ShapeDtypeStruct((m * n, 1, LANES), F32),
+            jax.ShapeDtypeStruct((2, cols), F32),
+            jax.ShapeDtypeStruct((rows + TILE, cols), F32),
+        ),
         in_specs=[VMEM] * 9,
         out_specs=[VMEM] * 3,
         compiler_params=PARAMS,
@@ -211,9 +223,9 @@
     )(f, part, rim, *halo)
 
 
-def final_kernel(m, n, got_ref, near_corner_ref, far_corner_ref, f_ref, drift_ref, *refs):
+def final_kernel(m, n, got_ref, near_corner_ref, far_b_ref, f_ref, drift_ref, *refs):
     halo_refs, (ratio_ref, res_out, grad_out, resid, grad, outer, rim, sem) = refs[:6], refs[6:]
-    halo = Halo(m, *halo_refs)
+    halo = Halo(m, *halo_refs, far_b_ref)
     count, rows, cols = f_ref.shape
     tiles = rows // TILE
     path = lax.axis_index("path")
@@ -257,7 +269,7 @@
     fixed = halo.tail(2), halo.head(2)
     corners = []
     for i in range(2):
-        near, far = near_corner_ref[i : i + 1, :], far_corner_ref[i : i + 1, :]
+        near, far = near_corner_ref[i : i + 1, :], far_b_ref[rows + i : rows + i + 1, :]
         low = pick(first, fixed[i][0:1], pick(halo.path, near, far))
         high = pick(last, fixed[i][1:2], pick(halo.path, far, near))
         corners.append((low, high))
@@ -266,14 +278,14 @@
         return pl.ds(TILE * k, TILE)
 
     for k in range(tiles):
-        outer[0, at(k), :] = halo.below(1, at(k))
-        outer[1, at(k), :] = halo.above(0, at(k))
+        outer[0, at(k), :] = halo.below(at(k))
+        outer[1, at(k), :] = halo.above(at(k))
 
     def value(s, k):
         if s == -2:
-            return halo.below(0, at(k))
+            return halo.below_2(at(k))
         if s == count + 1:
-            return halo.above(1, at(k))
+            return halo.above_2(at(k))
         ref, slot = {-1: (outer, 0), count: (outer, 1)}.get(s, (f_ref, s))
         return ref[slot, at(k), :]
 
@@ -359,27 +371,24 @@
     )(got, *corners, f, drift, *halo)
 
 
-def swap(x, axis, kind, wrap):
+def swap(x, axis, kind):
     size = lax.axis_size(axis)
-    pairs = [(i, i ^ 1) for i in range(size)]
-    if kind == 1:
-        pairs = [((i + 1) % size, (j + 1) % size) for i, j in pairs]
-        pairs = [(i, j) for i, j in pairs if wrap or abs(i - j) == 1]
-    return lax.ppermute(x, axis, pairs)
+    return lax.ppermute(x, axis, [((i + kind) % size, ((i ^ 1) + kind) % size) for i in range(size)])
 
 
 def body(m, n, f, start, end):
-    far, near_strip, far_strip = edges(f, start, end)
-    far = swap(far, "path", 1, False)
-    far_strip = swap(far_strip, "space", 1, True)
-    near_strip = swap(near_strip, "space", 0, True)
-    part, drift, rim, near = interior(f)
-    near = swap(near, "path", 0, False)
+    near, far = slices(f)
+    near_strip, far_strip = strips(f, start, end)
+    near = swap(near, "path", 0)
+    far = swap(far, "path", 1)
+    near_strip = swap(near_strip, "space", 0)
+    far_strip = swap(far_strip, "space", 1)
+    part, drift, rim = interior(f)
     halo = near, far, near_strip, far_strip, start, end
-    send, near_corner, far_corner = chunks(m, n, f, part, rim, halo)
+    send, near_corner, far_b = chunks(m, n, f, part, rim, halo)
     got = lax.all_to_all(send, ("space", "path"), 0, 0, tiled=True)
-    corners = swap(near_corner, "path", 0, False), swap(far_corner, "path", 1, False)
-    return final(m, n, got, corners, f, drift, halo)
+    later = swap(near_corner, "path", 0), swap(far_b, "path", 1)
+    return final(m, n, got, later, f, drift, halo)
 
 
 def solution(mesh):

time: 34.4 us -> 30.7 us (0.89)
  starting transfers between devices: 15.1 us -> 12.1 us
  local copies, waits for them, and re-layouts: 3.05 us -> 1.64 us
  waiting for transfers between devices: 9.87 us -> 11 us
    ppermute x6, starting transfers between devices: 11.2 us -> 7.99 us  [swap(): lax.ppermute(x, axis, [((i + kind) % size, ((i ^ 1) + kind) % size) for i...]
    unnamed x12 -> x8, local copies, waits for them, and re-layouts: 3.05 us -> 1.64 us
    ppermute x6, waiting for transfers between devices: 4.04 us -> 5.18 us  [swap(): lax.ppermute(x, axis, [((i + kind) % size, ((i ^ 1) + kind) % size) for i...]
  transfers between devices with their start and end apart: 7 -> 7, of which waited for: 4 -> 3; matrix products, arithmetic and copies ran while one was open for 0% -> 0% of each run, Pallas kernels for 4% -> 5%
where the time goes in v7:
time: 30.7 us; the launch traced here: 30.5 us
  starting transfers between devices  12.1 us (39%)
  waiting for transfers between devices  11 us (36%)
  Pallas kernels  5.1 us (17%)
  local copies, waits for them, and re-layouts  1.64 us (5%)
  between operations  0.68 us (2%)
    ppermute x6, starting transfers between devices, swap(): lax.ppermute(x, axis, [((i + kind) % size, ((i ^ 1) + kind) % size) for i...  7.99 us
    all_to_all x1, waiting for transfers between devices, body(): got = lax.all_to_all(send, ('space', 'path'), 0, 0, tiled=True)  5.84 us
    ppermute x6, waiting for transfers between devices, swap(): lax.ppermute(x, axis, [((i + kind) % size, ((i ^ 1) + kind) % size) for i...  5.18 us
    all_to_all x1, starting transfers between devices, body(): got = lax.all_to_all(send, ('space', 'path'), 0, 0, tiled=True)  4.09 us
    pallas_call x1, Pallas kernels, final(): pl.pallas_call(functools.partial(final_kernel, m, n), out_shape=(jax.Shap...  2.87 us
    unnamed x8, local copies, waits for them, and re-layouts  1.64 us
    pallas_call x1, Pallas kernels, interior(): pl.pallas_call(interior_kernel, out_shape=(jax.ShapeDtypeStruct((2 * coun...  1.38 us
    pallas_call x1, Pallas kernels, chunks(): pl.pallas_call(functools.partial(chunk_kernel, m, n), out_shape=(jax.Shap...  0.78 us
  transfers between devices with their start and end apart: 7, of which 3 were waited for; matrix products, arithmetic and copies ran while one was open for 0% of the time, Pallas kernels for 5%

profile of v7, /device:TPU:0, one launch (start us, length us, event | category | flops | bytes accessed | tf_op | source)
XLA Modules:
  0.0 30.5 jit_solution(18089829988959853330)
XLA Ops:
  0.6 0.0 copy-start
  0.6 1.2 %copy-done = f32[8,32,1024]{2,1,0:T(8,128)S(1)} copy-done((f32[8,32,1024]{2,1,0:T(8,128)S(1)}, f32[8,32,1024]{2,1,0:T(8,128)}, u32[]{:S(2)}) %copy-start) | copy-done | bytes 1048600
  1.9 0.0 copy-start.2
  1.9 0.0 copy-start.3
  1.9 0.5 %collective-permute-start = (f32[2,32,1024]{2,1,0:T(8,128)S(1)}, f32[2,32,1024]{2,1,0:T(8,128)S(1)}, u32[]{:S(2)}, u32[]{:S(2)}) collective-permute-start(f32[2,32,1024]{2,1,0:T(8,128)S(1)} %get-tuple-element.15), channel_id=1, source_target_pairs={{0,1},{1,0},{2,3},{3,2},{4,5},{5,4},{6,7},{7,6},{8,9},{9,8},{10,11... | collective-permute-start | bytes 786440 | tf_op jit(solution)/shard_map/ppermute | solution.py:376
  2.4 0.4 %copy-done.2 = f32[32,1024]{1,0:T(8,128)S(1)} copy-done((f32[32,1024]{1,0:T(8,128)S(1)}, f32[32,1024]{1,0:T(8,128)}, u32[]{:S(2)}) %copy-start.2) | copy-done | bytes 131096
  2.8 0.1 copy-done.3
  2.9 6.1 %collective-permute-start.3 = (f32[4,8,1024]{2,1,0:T(8,128)S(1)}, f32[4,8,1024]{2,1,0:T(8,128)S(1)}, u32[]{:S(2)}, u32[]{:S(2)}) collective-permute-start(f32[4,8,1024]{2,1,0:T(8,128)S(1)} %get-tuple-element.18), channel_id=1, source_target_pairs={{4,8},{8,4},{12,16},{16,12},{20,24},{24,20},{28,0},{0,28},{5,9},{9... | collective-permute-start | bytes 393224 | tf_op jit(solution)/shard_map/ppermute | solution.py:376
  8.9 0.7 %collective-permute-start.1 = (f32[32,1024]{1,0:T(8,128)S(1)}, f32[32,1024]{1,0:T(8,128)S(1)}, u32[]{:S(2)}, u32[]{:S(2)}) collective-permute-start(f32[32,1024]{1,0:T(8,128)S(1)} %get-tuple-element.16), channel_id=1, source_target_pairs={{1,2},{2,1},{3,0},{0,3},{5,6},{6,5},{7,4},{4,7},{9,10},{10,9},{11,... | collective-permute-start | bytes 393224 | tf_op jit(solution)/shard_map/ppermute | solution.py:376
  9.6 0.0 collective-permute-start.2
  9.6 1.4 %interior.1 = (f32[16,128]{1,0:T(8,128)S(1)}, f32[8,32,1024]{2,1,0:T(8,128)S(1)}, f32[2,8,1024]{2,1,0:T(8,128)S(1)}) custom-call(f32[8,32,1024]{2,1,0:T(8,128)S(1)} %copy-done), custom_call_target="tpu_custom_call" | custom-call | flops 5242880 | bytes 2097152 | tf_op jit(solution)/shard_map/interior/pallas_call | solution.py:159
  11.0 0.0 copy-start.1
  11.0 4.3 %collective-permute-done.2.refs_2_ = f32[3,8,1024]{2,1,0:T(8,128)S(1)} collective-permute-done((f32[3,8,1024]{2,1,0:T(8,128)S(1)}, f32[3,8,1024]{2,1,0:T(8,128)S(1)}, u32[]{:S(2)}, u32[]{:S(2)}) %collective-permute-start.2) | collective-permute-done | bytes 98336 | tf_op jit(solution)/shard_map/ppermute | solution.py:376
  15.3 0.0 collective-permute-done.3.refs_3_
  15.3 0.0 collective-permute-done.1.refs_1_
  15.3 0.0 collective-permute-done.refs_0_
  15.3 0.8 %chunks.1 = (f32[32,1,128]{2,1,0:T(1,128)}, f32[2,1024]{1,0:T(2,128)S(1)}, f32[40,1024]{1,0:T(8,128)S(1)}) custom-call(f32[8,32,1024]{2,1,0:T(8,128)S(1)} %copy-done, f32[16,128]{1,0:T(8,128)S(1)} %get-tuple-element.13.part_ref, f32[2,8,1024]{2,1,0:T(8,128)S(1)} %get-tuple-element.14.rim_ref, f32[2,32,1024]{2,1,0:T(8,128)S(1)} %collective-permute-done.refs_0_, ...), custom_call_target="tpu_custom_call" | custom-call | tf_op jit(solution)/shard_map/chunks/pallas_call | solution.py:212
  16.0 0.4 %collective-permute-start.5 = (f32[40,1024]{1,0:T(8,128)S(1)}, f32[40,1024]{1,0:T(8,128)S(1)}, u32[]{:S(2)}, u32[]{:S(2)}) collective-permute-start(f32[40,1024]{1,0:T(8,128)S(1)} %get-tuple-element.21), channel_id=1, source_target_pairs={{1,2},{2,1},{3,0},{0,3},{5,6},{6,5},{7,4},{4,7},{9,10},{10,9},{11,... | collective-permute-start | bytes 491528 | tf_op jit(solution)/shard_map/ppermute | solution.py:376
  16.5 4.1 %all-to-all-start = ((f32[32,1,128]{2,1,0:T(1,128)}), f32[32,1,128]{2,1,0:T(1,128)S(1)}, u32[]{:S(2)}, u32[]{:S(2)}) async-start(f32[32,1,128]{2,1,0:T(1,128)} %get-tuple-element.19), calls=%async_computation | async-start | bytes 32768 | tf_op jit(solution)/shard_map/all_to_all | solution.py:389
  20.6 0.3 %collective-permute-start.4 = (f32[2,1024]{1,0:T(2,128)S(1)}, f32[2,1024]{1,0:T(2,128)S(1)}, u32[]{:S(2)}, u32[]{:S(2)}) collective-permute-start(f32[2,1024]{1,0:T(2,128)S(1)} %get-tuple-element.20), channel_id=1, source_target_pairs={{0,1},{1,0},{2,3},{3,2},{4,5},{5,4},{6,7},{7,6},{8,9},{9,8},{10,11... | collective-permute-start | bytes 24584 | tf_op jit(solution)/shard_map/ppermute | solution.py:376
  20.9 0.9 %collective-permute-done.4.near_corner_ref = f32[2,1024]{1,0:T(2,128)S(1)} collective-permute-done((f32[2,1024]{1,0:T(2,128)S(1)}, f32[2,1024]{1,0:T(2,128)S(1)}, u32[]{:S(2)}, u32[]{:S(2)}) %collective-permute-start.4) | collective-permute-done | bytes 8224 | tf_op jit(solution)/shard_map/ppermute | solution.py:376
  21.8 5.8 %all-to-all-done.got_ref = f32[32,1,128]{2,1,0:T(1,128)S(1)} async-done(((f32[32,1,128]{2,1,0:T(1,128)}), f32[32,1,128]{2,1,0:T(1,128)S(1)}, u32[]{:S(2)}, u32[]{:S(2)}) %all-to-all-start) | async-done | bytes 16416 | tf_op jit(solution)/shard_map/all_to_all | solution.py:389
  27.7 0.0 collective-permute-done.5.far_b_ref
  27.7 0.0 copy-done.1
  27.7 2.9 %final.1 = (f32[8]{0:T(128)}, f32[8,32,1024]{2,1,0:T(8,128)}, f32[8,32,1024]{2,1,0:T(8,128)}) custom-call(f32[32,1,128]{2,1,0:T(1,128)S(1)} %all-to-all-done.got_ref, f32[2,1024]{1,0:T(2,128)S(1)} %collective-permute-done.4.near_corner_ref, f32[40,1024]{1,0:T(8,128)S(1)} %collective-permute-done.5.far_b_ref, f32[8,32,1024]{2,1,0:T(8,128)S(1)} %copy-done.1, ...), custom_call_target="tpu_custom_call" | custom-call | tf_op jit(solution)/shard_map/final/pallas_call | solution.py:357
  (2 shorter events, 0.1 us)
Async XLA Ops:
  0.6 1.2 %copy-start = (f32[8,32,1024]{2,1,0:T(8,128)S(1)}, f32[8,32,1024]{2,1,0:T(8,128)}, u32[]{:S(2)}) copy-start(f32[8,32,1024]{2,1,0:T(8,128)} %f_ref.9) | copy-start | bytes 3145732
  1.9 0.9 %copy-start.2 = (f32[32,1024]{1,0:T(8,128)S(1)}, f32[32,1024]{1,0:T(8,128)}, u32[]{:S(2)}) copy-start(f32[32,1024]{1,0:T(8,128)} %refs_4_.3) | copy-start | bytes 393220
  1.9 1.0 %copy-start.3 = (f32[32,1024]{1,0:T(8,128)S(1)}, f32[32,1024]{1,0:T(8,128)}, u32[]{:S(2)}) copy-start(f32[32,1024]{1,0:T(8,128)} %refs_5_.3) | copy-start | bytes 393220
  1.9 13.4 %collective-permute-start = (f32[2,32,1024]{2,1,0:T(8,128)S(1)}, f32[2,32,1024]{2,1,0:T(8,128)S(1)}, u32[]{:S(2)}, u32[]{:S(2)}) collective-permute-start(f32[2,32,1024]{2,1,0:T(8,128)S(1)} %get-tuple-element.15), channel_id=1, source_target_pairs={{0,1},{1,0},{2,3},{3,2},{4,5},{5,4},{6,7},{7,6},{8,9},{9,8},{10,11... | collective-permute-start | bytes 786440 | tf_op jit(solution)/shard_map/ppermute | solution.py:376
  2.9 12.4 %collective-permute-start.3 = (f32[4,8,1024]{2,1,0:T(8,128)S(1)}, f32[4,8,1024]{2,1,0:T(8,128)S(1)}, u32[]{:S(2)}, u32[]{:S(2)}) collective-permute-start(f32[4,8,1024]{2,1,0:T(8,128)S(1)} %get-tuple-element.18), channel_id=1, source_target_pairs={{4,8},{8,4},{12,16},{16,12},{20,24},{24,20},{28,0},{0,28},{5,9},{9... | collective-permute-start | bytes 393224 | tf_op jit(solution)/shard_map/ppermute | solution.py:376
  8.9 6.3 %collective-permute-start.1 = (f32[32,1024]{1,0:T(8,128)S(1)}, f32[32,1024]{1,0:T(8,128)S(1)}, u32[]{:S(2)}, u32[]{:S(2)}) collective-permute-start(f32[32,1024]{1,0:T(8,128)S(1)} %get-tuple-element.16), channel_id=1, source_target_pairs={{1,2},{2,1},{3,0},{0,3},{5,6},{6,5},{7,4},{4,7},{9,10},{10,9},{11,... | collective-permute-start | bytes 393224 | tf_op jit(solution)/shard_map/ppermute | solution.py:376
  9.6 5.7 %collective-permute-start.2 = (f32[3,8,1024]{2,1,0:T(8,128)S(1)}, f32[3,8,1024]{2,1,0:T(8,128)S(1)}, u32[]{:S(2)}, u32[]{:S(2)}) collective-permute-start(f32[3,8,1024]{2,1,0:T(8,128)S(1)} %get-tuple-element.17), channel_id=1, source_target_pairs={{0,4},{4,0},{8,12},{12,8},{16,20},{20,16},{24,28},{28,24},{1,5},{5... | collective-permute-start | bytes 294920 | tf_op jit(solution)/shard_map/ppermute | solution.py:376
  11.0 16.7 %copy-start.1 = (f32[8,32,1024]{2,1,0:T(8,128)S(1)}, f32[8,32,1024]{2,1,0:T(8,128)}, u32[]{:S(2)}) copy-start(f32[8,32,1024]{2,1,0:T(8,128)} %f_ref.9) | copy-start | bytes 3145732
  16.0 11.6 %collective-permute-start.5 = (f32[40,1024]{1,0:T(8,128)S(1)}, f32[40,1024]{1,0:T(8,128)S(1)}, u32[]{:S(2)}, u32[]{:S(2)}) collective-permute-start(f32[40,1024]{1,0:T(8,128)S(1)} %get-tuple-element.21), channel_id=1, source_target_pairs={{1,2},{2,1},{3,0},{0,3},{5,6},{6,5},{7,4},{4,7},{9,10},{10,9},{11,... | collective-permute-start | bytes 491528 | tf_op jit(solution)/shard_map/ppermute | solution.py:376
  16.5 11.2 %all-to-all-start = ((f32[32,1,128]{2,1,0:T(1,128)}), f32[32,1,128]{2,1,0:T(1,128)S(1)}, u32[]{:S(2)}, u32[]{:S(2)}) async-start(f32[32,1,128]{2,1,0:T(1,128)} %get-tuple-element.19), calls=%async_computation | async-start | bytes 32768 | tf_op jit(solution)/shard_map/all_to_all | solution.py:389
  20.6 1.2 %collective-permute-start.4 = (f32[2,1024]{1,0:T(2,128)S(1)}, f32[2,1024]{1,0:T(2,128)S(1)}, u32[]{:S(2)}, u32[]{:S(2)}) collective-permute-start(f32[2,1024]{1,0:T(2,128)S(1)} %get-tuple-element.20), channel_id=1, source_target_pairs={{0,1},{1,0},{2,3},{3,2},{4,5},{5,4},{6,7},{7,6},{8,9},{9,8},{10,11... | collective-permute-start | bytes 24584 | tf_op jit(solution)/shard_map/ppermute | solution.py:376

commit v8 on v7

--- a/solution.py
+++ b/solution.py
@@ -13,7 +13,6 @@
 EPS = 1e-06
 VMEM = pl.BlockSpec(memory_space=pltpu.VMEM)
 ANY = pl.BlockSpec(memory_space=pl.ANY)
-FAR_TILES = 4
 PARAMS = pltpu.CompilerParams(vmem_limit_bytes=16 * 2**20)
 
 
@@ -44,10 +43,10 @@
 def slices_kernel(f_ref, near_ref, far_ref):
     count = f_ref.shape[0]
     flag = odd("path")
-    base = pick(flag, 0, count - 2)
-    for s in range(2):
-        near_ref[s] = f_ref[base + s]
-    far_ref[...] = f_ref[pick(flag, count - 1, 0)]
+    for ref, low in ((far_ref, jnp.logical_not(flag)), (near_ref, flag)):
+        base = pick(low, 0, count - 2)
+        for s in range(2):
+            ref[s] = f_ref[base + s]
 
 
 def strips_kernel(f_ref, start_ref, end_ref, near_ref, far_ref):
@@ -56,19 +55,19 @@
     for ref, low in ((near_ref, flag), (far_ref, jnp.logical_not(flag))):
         at = pick(low, 0, rows - 2)
         face = pl.ds(pick(low, 0, rows - 1), 1)
-        ref[2:] = jnp.zeros_like(ref[2:])
-        ref[2, 0:1, :] = start_ref[face, :]
-        ref[2, 1:2, :] = end_ref[face, :]
+        ref[count:] = jnp.zeros_like(ref[count:])
+        ref[count, 0:1, :] = start_ref[face, :]
+        ref[count, 1:2, :] = end_ref[face, :]
         for s in range(count):
             for r in range(2):
-                ref[r, s : s + 1, :] = f_ref[s, pl.ds(at + r, 1), :]
+                ref[s, r : r + 1, :] = f_ref[s, pl.ds(at + r, 1), :]
 
 
 def slices(f):
     count, rows, cols = f.shape
     return pl.pallas_call(
         slices_kernel,
-        out_shape=(jax.ShapeDtypeStruct((2, rows, cols), F32), jax.ShapeDtypeStruct((rows, cols), F32)),
+        out_shape=(jax.ShapeDtypeStruct((2, rows, cols), F32),) * 2,
         in_specs=[VMEM],
         out_specs=[VMEM] * 2,
         compiler_params=PARAMS,
@@ -80,7 +79,7 @@
     count, rows, cols = f.shape
     return pl.pallas_call(
         strips_kernel,
-        out_shape=tuple(jax.ShapeDtypeStruct((k, count, cols), F32) for k in (3, FAR_TILES)),
+        out_shape=tuple(jax.ShapeDtypeStruct((count + k, 2, cols), F32) for k in (1, 2)),
         in_specs=[VMEM] * 3,
         out_specs=[VMEM] * 2,
         compiler_params=PARAMS,
@@ -89,31 +88,24 @@
 
 
 class Halo:
-    def __init__(self, m, near_ref, far_ref, near_strip_ref, far_strip_ref, start_ref, end_ref, far_b_ref=None):
-        self.path, self.space = odd("path"), odd("space")
+    def __init__(self, m, near_ref, far_ref, start_ref, end_ref):
+        self.odd = odd("path")
         self.first = lax.axis_index("path") == 0
         self.last = lax.axis_index("path") == m - 1
-        self.near, self.far, self.far_b = near_ref, far_ref, far_b_ref
-        self.strips = near_strip_ref, far_strip_ref
+        self.near, self.far = near_ref, far_ref
         self.start, self.end = start_ref, end_ref
 
     def below(self, at):
-        return pick(self.first, self.start[at, :], pick(self.path, self.near[1, at, :], self.far[at, :]))
+        return pick(self.first, self.start[at, :], pick(self.odd, self.near[1, at, :], self.far[1, at, :]))
 
     def above(self, at):
-        return pick(self.last, self.end[at, :], pick(self.path, self.far[at, :], self.near[0, at, :]))
+        return pick(self.last, self.end[at, :], pick(self.odd, self.far[0, at, :], self.near[0, at, :]))
 
     def below_2(self, at):
-        return pick(self.path, self.near[0, at, :], self.far_b[at, :])
+        return pick(self.odd, self.near[0, at, :], self.far[0, at, :])
 
     def above_2(self, at):
-        return pick(self.path, self.far_b[at, :], self.near[1, at, :])
-
-    def tail(self, *at):
-        return pick(self.space, self.strips[0][at], self.strips[1][at])
-
-    def head(self, *at):
-        return pick(self.space, self.strips[1][at], self.strips[0][at])
+        return pick(self.odd, self.far[1, at, :], self.near[1, at, :])
 
 
 def interior_kernel(f_ref, part_ref, drift_ref, rim_ref):
@@ -171,21 +163,28 @@
     )(f)
 
 
-def chunk_kernel(m, n, f_ref, part_ref, rim_ref, *refs):
-    halo_refs, (out_ref, near_corner_ref, far_b_ref) = refs[:6], refs[6:]
-    halo = Halo(m, *halo_refs)
+def chunk_kernel(
+    m, n, f_ref, part_ref, rim_ref, near_ref, far_ref, start_ref, end_ref, near_strip_ref, far_strip_ref,
+    out_ref, near_corner_ref, far_corner_ref, tail_ref, head_ref, face_ref,
+):
+    halo = Halo(m, near_ref, far_ref, start_ref, end_ref)
     count, rows, cols = f_ref.shape
     tiles = rows // TILE
 
-    for ref, low, at in ((near_corner_ref, halo.path, 0), (far_b_ref, jnp.logical_not(halo.path), rows)):
+    flag = odd("space")
+    for i, (ref, x_ref, y_ref) in enumerate(((tail_ref, near_strip_ref, far_strip_ref), (head_ref, far_strip_ref, near_strip_ref))):
+        for s in range(count):
+            both = pick(flag, x_ref[s], y_ref[s])
+            for r in range(2):
+                ref[r, s : s + 1, :] = both[r : r + 1]
+        face_ref[2 * i : 2 * i + 2, :] = pick(flag, x_ref[count], y_ref[count])
+    for ref, low in ((near_corner_ref, halo.odd), (far_corner_ref, jnp.logical_not(halo.odd))):
         s = pl.ds(pick(low, 0, count - 1), 1)
-        ref[at : at + 1, :] = halo.tail(1, s)
-        ref[at + 1 : at + 2, :] = halo.head(0, s)
-    far_b_ref[0:rows, :] = f_ref[pick(halo.path, count - 2, 1)]
-    far_b_ref[rows + 2 :, :] = jnp.zeros((TILE - 2, cols), F32)
-
-    drift_a = rim_ref[0] + halo.tail(1)
-    drift_b = rim_ref[1] + halo.head(0)
+        ref[0:1, :] = tail_ref[1, s, :]
+        ref[1:2, :] = head_ref[0, s, :]
+
+    drift_a = rim_ref[0] + tail_ref[1]
+    drift_b = rim_ref[1] + head_ref[0]
     drift = part_ref[0:count, :] + lanes_sum(drift_a * drift_a) + lanes_sum(drift_b * drift_b)
 
     totals = [jnp.zeros((TILE, LANES), F32) for _ in range(2)]
@@ -207,25 +206,32 @@
         out_ref[j] = line
 
 
-def chunks(m, n, f, part, rim, halo):
-    _, rows, cols = f.shape
+def chunks(m, n, f, part, rim, near, far, start, end, near_strip, far_strip):
+    count, rows, cols = f.shape
+    corner = jax.ShapeDtypeStruct((2, cols), F32)
+    strip = jax.ShapeDtypeStruct((2, count, cols), F32)
     return pl.pallas_call(
         functools.partial(chunk_kernel, m, n),
         out_shape=(
             jax.ShapeDtypeStruct((m * n, 1, LANES), F32),
-            jax.ShapeDtypeStruct((2, cols), F32),
-            jax.ShapeDtypeStruct((rows + TILE, cols), F32),
+            corner,
+            corner,
+            strip,
+            strip,
+            jax.ShapeDtypeStruct((4, cols), F32),
         ),
         in_specs=[VMEM] * 9,
-        out_specs=[VMEM] * 3,
+        out_specs=[VMEM] * 6,
         compiler_params=PARAMS,
         name="chunks",
-    )(f, part, rim, *halo)
-
-
-def final_kernel(m, n, got_ref, near_corner_ref, far_b_ref, f_ref, drift_ref, *refs):
-    halo_refs, (ratio_ref, res_out, grad_out, resid, grad, outer, rim, sem) = refs[:6], refs[6:]
-    halo = Halo(m, *halo_refs, far_b_ref)
+    )(f, part, rim, near, far, start, end, near_strip, far_strip)
+
+
+def final_kernel(
+    m, n, got_ref, near_corner_ref, far_corner_ref, f_ref, drift_ref, near_ref, far_ref, start_ref, end_ref,
+    tail_ref, head_ref, face_ref, ratio_ref, res_out, grad_out, resid, grad, outer, rim, sem,
+):
+    halo = Halo(m, near_ref, far_ref, start_ref, end_ref)
     count, rows, cols = f_ref.shape
     tiles = rows // TILE
     path = lax.axis_index("path")
@@ -266,12 +272,11 @@
     scale = [widen(splat(t)) for t in range(count + 2)]
     column = jnp.sum(jnp.where(lane == sub + 1, ratio, 0.0), axis=1, keepdims=True)
     row = iota((TILE, cols), 0)
-    fixed = halo.tail(2), halo.head(2)
     corners = []
     for i in range(2):
-        near, far = near_corner_ref[i : i + 1, :], far_b_ref[rows + i : rows + i + 1, :]
-        low = pick(first, fixed[i][0:1], pick(halo.path, near, far))
-        high = pick(last, fixed[i][1:2], pick(halo.path, far, near))
+        near, far = near_corner_ref[i : i + 1, :], far_corner_ref[i : i + 1, :]
+        low = pick(first, face_ref[2 * i : 2 * i + 1, :], pick(halo.odd, near, far))
+        high = pick(last, face_ref[2 * i + 1 : 2 * i + 2, :], pick(halo.odd, far, near))
         corners.append((low, high))
 
     def at(k):
@@ -293,8 +298,8 @@
         rim[0, s : s + 1, :] = f_ref[s, 0:1, :]
         rim[1, s : s + 1, :] = f_ref[s, rows - 1 : rows, :]
     for far, mid, near, (low, high), place in (
-        (halo.tail(0), halo.tail(1), rim[0], corners[0], TILE - 1),
-        (halo.head(1), halo.head(0), rim[1], corners[1], TILE + rows),
+        (tail_ref[0], tail_ref[1], rim[0], corners[0], TILE - 1),
+        (head_ref[1], head_ref[0], rim[1], corners[1], TILE + rows),
     ):
         ahead = jnp.where(row == count - 1, high, pltpu.roll(mid, count - 1, 0))
         behind = jnp.where(row == 0, low, pltpu.roll(mid, 1, 0))
@@ -307,7 +312,7 @@
             slot = 0 if s < 0 else 1
             top, bottom = corners[0][slot], corners[1][slot]
         else:
-            top, bottom = halo.tail(1, pl.ds(s, 1)), halo.head(0, pl.ds(s, 1))
+            top, bottom = tail_ref[1, s : s + 1, :], head_ref[0, s : s + 1, :]
         for k in range(tiles):
             if s in (-1, count):
                 c = outer[slot, at(k), :]
@@ -351,13 +356,13 @@
         copy.wait()
 
 
-def final(m, n, got, corners, f, drift, halo):
+def final(m, n, got, corners, f, drift, slabs, strips):
     count, rows, cols = f.shape
     big = jax.ShapeDtypeStruct(f.shape, F32)
     return pl.pallas_call(
         functools.partial(final_kernel, m, n),
         out_shape=(jax.ShapeDtypeStruct((count,), F32), big, big),
-        in_specs=[VMEM] * 11,
+        in_specs=[VMEM] * 12,
         out_specs=(VMEM, ANY, ANY),
         scratch_shapes=[
             pltpu.VMEM((count + 2, rows + 2 * TILE, cols), F32),
@@ -368,7 +373,7 @@
         ],
         compiler_params=PARAMS,
         name="final",
-    )(got, *corners, f, drift, *halo)
+    )(got, *corners, f, drift, *slabs, *strips)
 
 
 def swap(x, axis, kind):
@@ -379,16 +384,16 @@
 def body(m, n, f, start, end):
     near, far = slices(f)
     near_strip, far_strip = strips(f, start, end)
+    far = swap(far, "path", 1)
     near = swap(near, "path", 0)
-    far = swap(far, "path", 1)
+    far_strip = swap(far_strip, "space", 1)
     near_strip = swap(near_strip, "space", 0)
-    far_strip = swap(far_strip, "space", 1)
     part, drift, rim = interior(f)
-    halo = near, far, near_strip, far_strip, start, end
-    send, near_corner, far_b = chunks(m, n, f, part, rim, halo)
+    slabs = near, far, start, end
+    send, near_corner, far_corner, *sorted_strips = chunks(m, n, f, part, rim, *slabs, near_strip, far_strip)
     got = lax.all_to_all(send, ("space", "path"), 0, 0, tiled=True)
-    later = swap(near_corner, "path", 0), swap(far_b, "path", 1)
-    return final(m, n, got, later, f, drift, halo)
+    corners = swap(near_corner, "path", 0), swap(far_corner, "path", 1)
+    return final(m, n, got, corners, f, drift, slabs, sorted_strips)
 
 
 def solution(mesh):

time: 30.7 us -> 28.3 us (0.922)
  waiting for transfers between devices: 11 us -> 8.09 us
  starting transfers between devices: 12.1 us -> 13 us
  local copies, waits for them, and re-layouts: 1.64 us -> 1.23 us
    all_to_all x1, waiting for transfers between devices: 5.84 us -> 3.66 us  [body(): got = lax.all_to_all(send, ('space', 'path'), 0, 0, tiled=True)]
    ppermute x6, starting transfers between devices: 7.99 us -> 9.7 us  [swap(): lax.ppermute(x, axis, [((i + kind) % size, ((i ^ 1) + kind) % size) for i...]
    all_to_all x1, starting transfers between devices: 4.09 us -> 3.31 us  [body(): got = lax.all_to_all(send, ('space', 'path'), 0, 0, tiled=True)]
    ppermute x6, waiting for transfers between devices: 5.18 us -> 4.43 us  [swap(): lax.ppermute(x, axis, [((i + kind) % size, ((i ^ 1) + kind) % size) for i...]
    unnamed x8, local copies, waits for them, and re-layouts: 1.64 us -> 1.23 us
where the time goes in v8:
time: 28.3 us; the launch traced here: 28.1 us
  starting transfers between devices  13 us (46%)
  waiting for transfers between devices  8.09 us (29%)
  Pallas kernels  5.09 us (18%)
  local copies, waits for them, and re-layouts  1.23 us (4%)
  between operations  0.68 us (2%)
    ppermute x6, starting transfers between devices, swap(): lax.ppermute(x, axis, [((i + kind) % size, ((i ^ 1) + kind) % size) for i...  9.7 us
    ppermute x6, waiting for transfers between devices, swap(): lax.ppermute(x, axis, [((i + kind) % size, ((i ^ 1) + kind) % size) for i...  4.43 us
    all_to_all x1, waiting for transfers between devices, body(): got = lax.all_to_all(send, ('space', 'path'), 0, 0, tiled=True)  3.66 us
    all_to_all x1, starting transfers between devices, body(): got = lax.all_to_all(send, ('space', 'path'), 0, 0, tiled=True)  3.31 us
    pallas_call x1, Pallas kernels, final(): pl.pallas_call(functools.partial(final_kernel, m, n), out_shape=(jax.Shap...  2.83 us
    pallas_call x1, Pallas kernels, interior(): pl.pallas_call(interior_kernel, out_shape=(jax.ShapeDtypeStruct((2 * coun...  1.38 us
    unnamed x8, local copies, waits for them, and re-layouts  1.23 us
    pallas_call x1, Pallas kernels, chunks(): pl.pallas_call(functools.partial(chunk_kernel, m, n), out_shape=(jax.Shap...  0.8 us
  transfers between devices with their start and end apart: 7, of which 3 were waited for; matrix products, arithmetic and copies ran while one was open for 0% of the time, Pallas kernels for 5%

profile of v8, /device:TPU:0, one launch (start us, length us, event | category | flops | bytes accessed | tf_op | source)
XLA Modules:
  0.0 28.1 jit_solution(15731685745034575318)
XLA Ops:
  0.6 0.0 copy-start
  0.6 1.2 %copy-done = f32[8,32,1024]{2,1,0:T(8,128)S(1)} copy-done((f32[8,32,1024]{2,1,0:T(8,128)S(1)}, f32[8,32,1024]{2,1,0:T(8,128)}, u32[]{:S(2)}) %copy-start) | copy-done | bytes 1048600
  1.9 0.0 copy-start.2
  1.9 0.0 copy-start.3
  1.9 0.5 %collective-permute-start = (f32[2,32,1024]{2,1,0:T(8,128)S(1)}, f32[2,32,1024]{2,1,0:T(8,128)S(1)}, u32[]{:S(2)}, u32[]{:S(2)}) collective-permute-start(f32[2,32,1024]{2,1,0:T(8,128)S(1)} %get-tuple-element.18), channel_id=1, source_target_pairs={{0,1},{1,0},{2,3},{3,2},{4,5},{5,4},{6,7},{7,6},{8,9},{9,8},{10,11... | collective-permute-start | bytes 786440 | tf_op jit(solution)/shard_map/ppermute | solution.py:381
  2.4 2.6 %collective-permute-start.1 = (f32[2,32,1024]{2,1,0:T(8,128)S(1)}, f32[2,32,1024]{2,1,0:T(8,128)S(1)}, u32[]{:S(2)}, u32[]{:S(2)}) collective-permute-start(f32[2,32,1024]{2,1,0:T(8,128)S(1)} %get-tuple-element.19), channel_id=1, source_target_pairs={{1,2},{2,1},{3,0},{0,3},{5,6},{6,5},{7,4},{4,7},{9,10},{10,9},{11,... | collective-permute-start | bytes 786440 | tf_op jit(solution)/shard_map/ppermute | solution.py:381
  5.0 0.0 copy-done.2
  5.0 0.0 copy-done.3
  5.1 4.6 %collective-permute-start.3 = (f32[10,2,1024]{2,1,0:T(2,128)S(1)}, f32[10,2,1024]{2,1,0:T(2,128)S(1)}, u32[]{:S(2)}, u32[]{:S(2)}) collective-permute-start(f32[10,2,1024]{2,1,0:T(2,128)S(1)} %get-tuple-element.21), channel_id=1, source_target_pairs={{4,8},{8,4},{12,16},{16,12},{20,24},{24,20},{28,0},{0,28},{5,9},{9... | collective-permute-start | bytes 245768 | tf_op jit(solution)/shard_map/ppermute | solution.py:381
  9.7 0.0 collective-permute-start.2
  9.7 1.4 %interior.1 = (f32[16,128]{1,0:T(8,128)S(1)}, f32[8,32,1024]{2,1,0:T(8,128)S(1)}, f32[2,8,1024]{2,1,0:T(8,128)S(1)}) custom-call(f32[8,32,1024]{2,1,0:T(8,128)S(1)} %copy-done), custom_call_target="tpu_custom_call" | custom-call | flops 5242880 | bytes 2097152 | tf_op jit(solution)/shard_map/interior/pallas_call | solution.py:151
  11.1 3.0 %collective-permute-done.2.near_strip_ref = f32[9,2,1024]{2,1,0:T(2,128)S(1)} collective-permute-done((f32[9,2,1024]{2,1,0:T(2,128)S(1)}, f32[9,2,1024]{2,1,0:T(2,128)S(1)}, u32[]{:S(2)}, u32[]{:S(2)}) %collective-permute-start.2) | collective-permute-done | bytes 73760 | tf_op jit(solution)/shard_map/ppermute | solution.py:381
  14.1 0.0 collective-permute-done.3.far_strip_ref
  14.1 0.0 collective-permute-done.near_ref
  14.1 0.0 collective-permute-done.1.far_ref
  14.1 0.0 copy-start.1
  14.1 0.8 %chunks.1 = (f32[32,1,128]{2,1,0:T(1,128)}, f32[2,1024]{1,0:T(2,128)S(1)}, f32[2,1024]{1,0:T(2,128)S(1)}, f32[2,8,1024]{2,1,0:T(8,128)S(1)}, f32[2,8,1024]{2,1,0:T(8,128)S(1)}, /*index=5*/f32[4,1024]{1,0:T(4,128)S(1)}) custom-call(f32[8,32,1024]{2,1,0:T(8,128)S(1)} %copy-done, f32[16,128]{1,0:T(8,128)S(1)} %get-tuple-element.16.part_ref, ...), custom_call_target="tpu_custom_call" | custom-call | tf_op jit(solution)/shard_map/chunks/pallas_call | solution.py:213
  14.9 3.3 %all-to-all-start = ((f32[32,1,128]{2,1,0:T(1,128)}), f32[32,1,128]{2,1,0:T(1,128)S(1)}, u32[]{:S(2)}, u32[]{:S(2)}) async-start(f32[32,1,128]{2,1,0:T(1,128)} %get-tuple-element.22), calls=%async_computation | async-start | bytes 32768 | tf_op jit(solution)/shard_map/all_to_all | solution.py:394
  18.2 0.3 %collective-permute-start.4 = (f32[2,1024]{1,0:T(2,128)S(1)}, f32[2,1024]{1,0:T(2,128)S(1)}, u32[]{:S(2)}, u32[]{:S(2)}) collective-permute-start(f32[2,1024]{1,0:T(2,128)S(1)} %get-tuple-element.23), channel_id=1, source_target_pairs={{0,1},{1,0},{2,3},{3,2},{4,5},{5,4},{6,7},{7,6},{8,9},{9,8},{10,11... | collective-permute-start | bytes 24584 | tf_op jit(solution)/shard_map/ppermute | solution.py:381
  18.5 1.6 %collective-permute-start.5 = (f32[2,1024]{1,0:T(2,128)S(1)}, f32[2,1024]{1,0:T(2,128)S(1)}, u32[]{:S(2)}, u32[]{:S(2)}) collective-permute-start(f32[2,1024]{1,0:T(2,128)S(1)} %get-tuple-element.24), channel_id=1, source_target_pairs={{1,2},{2,1},{3,0},{0,3},{5,6},{6,5},{7,4},{4,7},{9,10},{10,9},{11,... | collective-permute-start | bytes 24584 | tf_op jit(solution)/shard_map/ppermute | solution.py:381
  20.2 0.0 collective-permute-done.4.near_corner_ref
  20.2 1.5 %collective-permute-done.5.far_corner_ref = f32[2,1024]{1,0:T(2,128)S(1)} collective-permute-done((f32[2,1024]{1,0:T(2,128)S(1)}, f32[2,1024]{1,0:T(2,128)S(1)}, u32[]{:S(2)}, u32[]{:S(2)}) %collective-permute-start.5) | collective-permute-done | bytes 8224 | tf_op jit(solution)/shard_map/ppermute | solution.py:381
  21.6 3.7 %all-to-all-done.got_ref = f32[32,1,128]{2,1,0:T(1,128)S(1)} async-done(((f32[32,1,128]{2,1,0:T(1,128)}), f32[32,1,128]{2,1,0:T(1,128)S(1)}, u32[]{:S(2)}, u32[]{:S(2)}) %all-to-all-start) | async-done | bytes 16416 | tf_op jit(solution)/shard_map/all_to_all | solution.py:394
  25.3 0.0 copy-done.1
  25.3 2.8 %final.1 = (f32[8]{0:T(128)}, f32[8,32,1024]{2,1,0:T(8,128)}, f32[8,32,1024]{2,1,0:T(8,128)}) custom-call(f32[32,1,128]{2,1,0:T(1,128)S(1)} %all-to-all-done.got_ref, f32[2,1024]{1,0:T(2,128)S(1)} %collective-permute-done.4.near_corner_ref, f32[2,1024]{1,0:T(2,128)S(1)} %collective-permute-done.5.far_corner_ref, f32[8,32,1024]{2,1,0:T(8,128)S(1)} %copy-done.1, ...), custom_call_target="tpu_custom_call" | custom-call | tf_op jit(solution)/shard_map/final/pallas_call | solution.py:362
  (2 shorter events, 0.1 us)
Async XLA Ops:
  0.6 1.2 %copy-start = (f32[8,32,1024]{2,1,0:T(8,128)S(1)}, f32[8,32,1024]{2,1,0:T(8,128)}, u32[]{:S(2)}) copy-start(f32[8,32,1024]{2,1,0:T(8,128)} %f_ref.9) | copy-start | bytes 3145732
  1.9 3.2 %copy-start.2 = (f32[32,1024]{1,0:T(8,128)S(1)}, f32[32,1024]{1,0:T(8,128)}, u32[]{:S(2)}) copy-start(f32[32,1024]{1,0:T(8,128)} %start_ref.5) | copy-start | bytes 393220
  1.9 3.2 %copy-start.3 = (f32[32,1024]{1,0:T(8,128)S(1)}, f32[32,1024]{1,0:T(8,128)}, u32[]{:S(2)}) copy-start(f32[32,1024]{1,0:T(8,128)} %end_ref.5) | copy-start | bytes 393220
  1.9 12.2 %collective-permute-start = (f32[2,32,1024]{2,1,0:T(8,128)S(1)}, f32[2,32,1024]{2,1,0:T(8,128)S(1)}, u32[]{:S(2)}, u32[]{:S(2)}) collective-permute-start(f32[2,32,1024]{2,1,0:T(8,128)S(1)} %get-tuple-element.18), channel_id=1, source_target_pairs={{0,1},{1,0},{2,3},{3,2},{4,5},{5,4},{6,7},{7,6},{8,9},{9,8},{10,11... | collective-permute-start | bytes 786440 | tf_op jit(solution)/shard_map/ppermute | solution.py:381
  2.4 11.7 %collective-permute-start.1 = (f32[2,32,1024]{2,1,0:T(8,128)S(1)}, f32[2,32,1024]{2,1,0:T(8,128)S(1)}, u32[]{:S(2)}, u32[]{:S(2)}) collective-permute-start(f32[2,32,1024]{2,1,0:T(8,128)S(1)} %get-tuple-element.19), channel_id=1, source_target_pairs={{1,2},{2,1},{3,0},{0,3},{5,6},{6,5},{7,4},{4,7},{9,10},{10,9},{11,... | collective-permute-start | bytes 786440 | tf_op jit(solution)/shard_map/ppermute | solution.py:381
  5.1 9.0 %collective-permute-start.3 = (f32[10,2,1024]{2,1,0:T(2,128)S(1)}, f32[10,2,1024]{2,1,0:T(2,128)S(1)}, u32[]{:S(2)}, u32[]{:S(2)}) collective-permute-start(f32[10,2,1024]{2,1,0:T(2,128)S(1)} %get-tuple-element.21), channel_id=1, source_target_pairs={{4,8},{8,4},{12,16},{16,12},{20,24},{24,20},{28,0},{0,28},{5,9},{9... | collective-permute-start | bytes 245768 | tf_op jit(solution)/shard_map/ppermute | solution.py:381
  9.7 4.4 %collective-permute-start.2 = (f32[9,2,1024]{2,1,0:T(2,128)S(1)}, f32[9,2,1024]{2,1,0:T(2,128)S(1)}, u32[]{:S(2)}, u32[]{:S(2)}) collective-permute-start(f32[9,2,1024]{2,1,0:T(2,128)S(1)} %get-tuple-element.20), channel_id=1, source_target_pairs={{0,4},{4,0},{8,12},{12,8},{16,20},{20,16},{24,28},{28,24},{1,5},{5... | collective-permute-start | bytes 221192 | tf_op jit(solution)/shard_map/ppermute | solution.py:381
  14.1 11.2 %copy-start.1 = (f32[8,32,1024]{2,1,0:T(8,128)S(1)}, f32[8,32,1024]{2,1,0:T(8,128)}, u32[]{:S(2)}) copy-start(f32[8,32,1024]{2,1,0:T(8,128)} %f_ref.9) | copy-start | bytes 3145732
  14.9 10.4 %all-to-all-start = ((f32[32,1,128]{2,1,0:T(1,128)}), f32[32,1,128]{2,1,0:T(1,128)S(1)}, u32[]{:S(2)}, u32[]{:S(2)}) async-start(f32[32,1,128]{2,1,0:T(1,128)} %get-tuple-element.22), calls=%async_computation | async-start | bytes 32768 | tf_op jit(solution)/shard_map/all_to_all | solution.py:394
  18.2 2.0 %collective-permute-start.4 = (f32[2,1024]{1,0:T(2,128)S(1)}, f32[2,1024]{1,0:T(2,128)S(1)}, u32[]{:S(2)}, u32[]{:S(2)}) collective-permute-start(f32[2,1024]{1,0:T(2,128)S(1)} %get-tuple-element.23), channel_id=1, source_target_pairs={{0,1},{1,0},{2,3},{3,2},{4,5},{5,4},{6,7},{7,6},{8,9},{9,8},{10,11... | collective-permute-start | bytes 24584 | tf_op jit(solution)/shard_map/ppermute | solution.py:381
  18.5 3.1 %collective-permute-start.5 = (f32[2,1024]{1,0:T(2,128)S(1)}, f32[2,1024]{1,0:T(2,128)S(1)}, u32[]{:S(2)}, u32[]{:S(2)}) collective-permute-start(f32[2,1024]{1,0:T(2,128)S(1)} %get-tuple-element.24), channel_id=1, source_target_pairs={{1,2},{2,1},{3,0},{0,3},{5,6},{6,5},{7,4},{4,7},{9,10},{10,9},{11,... | collective-permute-start | bytes 24584 | tf_op jit(solution)/shard_map/ppermute | solution.py:381

commit v9 on v8

--- a/solution.py
+++ b/solution.py
@@ -13,6 +13,7 @@
 EPS = 1e-06
 VMEM = pl.BlockSpec(memory_space=pltpu.VMEM)
 ANY = pl.BlockSpec(memory_space=pl.ANY)
+PIECES = 4
 PARAMS = pltpu.CompilerParams(vmem_limit_bytes=16 * 2**20)
 
 
@@ -165,23 +166,22 @@
 
 def chunk_kernel(
     m, n, f_ref, part_ref, rim_ref, near_ref, far_ref, start_ref, end_ref, near_strip_ref, far_strip_ref,
-    out_ref, near_corner_ref, far_corner_ref, tail_ref, head_ref, face_ref,
+    out_ref, near_corner_ref, far_corner_ref, tail_ref, head_ref, face_ref, lines, sem,
 ):
     halo = Halo(m, near_ref, far_ref, start_ref, end_ref)
     count, rows, cols = f_ref.shape
     tiles = rows // TILE
 
     flag = odd("space")
-    for i, (ref, x_ref, y_ref) in enumerate(((tail_ref, near_strip_ref, far_strip_ref), (head_ref, far_strip_ref, near_strip_ref))):
+    strips = (tail_ref, near_strip_ref, far_strip_ref), (head_ref, far_strip_ref, near_strip_ref)
+
+    def sort(i, r):
+        ref, x_ref, y_ref = strips[i]
         for s in range(count):
-            both = pick(flag, x_ref[s], y_ref[s])
-            for r in range(2):
-                ref[r, s : s + 1, :] = both[r : r + 1]
-        face_ref[2 * i : 2 * i + 2, :] = pick(flag, x_ref[count], y_ref[count])
-    for ref, low in ((near_corner_ref, halo.odd), (far_corner_ref, jnp.logical_not(halo.odd))):
-        s = pl.ds(pick(low, 0, count - 1), 1)
-        ref[0:1, :] = tail_ref[1, s, :]
-        ref[1:2, :] = head_ref[0, s, :]
+            ref[r, s : s + 1, :] = pick(flag, x_ref[s, r : r + 1, :], y_ref[s, r : r + 1, :])
+
+    sort(0, 1)
+    sort(1, 0)
 
     drift_a = rim_ref[0] + tail_ref[1]
     drift_b = rim_ref[1] + head_ref[0]
@@ -203,7 +203,19 @@
     line = jnp.sum(spread, axis=0, keepdims=True)
 
     for j in range(m * n):
-        out_ref[j] = line
+        lines[j] = line
+    copy = pltpu.make_async_copy(lines, out_ref, sem)
+    copy.start()
+
+    sort(0, 0)
+    sort(1, 1)
+    for i, (_, x_ref, y_ref) in enumerate(strips):
+        face_ref[2 * i : 2 * i + 2, :] = pick(flag, x_ref[count], y_ref[count])
+    for ref, low in ((near_corner_ref, halo.odd), (far_corner_ref, jnp.logical_not(halo.odd))):
+        s = pl.ds(pick(low, 0, count - 1), 1)
+        ref[0:1, :] = tail_ref[1, s, :]
+        ref[1:2, :] = head_ref[0, s, :]
+    copy.wait()
 
 
 def chunks(m, n, f, part, rim, near, far, start, end, near_strip, far_strip):
@@ -221,7 +233,8 @@
             jax.ShapeDtypeStruct((4, cols), F32),
         ),
         in_specs=[VMEM] * 9,
-        out_specs=[VMEM] * 6,
+        out_specs=[ANY] + [VMEM] * 5,
+        scratch_shapes=[pltpu.VMEM((m * n, 1, LANES), F32), pltpu.SemaphoreType.DMA],
         compiler_params=PARAMS,
         name="chunks",
     )(f, part, rim, near, far, start, end, near_strip, far_strip)
@@ -229,7 +242,7 @@
 
 def final_kernel(
     m, n, got_ref, near_corner_ref, far_corner_ref, f_ref, drift_ref, near_ref, far_ref, start_ref, end_ref,
-    tail_ref, head_ref, face_ref, ratio_ref, res_out, grad_out, resid, grad, outer, rim, sem,
+    tail_ref, head_ref, face_ref, ratio_out, res_out, grad_out, ratio_ref, resid, grad, outer, rim, sem,
 ):
     halo = Halo(m, near_ref, far_ref, start_ref, end_ref)
     count, rows, cols = f_ref.shape
@@ -261,6 +274,8 @@
     high = jnp.where(last, 0.0, shift(ratios(upper), count + 1))
     own = ratios(mine)
     ratio_ref[...] = own[0, 0:count]
+    copies = [pltpu.make_async_copy(ratio_ref, ratio_out, sem.at[2, 0])]
+    copies[0].start()
     ratio = jnp.where(lane == 0, low, jnp.where(lane == count + 1, high, shift(own, 1)))
 
     def splat(t):
@@ -282,17 +297,49 @@
     def at(k):
         return pl.ds(TILE * k, TILE)
 
+    def value(s, k):
+        if s < 0:
+            return halo.below(at(k)) if s == -1 else halo.below_2(at(k))
+        if s >= count:
+            return halo.above(at(k)) if s == count else halo.above_2(at(k))
+        return f_ref[s, at(k), :]
+
+    def residual_of(s):
+        for k in range(tiles):
+            if 0 <= s < count:
+                drift = drift_ref[s, at(k), :]
+                if k == 0:
+                    drift += jnp.where(row == 0, tail_ref[1, s : s + 1, :], 0.0)
+                if k == tiles - 1:
+                    drift += jnp.where(row == TILE - 1, head_ref[0, s : s + 1, :], 0.0)
+            else:
+                slot = 0 if s < 0 else 1
+                c = outer[slot, at(k), :]
+                above = outer[slot, TILE * k - 1 : TILE * k, :] if k > 0 else corners[0][slot]
+                under = outer[slot, TILE * (k + 1) : TILE * (k + 1) + 1, :] if k < tiles - 1 else corners[1][slot]
+                up = jnp.where(row == 0, above, pltpu.roll(c, 1, 0))
+                dn = jnp.where(row == TILE - 1, under, pltpu.roll(c, TILE - 1, 0))
+                drift = up + dn + sides(c) - 3.0 * c - c * c * c
+            resid[s + 1, at(k + 1), :] = scale[s + 1] * (value(s + 1, k) - value(s - 1, k)) - drift
+
+    def send(src, dst, slot):
+        copy = pltpu.make_async_copy(src, dst, slot)
+        copy.start()
+        copies.append(copy)
+
+    pieces = PIECES if count % PIECES == 0 else 1
+    step = count // pieces
+    for i in range(pieces):
+        for s in range(i * step, (i + 1) * step):
+            residual_of(s)
+        span = pl.ds(i * step, step)
+        send(resid.at[pl.ds(i * step + 1, step), pl.ds(TILE, rows)], res_out.at[span], sem.at[0, i])
+
     for k in range(tiles):
         outer[0, at(k), :] = halo.below(at(k))
         outer[1, at(k), :] = halo.above(at(k))
-
-    def value(s, k):
-        if s == -2:
-            return halo.below_2(at(k))
-        if s == count + 1:
-            return halo.above_2(at(k))
-        ref, slot = {-1: (outer, 0), count: (outer, 1)}.get(s, (f_ref, s))
-        return ref[slot, at(k), :]
+    residual_of(-1)
+    residual_of(count)
 
     for s in range(count):
         rim[0, s : s + 1, :] = f_ref[s, 0:1, :]
@@ -307,51 +354,21 @@
         for s in range(count):
             resid[s + 1, place : place + 1, :] = edge[s : s + 1, :]
 
-    def residual_of(s):
-        if s in (-1, count):
-            slot = 0 if s < 0 else 1
-            top, bottom = corners[0][slot], corners[1][slot]
-        else:
-            top, bottom = tail_ref[1, s : s + 1, :], head_ref[0, s : s + 1, :]
+    def gradient_of(s):
+        r = [resid[s + 1, at(k + 1), :] for k in range(tiles)]
+        down = [resid[s + 1, TILE - 1 : TILE, :]] + [pltpu.roll(x, 1, 0) for x in r]
+        up = [pltpu.roll(x, TILE - 1, 0) for x in r] + [resid[s + 1, TILE + rows : TILE + rows + 1, :]]
         for k in range(tiles):
-            if s in (-1, count):
-                c = outer[slot, at(k), :]
-                above = outer[slot, TILE * k - 1 : TILE * k, :] if k > 0 else top
-                under = outer[slot, TILE * (k + 1) : TILE * (k + 1) + 1, :] if k < tiles - 1 else bottom
-                up = jnp.where(row == 0, above, pltpu.roll(c, 1, 0))
-                dn = jnp.where(row == TILE - 1, under, pltpu.roll(c, TILE - 1, 0))
-                drift = up + dn + sides(c) - 3.0 * c - c * c * c
-            else:
-                drift = drift_ref[s, at(k), :]
-                if k == 0:
-                    drift += jnp.where(row == 0, top, 0.0)
-                if k == tiles - 1:
-                    drift += jnp.where(row == TILE - 1, bottom, 0.0)
-            resid[s + 1, at(k + 1), :] = scale[s + 1] * (value(s + 1, k) - value(s - 1, k)) - drift
-
-    def gradient_of(s):
-        for k in range(tiles):
-            base = TILE * (k + 1)
-            c = f_ref[s, pl.ds(TILE * k, TILE), :]
-            r = resid[s + 1, pl.ds(base, TILE), :]
-            around = resid[s + 1, pl.ds(base - 1, TILE), :] + resid[s + 1, pl.ds(base + 1, TILE), :] + sides(r)
-            out = scale[s] * resid[s, pl.ds(base, TILE), :] - scale[s + 2] * resid[s + 2, pl.ds(base, TILE), :]
-            grad[s, pl.ds(TILE * k, TILE), :] = out - (around - (3.0 + 3.0 * c * c) * r)
-
-    copies = []
-
-    def send(src, dst, slot):
-        copy = pltpu.make_async_copy(src, dst, slot)
-        copy.start()
-        copies.append(copy)
-
-    residual_of(-1)
-    residual_of(0)
-    for s in range(count):
-        residual_of(s + 1)
-        send(resid.at[s + 1, pl.ds(TILE, rows)], res_out.at[s], sem.at[0, s])
-        gradient_of(s)
-        send(grad.at[s], grad_out.at[s], sem.at[1, s])
+            c = f_ref[s, at(k), :]
+            around = jnp.where(row == 0, down[k], down[k + 1]) + jnp.where(row == TILE - 1, up[k + 1], up[k]) + sides(r[k])
+            out = scale[s] * resid[s, at(k + 1), :] - scale[s + 2] * resid[s + 2, at(k + 1), :]
+            grad[s, at(k), :] = out - (around - (3.0 + 3.0 * c * c) * r[k])
+
+    for i in range(pieces):
+        for s in range(i * step, (i + 1) * step):
+            gradient_of(s)
+        span = pl.ds(i * step, step)
+        send(grad.at[span], grad_out.at[span], sem.at[1, i])
     for copy in copies:
         copy.wait()
 
@@ -363,13 +380,14 @@
         functools.partial(final_kernel, m, n),
         out_shape=(jax.ShapeDtypeStruct((count,), F32), big, big),
         in_specs=[VMEM] * 12,
-        out_specs=(VMEM, ANY, ANY),
+        out_specs=(ANY, ANY, ANY),
         scratch_shapes=[
+            pltpu.VMEM((count,), F32),
             pltpu.VMEM((count + 2, rows + 2 * TILE, cols), F32),
             pltpu.VMEM(f.shape, F32),
             pltpu.VMEM((2, rows, cols), F32),
             pltpu.VMEM((2, count, cols), F32),
-            pltpu.SemaphoreType.DMA((2, count)),
+            pltpu.SemaphoreType.DMA((3, PIECES)),
         ],
         compiler_params=PARAMS,
         name="final",

time: 28.3 us -> 27.7 us (0.979)
  Pallas kernels: 5.09 us -> 4.46 us
    pallas_call x1, Pallas kernels: 2.83 us -> 2.2 us  [final(): pl.pallas_call(functools.partial(final_kernel, m, n), out_shape=(jax.Shap...]
where the time goes in v9:
time: 27.7 us; the launch traced here: 27.5 us
  starting transfers between devices  13 us (47%)
  waiting for transfers between devices  8.09 us (29%)
  Pallas kernels  4.46 us (16%)
  local copies, waits for them, and re-layouts  1.23 us (4%)
  between operations  0.69 us (2%)
    ppermute x6, starting transfers between devices, swap(): lax.ppermute(x, axis, [((i + kind) % size, ((i ^ 1) + kind) % size) for i...  9.7 us
    ppermute x6, waiting for transfers between devices, swap(): lax.ppermute(x, axis, [((i + kind) % size, ((i ^ 1) + kind) % size) for i...  4.43 us
    all_to_all x1, waiting for transfers between devices, body(): got = lax.all_to_all(send, ('space', 'path'), 0, 0, tiled=True)  3.66 us
    all_to_all x1, starting transfers between devices, body(): got = lax.all_to_all(send, ('space', 'path'), 0, 0, tiled=True)  3.32 us
    pallas_call x1, Pallas kernels, final(): pl.pallas_call(functools.partial(final_kernel, m, n), out_shape=(jax.Shap...  2.2 us
    pallas_call x1, Pallas kernels, interior(): pl.pallas_call(interior_kernel, out_shape=(jax.ShapeDtypeStruct((2 * coun...  1.38 us
    unnamed x8, local copies, waits for them, and re-layouts  1.23 us
    pallas_call x1, Pallas kernels, chunks(): pl.pallas_call(functools.partial(chunk_kernel, m, n), out_shape=(jax.Shap...  0.8 us
  transfers between devices with their start and end apart: 7, of which 3 were waited for; matrix products, arithmetic and copies ran while one was open for 0% of the time, Pallas kernels for 5%

profile of v9, /device:TPU:0, one launch (start us, length us, event | category | flops | bytes accessed | tf_op | source)
XLA Modules:
  0.0 27.5 jit_solution(15351720675844381065)
XLA Ops:
  0.6 0.0 copy-start
  0.6 1.2 %copy-done = f32[8,32,1024]{2,1,0:T(8,128)S(1)} copy-done((f32[8,32,1024]{2,1,0:T(8,128)S(1)}, f32[8,32,1024]{2,1,0:T(8,128)}, u32[]{:S(2)}) %copy-start) | copy-done | bytes 1048600
  1.9 0.0 copy-start.2
  1.9 0.0 copy-start.3
  1.9 0.5 %collective-permute-start = (f32[2,32,1024]{2,1,0:T(8,128)S(1)}, f32[2,32,1024]{2,1,0:T(8,128)S(1)}, u32[]{:S(2)}, u32[]{:S(2)}) collective-permute-start(f32[2,32,1024]{2,1,0:T(8,128)S(1)} %get-tuple-element.18), channel_id=1, source_target_pairs={{0,1},{1,0},{2,3},{3,2},{4,5},{5,4},{6,7},{7,6},{8,9},{9,8},{10,11... | collective-permute-start | bytes 786440 | tf_op jit(solution)/shard_map/ppermute | solution.py:399
  2.4 2.6 %collective-permute-start.1 = (f32[2,32,1024]{2,1,0:T(8,128)S(1)}, f32[2,32,1024]{2,1,0:T(8,128)S(1)}, u32[]{:S(2)}, u32[]{:S(2)}) collective-permute-start(f32[2,32,1024]{2,1,0:T(8,128)S(1)} %get-tuple-element.19), channel_id=1, source_target_pairs={{1,2},{2,1},{3,0},{0,3},{5,6},{6,5},{7,4},{4,7},{9,10},{10,9},{11,... | collective-permute-start | bytes 786440 | tf_op jit(solution)/shard_map/ppermute | solution.py:399
  5.0 0.0 copy-done.2
  5.0 0.0 copy-done.3
  5.1 4.6 %collective-permute-start.3 = (f32[10,2,1024]{2,1,0:T(2,128)S(1)}, f32[10,2,1024]{2,1,0:T(2,128)S(1)}, u32[]{:S(2)}, u32[]{:S(2)}) collective-permute-start(f32[10,2,1024]{2,1,0:T(2,128)S(1)} %get-tuple-element.21), channel_id=1, source_target_pairs={{4,8},{8,4},{12,16},{16,12},{20,24},{24,20},{28,0},{0,28},{5,9},{9... | collective-permute-start | bytes 245768 | tf_op jit(solution)/shard_map/ppermute | solution.py:399
  9.7 0.0 collective-permute-start.2
  9.7 1.4 %interior.1 = (f32[16,128]{1,0:T(8,128)S(1)}, f32[8,32,1024]{2,1,0:T(8,128)S(1)}, f32[2,8,1024]{2,1,0:T(8,128)S(1)}) custom-call(f32[8,32,1024]{2,1,0:T(8,128)S(1)} %copy-done), custom_call_target="tpu_custom_call" | custom-call | flops 5242880 | bytes 2097152 | tf_op jit(solution)/shard_map/interior/pallas_call | solution.py:152
  11.1 3.0 %collective-permute-done.2.near_strip_ref = f32[9,2,1024]{2,1,0:T(2,128)S(1)} collective-permute-done((f32[9,2,1024]{2,1,0:T(2,128)S(1)}, f32[9,2,1024]{2,1,0:T(2,128)S(1)}, u32[]{:S(2)}, u32[]{:S(2)}) %collective-permute-start.2) | collective-permute-done | bytes 73760 | tf_op jit(solution)/shard_map/ppermute | solution.py:399
  14.1 0.0 collective-permute-done.3.far_strip_ref
  14.1 0.0 collective-permute-done.near_ref
  14.1 0.0 collective-permute-done.1.far_ref
  14.1 0.0 copy-start.1
  14.1 0.8 %chunks.1 = (f32[32,1,128]{2,1,0:T(1,128)}, f32[2,1024]{1,0:T(2,128)S(1)}, f32[2,1024]{1,0:T(2,128)S(1)}, f32[2,8,1024]{2,1,0:T(8,128)S(1)}, f32[2,8,1024]{2,1,0:T(8,128)S(1)}, /*index=5*/f32[4,1024]{1,0:T(4,128)S(1)}) custom-call(f32[8,32,1024]{2,1,0:T(8,128)S(1)} %copy-done, f32[16,128]{1,0:T(8,128)S(1)} %get-tuple-element.16.part_ref, ...), custom_call_target="tpu_custom_call" | custom-call | tf_op jit(solution)/shard_map/chunks/pallas_call | solution.py:225
  14.9 3.3 %all-to-all-start = ((f32[32,1,128]{2,1,0:T(1,128)}), f32[32,1,128]{2,1,0:T(1,128)S(1)}, u32[]{:S(2)}, u32[]{:S(2)}) async-start(f32[32,1,128]{2,1,0:T(1,128)} %get-tuple-element.22), calls=%async_computation | async-start | bytes 32768 | tf_op jit(solution)/shard_map/all_to_all | solution.py:412
  18.2 0.3 %collective-permute-start.4 = (f32[2,1024]{1,0:T(2,128)S(1)}, f32[2,1024]{1,0:T(2,128)S(1)}, u32[]{:S(2)}, u32[]{:S(2)}) collective-permute-start(f32[2,1024]{1,0:T(2,128)S(1)} %get-tuple-element.23), channel_id=1, source_target_pairs={{0,1},{1,0},{2,3},{3,2},{4,5},{5,4},{6,7},{7,6},{8,9},{9,8},{10,11... | collective-permute-start | bytes 24584 | tf_op jit(solution)/shard_map/ppermute | solution.py:399
  18.5 1.6 %collective-permute-start.5 = (f32[2,1024]{1,0:T(2,128)S(1)}, f32[2,1024]{1,0:T(2,128)S(1)}, u32[]{:S(2)}, u32[]{:S(2)}) collective-permute-start(f32[2,1024]{1,0:T(2,128)S(1)} %get-tuple-element.24), channel_id=1, source_target_pairs={{1,2},{2,1},{3,0},{0,3},{5,6},{6,5},{7,4},{4,7},{9,10},{10,9},{11,... | collective-permute-start | bytes 24584 | tf_op jit(solution)/shard_map/ppermute | solution.py:399
  20.2 0.0 collective-permute-done.4.near_corner_ref
  20.2 1.5 %collective-permute-done.5.far_corner_ref = f32[2,1024]{1,0:T(2,128)S(1)} collective-permute-done((f32[2,1024]{1,0:T(2,128)S(1)}, f32[2,1024]{1,0:T(2,128)S(1)}, u32[]{:S(2)}, u32[]{:S(2)}) %collective-permute-start.5) | collective-permute-done | bytes 8224 | tf_op jit(solution)/shard_map/ppermute | solution.py:399
  21.6 3.7 %all-to-all-done.got_ref = f32[32,1,128]{2,1,0:T(1,128)S(1)} async-done(((f32[32,1,128]{2,1,0:T(1,128)}), f32[32,1,128]{2,1,0:T(1,128)S(1)}, u32[]{:S(2)}, u32[]{:S(2)}) %all-to-all-start) | async-done | bytes 16416 | tf_op jit(solution)/shard_map/all_to_all | solution.py:412
  25.3 0.0 copy-done.1
  25.3 2.2 %final.1 = (f32[8]{0:T(128)}, f32[8,32,1024]{2,1,0:T(8,128)}, f32[8,32,1024]{2,1,0:T(8,128)}) custom-call(f32[32,1,128]{2,1,0:T(1,128)S(1)} %all-to-all-done.got_ref, f32[2,1024]{1,0:T(2,128)S(1)} %collective-permute-done.4.near_corner_ref, f32[2,1024]{1,0:T(2,128)S(1)} %collective-permute-done.5.far_corner_ref, f32[8,32,1024]{2,1,0:T(8,128)S(1)} %copy-done.1, ...), custom_call_target="tpu_custom_call" | custom-call | tf_op jit(solution)/shard_map/final/pallas_call | solution.py:379
  (2 shorter events, 0.1 us)
Async XLA Ops:
  0.6 1.2 %copy-start = (f32[8,32,1024]{2,1,0:T(8,128)S(1)}, f32[8,32,1024]{2,1,0:T(8,128)}, u32[]{:S(2)}) copy-start(f32[8,32,1024]{2,1,0:T(8,128)} %f_ref.9) | copy-start | bytes 3145732
  1.9 3.2 %copy-start.2 = (f32[32,1024]{1,0:T(8,128)S(1)}, f32[32,1024]{1,0:T(8,128)}, u32[]{:S(2)}) copy-start(f32[32,1024]{1,0:T(8,128)} %start_ref.5) | copy-start | bytes 393220
  1.9 3.2 %copy-start.3 = (f32[32,1024]{1,0:T(8,128)S(1)}, f32[32,1024]{1,0:T(8,128)}, u32[]{:S(2)}) copy-start(f32[32,1024]{1,0:T(8,128)} %end_ref.5) | copy-start | bytes 393220
  1.9 12.2 %collective-permute-start = (f32[2,32,1024]{2,1,0:T(8,128)S(1)}, f32[2,32,1024]{2,1,0:T(8,128)S(1)}, u32[]{:S(2)}, u32[]{:S(2)}) collective-permute-start(f32[2,32,1024]{2,1,0:T(8,128)S(1)} %get-tuple-element.18), channel_id=1, source_target_pairs={{0,1},{1,0},{2,3},{3,2},{4,5},{5,4},{6,7},{7,6},{8,9},{9,8},{10,11... | collective-permute-start | bytes 786440 | tf_op jit(solution)/shard_map/ppermute | solution.py:399
  2.4 11.7 %collective-permute-start.1 = (f32[2,32,1024]{2,1,0:T(8,128)S(1)}, f32[2,32,1024]{2,1,0:T(8,128)S(1)}, u32[]{:S(2)}, u32[]{:S(2)}) collective-permute-start(f32[2,32,1024]{2,1,0:T(8,128)S(1)} %get-tuple-element.19), channel_id=1, source_target_pairs={{1,2},{2,1},{3,0},{0,3},{5,6},{6,5},{7,4},{4,7},{9,10},{10,9},{11,... | collective-permute-start | bytes 786440 | tf_op jit(solution)/shard_map/ppermute | solution.py:399
  5.1 9.0 %collective-permute-start.3 = (f32[10,2,1024]{2,1,0:T(2,128)S(1)}, f32[10,2,1024]{2,1,0:T(2,128)S(1)}, u32[]{:S(2)}, u32[]{:S(2)}) collective-permute-start(f32[10,2,1024]{2,1,0:T(2,128)S(1)} %get-tuple-element.21), channel_id=1, source_target_pairs={{4,8},{8,4},{12,16},{16,12},{20,24},{24,20},{28,0},{0,28},{5,9},{9... | collective-permute-start | bytes 245768 | tf_op jit(solution)/shard_map/ppermute | solution.py:399
  9.7 4.4 %collective-permute-start.2 = (f32[9,2,1024]{2,1,0:T(2,128)S(1)}, f32[9,2,1024]{2,1,0:T(2,128)S(1)}, u32[]{:S(2)}, u32[]{:S(2)}) collective-permute-start(f32[9,2,1024]{2,1,0:T(2,128)S(1)} %get-tuple-element.20), channel_id=1, source_target_pairs={{0,4},{4,0},{8,12},{12,8},{16,20},{20,16},{24,28},{28,24},{1,5},{5... | collective-permute-start | bytes 221192 | tf_op jit(solution)/shard_map/ppermute | solution.py:399
  14.1 11.2 %copy-start.1 = (f32[8,32,1024]{2,1,0:T(8,128)S(1)}, f32[8,32,1024]{2,1,0:T(8,128)}, u32[]{:S(2)}) copy-start(f32[8,32,1024]{2,1,0:T(8,128)} %f_ref.9) | copy-start | bytes 3145732
  14.9 10.4 %all-to-all-start = ((f32[32,1,128]{2,1,0:T(1,128)}), f32[32,1,128]{2,1,0:T(1,128)S(1)}, u32[]{:S(2)}, u32[]{:S(2)}) async-start(f32[32,1,128]{2,1,0:T(1,128)} %get-tuple-element.22), calls=%async_computation | async-start | bytes 32768 | tf_op jit(solution)/shard_map/all_to_all | solution.py:412
  18.2 2.0 %collective-permute-start.4 = (f32[2,1024]{1,0:T(2,128)S(1)}, f32[2,1024]{1,0:T(2,128)S(1)}, u32[]{:S(2)}, u32[]{:S(2)}) collective-permute-start(f32[2,1024]{1,0:T(2,128)S(1)} %get-tuple-element.23), channel_id=1, source_target_pairs={{0,1},{1,0},{2,3},{3,2},{4,5},{5,4},{6,7},{7,6},{8,9},{9,8},{10,11... | collective-permute-start | bytes 24584 | tf_op jit(solution)/shard_map/ppermute | solution.py:399
  18.5 3.1 %collective-permute-start.5 = (f32[2,1024]{1,0:T(2,128)S(1)}, f32[2,1024]{1,0:T(2,128)S(1)}, u32[]{:S(2)}, u32[]{:S(2)}) collective-permute-start(f32[2,1024]{1,0:T(2,128)S(1)} %get-tuple-element.24), channel_id=1, source_target_pairs={{1,2},{2,1},{3,0},{0,3},{5,6},{6,5},{7,4},{4,7},{9,10},{10,9},{11,... | collective-permute-start | bytes 24584 | tf_op jit(solution)/shard_map/ppermute | solution.py:399

commit v10 on v9

--- a/solution.py
+++ b/solution.py
@@ -14,6 +14,7 @@
 VMEM = pl.BlockSpec(memory_space=pltpu.VMEM)
 ANY = pl.BlockSpec(memory_space=pl.ANY)
 PIECES = 4
+WIDTH = 384
 PARAMS = pltpu.CompilerParams(vmem_limit_bytes=16 * 2**20)
 
 
@@ -50,18 +51,12 @@
             ref[s] = f_ref[base + s]
 
 
-def strips_kernel(f_ref, start_ref, end_ref, near_ref, far_ref):
+def tail_kernel(f_ref, start_ref, end_ref, tail_ref):
     count, rows, _ = f_ref.shape
-    flag = odd("space")
-    for ref, low in ((near_ref, flag), (far_ref, jnp.logical_not(flag))):
-        at = pick(low, 0, rows - 2)
-        face = pl.ds(pick(low, 0, rows - 1), 1)
-        ref[count:] = jnp.zeros_like(ref[count:])
-        ref[count, 0:1, :] = start_ref[face, :]
-        ref[count, 1:2, :] = end_ref[face, :]
-        for s in range(count):
-            for r in range(2):
-                ref[s, r : r + 1, :] = f_ref[s, pl.ds(at + r, 1), :]
+    tail_ref[count, 0:1, :] = start_ref[rows - 1 :, :]
+    tail_ref[count, 1:2, :] = end_ref[rows - 1 :, :]
+    for s in range(count):
+        tail_ref[s] = f_ref[s, rows - 2 :, :]
 
 
 def slices(f):
@@ -76,15 +71,15 @@
     )(f)
 
 
-def strips(f, start, end):
+def tail_rows(f, start, end):
     count, rows, cols = f.shape
     return pl.pallas_call(
-        strips_kernel,
-        out_shape=tuple(jax.ShapeDtypeStruct((count + k, 2, cols), F32) for k in (1, 2)),
+        tail_kernel,
+        out_shape=jax.ShapeDtypeStruct((count + 1, 2, cols), F32),
         in_specs=[VMEM] * 3,
-        out_specs=[VMEM] * 2,
+        out_specs=VMEM,
         compiler_params=PARAMS,
-        name="strips",
+        name="tail_rows",
     )(f, start, end)
 
 
@@ -127,9 +122,9 @@
             drift_ref[s, pl.ds(TILE * k, TILE), :] = drift
             if k == 0:
                 rim_ref[0, pl.ds(s, 1), :] = drift[0:1]
+                rim_ref[1, pl.ds(s, 1), :] = c[0:1]
                 drift = jnp.where(row == 0, 0.0, drift)
             if k == tiles - 1:
-                rim_ref[1, pl.ds(s, 1), :] = drift[TILE - 1 : TILE]
                 drift = jnp.where(row == TILE - 1, 0.0, drift)
             total += lanes_sum(drift * drift)
         part_ref[pl.ds(s, 1), :] = jnp.sum(total, axis=0, keepdims=True)
@@ -165,26 +160,20 @@
 
 
 def chunk_kernel(
-    m, n, f_ref, part_ref, rim_ref, near_ref, far_ref, start_ref, end_ref, near_strip_ref, far_strip_ref,
-    out_ref, near_corner_ref, far_corner_ref, tail_ref, head_ref, face_ref, lines, sem,
+    m, n, f_ref, part_ref, rim_ref, near_ref, far_ref, start_ref, end_ref, strip_ref,
+    out_ref, near_corner_ref, far_corner_ref, tail_ref, head_ref, lines, sem,
 ):
     halo = Halo(m, near_ref, far_ref, start_ref, end_ref)
     count, rows, cols = f_ref.shape
     tiles = rows // TILE
 
-    flag = odd("space")
-    strips = (tail_ref, near_strip_ref, far_strip_ref), (head_ref, far_strip_ref, near_strip_ref)
-
-    def sort(i, r):
-        ref, x_ref, y_ref = strips[i]
-        for s in range(count):
-            ref[r, s : s + 1, :] = pick(flag, x_ref[s, r : r + 1, :], y_ref[s, r : r + 1, :])
-
-    sort(0, 1)
-    sort(1, 0)
-
-    drift_a = rim_ref[0] + tail_ref[1]
-    drift_b = rim_ref[1] + head_ref[0]
+    for s in range(count):
+        for r in range(2):
+            tail_ref[r, s : s + 1, :] = strip_ref[s, r : r + 1, :]
+    r0, r1 = tail_ref[0], tail_ref[1]
+
+    drift_a = r0 + rim_ref[1] + sides(r1) - 3.0 * r1 - r1 * r1 * r1
+    drift_b = rim_ref[0] + r1
     drift = part_ref[0:count, :] + lanes_sum(drift_a * drift_a) + lanes_sum(drift_b * drift_b)
 
     totals = [jnp.zeros((TILE, LANES), F32) for _ in range(2)]
@@ -202,47 +191,45 @@
     spread += jnp.where(lane == sub + count, jnp.sum(tangent, axis=1, keepdims=True), 0.0)
     line = jnp.sum(spread, axis=0, keepdims=True)
 
+    if WIDTH > LANES:
+        line = jnp.concatenate([line, jnp.zeros((1, WIDTH - LANES), F32)], axis=1)
     for j in range(m * n):
         lines[j] = line
     copy = pltpu.make_async_copy(lines, out_ref, sem)
     copy.start()
 
-    sort(0, 0)
-    sort(1, 1)
-    for i, (_, x_ref, y_ref) in enumerate(strips):
-        face_ref[2 * i : 2 * i + 2, :] = pick(flag, x_ref[count], y_ref[count])
     for ref, low in ((near_corner_ref, halo.odd), (far_corner_ref, jnp.logical_not(halo.odd))):
-        s = pl.ds(pick(low, 0, count - 1), 1)
-        ref[0:1, :] = tail_ref[1, s, :]
-        ref[1:2, :] = head_ref[0, s, :]
+        ref[...] = tail_ref[1, pl.ds(pick(low, 0, count - 1), 1), :]
+    for s in range(count):
+        head_ref[s] = f_ref[s, 0:2, :]
+    head_ref[count, 0:1, :] = halo.below(pl.ds(0, 1))
+    head_ref[count, 1:2, :] = halo.above(pl.ds(0, 1))
     copy.wait()
 
 
-def chunks(m, n, f, part, rim, near, far, start, end, near_strip, far_strip):
+def chunks(m, n, f, part, rim, near, far, start, end, strip):
     count, rows, cols = f.shape
-    corner = jax.ShapeDtypeStruct((2, cols), F32)
-    strip = jax.ShapeDtypeStruct((2, count, cols), F32)
+    corner = jax.ShapeDtypeStruct((1, cols), F32)
     return pl.pallas_call(
         functools.partial(chunk_kernel, m, n),
         out_shape=(
-            jax.ShapeDtypeStruct((m * n, 1, LANES), F32),
+            jax.ShapeDtypeStruct((m * n, 1, WIDTH), F32),
             corner,
             corner,
-            strip,
-            strip,
-            jax.ShapeDtypeStruct((4, cols), F32),
+            jax.ShapeDtypeStruct((2, count, cols), F32),
+            jax.ShapeDtypeStruct((count + 1, 2, cols), F32),
         ),
-        in_specs=[VMEM] * 9,
-        out_specs=[ANY] + [VMEM] * 5,
-        scratch_shapes=[pltpu.VMEM((m * n, 1, LANES), F32), pltpu.SemaphoreType.DMA],
+        in_specs=[VMEM] * 8,
+        out_specs=[ANY] + [VMEM] * 4,
+        scratch_shapes=[pltpu.VMEM((m * n, 1, WIDTH), F32), pltpu.SemaphoreType.DMA],
         compiler_params=PARAMS,
         name="chunks",
-    )(f, part, rim, near, far, start, end, near_strip, far_strip)
+    )(f, part, rim, near, far, start, end, strip)
 
 
 def final_kernel(
     m, n, got_ref, near_corner_ref, far_corner_ref, f_ref, drift_ref, near_ref, far_ref, start_ref, end_ref,
-    tail_ref, head_ref, face_ref, ratio_out, res_out, grad_out, ratio_ref, resid, grad, outer, rim, sem,
+    strip_ref, tail_ref, lead_ref, ratio_out, res_out, grad_out, ratio_ref, resid, grad, outer, rim, head_ref, sem,
 ):
     halo = Halo(m, near_ref, far_ref, start_ref, end_ref)
     count, rows, cols = f_ref.shape
@@ -253,9 +240,9 @@
     path_hi = jnp.where(last, path, path + 1)
 
     def gathered(p):
-        total = got_ref[p]
+        total = got_ref[p, :, 0:LANES]
         for i in range(1, n):
-            total += got_ref[i * m + p]
+            total += got_ref[i * m + p, :, 0:LANES]
         return jnp.broadcast_to(total, (TILE, LANES))
 
     mine = gathered(path)
@@ -287,12 +274,14 @@
     scale = [widen(splat(t)) for t in range(count + 2)]
     column = jnp.sum(jnp.where(lane == sub + 1, ratio, 0.0), axis=1, keepdims=True)
     row = iota((TILE, cols), 0)
-    corners = []
-    for i in range(2):
-        near, far = near_corner_ref[i : i + 1, :], far_corner_ref[i : i + 1, :]
-        low = pick(first, face_ref[2 * i : 2 * i + 1, :], pick(halo.odd, near, far))
-        high = pick(last, face_ref[2 * i + 1 : 2 * i + 2, :], pick(halo.odd, far, near))
-        corners.append((low, high))
+    near, far = near_corner_ref[...], far_corner_ref[...]
+    corners = (
+        (
+            pick(first, strip_ref[count, 0:1, :], pick(halo.odd, near, far)),
+            pick(last, strip_ref[count, 1:2, :], pick(halo.odd, far, near)),
+        ),
+        (lead_ref[count, 0:1, :], lead_ref[count, 1:2, :]),
+    )
 
     def at(k):
         return pl.ds(TILE * k, TILE)
@@ -311,7 +300,7 @@
                 if k == 0:
                     drift += jnp.where(row == 0, tail_ref[1, s : s + 1, :], 0.0)
                 if k == tiles - 1:
-                    drift += jnp.where(row == TILE - 1, head_ref[0, s : s + 1, :], 0.0)
+                    drift += jnp.where(row == TILE - 1, lead_ref[s, 0:1, :], 0.0)
             else:
                 slot = 0 if s < 0 else 1
                 c = outer[slot, at(k), :]
@@ -344,6 +333,8 @@
     for s in range(count):
         rim[0, s : s + 1, :] = f_ref[s, 0:1, :]
         rim[1, s : s + 1, :] = f_ref[s, rows - 1 : rows, :]
+        for r in range(2):
+            head_ref[r, s : s + 1, :] = lead_ref[s, r : r + 1, :]
     for far, mid, near, (low, high), place in (
         (tail_ref[0], tail_ref[1], rim[0], corners[0], TILE - 1),
         (head_ref[1], head_ref[0], rim[1], corners[1], TILE + rows),
@@ -387,6 +378,7 @@
             pltpu.VMEM(f.shape, F32),
             pltpu.VMEM((2, rows, cols), F32),
             pltpu.VMEM((2, count, cols), F32),
+            pltpu.VMEM((2, count, cols), F32),
             pltpu.SemaphoreType.DMA((3, PIECES)),
         ],
         compiler_params=PARAMS,
@@ -394,24 +386,28 @@
     )(got, *corners, f, drift, *slabs, *strips)
 
 
-def swap(x, axis, kind):
-    size = lax.axis_size(axis)
-    return lax.ppermute(x, axis, [((i + kind) % size, ((i ^ 1) + kind) % size) for i in range(size)])
+def swap(x, kind):
+    size = lax.axis_size("path")
+    return lax.ppermute(x, "path", [((i + kind) % size, ((i ^ 1) + kind) % size) for i in range(size)])
+
+
+def ring(x, step):
+    size = lax.axis_size("space")
+    return lax.ppermute(x, "space", [(i, (i + step) % size) for i in range(size)])
 
 
 def body(m, n, f, start, end):
     near, far = slices(f)
-    near_strip, far_strip = strips(f, start, end)
-    far = swap(far, "path", 1)
-    near = swap(near, "path", 0)
-    far_strip = swap(far_strip, "space", 1)
-    near_strip = swap(near_strip, "space", 0)
+    strip = ring(tail_rows(f, start, end), 1)
+    far = swap(far, 1)
+    near = swap(near, 0)
     part, drift, rim = interior(f)
     slabs = near, far, start, end
-    send, near_corner, far_corner, *sorted_strips = chunks(m, n, f, part, rim, *slabs, near_strip, far_strip)
+    send, near_corner, far_corner, tail, head = chunks(m, n, f, part, rim, *slabs, strip)
     got = lax.all_to_all(send, ("space", "path"), 0, 0, tiled=True)
-    corners = swap(near_corner, "path", 0), swap(far_corner, "path", 1)
-    return final(m, n, got, corners, f, drift, slabs, sorted_strips)
+    lead = ring(head, -1)
+    corners = swap(near_corner, 0), swap(far_corner, 1)
+    return final(m, n, got, corners, f, drift, slabs, (strip, tail, lead))
 
 
 def solution(mesh):

time: 27.7 us -> 28.4 us (1.025)
  starting transfers between devices: 13 us -> 16.1 us
  waiting for transfers between devices: 8.09 us -> 5.59 us
    all_to_all x1, waiting for transfers between devices: 3.66 us -> 0.01 us  [body(): got = lax.all_to_all(send, ('space', 'path'), 0, 0, tiled=True)]
    all_to_all x1, starting transfers between devices: 3.32 us -> 5.24 us  [body(): got = lax.all_to_all(send, ('space', 'path'), 0, 0, tiled=True)]
    ppermute x6, starting transfers between devices: 9.7 us -> 10.9 us  [the longest x2 6.18 us: ring(): lax.ppermute(x, 'space', [(i, (i + step) % size) for i in range(size)])]
    ppermute x6, waiting for transfers between devices: 4.43 us -> 5.59 us  [the longest x2 4.14 us: ring(): lax.ppermute(x, 'space', [(i, (i + step) % size) for i in range(size)])]
  transfers between devices with their start and end apart: 7 -> 7, of which waited for: 3 -> 2; matrix products, arithmetic and copies ran while one was open for 0% -> 0% of each run, Pallas kernels for 5% -> 5%
where the time goes in v10:
time: 28.4 us; the launch traced here: 28.1 us
  starting transfers between devices  16.1 us (57%)
  waiting for transfers between devices  5.59 us (20%)
  Pallas kernels  4.49 us (16%)
  local copies, waits for them, and re-layouts  1.23 us (4%)
  between operations  0.69 us (2%)
    ppermute x2, starting transfers between devices, ring(): lax.ppermute(x, 'space', [(i, (i + step) % size) for i in range(size)])  6.18 us
    all_to_all x1, starting transfers between devices, body(): got = lax.all_to_all(send, ('space', 'path'), 0, 0, tiled=True)  5.24 us
    ppermute x4, starting transfers between devices, swap(): lax.ppermute(x, 'path', [((i + kind) % size, ((i ^ 1) + kind) % size) for...  4.73 us
    ppermute x2, waiting for transfers between devices, ring(): lax.ppermute(x, 'space', [(i, (i + step) % size) for i in range(size)])  4.14 us
    pallas_call x1, Pallas kernels, final(): pl.pallas_call(functools.partial(final_kernel, m, n), out_shape=(jax.Shap...  2.22 us
    ppermute x4, waiting for transfers between devices, swap(): lax.ppermute(x, 'path', [((i + kind) % size, ((i ^ 1) + kind) % size) for...  1.45 us
    pallas_call x1, Pallas kernels, interior(): pl.pallas_call(interior_kernel, out_shape=(jax.ShapeDtypeStruct((2 * coun...  1.38 us
    unnamed x8, local copies, waits for them, and re-layouts  1.23 us
  transfers between devices with their start and end apart: 7, of which 2 were waited for; matrix products, arithmetic and copies ran while one was open for 0% of the time, Pallas kernels for 5%

profile of v10, /device:TPU:0, one launch (start us, length us, event | category | flops | bytes accessed | tf_op | source)
XLA Modules:
  0.0 28.1 jit_solution(17947781686624022889)
XLA Ops:
  0.6 0.0 copy-start
  0.6 1.2 %copy-done = f32[8,32,1024]{2,1,0:T(8,128)S(1)} copy-done((f32[8,32,1024]{2,1,0:T(8,128)S(1)}, f32[8,32,1024]{2,1,0:T(8,128)}, u32[]{:S(2)}) %copy-start) | copy-done | bytes 1048600
  1.9 0.0 copy-start.2
  1.9 0.0 copy-start.3
  1.9 0.5 %collective-permute-start = (f32[2,32,1024]{2,1,0:T(8,128)S(1)}, f32[2,32,1024]{2,1,0:T(8,128)S(1)}, u32[]{:S(2)}, u32[]{:S(2)}) collective-permute-start(f32[2,32,1024]{2,1,0:T(8,128)S(1)} %get-tuple-element.15), channel_id=1, source_target_pairs={{0,1},{1,0},{2,3},{3,2},{4,5},{5,4},{6,7},{7,6},{8,9},{9,8},{10,11... | collective-permute-start | bytes 786440 | tf_op jit(solution)/shard_map/ppermute | solution.py:391
  2.4 2.6 %collective-permute-start.1 = (f32[2,32,1024]{2,1,0:T(8,128)S(1)}, f32[2,32,1024]{2,1,0:T(8,128)S(1)}, u32[]{:S(2)}, u32[]{:S(2)}) collective-permute-start(f32[2,32,1024]{2,1,0:T(8,128)S(1)} %get-tuple-element.16), channel_id=1, source_target_pairs={{1,2},{2,1},{3,0},{0,3},{5,6},{6,5},{7,4},{4,7},{9,10},{10,9},{11,... | collective-permute-start | bytes 786440 | tf_op jit(solution)/shard_map/ppermute | solution.py:391
  5.0 0.0 copy-done.2
  5.0 0.0 copy-done.3
  5.1 1.6 %collective-permute-start.2 = (f32[9,2,1024]{2,1,0:T(2,128)S(1)}, f32[9,2,1024]{2,1,0:T(2,128)S(1)}, u32[]{:S(2)}, u32[]{:S(2)}) collective-permute-start(f32[9,2,1024]{2,1,0:T(2,128)S(1)} %tail_rows.1), channel_id=1, source_target_pairs={{0,4},{4,8},{8,12},{12,16},{16,20},{20,24},{24,28},{28,0},{1,5},{5... | collective-permute-start | bytes 221192 | tf_op jit(solution)/shard_map/ppermute | solution.py:396
  6.6 1.4 %interior.1 = (f32[16,128]{1,0:T(8,128)S(1)}, f32[8,32,1024]{2,1,0:T(8,128)S(1)}, f32[2,8,1024]{2,1,0:T(8,128)S(1)}) custom-call(f32[8,32,1024]{2,1,0:T(8,128)S(1)} %copy-done), custom_call_target="tpu_custom_call" | custom-call | flops 5242880 | bytes 2097152 | tf_op jit(solution)/shard_map/interior/pallas_call | solution.py:147
  8.0 0.0 copy-start.1
  8.0 4.1 %collective-permute-done.2.strip_ref = f32[9,2,1024]{2,1,0:T(2,128)S(1)} collective-permute-done((f32[9,2,1024]{2,1,0:T(2,128)S(1)}, f32[9,2,1024]{2,1,0:T(2,128)S(1)}, u32[]{:S(2)}, u32[]{:S(2)}) %collective-permute-start.2) | collective-permute-done | bytes 73760 | tf_op jit(solution)/shard_map/ppermute | solution.py:396
  12.2 0.0 collective-permute-done.near_ref
  12.2 0.0 collective-permute-done.1.far_ref
  12.2 0.8 %chunks.1 = (f32[32,1,384]{2,1,0:T(1,128)}, f32[1,1024]{1,0:T(1,128)S(1)}, f32[1,1024]{1,0:T(1,128)S(1)}, f32[2,8,1024]{2,1,0:T(8,128)S(1)}, f32[9,2,1024]{2,1,0:T(2,128)S(1)}) custom-call(f32[8,32,1024]{2,1,0:T(8,128)S(1)} %copy-done, f32[16,128]{1,0:T(8,128)S(1)} %get-tuple-element.13.part_ref, f32[2,8,1024]{2,1,0:T(8,128)S(1)} %get-tuple-element.14.rim_ref, ...), custom_call_target="tpu_custom_call" | custom-call | tf_op jit(solution)/shard_map/chunks/pallas_call | solution.py:213
  13.0 5.2 %all-to-all-start = ((f32[32,1,384]{2,1,0:T(1,128)}), f32[32,1,384]{2,1,0:T(1,128)S(1)}, u32[]{:S(2)}, u32[]{:S(2)}) async-start(f32[32,1,384]{2,1,0:T(1,128)} %get-tuple-element.17), calls=%async_computation | async-start | bytes 98304 | tf_op jit(solution)/shard_map/all_to_all | solution.py:407
  18.3 4.6 %collective-permute-start.5 = (f32[9,2,1024]{2,1,0:T(2,128)S(1)}, f32[9,2,1024]{2,1,0:T(2,128)S(1)}, u32[]{:S(2)}, u32[]{:S(2)}) collective-permute-start(f32[9,2,1024]{2,1,0:T(2,128)S(1)} %get-tuple-element.22), channel_id=1, source_target_pairs={{0,28},{4,0},{8,4},{12,8},{16,12},{20,16},{24,20},{28,24},{1,29},{... | collective-permute-start | bytes 221192 | tf_op jit(solution)/shard_map/ppermute | solution.py:396
  22.9 0.0 collective-permute-start.3
  22.9 1.6 %collective-permute-start.4 = (f32[1,1024]{1,0:T(1,128)S(1)}, f32[1,1024]{1,0:T(1,128)S(1)}, u32[]{:S(2)}, u32[]{:S(2)}) collective-permute-start(f32[1,1024]{1,0:T(1,128)S(1)} %get-tuple-element.19), channel_id=1, source_target_pairs={{1,2},{2,1},{3,0},{0,3},{5,6},{6,5},{7,4},{4,7},{9,10},{10,9},{11,... | collective-permute-start | bytes 12296 | tf_op jit(solution)/shard_map/ppermute | solution.py:391
  24.5 0.0 collective-permute-done.3.near_corner_ref
  24.5 1.4 %collective-permute-done.4.far_corner_ref = f32[1,1024]{1,0:T(1,128)S(1)} collective-permute-done((f32[1,1024]{1,0:T(1,128)S(1)}, f32[1,1024]{1,0:T(1,128)S(1)}, u32[]{:S(2)}, u32[]{:S(2)}) %collective-permute-start.4) | collective-permute-done | bytes 4128 | tf_op jit(solution)/shard_map/ppermute | solution.py:391
  25.9 0.0 collective-permute-done.5.lead_ref
  25.9 0.0 all-to-all-done.got_ref
  25.9 0.0 copy-done.1
  25.9 2.2 %final.1 = (f32[8]{0:T(128)}, f32[8,32,1024]{2,1,0:T(8,128)}, f32[8,32,1024]{2,1,0:T(8,128)}) custom-call(f32[32,1,384]{2,1,0:T(1,128)S(1)} %all-to-all-done.got_ref, f32[1,1024]{1,0:T(1,128)S(1)} %collective-permute-done.3.near_corner_ref, f32[1,1024]{1,0:T(1,128)S(1)} %collective-permute-done.4.far_corner_ref, f32[8,32,1024]{2,1,0:T(8,128)S(1)} %copy-done.1, ...), custom_call_target="tpu_custom_call" | custom-call | tf_op jit(solution)/shard_map/final/pallas_call | solution.py:370
  (2 shorter events, 0.1 us)
Async XLA Ops:
  0.6 1.2 %copy-start = (f32[8,32,1024]{2,1,0:T(8,128)S(1)}, f32[8,32,1024]{2,1,0:T(8,128)}, u32[]{:S(2)}) copy-start(f32[8,32,1024]{2,1,0:T(8,128)} %f_ref.9) | copy-start | bytes 3145732
  1.9 3.2 %copy-start.2 = (f32[32,1024]{1,0:T(8,128)S(1)}, f32[32,1024]{1,0:T(8,128)}, u32[]{:S(2)}) copy-start(f32[32,1024]{1,0:T(8,128)} %start_ref.5) | copy-start | bytes 393220
  1.9 3.2 %copy-start.3 = (f32[32,1024]{1,0:T(8,128)S(1)}, f32[32,1024]{1,0:T(8,128)}, u32[]{:S(2)}) copy-start(f32[32,1024]{1,0:T(8,128)} %end_ref.5) | copy-start | bytes 393220
  1.9 10.3 %collective-permute-start = (f32[2,32,1024]{2,1,0:T(8,128)S(1)}, f32[2,32,1024]{2,1,0:T(8,128)S(1)}, u32[]{:S(2)}, u32[]{:S(2)}) collective-permute-start(f32[2,32,1024]{2,1,0:T(8,128)S(1)} %get-tuple-element.15), channel_id=1, source_target_pairs={{0,1},{1,0},{2,3},{3,2},{4,5},{5,4},{6,7},{7,6},{8,9},{9,8},{10,11... | collective-permute-start | bytes 786440 | tf_op jit(solution)/shard_map/ppermute | solution.py:391
  2.4 9.8 %collective-permute-start.1 = (f32[2,32,1024]{2,1,0:T(8,128)S(1)}, f32[2,32,1024]{2,1,0:T(8,128)S(1)}, u32[]{:S(2)}, u32[]{:S(2)}) collective-permute-start(f32[2,32,1024]{2,1,0:T(8,128)S(1)} %get-tuple-element.16), channel_id=1, source_target_pairs={{1,2},{2,1},{3,0},{0,3},{5,6},{6,5},{7,4},{4,7},{9,10},{10,9},{11,... | collective-permute-start | bytes 786440 | tf_op jit(solution)/shard_map/ppermute | solution.py:391
  5.1 7.1 %collective-permute-start.2 = (f32[9,2,1024]{2,1,0:T(2,128)S(1)}, f32[9,2,1024]{2,1,0:T(2,128)S(1)}, u32[]{:S(2)}, u32[]{:S(2)}) collective-permute-start(f32[9,2,1024]{2,1,0:T(2,128)S(1)} %tail_rows.1), channel_id=1, source_target_pairs={{0,4},{4,8},{8,12},{12,16},{16,20},{20,24},{24,28},{28,0},{1,5},{5... | collective-permute-start | bytes 221192 | tf_op jit(solution)/shard_map/ppermute | solution.py:396
  8.0 17.9 %copy-start.1 = (f32[8,32,1024]{2,1,0:T(8,128)S(1)}, f32[8,32,1024]{2,1,0:T(8,128)}, u32[]{:S(2)}) copy-start(f32[8,32,1024]{2,1,0:T(8,128)} %f_ref.9) | copy-start | bytes 3145732
  13.0 12.9 %all-to-all-start = ((f32[32,1,384]{2,1,0:T(1,128)}), f32[32,1,384]{2,1,0:T(1,128)S(1)}, u32[]{:S(2)}, u32[]{:S(2)}) async-start(f32[32,1,384]{2,1,0:T(1,128)} %get-tuple-element.17), calls=%async_computation | async-start | bytes 98304 | tf_op jit(solution)/shard_map/all_to_all | solution.py:407
  18.3 7.6 %collective-permute-start.5 = (f32[9,2,1024]{2,1,0:T(2,128)S(1)}, f32[9,2,1024]{2,1,0:T(2,128)S(1)}, u32[]{:S(2)}, u32[]{:S(2)}) collective-permute-start(f32[9,2,1024]{2,1,0:T(2,128)S(1)} %get-tuple-element.22), channel_id=1, source_target_pairs={{0,28},{4,0},{8,4},{12,8},{16,12},{20,16},{24,20},{28,24},{1,29},{... | collective-permute-start | bytes 221192 | tf_op jit(solution)/shard_map/ppermute | solution.py:396
  22.9 1.6 %collective-permute-start.3 = (f32[1,1024]{1,0:T(1,128)S(1)}, f32[1,1024]{1,0:T(1,128)S(1)}, u32[]{:S(2)}, u32[]{:S(2)}) collective-permute-start(f32[1,1024]{1,0:T(1,128)S(1)} %get-tuple-element.18), channel_id=1, source_target_pairs={{0,1},{1,0},{2,3},{3,2},{4,5},{5,4},{6,7},{7,6},{8,9},{9,8},{10,11... | collective-permute-start | bytes 12296 | tf_op jit(solution)/shard_map/ppermute | solution.py:391
  22.9 3.0 %collective-permute-start.4 = (f32[1,1024]{1,0:T(1,128)S(1)}, f32[1,1024]{1,0:T(1,128)S(1)}, u32[]{:S(2)}, u32[]{:S(2)}) collective-permute-start(f32[1,1024]{1,0:T(1,128)S(1)} %get-tuple-element.19), channel_id=1, source_target_pairs={{1,2},{2,1},{3,0},{0,3},{5,6},{6,5},{7,4},{4,7},{9,10},{10,9},{11,... | collective-permute-start | bytes 12296 | tf_op jit(solution)/shard_map/ppermute | solution.py:391

commit v11 on v10

--- a/solution.py
+++ b/solution.py
@@ -45,10 +45,10 @@
 def slices_kernel(f_ref, near_ref, far_ref):
     count = f_ref.shape[0]
     flag = odd("path")
-    for ref, low in ((far_ref, jnp.logical_not(flag)), (near_ref, flag)):
-        base = pick(low, 0, count - 2)
-        for s in range(2):
-            ref[s] = f_ref[base + s]
+    base = pick(flag, 0, count - 2)
+    for s in range(2):
+        near_ref[s] = f_ref[base + s]
+    far_ref[...] = f_ref[pick(flag, count - 1, 0)]
 
 
 def tail_kernel(f_ref, start_ref, end_ref, tail_ref):
@@ -63,7 +63,7 @@
     count, rows, cols = f.shape
     return pl.pallas_call(
         slices_kernel,
-        out_shape=(jax.ShapeDtypeStruct((2, rows, cols), F32),) * 2,
+        out_shape=(jax.ShapeDtypeStruct((2, rows, cols), F32), jax.ShapeDtypeStruct((rows, cols), F32)),
         in_specs=[VMEM],
         out_specs=[VMEM] * 2,
         compiler_params=PARAMS,
@@ -84,24 +84,24 @@
 
 
 class Halo:
-    def __init__(self, m, near_ref, far_ref, start_ref, end_ref):
+    def __init__(self, m, near_ref, far_ref, start_ref, end_ref, rest_ref=None):
         self.odd = odd("path")
         self.first = lax.axis_index("path") == 0
         self.last = lax.axis_index("path") == m - 1
-        self.near, self.far = near_ref, far_ref
+        self.near, self.far, self.rest = near_ref, far_ref, rest_ref
         self.start, self.end = start_ref, end_ref
 
     def below(self, at):
-        return pick(self.first, self.start[at, :], pick(self.odd, self.near[1, at, :], self.far[1, at, :]))
+        return pick(self.first, self.start[at, :], pick(self.odd, self.near[1, at, :], self.far[at, :]))
 
     def above(self, at):
-        return pick(self.last, self.end[at, :], pick(self.odd, self.far[0, at, :], self.near[0, at, :]))
+        return pick(self.last, self.end[at, :], pick(self.odd, self.far[at, :], self.near[0, at, :]))
 
     def below_2(self, at):
-        return pick(self.odd, self.near[0, at, :], self.far[0, at, :])
+        return pick(self.odd, self.near[0, at, :], self.rest[at, :])
 
     def above_2(self, at):
-        return pick(self.odd, self.far[1, at, :], self.near[1, at, :])
+        return pick(self.odd, self.rest[at, :], self.near[1, at, :])
 
 
 def interior_kernel(f_ref, part_ref, drift_ref, rim_ref):
@@ -161,7 +161,7 @@
 
 def chunk_kernel(
     m, n, f_ref, part_ref, rim_ref, near_ref, far_ref, start_ref, end_ref, strip_ref,
-    out_ref, near_corner_ref, far_corner_ref, tail_ref, head_ref, lines, sem,
+    out_ref, near_corner_ref, rest_ref, tail_ref, head_ref, lines, sem,
 ):
     halo = Halo(m, near_ref, far_ref, start_ref, end_ref)
     count, rows, cols = f_ref.shape
@@ -198,8 +198,9 @@
     copy = pltpu.make_async_copy(lines, out_ref, sem)
     copy.start()
 
-    for ref, low in ((near_corner_ref, halo.odd), (far_corner_ref, jnp.logical_not(halo.odd))):
-        ref[...] = tail_ref[1, pl.ds(pick(low, 0, count - 1), 1), :]
+    near_corner_ref[...] = tail_ref[1, pl.ds(pick(halo.odd, 0, count - 1), 1), :]
+    rest_ref[0:rows, :] = f_ref[pick(halo.odd, count - 2, 1)]
+    rest_ref[rows:, :] = jnp.broadcast_to(tail_ref[1, pl.ds(pick(halo.odd, count - 1, 0), 1), :], (TILE, cols))
     for s in range(count):
         head_ref[s] = f_ref[s, 0:2, :]
     head_ref[count, 0:1, :] = halo.below(pl.ds(0, 1))
@@ -209,13 +210,12 @@
 
 def chunks(m, n, f, part, rim, near, far, start, end, strip):
     count, rows, cols = f.shape
-    corner = jax.ShapeDtypeStruct((1, cols), F32)
     return pl.pallas_call(
         functools.partial(chunk_kernel, m, n),
         out_shape=(
             jax.ShapeDtypeStruct((m * n, 1, WIDTH), F32),
-            corner,
-            corner,
+            jax.ShapeDtypeStruct((1, cols), F32),
+            jax.ShapeDtypeStruct((rows + TILE, cols), F32),
             jax.ShapeDtypeStruct((2, count, cols), F32),
             jax.ShapeDtypeStruct((count + 1, 2, cols), F32),
         ),
@@ -228,10 +228,10 @@
 
 
 def final_kernel(
-    m, n, got_ref, near_corner_ref, far_corner_ref, f_ref, drift_ref, near_ref, far_ref, start_ref, end_ref,
+    m, n, got_ref, near_corner_ref, rest_ref, f_ref, drift_ref, near_ref, far_ref, start_ref, end_ref,
     strip_ref, tail_ref, lead_ref, ratio_out, res_out, grad_out, ratio_ref, resid, grad, outer, rim, head_ref, sem,
 ):
-    halo = Halo(m, near_ref, far_ref, start_ref, end_ref)
+    halo = Halo(m, near_ref, far_ref, start_ref, end_ref, rest_ref)
     count, rows, cols = f_ref.shape
     tiles = rows // TILE
     path = lax.axis_index("path")
@@ -274,7 +274,7 @@
     scale = [widen(splat(t)) for t in range(count + 2)]
     column = jnp.sum(jnp.where(lane == sub + 1, ratio, 0.0), axis=1, keepdims=True)
     row = iota((TILE, cols), 0)
-    near, far = near_corner_ref[...], far_corner_ref[...]
+    near, far = near_corner_ref[...], rest_ref[rows : rows + 1, :]
     corners = (
         (
             pick(first, strip_ref[count, 0:1, :], pick(halo.odd, near, far)),
@@ -403,11 +403,11 @@
     near = swap(near, 0)
     part, drift, rim = interior(f)
     slabs = near, far, start, end
-    send, near_corner, far_corner, tail, head = chunks(m, n, f, part, rim, *slabs, strip)
+    send, near_corner, rest, tail, head = chunks(m, n, f, part, rim, *slabs, strip)
     got = lax.all_to_all(send, ("space", "path"), 0, 0, tiled=True)
     lead = ring(head, -1)
-    corners = swap(near_corner, 0), swap(far_corner, 1)
-    return final(m, n, got, corners, f, drift, slabs, (strip, tail, lead))
+    late = swap(near_corner, 0), swap(rest, 1)
+    return final(m, n, got, late, f, drift, slabs, (strip, tail, lead))
 
 
 def solution(mesh):

time: 28.4 us -> 26.3 us (0.926)
  starting transfers between devices: 16.1 us -> 12.8 us
  waiting for transfers between devices: 5.59 us -> 6.87 us
    all_to_all x1, starting transfers between devices: 5.24 us -> 3.39 us  [body(): got = lax.all_to_all(send, ('space', 'path'), 0, 0, tiled=True)]
    ppermute x4, starting transfers between devices: 4.73 us -> 3.21 us  [swap(): lax.ppermute(x, 'path', [((i + kind) % size, ((i ^ 1) + kind) % size) for...]
    ppermute x2, waiting for transfers between devices: 4.14 us -> 4.96 us  [ring(): lax.ppermute(x, 'space', [(i, (i + step) % size) for i in range(size)])]
    all_to_all x1, waiting for transfers between devices: 0.01 us -> 0.74 us  [body(): got = lax.all_to_all(send, ('space', 'path'), 0, 0, tiled=True)]
  transfers between devices with their start and end apart: 7 -> 7, of which waited for: 2 -> 4; matrix products, arithmetic and copies ran while one was open for 0% -> 0% of each run, Pallas kernels for 5% -> 5%
where the time goes in v11:
time: 26.3 us; the launch traced here: 26.1 us
  starting transfers between devices  12.8 us (49%)
  waiting for transfers between devices  6.87 us (26%)
  Pallas kernels  4.49 us (17%)
  local copies, waits for them, and re-layouts  1.23 us (5%)
  between operations  0.69 us (3%)
    ppermute x2, starting transfers between devices, ring(): lax.ppermute(x, 'space', [(i, (i + step) % size) for i in range(size)])  6.18 us
    ppermute x2, waiting for transfers between devices, ring(): lax.ppermute(x, 'space', [(i, (i + step) % size) for i in range(size)])  4.96 us
    all_to_all x1, starting transfers between devices, body(): got = lax.all_to_all(send, ('space', 'path'), 0, 0, tiled=True)  3.39 us
    ppermute x4, starting transfers between devices, swap(): lax.ppermute(x, 'path', [((i + kind) % size, ((i ^ 1) + kind) % size) for...  3.21 us
    pallas_call x1, Pallas kernels, final(): pl.pallas_call(functools.partial(final_kernel, m, n), out_shape=(jax.Shap...  2.24 us
    pallas_call x1, Pallas kernels, interior(): pl.pallas_call(interior_kernel, out_shape=(jax.ShapeDtypeStruct((2 * coun...  1.38 us
    unnamed x8, local copies, waits for them, and re-layouts  1.23 us
    ppermute x4, waiting for transfers between devices, swap(): lax.ppermute(x, 'path', [((i + kind) % size, ((i ^ 1) + kind) % size) for...  1.17 us
  transfers between devices with their start and end apart: 7, of which 4 were waited for; matrix products, arithmetic and copies ran while one was open for 0% of the time, Pallas kernels for 5%

profile of v11, /device:TPU:0, one launch (start us, length us, event | category | flops | bytes accessed | tf_op | source)
XLA Modules:
  0.0 26.1 jit_solution(13051855507937219690)
XLA Ops:
  0.6 0.0 copy-start
  0.6 1.2 %copy-done = f32[8,32,1024]{2,1,0:T(8,128)S(1)} copy-done((f32[8,32,1024]{2,1,0:T(8,128)S(1)}, f32[8,32,1024]{2,1,0:T(8,128)}, u32[]{:S(2)}) %copy-start) | copy-done | bytes 1048600
  1.9 0.0 copy-start.2
  1.9 0.0 copy-start.3
  1.9 0.5 %collective-permute-start = (f32[2,32,1024]{2,1,0:T(8,128)S(1)}, f32[2,32,1024]{2,1,0:T(8,128)S(1)}, u32[]{:S(2)}, u32[]{:S(2)}) collective-permute-start(f32[2,32,1024]{2,1,0:T(8,128)S(1)} %get-tuple-element.15), channel_id=1, source_target_pairs={{0,1},{1,0},{2,3},{3,2},{4,5},{5,4},{6,7},{7,6},{8,9},{9,8},{10,11... | collective-permute-start | bytes 786440 | tf_op jit(solution)/shard_map/ppermute | solution.py:391
  2.4 2.6 %collective-permute-start.1 = (f32[32,1024]{1,0:T(8,128)S(1)}, f32[32,1024]{1,0:T(8,128)S(1)}, u32[]{:S(2)}, u32[]{:S(2)}) collective-permute-start(f32[32,1024]{1,0:T(8,128)S(1)} %get-tuple-element.16), channel_id=1, source_target_pairs={{1,2},{2,1},{3,0},{0,3},{5,6},{6,5},{7,4},{4,7},{9,10},{10,9},{11,... | collective-permute-start | bytes 393224 | tf_op jit(solution)/shard_map/ppermute | solution.py:391
  5.0 0.0 copy-done.2
  5.0 0.0 copy-done.3
  5.1 1.6 %collective-permute-start.2 = (f32[9,2,1024]{2,1,0:T(2,128)S(1)}, f32[9,2,1024]{2,1,0:T(2,128)S(1)}, u32[]{:S(2)}, u32[]{:S(2)}) collective-permute-start(f32[9,2,1024]{2,1,0:T(2,128)S(1)} %tail_rows.1), channel_id=1, source_target_pairs={{0,4},{4,8},{8,12},{12,16},{16,20},{20,24},{24,28},{28,0},{1,5},{5... | collective-permute-start | bytes 221192 | tf_op jit(solution)/shard_map/ppermute | solution.py:396
  6.6 1.4 %interior.1 = (f32[16,128]{1,0:T(8,128)S(1)}, f32[8,32,1024]{2,1,0:T(8,128)S(1)}, f32[2,8,1024]{2,1,0:T(8,128)S(1)}) custom-call(f32[8,32,1024]{2,1,0:T(8,128)S(1)} %copy-done), custom_call_target="tpu_custom_call" | custom-call | flops 5242880 | bytes 2097152 | tf_op jit(solution)/shard_map/interior/pallas_call | solution.py:147
  8.0 0.0 copy-start.1
  8.0 4.1 %collective-permute-done.2.strip_ref = f32[9,2,1024]{2,1,0:T(2,128)S(1)} collective-permute-done((f32[9,2,1024]{2,1,0:T(2,128)S(1)}, f32[9,2,1024]{2,1,0:T(2,128)S(1)}, u32[]{:S(2)}, u32[]{:S(2)}) %collective-permute-start.2) | collective-permute-done | bytes 73760 | tf_op jit(solution)/shard_map/ppermute | solution.py:396
  12.2 0.0 collective-permute-done.1.far_ref
  12.2 0.0 collective-permute-done.near_ref
  12.2 0.8 %chunks.1 = (f32[32,1,384]{2,1,0:T(1,128)}, f32[1,1024]{1,0:T(1,128)S(1)}, f32[40,1024]{1,0:T(8,128)S(1)}, f32[2,8,1024]{2,1,0:T(8,128)S(1)}, f32[9,2,1024]{2,1,0:T(2,128)S(1)}) custom-call(f32[8,32,1024]{2,1,0:T(8,128)S(1)} %copy-done, f32[16,128]{1,0:T(8,128)S(1)} %get-tuple-element.13.part_ref, f32[2,8,1024]{2,1,0:T(8,128)S(1)} %get-tuple-element.14.rim_ref, ...), custom_call_target="tpu_custom_call" | custom-call | tf_op jit(solution)/shard_map/chunks/pallas_call | solution.py:213
  13.0 0.1 collective-permute-start.4
  13.1 3.4 %all-to-all-start = ((f32[32,1,384]{2,1,0:T(1,128)}), f32[32,1,384]{2,1,0:T(1,128)S(1)}, u32[]{:S(2)}, u32[]{:S(2)}) async-start(f32[32,1,384]{2,1,0:T(1,128)} %get-tuple-element.17), calls=%async_computation | async-start | bytes 98304 | tf_op jit(solution)/shard_map/all_to_all | solution.py:407
  16.5 4.6 %collective-permute-start.5 = (f32[9,2,1024]{2,1,0:T(2,128)S(1)}, f32[9,2,1024]{2,1,0:T(2,128)S(1)}, u32[]{:S(2)}, u32[]{:S(2)}) collective-permute-start(f32[9,2,1024]{2,1,0:T(2,128)S(1)} %get-tuple-element.22), channel_id=1, source_target_pairs={{0,28},{4,0},{8,4},{12,8},{16,12},{20,16},{24,20},{28,24},{1,29},{... | collective-permute-start | bytes 221192 | tf_op jit(solution)/shard_map/ppermute | solution.py:396
  21.1 0.0 collective-permute-start.3
  21.1 1.2 %collective-permute-done.3.near_corner_ref = f32[1,1024]{1,0:T(1,128)S(1)} collective-permute-done((f32[1,1024]{1,0:T(1,128)S(1)}, f32[1,1024]{1,0:T(1,128)S(1)}, u32[]{:S(2)}, u32[]{:S(2)}) %collective-permute-start.3) | collective-permute-done | bytes 4128 | tf_op jit(solution)/shard_map/ppermute | solution.py:391
  22.3 0.8 %collective-permute-done.5.lead_ref = f32[9,2,1024]{2,1,0:T(2,128)S(1)} collective-permute-done((f32[9,2,1024]{2,1,0:T(2,128)S(1)}, f32[9,2,1024]{2,1,0:T(2,128)S(1)}, u32[]{:S(2)}, u32[]{:S(2)}) %collective-permute-start.5) | collective-permute-done | bytes 73760 | tf_op jit(solution)/shard_map/ppermute | solution.py:396
  23.1 0.7 %all-to-all-done.got_ref = f32[32,1,384]{2,1,0:T(1,128)S(1)} async-done(((f32[32,1,384]{2,1,0:T(1,128)}), f32[32,1,384]{2,1,0:T(1,128)S(1)}, u32[]{:S(2)}, u32[]{:S(2)}) %all-to-all-start) | async-done | bytes 49184 | tf_op jit(solution)/shard_map/all_to_all | solution.py:407
  23.8 0.0 collective-permute-done.4.rest_ref
  23.8 0.0 copy-done.1
  23.8 2.2 %final.1 = (f32[8]{0:T(128)}, f32[8,32,1024]{2,1,0:T(8,128)}, f32[8,32,1024]{2,1,0:T(8,128)}) custom-call(f32[32,1,384]{2,1,0:T(1,128)S(1)} %all-to-all-done.got_ref, f32[1,1024]{1,0:T(1,128)S(1)} %collective-permute-done.3.near_corner_ref, f32[40,1024]{1,0:T(8,128)S(1)} %collective-permute-done.4.rest_ref, f32[8,32,1024]{2,1,0:T(8,128)S(1)} %copy-done.1, ...), custom_call_target="tpu_custom_call" | custom-call | tf_op jit(solution)/shard_map/final/pallas_call | solution.py:370
  (2 shorter events, 0.0 us)
Async XLA Ops:
  0.6 1.2 %copy-start = (f32[8,32,1024]{2,1,0:T(8,128)S(1)}, f32[8,32,1024]{2,1,0:T(8,128)}, u32[]{:S(2)}) copy-start(f32[8,32,1024]{2,1,0:T(8,128)} %f_ref.9) | copy-start | bytes 3145732
  1.9 3.2 %copy-start.2 = (f32[32,1024]{1,0:T(8,128)S(1)}, f32[32,1024]{1,0:T(8,128)}, u32[]{:S(2)}) copy-start(f32[32,1024]{1,0:T(8,128)} %start_ref.5) | copy-start | bytes 393220
  1.9 3.2 %copy-start.3 = (f32[32,1024]{1,0:T(8,128)S(1)}, f32[32,1024]{1,0:T(8,128)}, u32[]{:S(2)}) copy-start(f32[32,1024]{1,0:T(8,128)} %end_ref.5) | copy-start | bytes 393220
  1.9 10.3 %collective-permute-start = (f32[2,32,1024]{2,1,0:T(8,128)S(1)}, f32[2,32,1024]{2,1,0:T(8,128)S(1)}, u32[]{:S(2)}, u32[]{:S(2)}) collective-permute-start(f32[2,32,1024]{2,1,0:T(8,128)S(1)} %get-tuple-element.15), channel_id=1, source_target_pairs={{0,1},{1,0},{2,3},{3,2},{4,5},{5,4},{6,7},{7,6},{8,9},{9,8},{10,11... | collective-permute-start | bytes 786440 | tf_op jit(solution)/shard_map/ppermute | solution.py:391
  2.4 9.8 %collective-permute-start.1 = (f32[32,1024]{1,0:T(8,128)S(1)}, f32[32,1024]{1,0:T(8,128)S(1)}, u32[]{:S(2)}, u32[]{:S(2)}) collective-permute-start(f32[32,1024]{1,0:T(8,128)S(1)} %get-tuple-element.16), channel_id=1, source_target_pairs={{1,2},{2,1},{3,0},{0,3},{5,6},{6,5},{7,4},{4,7},{9,10},{10,9},{11,... | collective-permute-start | bytes 393224 | tf_op jit(solution)/shard_map/ppermute | solution.py:391
  5.1 7.1 %collective-permute-start.2 = (f32[9,2,1024]{2,1,0:T(2,128)S(1)}, f32[9,2,1024]{2,1,0:T(2,128)S(1)}, u32[]{:S(2)}, u32[]{:S(2)}) collective-permute-start(f32[9,2,1024]{2,1,0:T(2,128)S(1)} %tail_rows.1), channel_id=1, source_target_pairs={{0,4},{4,8},{8,12},{12,16},{16,20},{20,24},{24,28},{28,0},{1,5},{5... | collective-permute-start | bytes 221192 | tf_op jit(solution)/shard_map/ppermute | solution.py:396
  8.0 15.8 %copy-start.1 = (f32[8,32,1024]{2,1,0:T(8,128)S(1)}, f32[8,32,1024]{2,1,0:T(8,128)}, u32[]{:S(2)}) copy-start(f32[8,32,1024]{2,1,0:T(8,128)} %f_ref.9) | copy-start | bytes 3145732
  13.0 10.8 %collective-permute-start.4 = (f32[40,1024]{1,0:T(8,128)S(1)}, f32[40,1024]{1,0:T(8,128)S(1)}, u32[]{:S(2)}, u32[]{:S(2)}) collective-permute-start(f32[40,1024]{1,0:T(8,128)S(1)} %get-tuple-element.19), channel_id=1, source_target_pairs={{1,2},{2,1},{3,0},{0,3},{5,6},{6,5},{7,4},{4,7},{9,10},{10,9},{11,... | collective-permute-start | bytes 491528 | tf_op jit(solution)/shard_map/ppermute | solution.py:391
  13.1 10.7 %all-to-all-start = ((f32[32,1,384]{2,1,0:T(1,128)}), f32[32,1,384]{2,1,0:T(1,128)S(1)}, u32[]{:S(2)}, u32[]{:S(2)}) async-start(f32[32,1,384]{2,1,0:T(1,128)} %get-tuple-element.17), calls=%async_computation | async-start | bytes 98304 | tf_op jit(solution)/shard_map/all_to_all | solution.py:407
  16.5 6.6 %collective-permute-start.5 = (f32[9,2,1024]{2,1,0:T(2,128)S(1)}, f32[9,2,1024]{2,1,0:T(2,128)S(1)}, u32[]{:S(2)}, u32[]{:S(2)}) collective-permute-start(f32[9,2,1024]{2,1,0:T(2,128)S(1)} %get-tuple-element.22), channel_id=1, source_target_pairs={{0,28},{4,0},{8,4},{12,8},{16,12},{20,16},{24,20},{28,24},{1,29},{... | collective-permute-start | bytes 221192 | tf_op jit(solution)/shard_map/ppermute | solution.py:396
  21.1 1.2 %collective-permute-start.3 = (f32[1,1024]{1,0:T(1,128)S(1)}, f32[1,1024]{1,0:T(1,128)S(1)}, u32[]{:S(2)}, u32[]{:S(2)}) collective-permute-start(f32[1,1024]{1,0:T(1,128)S(1)} %get-tuple-element.18), channel_id=1, source_target_pairs={{0,1},{1,0},{2,3},{3,2},{4,5},{5,4},{6,7},{7,6},{8,9},{9,8},{10,11... | collective-permute-start | bytes 12296 | tf_op jit(solution)/shard_map/ppermute | solution.py:391

commit v12 on v11

--- a/solution.py
+++ b/solution.py
@@ -42,13 +42,14 @@
     return jnp.where(flag, x, y)
 
 
-def slices_kernel(f_ref, near_ref, far_ref):
+def slices_kernel(f_ref, near_ref, far_ref, rest_ref):
     count = f_ref.shape[0]
     flag = odd("path")
     base = pick(flag, 0, count - 2)
     for s in range(2):
         near_ref[s] = f_ref[base + s]
     far_ref[...] = f_ref[pick(flag, count - 1, 0)]
+    rest_ref[...] = f_ref[pick(flag, count - 2, 1)]
 
 
 def tail_kernel(f_ref, start_ref, end_ref, tail_ref):
@@ -63,9 +64,9 @@
     count, rows, cols = f.shape
     return pl.pallas_call(
         slices_kernel,
-        out_shape=(jax.ShapeDtypeStruct((2, rows, cols), F32), jax.ShapeDtypeStruct((rows, cols), F32)),
+        out_shape=(jax.ShapeDtypeStruct((2, rows, cols), F32),) + (jax.ShapeDtypeStruct((rows, cols), F32),) * 2,
         in_specs=[VMEM],
-        out_specs=[VMEM] * 2,
+        out_specs=[VMEM] * 3,
         compiler_params=PARAMS,
         name="slices",
     )(f)
@@ -161,7 +162,7 @@
 
 def chunk_kernel(
     m, n, f_ref, part_ref, rim_ref, near_ref, far_ref, start_ref, end_ref, strip_ref,
-    out_ref, near_corner_ref, rest_ref, tail_ref, head_ref, lines, sem,
+    out_ref, near_corner_ref, far_corner_ref, tail_ref, head_ref, lines, sem,
 ):
     halo = Halo(m, near_ref, far_ref, start_ref, end_ref)
     count, rows, cols = f_ref.shape
@@ -198,9 +199,8 @@
     copy = pltpu.make_async_copy(lines, out_ref, sem)
     copy.start()
 
-    near_corner_ref[...] = tail_ref[1, pl.ds(pick(halo.odd, 0, count - 1), 1), :]
-    rest_ref[0:rows, :] = f_ref[pick(halo.odd, count - 2, 1)]
-    rest_ref[rows:, :] = jnp.broadcast_to(tail_ref[1, pl.ds(pick(halo.odd, count - 1, 0), 1), :], (TILE, cols))
+    for ref, low in ((near_corner_ref, halo.odd), (far_corner_ref, jnp.logical_not(halo.odd))):
+        ref[...] = tail_ref[1, pl.ds(pick(low, 0, count - 1), 1), :]
     for s in range(count):
         head_ref[s] = f_ref[s, 0:2, :]
     head_ref[count, 0:1, :] = halo.below(pl.ds(0, 1))
@@ -215,7 +215,7 @@
         out_shape=(
             jax.ShapeDtypeStruct((m * n, 1, WIDTH), F32),
             jax.ShapeDtypeStruct((1, cols), F32),
-            jax.ShapeDtypeStruct((rows + TILE, cols), F32),
+            jax.ShapeDtypeStruct((1, cols), F32),
             jax.ShapeDtypeStruct((2, count, cols), F32),
             jax.ShapeDtypeStruct((count + 1, 2, cols), F32),
         ),
@@ -228,7 +228,7 @@
 
 
 def final_kernel(
-    m, n, got_ref, near_corner_ref, rest_ref, f_ref, drift_ref, near_ref, far_ref, start_ref, end_ref,
+    m, n, got_ref, near_corner_ref, far_corner_ref, rest_ref, f_ref, drift_ref, near_ref, far_ref, start_ref, end_ref,
     strip_ref, tail_ref, lead_ref, ratio_out, res_out, grad_out, ratio_ref, resid, grad, outer, rim, head_ref, sem,
 ):
     halo = Halo(m, near_ref, far_ref, start_ref, end_ref, rest_ref)
@@ -274,7 +274,7 @@
     scale = [widen(splat(t)) for t in range(count + 2)]
     column = jnp.sum(jnp.where(lane == sub + 1, ratio, 0.0), axis=1, keepdims=True)
     row = iota((TILE, cols), 0)
-    near, far = near_corner_ref[...], rest_ref[rows : rows + 1, :]
+    near, far = near_corner_ref[...], far_corner_ref[...]
     corners = (
         (
             pick(first, strip_ref[count, 0:1, :], pick(halo.odd, near, far)),
@@ -370,7 +370,7 @@
     return pl.pallas_call(
         functools.partial(final_kernel, m, n),
         out_shape=(jax.ShapeDtypeStruct((count,), F32), big, big),
-        in_specs=[VMEM] * 12,
+        in_specs=[VMEM] * 13,
         out_specs=(ANY, ANY, ANY),
         scratch_shapes=[
             pltpu.VMEM((count,), F32),
@@ -397,17 +397,19 @@
 
 
 def body(m, n, f, start, end):
-    near, far = slices(f)
+    near, far, rest = slices(f)
     strip = ring(tail_rows(f, start, end), 1)
     far = swap(far, 1)
     near = swap(near, 0)
+    rest = swap(rest, 1)
     part, drift, rim = interior(f)
     slabs = near, far, start, end
-    send, near_corner, rest, tail, head = chunks(m, n, f, part, rim, *slabs, strip)
+    send, near_corner, far_corner, tail, head = chunks(m, n, f, part, rim, *slabs, strip)
     got = lax.all_to_all(send, ("space", "path"), 0, 0, tiled=True)
+    near_corner, far_corner = swap(near_corner, 0), swap(far_corner, 1)
+    head, near_corner, far_corner = lax.optimization_barrier((head, near_corner, far_corner))
     lead = ring(head, -1)
-    late = swap(near_corner, 0), swap(rest, 1)
-    return final(m, n, got, late, f, drift, slabs, (strip, tail, lead))
+    return final(m, n, got, (near_corner, far_corner, rest), f, drift, slabs, (strip, tail, lead))
 
 
 def solution(mesh):

time: 26.3 us -> 28.6 us (1.087)
  starting transfers between devices: 12.8 us -> 14.4 us
  waiting for transfers between devices: 6.87 us -> 7.53 us
    ppermute x4 -> x5, starting transfers between devices: 3.21 us -> 5.08 us  [swap(): lax.ppermute(x, 'path', [((i + kind) % size, ((i ^ 1) + kind) % size) for...]
    ppermute x2, waiting for transfers between devices: 4.96 us -> 6.12 us  [ring(): lax.ppermute(x, 'space', [(i, (i + step) % size) for i in range(size)])]
    all_to_all x1, waiting for transfers between devices: 0.74 us -> 0.01 us  [body(): got = lax.all_to_all(send, ('space', 'path'), 0, 0, tiled=True)]
    ppermute x4 -> x5, waiting for transfers between devices: 1.17 us -> 1.41 us  [swap(): lax.ppermute(x, 'path', [((i + kind) % size, ((i ^ 1) + kind) % size) for...]
  transfers between devices with their start and end apart: 7 -> 8, of which waited for: 4 -> 3; matrix products, arithmetic and copies ran while one was open for 0% -> 0% of each run, Pallas kernels for 5% -> 8%
where the time goes in v12:
time: 28.6 us; the launch traced here: 28.4 us
  starting transfers between devices  14.4 us (50%)
  waiting for transfers between devices  7.53 us (26%)
  Pallas kernels  4.5 us (16%)
  local copies, waits for them, and re-layouts  1.23 us (4%)
  between operations  0.69 us (2%)
    ppermute x2, waiting for transfers between devices, ring(): lax.ppermute(x, 'space', [(i, (i + step) % size) for i in range(size)])  6.12 us
    ppermute x2, starting transfers between devices, ring(): lax.ppermute(x, 'space', [(i, (i + step) % size) for i in range(size)])  6.11 us
    ppermute x5, starting transfers between devices, swap(): lax.ppermute(x, 'path', [((i + kind) % size, ((i ^ 1) + kind) % size) for...  5.08 us
    all_to_all x1, starting transfers between devices, body(): got = lax.all_to_all(send, ('space', 'path'), 0, 0, tiled=True)  3.26 us
    pallas_call x1, Pallas kernels, final(): pl.pallas_call(functools.partial(final_kernel, m, n), out_shape=(jax.Shap...  2.23 us
    ppermute x5, waiting for transfers between devices, swap(): lax.ppermute(x, 'path', [((i + kind) % size, ((i ^ 1) + kind) % size) for...  1.41 us
    pallas_call x1, Pallas kernels, interior(): pl.pallas_call(interior_kernel, out_shape=(jax.ShapeDtypeStruct((2 * coun...  1.38 us
    unnamed x8, local copies, waits for them, and re-layouts  1.23 us
  transfers between devices with their start and end apart: 8, of which 3 were waited for; matrix products, arithmetic and copies ran while one was open for 0% of the time, Pallas kernels for 8%

profile of v12, /device:TPU:0, one launch (start us, length us, event | category | flops | bytes accessed | tf_op | source)
XLA Modules:
  0.0 28.4 jit_solution(4412950224265387863)
XLA Ops:
  0.6 0.0 copy-start
  0.6 1.2 %copy-done = f32[8,32,1024]{2,1,0:T(8,128)S(1)} copy-done((f32[8,32,1024]{2,1,0:T(8,128)S(1)}, f32[8,32,1024]{2,1,0:T(8,128)}, u32[]{:S(2)}) %copy-start) | copy-done | bytes 1048600
  1.9 0.0 copy-start.2
  1.9 0.0 copy-start.3
  1.9 0.5 %collective-permute-start = (f32[2,32,1024]{2,1,0:T(8,128)S(1)}, f32[2,32,1024]{2,1,0:T(8,128)S(1)}, u32[]{:S(2)}, u32[]{:S(2)}) collective-permute-start(f32[2,32,1024]{2,1,0:T(8,128)S(1)} %get-tuple-element.19), channel_id=1, source_target_pairs={{0,1},{1,0},{2,3},{3,2},{4,5},{5,4},{6,7},{7,6},{8,9},{9,8},{10,11... | collective-permute-start | bytes 786440 | tf_op jit(solution)/shard_map/ppermute | solution.py:391
  2.4 2.6 %collective-permute-start.1 = (f32[32,1024]{1,0:T(8,128)S(1)}, f32[32,1024]{1,0:T(8,128)S(1)}, u32[]{:S(2)}, u32[]{:S(2)}) collective-permute-start(f32[32,1024]{1,0:T(8,128)S(1)} %get-tuple-element.20), channel_id=1, source_target_pairs={{1,2},{2,1},{3,0},{0,3},{5,6},{6,5},{7,4},{4,7},{9,10},{10,9},{11,... | collective-permute-start | bytes 393224 | tf_op jit(solution)/shard_map/ppermute | solution.py:391
  5.0 0.0 copy-done.2
  5.0 0.0 copy-done.3
  5.1 1.6 %collective-permute-start.2 = (f32[9,2,1024]{2,1,0:T(2,128)S(1)}, f32[9,2,1024]{2,1,0:T(2,128)S(1)}, u32[]{:S(2)}, u32[]{:S(2)}) collective-permute-start(f32[9,2,1024]{2,1,0:T(2,128)S(1)} %tail_rows.1), channel_id=1, source_target_pairs={{0,4},{4,8},{8,12},{12,16},{16,20},{20,24},{24,28},{28,0},{1,5},{5... | collective-permute-start | bytes 221192 | tf_op jit(solution)/shard_map/ppermute | solution.py:396
  6.6 0.0 collective-permute-start.5
  6.6 1.4 %interior.1 = (f32[16,128]{1,0:T(8,128)S(1)}, f32[8,32,1024]{2,1,0:T(8,128)S(1)}, f32[2,8,1024]{2,1,0:T(8,128)S(1)}) custom-call(f32[8,32,1024]{2,1,0:T(8,128)S(1)} %copy-done), custom_call_target="tpu_custom_call" | custom-call | flops 5242880 | bytes 2097152 | tf_op jit(solution)/shard_map/interior/pallas_call | solution.py:148
  8.0 0.0 copy-start.1
  8.0 4.1 %collective-permute-done.2.strip_ref = f32[9,2,1024]{2,1,0:T(2,128)S(1)} collective-permute-done((f32[9,2,1024]{2,1,0:T(2,128)S(1)}, f32[9,2,1024]{2,1,0:T(2,128)S(1)}, u32[]{:S(2)}, u32[]{:S(2)}) %collective-permute-start.2) | collective-permute-done | bytes 73760 | tf_op jit(solution)/shard_map/ppermute | solution.py:396
  12.2 0.0 collective-permute-done.1.far_ref
  12.2 0.0 collective-permute-done.near_ref
  12.2 0.8 %chunks.1 = (f32[32,1,384]{2,1,0:T(1,128)}, f32[1,1024]{1,0:T(1,128)S(1)}, f32[1,1024]{1,0:T(1,128)S(1)}, f32[2,8,1024]{2,1,0:T(8,128)S(1)}, f32[9,2,1024]{2,1,0:T(2,128)S(1)}) custom-call(f32[8,32,1024]{2,1,0:T(8,128)S(1)} %copy-done, f32[16,128]{1,0:T(8,128)S(1)} %get-tuple-element.17.part_ref, f32[2,8,1024]{2,1,0:T(8,128)S(1)} %get-tuple-element.18.rim_ref, ...), custom_call_target="tpu_custom_call" | custom-call | tf_op jit(solution)/shard_map/chunks/pallas_call | solution.py:213
  13.0 3.3 %all-to-all-start = ((f32[32,1,384]{2,1,0:T(1,128)}), f32[32,1,384]{2,1,0:T(1,128)S(1)}, u32[]{:S(2)}, u32[]{:S(2)}) async-start(f32[32,1,384]{2,1,0:T(1,128)} %get-tuple-element.21), calls=%async_computation | async-start | bytes 98304 | tf_op jit(solution)/shard_map/all_to_all | solution.py:408
  16.3 0.3 %collective-permute-start.3 = (f32[1,1024]{1,0:T(1,128)S(1)}, f32[1,1024]{1,0:T(1,128)S(1)}, u32[]{:S(2)}, u32[]{:S(2)}) collective-permute-start(f32[1,1024]{1,0:T(1,128)S(1)} %get-tuple-element.23), channel_id=1, source_target_pairs={{0,1},{1,0},{2,3},{3,2},{4,5},{5,4},{6,7},{7,6},{8,9},{9,8},{10,11... | collective-permute-start | bytes 12296 | tf_op jit(solution)/shard_map/ppermute | solution.py:391
  16.6 1.6 %collective-permute-start.4 = (f32[1,1024]{1,0:T(1,128)S(1)}, f32[1,1024]{1,0:T(1,128)S(1)}, u32[]{:S(2)}, u32[]{:S(2)}) collective-permute-start(f32[1,1024]{1,0:T(1,128)S(1)} %get-tuple-element.24), channel_id=1, source_target_pairs={{1,2},{2,1},{3,0},{0,3},{5,6},{6,5},{7,4},{4,7},{9,10},{10,9},{11,... | collective-permute-start | bytes 12296 | tf_op jit(solution)/shard_map/ppermute | solution.py:391
  18.2 0.0 collective-permute-done.3.near_corner_ref
  18.2 1.4 %collective-permute-done.4.far_corner_ref = f32[1,1024]{1,0:T(1,128)S(1)} collective-permute-done((f32[1,1024]{1,0:T(1,128)S(1)}, f32[1,1024]{1,0:T(1,128)S(1)}, u32[]{:S(2)}, u32[]{:S(2)}) %collective-permute-start.4) | collective-permute-done | bytes 4128 | tf_op jit(solution)/shard_map/ppermute | solution.py:391
  19.6 4.5 %collective-permute-start.6 = (f32[9,2,1024]{2,1,0:T(2,128)S(1)}, f32[9,2,1024]{2,1,0:T(2,128)S(1)}, u32[]{:S(2)}, u32[]{:S(2)}) collective-permute-start(f32[9,2,1024]{2,1,0:T(2,128)S(1)} %get-tuple-element.30), channel_id=1, source_target_pairs={{0,28},{4,0},{8,4},{12,8},{16,12},{20,16},{24,20},{28,24},{1,29},{... | collective-permute-start | bytes 221192 | tf_op jit(solution)/shard_map/ppermute | solution.py:396
  24.2 0.0 collective-permute-done.5.rest_ref
  24.2 2.0 %collective-permute-done.6.lead_ref = f32[9,2,1024]{2,1,0:T(2,128)S(1)} collective-permute-done((f32[9,2,1024]{2,1,0:T(2,128)S(1)}, f32[9,2,1024]{2,1,0:T(2,128)S(1)}, u32[]{:S(2)}, u32[]{:S(2)}) %collective-permute-start.6) | collective-permute-done | bytes 73760 | tf_op jit(solution)/shard_map/ppermute | solution.py:396
  26.2 0.0 all-to-all-done.got_ref
  26.2 0.0 copy-done.1
  26.2 2.2 %final.1 = (f32[8]{0:T(128)}, f32[8,32,1024]{2,1,0:T(8,128)}, f32[8,32,1024]{2,1,0:T(8,128)}) custom-call(f32[32,1,384]{2,1,0:T(1,128)S(1)} %all-to-all-done.got_ref, f32[1,1024]{1,0:T(1,128)S(1)} %collective-permute-done.3.near_corner_ref, f32[1,1024]{1,0:T(1,128)S(1)} %collective-permute-done.4.far_corner_ref, ...), custom_call_target="tpu_custom_call" | custom-call | tf_op jit(solution)/shard_map/final/pallas_call | solution.py:370
  (2 shorter events, 0.1 us)
Async XLA Ops:
  0.6 1.2 %copy-start = (f32[8,32,1024]{2,1,0:T(8,128)S(1)}, f32[8,32,1024]{2,1,0:T(8,128)}, u32[]{:S(2)}) copy-start(f32[8,32,1024]{2,1,0:T(8,128)} %f_ref.9) | copy-start | bytes 3145732
  1.9 3.2 %copy-start.2 = (f32[32,1024]{1,0:T(8,128)S(1)}, f32[32,1024]{1,0:T(8,128)}, u32[]{:S(2)}) copy-start(f32[32,1024]{1,0:T(8,128)} %start_ref.5) | copy-start | bytes 393220
  1.9 3.2 %copy-start.3 = (f32[32,1024]{1,0:T(8,128)S(1)}, f32[32,1024]{1,0:T(8,128)}, u32[]{:S(2)}) copy-start(f32[32,1024]{1,0:T(8,128)} %end_ref.5) | copy-start | bytes 393220
  1.9 10.3 %collective-permute-start = (f32[2,32,1024]{2,1,0:T(8,128)S(1)}, f32[2,32,1024]{2,1,0:T(8,128)S(1)}, u32[]{:S(2)}, u32[]{:S(2)}) collective-permute-start(f32[2,32,1024]{2,1,0:T(8,128)S(1)} %get-tuple-element.19), channel_id=1, source_target_pairs={{0,1},{1,0},{2,3},{3,2},{4,5},{5,4},{6,7},{7,6},{8,9},{9,8},{10,11... | collective-permute-start | bytes 786440 | tf_op jit(solution)/shard_map/ppermute | solution.py:391
  2.4 9.8 %collective-permute-start.1 = (f32[32,1024]{1,0:T(8,128)S(1)}, f32[32,1024]{1,0:T(8,128)S(1)}, u32[]{:S(2)}, u32[]{:S(2)}) collective-permute-start(f32[32,1024]{1,0:T(8,128)S(1)} %get-tuple-element.20), channel_id=1, source_target_pairs={{1,2},{2,1},{3,0},{0,3},{5,6},{6,5},{7,4},{4,7},{9,10},{10,9},{11,... | collective-permute-start | bytes 393224 | tf_op jit(solution)/shard_map/ppermute | solution.py:391
  5.1 7.1 %collective-permute-start.2 = (f32[9,2,1024]{2,1,0:T(2,128)S(1)}, f32[9,2,1024]{2,1,0:T(2,128)S(1)}, u32[]{:S(2)}, u32[]{:S(2)}) collective-permute-start(f32[9,2,1024]{2,1,0:T(2,128)S(1)} %tail_rows.1), channel_id=1, source_target_pairs={{0,4},{4,8},{8,12},{12,16},{16,20},{20,24},{24,28},{28,0},{1,5},{5... | collective-permute-start | bytes 221192 | tf_op jit(solution)/shard_map/ppermute | solution.py:396
  6.6 17.5 %collective-permute-start.5 = (f32[32,1024]{1,0:T(8,128)S(1)}, f32[32,1024]{1,0:T(8,128)S(1)}, u32[]{:S(2)}, u32[]{:S(2)}) collective-permute-start(f32[32,1024]{1,0:T(8,128)S(1)} %get-tuple-element.27), channel_id=1, source_target_pairs={{1,2},{2,1},{3,0},{0,3},{5,6},{6,5},{7,4},{4,7},{9,10},{10,9},{11,... | collective-permute-start | bytes 393224 | tf_op jit(solution)/shard_map/ppermute | solution.py:391
  8.0 18.1 %copy-start.1 = (f32[8,32,1024]{2,1,0:T(8,128)S(1)}, f32[8,32,1024]{2,1,0:T(8,128)}, u32[]{:S(2)}) copy-start(f32[8,32,1024]{2,1,0:T(8,128)} %f_ref.9) | copy-start | bytes 3145732
  13.0 13.1 %all-to-all-start = ((f32[32,1,384]{2,1,0:T(1,128)}), f32[32,1,384]{2,1,0:T(1,128)S(1)}, u32[]{:S(2)}, u32[]{:S(2)}) async-start(f32[32,1,384]{2,1,0:T(1,128)} %get-tuple-element.21), calls=%async_computation | async-start | bytes 98304 | tf_op jit(solution)/shard_map/all_to_all | solution.py:408
  16.3 2.0 %collective-permute-start.3 = (f32[1,1024]{1,0:T(1,128)S(1)}, f32[1,1024]{1,0:T(1,128)S(1)}, u32[]{:S(2)}, u32[]{:S(2)}) collective-permute-start(f32[1,1024]{1,0:T(1,128)S(1)} %get-tuple-element.23), channel_id=1, source_target_pairs={{0,1},{1,0},{2,3},{3,2},{4,5},{5,4},{6,7},{7,6},{8,9},{9,8},{10,11... | collective-permute-start | bytes 12296 | tf_op jit(solution)/shard_map/ppermute | solution.py:391
  16.6 3.0 %collective-permute-start.4 = (f32[1,1024]{1,0:T(1,128)S(1)}, f32[1,1024]{1,0:T(1,128)S(1)}, u32[]{:S(2)}, u32[]{:S(2)}) collective-permute-start(f32[1,1024]{1,0:T(1,128)S(1)} %get-tuple-element.24), channel_id=1, source_target_pairs={{1,2},{2,1},{3,0},{0,3},{5,6},{6,5},{7,4},{4,7},{9,10},{10,9},{11,... | collective-permute-start | bytes 12296 | tf_op jit(solution)/shard_map/ppermute | solution.py:391
  19.6 6.5 %collective-permute-start.6 = (f32[9,2,1024]{2,1,0:T(2,128)S(1)}, f32[9,2,1024]{2,1,0:T(2,128)S(1)}, u32[]{:S(2)}, u32[]{:S(2)}) collective-permute-start(f32[9,2,1024]{2,1,0:T(2,128)S(1)} %get-tuple-element.30), channel_id=1, source_target_pairs={{0,28},{4,0},{8,4},{12,8},{16,12},{20,16},{24,20},{28,24},{1,29},{... | collective-permute-start | bytes 221192 | tf_op jit(solution)/shard_map/ppermute | solution.py:396

commit v13 on v12

--- a/solution.py
+++ b/solution.py
@@ -42,13 +42,15 @@
     return jnp.where(flag, x, y)
 
 
-def slices_kernel(f_ref, near_ref, far_ref, rest_ref):
+def slices_kernel(f_ref, near_ref, far_lo_ref, far_hi_ref, rest_ref):
     count = f_ref.shape[0]
     flag = odd("path")
     base = pick(flag, 0, count - 2)
     for s in range(2):
         near_ref[s] = f_ref[base + s]
-    far_ref[...] = f_ref[pick(flag, count - 1, 0)]
+    half = far_lo_ref.shape[0]
+    far_lo_ref[...] = f_ref[pick(flag, count - 1, 0), :half]
+    far_hi_ref[...] = f_ref[pick(flag, count - 1, 0), half:]
     rest_ref[...] = f_ref[pick(flag, count - 2, 1)]
 
 
@@ -64,9 +66,14 @@
     count, rows, cols = f.shape
     return pl.pallas_call(
         slices_kernel,
-        out_shape=(jax.ShapeDtypeStruct((2, rows, cols), F32),) + (jax.ShapeDtypeStruct((rows, cols), F32),) * 2,
+        out_shape=(
+            jax.ShapeDtypeStruct((2, rows, cols), F32),
+            jax.ShapeDtypeStruct((rows // 2, cols), F32),
+            jax.ShapeDtypeStruct((rows // 2, cols), F32),
+            jax.ShapeDtypeStruct((rows, cols), F32),
+        ),
         in_specs=[VMEM],
-        out_specs=[VMEM] * 3,
+        out_specs=[VMEM] * 4,
         compiler_params=PARAMS,
         name="slices",
     )(f)
@@ -85,18 +92,22 @@
 
 
 class Halo:
-    def __init__(self, m, near_ref, far_ref, start_ref, end_ref, rest_ref=None):
+    def __init__(self, m, near_ref, far_lo_ref, far_hi_ref, start_ref, end_ref, rest_ref=None):
         self.odd = odd("path")
         self.first = lax.axis_index("path") == 0
         self.last = lax.axis_index("path") == m - 1
-        self.near, self.far, self.rest = near_ref, far_ref, rest_ref
+        self.near, self.halves, self.rest = near_ref, (far_lo_ref, far_hi_ref), rest_ref
         self.start, self.end = start_ref, end_ref
 
+    def far(self, at):
+        half = self.halves[0].shape[0]
+        return self.halves[at.start // half][pl.ds(at.start % half, at.size), :]
+
     def below(self, at):
-        return pick(self.first, self.start[at, :], pick(self.odd, self.near[1, at, :], self.far[at, :]))
+        return pick(self.first, self.start[at, :], pick(self.odd, self.near[1, at, :], self.far(at)))
 
     def above(self, at):
-        return pick(self.last, self.end[at, :], pick(self.odd, self.far[at, :], self.near[0, at, :]))
+        return pick(self.last, self.end[at, :], pick(self.odd, self.far(at), self.near[0, at, :]))
 
     def below_2(self, at):
         return pick(self.odd, self.near[0, at, :], self.rest[at, :])
@@ -161,10 +172,10 @@
 
 
 def chunk_kernel(
-    m, n, f_ref, part_ref, rim_ref, near_ref, far_ref, start_ref, end_ref, strip_ref,
+    m, n, f_ref, part_ref, rim_ref, near_ref, far_lo_ref, far_hi_ref, start_ref, end_ref, strip_ref,
     out_ref, near_corner_ref, far_corner_ref, tail_ref, head_ref, lines, sem,
 ):
-    halo = Halo(m, near_ref, far_ref, start_ref, end_ref)
+    halo = Halo(m, near_ref, far_lo_ref, far_hi_ref, start_ref, end_ref)
     count, rows, cols = f_ref.shape
     tiles = rows // TILE
 
@@ -208,7 +219,7 @@
     copy.wait()
 
 
-def chunks(m, n, f, part, rim, near, far, start, end, strip):
+def chunks(m, n, f, part, rim, *halo):
     count, rows, cols = f.shape
     return pl.pallas_call(
         functools.partial(chunk_kernel, m, n),
@@ -219,19 +230,19 @@
             jax.ShapeDtypeStruct((2, count, cols), F32),
             jax.ShapeDtypeStruct((count + 1, 2, cols), F32),
         ),
-        in_specs=[VMEM] * 8,
+        in_specs=[VMEM] * 9,
         out_specs=[ANY] + [VMEM] * 4,
         scratch_shapes=[pltpu.VMEM((m * n, 1, WIDTH), F32), pltpu.SemaphoreType.DMA],
         compiler_params=PARAMS,
         name="chunks",
-    )(f, part, rim, near, far, start, end, strip)
+    )(f, part, rim, *halo)
 
 
 def final_kernel(
-    m, n, got_ref, near_corner_ref, far_corner_ref, rest_ref, f_ref, drift_ref, near_ref, far_ref, start_ref, end_ref,
+    m, n, got_ref, near_corner_ref, far_corner_ref, rest_ref, f_ref, drift_ref, near_ref, far_lo_ref, far_hi_ref, start_ref, end_ref,
     strip_ref, tail_ref, lead_ref, ratio_out, res_out, grad_out, ratio_ref, resid, grad, outer, rim, head_ref, sem,
 ):
-    halo = Halo(m, near_ref, far_ref, start_ref, end_ref, rest_ref)
+    halo = Halo(m, near_ref, far_lo_ref, far_hi_ref, start_ref, end_ref, rest_ref)
     count, rows, cols = f_ref.shape
     tiles = rows // TILE
     path = lax.axis_index("path")
@@ -370,7 +381,7 @@
     return pl.pallas_call(
         functools.partial(final_kernel, m, n),
         out_shape=(jax.ShapeDtypeStruct((count,), F32), big, big),
-        in_specs=[VMEM] * 13,
+        in_specs=[VMEM] * 14,
         out_specs=(ANY, ANY, ANY),
         scratch_shapes=[
             pltpu.VMEM((count,), F32),
@@ -397,17 +408,16 @@
 
 
 def body(m, n, f, start, end):
-    near, far, rest = slices(f)
+    near, far_lo, far_hi, rest = slices(f)
     strip = ring(tail_rows(f, start, end), 1)
-    far = swap(far, 1)
+    far_lo, far_hi = swap(far_lo, 1), swap(far_hi, 1)
     near = swap(near, 0)
     rest = swap(rest, 1)
     part, drift, rim = interior(f)
-    slabs = near, far, start, end
+    slabs = near, far_lo, far_hi, start, end
     send, near_corner, far_corner, tail, head = chunks(m, n, f, part, rim, *slabs, strip)
     got = lax.all_to_all(send, ("space", "path"), 0, 0, tiled=True)
     near_corner, far_corner = swap(near_corner, 0), swap(far_corner, 1)
-    head, near_corner, far_corner = lax.optimization_barrier((head, near_corner, far_corner))
     lead = ring(head, -1)
     return final(m, n, got, (near_corner, far_corner, rest), f, drift, slabs, (strip, tail, lead))
 

time: 28.6 us -> 27.6 us (0.965)
  waiting for transfers between devices: 7.53 us -> 3.02 us
  starting transfers between devices: 14.4 us -> 17.5 us
  local copies, waits for them, and re-layouts: 1.23 us -> 1.64 us
    ppermute x2, waiting for transfers between devices: 6.12 us -> 0.02 us  [ring(): lax.ppermute(x, 'space', [(i, (i + step) % size) for i in range(size)])]
    all_to_all x1, starting transfers between devices: 3.26 us -> 5.33 us  [body(): got = lax.all_to_all(send, ('space', 'path'), 0, 0, tiled=True)]
    ppermute x5 -> x6, waiting for transfers between devices: 1.41 us -> 3 us  [swap(): lax.ppermute(x, 'path', [((i + kind) % size, ((i ^ 1) + kind) % size) for...]
    ppermute x2, starting transfers between devices: 6.11 us -> 7.62 us  [ring(): lax.ppermute(x, 'space', [(i, (i + step) % size) for i in range(size)])]
    ppermute x5 -> x6, starting transfers between devices: 5.08 us -> 4.51 us  [swap(): lax.ppermute(x, 'path', [((i + kind) % size, ((i ^ 1) + kind) % size) for...]
    unnamed x8, local copies, waits for them, and re-layouts: 1.23 us -> 1.64 us
  transfers between devices with their start and end apart: 8 -> 9, of which waited for: 3 -> 3; matrix products, arithmetic and copies ran while one was open for 0% -> 0% of each run, Pallas kernels for 8% -> 8%
where the time goes in v13:
time: 27.6 us; the launch traced here: 27.3 us
  starting transfers between devices  17.5 us (63%)
  Pallas kernels  4.53 us (16%)
  waiting for transfers between devices  3.02 us (11%)
  local copies, waits for them, and re-layouts  1.64 us (6%)
  between operations  0.69 us (2%)
    ppermute x2, starting transfers between devices, ring(): lax.ppermute(x, 'space', [(i, (i + step) % size) for i in range(size)])  7.62 us
    all_to_all x1, starting transfers between devices, body(): got = lax.all_to_all(send, ('space', 'path'), 0, 0, tiled=True)  5.33 us
    ppermute x6, starting transfers between devices, swap(): lax.ppermute(x, 'path', [((i + kind) % size, ((i ^ 1) + kind) % size) for...  4.51 us
    ppermute x6, waiting for transfers between devices, swap(): lax.ppermute(x, 'path', [((i + kind) % size, ((i ^ 1) + kind) % size) for...  3 us
    pallas_call x1, Pallas kernels, final(): pl.pallas_call(functools.partial(final_kernel, m, n), out_shape=(jax.Shap...  2.26 us
    unnamed x8, local copies, waits for them, and re-layouts  1.64 us
    pallas_call x1, Pallas kernels, interior(): pl.pallas_call(interior_kernel, out_shape=(jax.ShapeDtypeStruct((2 * coun...  1.38 us
    pallas_call x1, Pallas kernels, chunks(): pl.pallas_call(functools.partial(chunk_kernel, m, n), out_shape=(jax.Shap...  0.84 us
  transfers between devices with their start and end apart: 9, of which 3 were waited for; matrix products, arithmetic and copies ran while one was open for 0% of the time, Pallas kernels for 8%

profile of v13, /device:TPU:0, one launch (start us, length us, event | category | flops | bytes accessed | tf_op | source)
XLA Modules:
  0.0 27.3 jit_solution(9816627019551531015)
XLA Ops:
  0.6 0.0 copy-start
  0.6 1.2 %copy-done = f32[8,32,1024]{2,1,0:T(8,128)S(1)} copy-done((f32[8,32,1024]{2,1,0:T(8,128)S(1)}, f32[8,32,1024]{2,1,0:T(8,128)}, u32[]{:S(2)}) %copy-start) | copy-done | bytes 1048600
  1.9 0.0 copy-start.2
  1.9 0.0 copy-start.3
  1.9 0.5 %collective-permute-start = (f32[2,32,1024]{2,1,0:T(8,128)S(1)}, f32[2,32,1024]{2,1,0:T(8,128)S(1)}, u32[]{:S(2)}, u32[]{:S(2)}) collective-permute-start(f32[2,32,1024]{2,1,0:T(8,128)S(1)} %get-tuple-element.17), channel_id=1, source_target_pairs={{0,1},{1,0},{2,3},{3,2},{4,5},{5,4},{6,7},{7,6},{8,9},{9,8},{10,11... | collective-permute-start | bytes 786440 | tf_op jit(solution)/shard_map/ppermute | solution.py:402
  2.4 0.3 %copy-done.2 = f32[32,1024]{1,0:T(8,128)S(1)} copy-done((f32[32,1024]{1,0:T(8,128)S(1)}, f32[32,1024]{1,0:T(8,128)}, u32[]{:S(2)}) %copy-start.2) | copy-done | bytes 131096
  2.8 0.1 copy-done.3
  2.8 3.0 %collective-permute-start.3 = (f32[9,2,1024]{2,1,0:T(2,128)S(1)}, f32[9,2,1024]{2,1,0:T(2,128)S(1)}, u32[]{:S(2)}, u32[]{:S(2)}) collective-permute-start(f32[9,2,1024]{2,1,0:T(2,128)S(1)} %tail_rows.1), channel_id=1, source_target_pairs={{0,4},{4,8},{8,12},{12,16},{16,20},{20,24},{24,28},{28,0},{1,5},{5... | collective-permute-start | bytes 221192 | tf_op jit(solution)/shard_map/ppermute | solution.py:407
  5.9 0.7 %collective-permute-start.1 = (f32[16,1024]{1,0:T(8,128)S(1)}, f32[16,1024]{1,0:T(8,128)S(1)}, u32[]{:S(2)}, u32[]{:S(2)}) collective-permute-start(f32[16,1024]{1,0:T(8,128)S(1)} %get-tuple-element.18), channel_id=1, source_target_pairs={{1,2},{2,1},{3,0},{0,3},{5,6},{6,5},{7,4},{4,7},{9,10},{10,9},{11,... | collective-permute-start | bytes 196616 | tf_op jit(solution)/shard_map/ppermute | solution.py:402
  6.5 1.1 %collective-permute-start.2 = (f32[16,1024]{1,0:T(8,128)S(1)}, f32[16,1024]{1,0:T(8,128)S(1)}, u32[]{:S(2)}, u32[]{:S(2)}) collective-permute-start(f32[16,1024]{1,0:T(8,128)S(1)} %get-tuple-element.19), channel_id=1, source_target_pairs={{1,2},{2,1},{3,0},{0,3},{5,6},{6,5},{7,4},{4,7},{9,10},{10,9},{11,... | collective-permute-start | bytes 196616 | tf_op jit(solution)/shard_map/ppermute | solution.py:402
  7.6 0.7 %collective-permute-start.6 = (f32[32,1024]{1,0:T(8,128)S(1)}, f32[32,1024]{1,0:T(8,128)S(1)}, u32[]{:S(2)}, u32[]{:S(2)}) collective-permute-start(f32[32,1024]{1,0:T(8,128)S(1)} %get-tuple-element.23), channel_id=1, source_target_pairs={{1,2},{2,1},{3,0},{0,3},{5,6},{6,5},{7,4},{4,7},{9,10},{10,9},{11,... | collective-permute-start | bytes 393224 | tf_op jit(solution)/shard_map/ppermute | solution.py:402
  8.3 1.4 %interior.1 = (f32[16,128]{1,0:T(8,128)S(1)}, f32[8,32,1024]{2,1,0:T(8,128)S(1)}, f32[2,8,1024]{2,1,0:T(8,128)S(1)}) custom-call(f32[8,32,1024]{2,1,0:T(8,128)S(1)} %copy-done), custom_call_target="tpu_custom_call" | custom-call | flops 5242880 | bytes 2097152 | tf_op jit(solution)/shard_map/interior/pallas_call | solution.py:159
  9.6 0.0 copy-start.1
  9.7 0.6 %collective-permute-done.1.far_lo_ref = f32[16,1024]{1,0:T(8,128)S(1)} collective-permute-done((f32[16,1024]{1,0:T(8,128)S(1)}, f32[16,1024]{1,0:T(8,128)S(1)}, u32[]{:S(2)}, u32[]{:S(2)}) %collective-permute-start.1) | collective-permute-done | bytes 65568 | tf_op jit(solution)/shard_map/ppermute | solution.py:402
  10.2 1.0 %collective-permute-done.2.far_hi_ref = f32[16,1024]{1,0:T(8,128)S(1)} collective-permute-done((f32[16,1024]{1,0:T(8,128)S(1)}, f32[16,1024]{1,0:T(8,128)S(1)}, u32[]{:S(2)}, u32[]{:S(2)}) %collective-permute-start.2) | collective-permute-done | bytes 65568 | tf_op jit(solution)/shard_map/ppermute | solution.py:402
  11.2 0.0 collective-permute-done.3.strip_ref
  11.2 0.0 collective-permute-done.near_ref
  11.2 0.8 %chunks.1 = (f32[32,1,384]{2,1,0:T(1,128)}, f32[1,1024]{1,0:T(1,128)S(1)}, f32[1,1024]{1,0:T(1,128)S(1)}, f32[2,8,1024]{2,1,0:T(8,128)S(1)}, f32[9,2,1024]{2,1,0:T(2,128)S(1)}) custom-call(f32[8,32,1024]{2,1,0:T(8,128)S(1)} %copy-done, f32[16,128]{1,0:T(8,128)S(1)} %get-tuple-element.15.part_ref, f32[2,8,1024]{2,1,0:T(8,128)S(1)} %get-tuple-element.16.rim_ref, ...), custom_call_target="tpu_custom_call" | custom-call | tf_op jit(solution)/shard_map/chunks/pallas_call | solution.py:224
  12.1 5.3 %all-to-all-start = ((f32[32,1,384]{2,1,0:T(1,128)}), f32[32,1,384]{2,1,0:T(1,128)S(1)}, u32[]{:S(2)}, u32[]{:S(2)}) async-start(f32[32,1,384]{2,1,0:T(1,128)} %get-tuple-element.20), calls=%async_computation | async-start | bytes 98304 | tf_op jit(solution)/shard_map/all_to_all | solution.py:419
  17.4 4.6 %collective-permute-start.7 = (f32[9,2,1024]{2,1,0:T(2,128)S(1)}, f32[9,2,1024]{2,1,0:T(2,128)S(1)}, u32[]{:S(2)}, u32[]{:S(2)}) collective-permute-start(f32[9,2,1024]{2,1,0:T(2,128)S(1)} %get-tuple-element.26), channel_id=1, source_target_pairs={{0,28},{4,0},{8,4},{12,8},{16,12},{20,16},{24,20},{28,24},{1,29},{... | collective-permute-start | bytes 221192 | tf_op jit(solution)/shard_map/ppermute | solution.py:407
  22.0 0.0 collective-permute-start.4
  22.0 1.6 %collective-permute-start.5 = (f32[1,1024]{1,0:T(1,128)S(1)}, f32[1,1024]{1,0:T(1,128)S(1)}, u32[]{:S(2)}, u32[]{:S(2)}) collective-permute-start(f32[1,1024]{1,0:T(1,128)S(1)} %get-tuple-element.22), channel_id=1, source_target_pairs={{1,2},{2,1},{3,0},{0,3},{5,6},{6,5},{7,4},{4,7},{9,10},{10,9},{11,... | collective-permute-start | bytes 12296 | tf_op jit(solution)/shard_map/ppermute | solution.py:402
  23.6 0.0 collective-permute-done.6.rest_ref
  23.6 0.0 collective-permute-done.4.near_corner_ref
  23.6 1.4 %collective-permute-done.5.far_corner_ref = f32[1,1024]{1,0:T(1,128)S(1)} collective-permute-done((f32[1,1024]{1,0:T(1,128)S(1)}, f32[1,1024]{1,0:T(1,128)S(1)}, u32[]{:S(2)}, u32[]{:S(2)}) %collective-permute-start.5) | collective-permute-done | bytes 4128 | tf_op jit(solution)/shard_map/ppermute | solution.py:402
  25.1 0.0 collective-permute-done.7.lead_ref
  25.1 0.0 all-to-all-done.got_ref
  25.1 0.0 copy-done.1
  25.1 2.3 %final.1 = (f32[8]{0:T(128)}, f32[8,32,1024]{2,1,0:T(8,128)}, f32[8,32,1024]{2,1,0:T(8,128)}) custom-call(f32[32,1,384]{2,1,0:T(1,128)S(1)} %all-to-all-done.got_ref, f32[1,1024]{1,0:T(1,128)S(1)} %collective-permute-done.4.near_corner_ref, f32[1,1024]{1,0:T(1,128)S(1)} %collective-permute-done.5.far_corner_ref, ...), custom_call_target="tpu_custom_call" | custom-call | tf_op jit(solution)/shard_map/final/pallas_call | solution.py:381
  (2 shorter events, 0.1 us)
Async XLA Ops:
  0.6 1.2 %copy-start = (f32[8,32,1024]{2,1,0:T(8,128)S(1)}, f32[8,32,1024]{2,1,0:T(8,128)}, u32[]{:S(2)}) copy-start(f32[8,32,1024]{2,1,0:T(8,128)} %f_ref.9) | copy-start | bytes 3145732
  1.9 0.9 %copy-start.2 = (f32[32,1024]{1,0:T(8,128)S(1)}, f32[32,1024]{1,0:T(8,128)}, u32[]{:S(2)}) copy-start(f32[32,1024]{1,0:T(8,128)} %start_ref.5) | copy-start | bytes 393220
  1.9 1.0 %copy-start.3 = (f32[32,1024]{1,0:T(8,128)S(1)}, f32[32,1024]{1,0:T(8,128)}, u32[]{:S(2)}) copy-start(f32[32,1024]{1,0:T(8,128)} %end_ref.5) | copy-start | bytes 393220
  1.9 9.3 %collective-permute-start = (f32[2,32,1024]{2,1,0:T(8,128)S(1)}, f32[2,32,1024]{2,1,0:T(8,128)S(1)}, u32[]{:S(2)}, u32[]{:S(2)}) collective-permute-start(f32[2,32,1024]{2,1,0:T(8,128)S(1)} %get-tuple-element.17), channel_id=1, source_target_pairs={{0,1},{1,0},{2,3},{3,2},{4,5},{5,4},{6,7},{7,6},{8,9},{9,8},{10,11... | collective-permute-start | bytes 786440 | tf_op jit(solution)/shard_map/ppermute | solution.py:402
  2.8 8.4 %collective-permute-start.3 = (f32[9,2,1024]{2,1,0:T(2,128)S(1)}, f32[9,2,1024]{2,1,0:T(2,128)S(1)}, u32[]{:S(2)}, u32[]{:S(2)}) collective-permute-start(f32[9,2,1024]{2,1,0:T(2,128)S(1)} %tail_rows.1), channel_id=1, source_target_pairs={{0,4},{4,8},{8,12},{12,16},{16,20},{20,24},{24,28},{28,0},{1,5},{5... | collective-permute-start | bytes 221192 | tf_op jit(solution)/shard_map/ppermute | solution.py:407
  5.9 4.3 %collective-permute-start.1 = (f32[16,1024]{1,0:T(8,128)S(1)}, f32[16,1024]{1,0:T(8,128)S(1)}, u32[]{:S(2)}, u32[]{:S(2)}) collective-permute-start(f32[16,1024]{1,0:T(8,128)S(1)} %get-tuple-element.18), channel_id=1, source_target_pairs={{1,2},{2,1},{3,0},{0,3},{5,6},{6,5},{7,4},{4,7},{9,10},{10,9},{11,... | collective-permute-start | bytes 196616 | tf_op jit(solution)/shard_map/ppermute | solution.py:402
  6.5 4.7 %collective-permute-start.2 = (f32[16,1024]{1,0:T(8,128)S(1)}, f32[16,1024]{1,0:T(8,128)S(1)}, u32[]{:S(2)}, u32[]{:S(2)}) collective-permute-start(f32[16,1024]{1,0:T(8,128)S(1)} %get-tuple-element.19), channel_id=1, source_target_pairs={{1,2},{2,1},{3,0},{0,3},{5,6},{6,5},{7,4},{4,7},{9,10},{10,9},{11,... | collective-permute-start | bytes 196616 | tf_op jit(solution)/shard_map/ppermute | solution.py:402
  7.6 16.0 %collective-permute-start.6 = (f32[32,1024]{1,0:T(8,128)S(1)}, f32[32,1024]{1,0:T(8,128)S(1)}, u32[]{:S(2)}, u32[]{:S(2)}) collective-permute-start(f32[32,1024]{1,0:T(8,128)S(1)} %get-tuple-element.23), channel_id=1, source_target_pairs={{1,2},{2,1},{3,0},{0,3},{5,6},{6,5},{7,4},{4,7},{9,10},{10,9},{11,... | collective-permute-start | bytes 393224 | tf_op jit(solution)/shard_map/ppermute | solution.py:402
  9.6 15.4 %copy-start.1 = (f32[8,32,1024]{2,1,0:T(8,128)S(1)}, f32[8,32,1024]{2,1,0:T(8,128)}, u32[]{:S(2)}) copy-start(f32[8,32,1024]{2,1,0:T(8,128)} %f_ref.9) | copy-start | bytes 3145732
  12.1 13.0 %all-to-all-start = ((f32[32,1,384]{2,1,0:T(1,128)}), f32[32,1,384]{2,1,0:T(1,128)S(1)}, u32[]{:S(2)}, u32[]{:S(2)}) async-start(f32[32,1,384]{2,1,0:T(1,128)} %get-tuple-element.20), calls=%async_computation | async-start | bytes 98304 | tf_op jit(solution)/shard_map/all_to_all | solution.py:419
  17.4 7.6 %collective-permute-start.7 = (f32[9,2,1024]{2,1,0:T(2,128)S(1)}, f32[9,2,1024]{2,1,0:T(2,128)S(1)}, u32[]{:S(2)}, u32[]{:S(2)}) collective-permute-start(f32[9,2,1024]{2,1,0:T(2,128)S(1)} %get-tuple-element.26), channel_id=1, source_target_pairs={{0,28},{4,0},{8,4},{12,8},{16,12},{20,16},{24,20},{28,24},{1,29},{... | collective-permute-start | bytes 221192 | tf_op jit(solution)/shard_map/ppermute | solution.py:407
  22.0 1.6 %collective-permute-start.4 = (f32[1,1024]{1,0:T(1,128)S(1)}, f32[1,1024]{1,0:T(1,128)S(1)}, u32[]{:S(2)}, u32[]{:S(2)}) collective-permute-start(f32[1,1024]{1,0:T(1,128)S(1)} %get-tuple-element.21), channel_id=1, source_target_pairs={{0,1},{1,0},{2,3},{3,2},{4,5},{5,4},{6,7},{7,6},{8,9},{9,8},{10,11... | collective-permute-start | bytes 12296 | tf_op jit(solution)/shard_map/ppermute | solution.py:402
  22.0 3.0 %collective-permute-start.5 = (f32[1,1024]{1,0:T(1,128)S(1)}, f32[1,1024]{1,0:T(1,128)S(1)}, u32[]{:S(2)}, u32[]{:S(2)}) collective-permute-start(f32[1,1024]{1,0:T(1,128)S(1)} %get-tuple-element.22), channel_id=1, source_target_pairs={{1,2},{2,1},{3,0},{0,3},{5,6},{6,5},{7,4},{4,7},{9,10},{10,9},{11,... | collective-permute-start | bytes 12296 | tf_op jit(solution)/shard_map/ppermute | solution.py:402

commit v14 on v11

--- a/solution.py
+++ b/solution.py
@@ -14,7 +14,7 @@
 VMEM = pl.BlockSpec(memory_space=pltpu.VMEM)
 ANY = pl.BlockSpec(memory_space=pl.ANY)
 PIECES = 4
-WIDTH = 384
+WIDTH = 256
 PARAMS = pltpu.CompilerParams(vmem_limit_bytes=16 * 2**20)
 
 
@@ -161,7 +161,7 @@
 
 def chunk_kernel(
     m, n, f_ref, part_ref, rim_ref, near_ref, far_ref, start_ref, end_ref, strip_ref,
-    out_ref, near_corner_ref, rest_ref, tail_ref, head_ref, lines, sem,
+    out_ref, near_corner_ref, rest_ref, tail_ref, head_ref, second_ref, lines, sem,
 ):
     halo = Halo(m, near_ref, far_ref, start_ref, end_ref)
     count, rows, cols = f_ref.shape
@@ -202,9 +202,10 @@
     rest_ref[0:rows, :] = f_ref[pick(halo.odd, count - 2, 1)]
     rest_ref[rows:, :] = jnp.broadcast_to(tail_ref[1, pl.ds(pick(halo.odd, count - 1, 0), 1), :], (TILE, cols))
     for s in range(count):
-        head_ref[s] = f_ref[s, 0:2, :]
-    head_ref[count, 0:1, :] = halo.below(pl.ds(0, 1))
-    head_ref[count, 1:2, :] = halo.above(pl.ds(0, 1))
+        head_ref[s // 2, s % 2 : s % 2 + 1, :] = f_ref[s, 0:1, :]
+        second_ref[s // 2, s % 2 : s % 2 + 1, :] = f_ref[s, 1:2, :]
+    head_ref[count // 2, 0:1, :] = halo.below(pl.ds(0, 1))
+    head_ref[count // 2, 1:2, :] = halo.above(pl.ds(0, 1))
     copy.wait()
 
 
@@ -217,10 +218,11 @@
             jax.ShapeDtypeStruct((1, cols), F32),
             jax.ShapeDtypeStruct((rows + TILE, cols), F32),
             jax.ShapeDtypeStruct((2, count, cols), F32),
-            jax.ShapeDtypeStruct((count + 1, 2, cols), F32),
+            jax.ShapeDtypeStruct((count // 2 + 1, 2, cols), F32),
+            jax.ShapeDtypeStruct((count // 2, 2, cols), F32),
         ),
         in_specs=[VMEM] * 8,
-        out_specs=[ANY] + [VMEM] * 4,
+        out_specs=[ANY] + [VMEM] * 5,
         scratch_shapes=[pltpu.VMEM((m * n, 1, WIDTH), F32), pltpu.SemaphoreType.DMA],
         compiler_params=PARAMS,
         name="chunks",
@@ -229,7 +231,7 @@
 
 def final_kernel(
     m, n, got_ref, near_corner_ref, rest_ref, f_ref, drift_ref, near_ref, far_ref, start_ref, end_ref,
-    strip_ref, tail_ref, lead_ref, ratio_out, res_out, grad_out, ratio_ref, resid, grad, outer, rim, head_ref, sem,
+    strip_ref, tail_ref, lead_ref, lead_b_ref, ratio_out, res_out, grad_out, ratio_ref, resid, grad, outer, rim, head_ref, sem,
 ):
     halo = Halo(m, near_ref, far_ref, start_ref, end_ref, rest_ref)
     count, rows, cols = f_ref.shape
@@ -280,7 +282,7 @@
             pick(first, strip_ref[count, 0:1, :], pick(halo.odd, near, far)),
             pick(last, strip_ref[count, 1:2, :], pick(halo.odd, far, near)),
         ),
-        (lead_ref[count, 0:1, :], lead_ref[count, 1:2, :]),
+        (lead_ref[count // 2, 0:1, :], lead_ref[count // 2, 1:2, :]),
     )
 
     def at(k):
@@ -300,7 +302,7 @@
                 if k == 0:
                     drift += jnp.where(row == 0, tail_ref[1, s : s + 1, :], 0.0)
                 if k == tiles - 1:
-                    drift += jnp.where(row == TILE - 1, lead_ref[s, 0:1, :], 0.0)
+                    drift += jnp.where(row == TILE - 1, lead_ref[s // 2, s % 2 : s % 2 + 1, :], 0.0)
             else:
                 slot = 0 if s < 0 else 1
                 c = outer[slot, at(k), :]
@@ -333,8 +335,8 @@
     for s in range(count):
         rim[0, s : s + 1, :] = f_ref[s, 0:1, :]
         rim[1, s : s + 1, :] = f_ref[s, rows - 1 : rows, :]
-        for r in range(2):
-            head_ref[r, s : s + 1, :] = lead_ref[s, r : r + 1, :]
+        for r, ref in enumerate((lead_ref, lead_b_ref)):
+            head_ref[r, s : s + 1, :] = ref[s // 2, s % 2 : s % 2 + 1, :]
     for far, mid, near, (low, high), place in (
         (tail_ref[0], tail_ref[1], rim[0], corners[0], TILE - 1),
         (head_ref[1], head_ref[0], rim[1], corners[1], TILE + rows),
@@ -370,7 +372,7 @@
     return pl.pallas_call(
         functools.partial(final_kernel, m, n),
         out_shape=(jax.ShapeDtypeStruct((count,), F32), big, big),
-        in_specs=[VMEM] * 12,
+        in_specs=[VMEM] * 13,
         out_specs=(ANY, ANY, ANY),
         scratch_shapes=[
             pltpu.VMEM((count,), F32),
@@ -403,11 +405,11 @@
     near = swap(near, 0)
     part, drift, rim = interior(f)
     slabs = near, far, start, end
-    send, near_corner, rest, tail, head = chunks(m, n, f, part, rim, *slabs, strip)
+    send, near_corner, rest, tail, head, second = chunks(m, n, f, part, rim, *slabs, strip)
     got = lax.all_to_all(send, ("space", "path"), 0, 0, tiled=True)
-    lead = ring(head, -1)
+    lead, lead_b = ring(head, -1), ring(second, -1)
     late = swap(near_corner, 0), swap(rest, 1)
-    return final(m, n, got, late, f, drift, slabs, (strip, tail, lead))
+    return final(m, n, got, late, f, drift, slabs, (strip, tail, lead, lead_b))
 
 
 def solution(mesh):

time: 26.3 us -> 27.4 us (1.042)
  waiting for transfers between devices: 6.87 us -> 7.53 us
  starting transfers between devices: 12.8 us -> 13.3 us
    ppermute x2 -> x3, waiting for transfers between devices: 4.96 us -> 6.36 us  [ring(): lax.ppermute(x, 'space', [(i, (i + step) % size) for i in range(size)])]
    all_to_all x1, waiting for transfers between devices: 0.74 us -> 0.01 us  [body(): got = lax.all_to_all(send, ('space', 'path'), 0, 0, tiled=True)]
    ppermute x2 -> x3, starting transfers between devices: 6.18 us -> 6.71 us  [ring(): lax.ppermute(x, 'space', [(i, (i + step) % size) for i in range(size)])]
  transfers between devices with their start and end apart: 7 -> 8, of which waited for: 4 -> 3; matrix products, arithmetic and copies ran while one was open for 0% -> 0% of each run, Pallas kernels for 5% -> 5%
where the time goes in v14:
time: 27.4 us; the launch traced here: 27.2 us
  starting transfers between devices  13.3 us (49%)
  waiting for transfers between devices  7.53 us (27%)
  Pallas kernels  4.45 us (16%)
  local copies, waits for them, and re-layouts  1.23 us (4%)
  between operations  0.7 us (3%)
    ppermute x3, starting transfers between devices, ring(): lax.ppermute(x, 'space', [(i, (i + step) % size) for i in range(size)])  6.71 us
    ppermute x3, waiting for transfers between devices, ring(): lax.ppermute(x, 'space', [(i, (i + step) % size) for i in range(size)])  6.36 us
    all_to_all x1, starting transfers between devices, body(): got = lax.all_to_all(send, ('space', 'path'), 0, 0, tiled=True)  3.39 us
    ppermute x4, starting transfers between devices, swap(): lax.ppermute(x, 'path', [((i + kind) % size, ((i ^ 1) + kind) % size) for...  3.21 us
    pallas_call x1, Pallas kernels, final(): pl.pallas_call(functools.partial(final_kernel, m, n), out_shape=(jax.Shap...  2.2 us
    pallas_call x1, Pallas kernels, interior(): pl.pallas_call(interior_kernel, out_shape=(jax.ShapeDtypeStruct((2 * coun...  1.38 us
    unnamed x8, local copies, waits for them, and re-layouts  1.23 us
    ppermute x4, waiting for transfers between devices, swap(): lax.ppermute(x, 'path', [((i + kind) % size, ((i ^ 1) + kind) % size) for...  1.17 us
  transfers between devices with their start and end apart: 8, of which 3 were waited for; matrix products, arithmetic and copies ran while one was open for 0% of the time, Pallas kernels for 5%

profile of v14, /device:TPU:0, one launch (start us, length us, event | category | flops | bytes accessed | tf_op | source)
XLA Modules:
  0.0 27.2 jit_solution(7243554259483523249)
XLA Ops:
  0.6 0.0 copy-start
  0.6 1.2 %copy-done = f32[8,32,1024]{2,1,0:T(8,128)S(1)} copy-done((f32[8,32,1024]{2,1,0:T(8,128)S(1)}, f32[8,32,1024]{2,1,0:T(8,128)}, u32[]{:S(2)}) %copy-start) | copy-done | bytes 1048600
  1.9 0.0 copy-start.2
  1.9 0.0 copy-start.3
  1.9 0.5 %collective-permute-start = (f32[2,32,1024]{2,1,0:T(8,128)S(1)}, f32[2,32,1024]{2,1,0:T(8,128)S(1)}, u32[]{:S(2)}, u32[]{:S(2)}) collective-permute-start(f32[2,32,1024]{2,1,0:T(8,128)S(1)} %get-tuple-element.16), channel_id=1, source_target_pairs={{0,1},{1,0},{2,3},{3,2},{4,5},{5,4},{6,7},{7,6},{8,9},{9,8},{10,11... | collective-permute-start | bytes 786440 | tf_op jit(solution)/shard_map/ppermute | solution.py:393
  2.4 2.6 %collective-permute-start.1 = (f32[32,1024]{1,0:T(8,128)S(1)}, f32[32,1024]{1,0:T(8,128)S(1)}, u32[]{:S(2)}, u32[]{:S(2)}) collective-permute-start(f32[32,1024]{1,0:T(8,128)S(1)} %get-tuple-element.17), channel_id=1, source_target_pairs={{1,2},{2,1},{3,0},{0,3},{5,6},{6,5},{7,4},{4,7},{9,10},{10,9},{11,... | collective-permute-start | bytes 393224 | tf_op jit(solution)/shard_map/ppermute | solution.py:393
  5.0 0.0 copy-done.2
  5.0 0.0 copy-done.3
  5.1 1.6 %collective-permute-start.2 = (f32[9,2,1024]{2,1,0:T(2,128)S(1)}, f32[9,2,1024]{2,1,0:T(2,128)S(1)}, u32[]{:S(2)}, u32[]{:S(2)}) collective-permute-start(f32[9,2,1024]{2,1,0:T(2,128)S(1)} %tail_rows.1), channel_id=1, source_target_pairs={{0,4},{4,8},{8,12},{12,16},{16,20},{20,24},{24,28},{28,0},{1,5},{5... | collective-permute-start | bytes 221192 | tf_op jit(solution)/shard_map/ppermute | solution.py:398
  6.6 1.4 %interior.1 = (f32[16,128]{1,0:T(8,128)S(1)}, f32[8,32,1024]{2,1,0:T(8,128)S(1)}, f32[2,8,1024]{2,1,0:T(8,128)S(1)}) custom-call(f32[8,32,1024]{2,1,0:T(8,128)S(1)} %copy-done), custom_call_target="tpu_custom_call" | custom-call | flops 5242880 | bytes 2097152 | tf_op jit(solution)/shard_map/interior/pallas_call | solution.py:147
  8.0 0.0 copy-start.1
  8.0 4.1 %collective-permute-done.2.strip_ref = f32[9,2,1024]{2,1,0:T(2,128)S(1)} collective-permute-done((f32[9,2,1024]{2,1,0:T(2,128)S(1)}, f32[9,2,1024]{2,1,0:T(2,128)S(1)}, u32[]{:S(2)}, u32[]{:S(2)}) %collective-permute-start.2) | collective-permute-done | bytes 73760 | tf_op jit(solution)/shard_map/ppermute | solution.py:398
  12.2 0.0 collective-permute-done.1.far_ref
  12.2 0.0 collective-permute-done.near_ref
  12.2 0.8 %chunks.1 = (f32[32,1,256]{2,1,0:T(1,128)}, f32[1,1024]{1,0:T(1,128)S(1)}, f32[40,1024]{1,0:T(8,128)S(1)}, f32[2,8,1024]{2,1,0:T(8,128)S(1)}, f32[5,2,1024]{2,1,0:T(2,128)S(1)}, /*index=5*/f32[4,2,1024]{2,1,0:T(2,128)S(1)}) custom-call(f32[8,32,1024]{2,1,0:T(8,128)S(1)} %copy-done, f32[16,128]{1,0:T(8,128)S(1)} %get-tuple-element.14.part_ref, ...), custom_call_target="tpu_custom_call" | custom-call | tf_op jit(solution)/shard_map/chunks/pallas_call | solution.py:214
  13.0 0.1 collective-permute-start.4
  13.1 3.4 %all-to-all-start = ((f32[32,1,256]{2,1,0:T(1,128)}), f32[32,1,256]{2,1,0:T(1,128)S(1)}, u32[]{:S(2)}, u32[]{:S(2)}) async-start(f32[32,1,256]{2,1,0:T(1,128)} %get-tuple-element.18), calls=%async_computation | async-start | bytes 65536 | tf_op jit(solution)/shard_map/all_to_all | solution.py:409
  16.5 4.6 %collective-permute-start.5 = (f32[5,2,1024]{2,1,0:T(2,128)S(1)}, f32[5,2,1024]{2,1,0:T(2,128)S(1)}, u32[]{:S(2)}, u32[]{:S(2)}) collective-permute-start(f32[5,2,1024]{2,1,0:T(2,128)S(1)} %get-tuple-element.23), channel_id=1, source_target_pairs={{0,28},{4,0},{8,4},{12,8},{16,12},{20,16},{24,20},{28,24},{1,29},{... | collective-permute-start | bytes 122888 | tf_op jit(solution)/shard_map/ppermute | solution.py:398
  21.1 0.5 %collective-permute-start.6 = (f32[4,2,1024]{2,1,0:T(2,128)S(1)}, f32[4,2,1024]{2,1,0:T(2,128)S(1)}, u32[]{:S(2)}, u32[]{:S(2)}) collective-permute-start(f32[4,2,1024]{2,1,0:T(2,128)S(1)} %get-tuple-element.24), channel_id=1, source_target_pairs={{0,28},{4,0},{8,4},{12,8},{16,12},{20,16},{24,20},{28,24},{1,29},{... | collective-permute-start | bytes 98312 | tf_op jit(solution)/shard_map/ppermute | solution.py:398
  21.6 0.0 collective-permute-start.3
  21.6 1.2 %collective-permute-done.3.near_corner_ref = f32[1,1024]{1,0:T(1,128)S(1)} collective-permute-done((f32[1,1024]{1,0:T(1,128)S(1)}, f32[1,1024]{1,0:T(1,128)S(1)}, u32[]{:S(2)}, u32[]{:S(2)}) %collective-permute-start.3) | collective-permute-done | bytes 4128 | tf_op jit(solution)/shard_map/ppermute | solution.py:393
  22.8 2.2 %collective-permute-done.6.lead_b_ref = f32[4,2,1024]{2,1,0:T(2,128)S(1)} collective-permute-done((f32[4,2,1024]{2,1,0:T(2,128)S(1)}, f32[4,2,1024]{2,1,0:T(2,128)S(1)}, u32[]{:S(2)}, u32[]{:S(2)}) %collective-permute-start.6) | collective-permute-done | bytes 32800 | tf_op jit(solution)/shard_map/ppermute | solution.py:398
  25.0 0.0 collective-permute-done.5.lead_ref
  25.0 0.0 all-to-all-done.got_ref
  25.0 0.0 collective-permute-done.4.rest_ref
  25.0 0.0 copy-done.1
  25.0 2.2 %final.1 = (f32[8]{0:T(128)}, f32[8,32,1024]{2,1,0:T(8,128)}, f32[8,32,1024]{2,1,0:T(8,128)}) custom-call(f32[32,1,256]{2,1,0:T(1,128)S(1)} %all-to-all-done.got_ref, f32[1,1024]{1,0:T(1,128)S(1)} %collective-permute-done.3.near_corner_ref, f32[40,1024]{1,0:T(8,128)S(1)} %collective-permute-done.4.rest_ref, f32[8,32,1024]{2,1,0:T(8,128)S(1)} %copy-done.1, ...), custom_call_target="tpu_custom_call" | custom-call | tf_op jit(solution)/shard_map/final/pallas_call | solution.py:372
  (2 shorter events, 0.0 us)
Async XLA Ops:
  0.6 1.2 %copy-start = (f32[8,32,1024]{2,1,0:T(8,128)S(1)}, f32[8,32,1024]{2,1,0:T(8,128)}, u32[]{:S(2)}) copy-start(f32[8,32,1024]{2,1,0:T(8,128)} %f_ref.9) | copy-start | bytes 3145732
  1.9 3.2 %copy-start.2 = (f32[32,1024]{1,0:T(8,128)S(1)}, f32[32,1024]{1,0:T(8,128)}, u32[]{:S(2)}) copy-start(f32[32,1024]{1,0:T(8,128)} %start_ref.5) | copy-start | bytes 393220
  1.9 3.2 %copy-start.3 = (f32[32,1024]{1,0:T(8,128)S(1)}, f32[32,1024]{1,0:T(8,128)}, u32[]{:S(2)}) copy-start(f32[32,1024]{1,0:T(8,128)} %end_ref.5) | copy-start | bytes 393220
  1.9 10.3 %collective-permute-start = (f32[2,32,1024]{2,1,0:T(8,128)S(1)}, f32[2,32,1024]{2,1,0:T(8,128)S(1)}, u32[]{:S(2)}, u32[]{:S(2)}) collective-permute-start(f32[2,32,1024]{2,1,0:T(8,128)S(1)} %get-tuple-element.16), channel_id=1, source_target_pairs={{0,1},{1,0},{2,3},{3,2},{4,5},{5,4},{6,7},{7,6},{8,9},{9,8},{10,11... | collective-permute-start | bytes 786440 | tf_op jit(solution)/shard_map/ppermute | solution.py:393
  2.4 9.8 %collective-permute-start.1 = (f32[32,1024]{1,0:T(8,128)S(1)}, f32[32,1024]{1,0:T(8,128)S(1)}, u32[]{:S(2)}, u32[]{:S(2)}) collective-permute-start(f32[32,1024]{1,0:T(8,128)S(1)} %get-tuple-element.17), channel_id=1, source_target_pairs={{1,2},{2,1},{3,0},{0,3},{5,6},{6,5},{7,4},{4,7},{9,10},{10,9},{11,... | collective-permute-start | bytes 393224 | tf_op jit(solution)/shard_map/ppermute | solution.py:393
  5.1 7.1 %collective-permute-start.2 = (f32[9,2,1024]{2,1,0:T(2,128)S(1)}, f32[9,2,1024]{2,1,0:T(2,128)S(1)}, u32[]{:S(2)}, u32[]{:S(2)}) collective-permute-start(f32[9,2,1024]{2,1,0:T(2,128)S(1)} %tail_rows.1), channel_id=1, source_target_pairs={{0,4},{4,8},{8,12},{12,16},{16,20},{20,24},{24,28},{28,0},{1,5},{5... | collective-permute-start | bytes 221192 | tf_op jit(solution)/shard_map/ppermute | solution.py:398
  8.0 17.0 %copy-start.1 = (f32[8,32,1024]{2,1,0:T(8,128)S(1)}, f32[8,32,1024]{2,1,0:T(8,128)}, u32[]{:S(2)}) copy-start(f32[8,32,1024]{2,1,0:T(8,128)} %f_ref.9) | copy-start | bytes 3145732
  13.0 12.0 %collective-permute-start.4 = (f32[40,1024]{1,0:T(8,128)S(1)}, f32[40,1024]{1,0:T(8,128)S(1)}, u32[]{:S(2)}, u32[]{:S(2)}) collective-permute-start(f32[40,1024]{1,0:T(8,128)S(1)} %get-tuple-element.20), channel_id=1, source_target_pairs={{1,2},{2,1},{3,0},{0,3},{5,6},{6,5},{7,4},{4,7},{9,10},{10,9},{11,... | collective-permute-start | bytes 491528 | tf_op jit(solution)/shard_map/ppermute | solution.py:393
  13.1 11.9 %all-to-all-start = ((f32[32,1,256]{2,1,0:T(1,128)}), f32[32,1,256]{2,1,0:T(1,128)S(1)}, u32[]{:S(2)}, u32[]{:S(2)}) async-start(f32[32,1,256]{2,1,0:T(1,128)} %get-tuple-element.18), calls=%async_computation | async-start | bytes 65536 | tf_op jit(solution)/shard_map/all_to_all | solution.py:409
  16.5 8.5 %collective-permute-start.5 = (f32[5,2,1024]{2,1,0:T(2,128)S(1)}, f32[5,2,1024]{2,1,0:T(2,128)S(1)}, u32[]{:S(2)}, u32[]{:S(2)}) collective-permute-start(f32[5,2,1024]{2,1,0:T(2,128)S(1)} %get-tuple-element.23), channel_id=1, source_target_pairs={{0,28},{4,0},{8,4},{12,8},{16,12},{20,16},{24,20},{28,24},{1,29},{... | collective-permute-start | bytes 122888 | tf_op jit(solution)/shard_map/ppermute | solution.py:398
  21.1 3.9 %collective-permute-start.6 = (f32[4,2,1024]{2,1,0:T(2,128)S(1)}, f32[4,2,1024]{2,1,0:T(2,128)S(1)}, u32[]{:S(2)}, u32[]{:S(2)}) collective-permute-start(f32[4,2,1024]{2,1,0:T(2,128)S(1)} %get-tuple-element.24), channel_id=1, source_target_pairs={{0,28},{4,0},{8,4},{12,8},{16,12},{20,16},{24,20},{28,24},{1,29},{... | collective-permute-start | bytes 98312 | tf_op jit(solution)/shard_map/ppermute | solution.py:398
  21.6 1.2 %collective-permute-start.3 = (f32[1,1024]{1,0:T(1,128)S(1)}, f32[1,1024]{1,0:T(1,128)S(1)}, u32[]{:S(2)}, u32[]{:S(2)}) collective-permute-start(f32[1,1024]{1,0:T(1,128)S(1)} %get-tuple-element.19), channel_id=1, source_target_pairs={{0,1},{1,0},{2,3},{3,2},{4,5},{5,4},{6,7},{7,6},{8,9},{9,8},{10,11... | collective-permute-start | bytes 12296 | tf_op jit(solution)/shard_map/ppermute | solution.py:393

commit v15 on v11

--- a/solution.py
+++ b/solution.py
@@ -14,7 +14,8 @@
 VMEM = pl.BlockSpec(memory_space=pltpu.VMEM)
 ANY = pl.BlockSpec(memory_space=pl.ANY)
 PIECES = 4
-WIDTH = 384
+WIDTH = 128
+RATIO_FLOPS = 10**9
 PARAMS = pltpu.CompilerParams(vmem_limit_bytes=16 * 2**20)
 
 
@@ -227,52 +228,75 @@
     )(f, part, rim, near, far, start, end, strip)
 
 
+def ratio_kernel(m, n, got_ref, scale_ref):
+    count = scale_ref.shape[0] - 4
+    path = lax.axis_index("path")
+    first, last = path == 0, path == m - 1
+    path_lo = jnp.where(first, path, path - 1)
+    path_hi = jnp.where(last, path, path + 1)
+
+    def gathered(p):
+        total = got_ref[p, :, 0:LANES]
+        for i in range(1, n):
+            total += got_ref[i * m + p, :, 0:LANES]
+        return jnp.broadcast_to(total, (TILE, LANES))
+
+    mine = gathered(path)
+    lower = gathered(path_lo)
+    upper = gathered(path_hi)
+    lane = iota((TILE, LANES), 1)
+    sub = iota((TILE, LANES), 0)
+
+    def shift(x, k):
+        return pltpu.roll(x, k % LANES, 1)
+
+    def ratios(x):
+        return jnp.sqrt(x + EPS) / jnp.sqrt(shift(x, -count) + EPS)
+
+    low = jnp.where(first, 0.0, shift(ratios(lower), 1 - count))
+    high = jnp.where(last, 0.0, shift(ratios(upper), count + 1))
+    own = ratios(mine)
+    ratio = jnp.where(lane == 0, low, jnp.where(lane == count + 1, high, shift(own, 1)))
+
+    def splat(t):
+        return jnp.broadcast_to(jnp.sum(jnp.where(lane == t, ratio, 0.0), axis=1, keepdims=True), (TILE, LANES))
+
+    for t in range(count + 2):
+        scale_ref[t] = splat(t)
+    column = jnp.sum(jnp.where(lane == sub + 1, ratio, 0.0), axis=1, keepdims=True)
+    scale_ref[count + 2] = jnp.broadcast_to(column, (TILE, LANES))
+    scale_ref[count + 3] = own
+
+
+def speed_ratios(m, n, count, got):
+    return pl.pallas_call(
+        functools.partial(ratio_kernel, m, n),
+        out_shape=jax.ShapeDtypeStruct((count + 4, TILE, LANES), F32),
+        in_specs=[VMEM],
+        out_specs=VMEM,
+        cost_estimate=pl.CostEstimate(flops=RATIO_FLOPS, transcendentals=0, bytes_accessed=0),
+        compiler_params=PARAMS,
+        name="speed_ratios",
+    )(got)
+
+
 def final_kernel(
-    m, n, got_ref, near_corner_ref, rest_ref, f_ref, drift_ref, near_ref, far_ref, start_ref, end_ref,
+    m, scale_ref, near_corner_ref, rest_ref, f_ref, drift_ref, near_ref, far_ref, start_ref, end_ref,
     strip_ref, tail_ref, lead_ref, ratio_out, res_out, grad_out, ratio_ref, resid, grad, outer, rim, head_ref, sem,
 ):
     halo = Halo(m, near_ref, far_ref, start_ref, end_ref, rest_ref)
     count, rows, cols = f_ref.shape
     tiles = rows // TILE
-    path = lax.axis_index("path")
     first, last = halo.first, halo.last
-    path_lo = jnp.where(first, path, path - 1)
-    path_hi = jnp.where(last, path, path + 1)
-
-    def gathered(p):
-        total = got_ref[p, :, 0:LANES]
-        for i in range(1, n):
-            total += got_ref[i * m + p, :, 0:LANES]
-        return jnp.broadcast_to(total, (TILE, LANES))
-
-    mine = gathered(path)
-    lower = gathered(path_lo)
-    upper = gathered(path_hi)
-    lane = iota((TILE, LANES), 1)
-    sub = iota((TILE, LANES), 0)
-
-    def shift(x, k):
-        return pltpu.roll(x, k % LANES, 1)
-
-    def ratios(x):
-        return jnp.sqrt(x + EPS) / jnp.sqrt(shift(x, -count) + EPS)
-
-    low = jnp.where(first, 0.0, shift(ratios(lower), 1 - count))
-    high = jnp.where(last, 0.0, shift(ratios(upper), count + 1))
-    own = ratios(mine)
-    ratio_ref[...] = own[0, 0:count]
+    ratio_ref[...] = scale_ref[count + 3][0, 0:count]
     copies = [pltpu.make_async_copy(ratio_ref, ratio_out, sem.at[2, 0])]
     copies[0].start()
-    ratio = jnp.where(lane == 0, low, jnp.where(lane == count + 1, high, shift(own, 1)))
-
-    def splat(t):
-        return jnp.broadcast_to(jnp.sum(jnp.where(lane == t, ratio, 0.0), axis=1, keepdims=True), (TILE, LANES))
 
     def widen(x):
         return jnp.concatenate([x] * (cols // LANES), axis=1)
 
-    scale = [widen(splat(t)) for t in range(count + 2)]
-    column = jnp.sum(jnp.where(lane == sub + 1, ratio, 0.0), axis=1, keepdims=True)
+    scale = [widen(scale_ref[t]) for t in range(count + 2)]
+    column = widen(scale_ref[count + 2])
     row = iota((TILE, cols), 0)
     near, far = near_corner_ref[...], rest_ref[rows : rows + 1, :]
     corners = (
@@ -364,11 +388,11 @@
         copy.wait()
 
 
-def final(m, n, got, corners, f, drift, slabs, strips):
+def final(m, scale, corners, f, drift, slabs, strips):
     count, rows, cols = f.shape
     big = jax.ShapeDtypeStruct(f.shape, F32)
     return pl.pallas_call(
-        functools.partial(final_kernel, m, n),
+        functools.partial(final_kernel, m),
         out_shape=(jax.ShapeDtypeStruct((count,), F32), big, big),
         in_specs=[VMEM] * 12,
         out_specs=(ANY, ANY, ANY),
@@ -383,7 +407,7 @@
         ],
         compiler_params=PARAMS,
         name="final",
-    )(got, *corners, f, drift, *slabs, *strips)
+    )(scale, *corners, f, drift, *slabs, *strips)
 
 
 def swap(x, kind):
@@ -407,7 +431,8 @@
     got = lax.all_to_all(send, ("space", "path"), 0, 0, tiled=True)
     lead = ring(head, -1)
     late = swap(near_corner, 0), swap(rest, 1)
-    return final(m, n, got, late, f, drift, slabs, (strip, tail, lead))
+    scale = speed_ratios(m, n, f.shape[0], got)
+    return final(m, scale, late, f, drift, slabs, (strip, tail, lead))
 
 
 def solution(mesh):

time: 26.3 us -> 26 us (0.989)
  waiting for transfers between devices: 6.87 us -> 6.45 us
    all_to_all x1, waiting for transfers between devices: 0.74 us -> 2.29 us  [body(): got = lax.all_to_all(send, ('space', 'path'), 0, 0, tiled=True)]
    ppermute x4, waiting for transfers between devices: 1.17 us -> 0.01 us  [swap(): lax.ppermute(x, 'path', [((i + kind) % size, ((i ^ 1) + kind) % size) for...]
    ppermute x2, waiting for transfers between devices: 4.96 us -> 4.15 us  [ring(): lax.ppermute(x, 'space', [(i, (i + step) % size) for i in range(size)])]
    ppermute x4, starting transfers between devices: 3.21 us -> 3.52 us  [swap(): lax.ppermute(x, 'path', [((i + kind) % size, ((i ^ 1) + kind) % size) for...]
    pallas_call x1 -> x2, Pallas kernels: 2.24 us -> 2.25 us  [the longest x1 2.01 us: final(): pl.pallas_call(functools.partial(final_kernel, m), out_shape=(jax.ShapeDt...]
  transfers between devices with their start and end apart: 7 -> 7, of which waited for: 4 -> 2; matrix products, arithmetic and copies ran while one was open for 0% -> 0% of each run, Pallas kernels for 5% -> 6%
where the time goes in v15:
time: 26 us; the launch traced here: 25.8 us
  starting transfers between devices  12.9 us (50%)
  waiting for transfers between devices  6.45 us (25%)
  Pallas kernels  4.49 us (17%)
  local copies, waits for them, and re-layouts  1.23 us (5%)
  between operations  0.71 us (3%)
    ppermute x2, starting transfers between devices, ring(): lax.ppermute(x, 'space', [(i, (i + step) % size) for i in range(size)])  6.04 us
    ppermute x2, waiting for transfers between devices, ring(): lax.ppermute(x, 'space', [(i, (i + step) % size) for i in range(size)])  4.15 us
    ppermute x4, starting transfers between devices, swap(): lax.ppermute(x, 'path', [((i + kind) % size, ((i ^ 1) + kind) % size) for...  3.52 us
    all_to_all x1, starting transfers between devices, body(): got = lax.all_to_all(send, ('space', 'path'), 0, 0, tiled=True)  3.39 us
    all_to_all x1, waiting for transfers between devices, body(): got = lax.all_to_all(send, ('space', 'path'), 0, 0, tiled=True)  2.29 us
    pallas_call x1, Pallas kernels, final(): pl.pallas_call(functools.partial(final_kernel, m), out_shape=(jax.ShapeDt...  2.01 us
    pallas_call x1, Pallas kernels, interior(): pl.pallas_call(interior_kernel, out_shape=(jax.ShapeDtypeStruct((2 * coun...  1.38 us
    unnamed x8, local copies, waits for them, and re-layouts  1.23 us
  transfers between devices with their start and end apart: 7, of which 2 were waited for; matrix products, arithmetic and copies ran while one was open for 0% of the time, Pallas kernels for 6%

profile of v15, /device:TPU:0, one launch (start us, length us, event | category | flops | bytes accessed | tf_op | source)
XLA Modules:
  0.0 25.8 jit_solution(17145601400218851210)
XLA Ops:
  0.6 0.0 copy-start
  0.6 1.2 %copy-done = f32[8,32,1024]{2,1,0:T(8,128)S(1)} copy-done((f32[8,32,1024]{2,1,0:T(8,128)S(1)}, f32[8,32,1024]{2,1,0:T(8,128)}, u32[]{:S(2)}) %copy-start) | copy-done | bytes 1048600
  1.9 0.0 copy-start.2
  1.9 0.0 copy-start.3
  1.9 0.5 %collective-permute-start = (f32[2,32,1024]{2,1,0:T(8,128)S(1)}, f32[2,32,1024]{2,1,0:T(8,128)S(1)}, u32[]{:S(2)}, u32[]{:S(2)}) collective-permute-start(f32[2,32,1024]{2,1,0:T(8,128)S(1)} %get-tuple-element.15), channel_id=1, source_target_pairs={{0,1},{1,0},{2,3},{3,2},{4,5},{5,4},{6,7},{7,6},{8,9},{9,8},{10,11... | collective-permute-start | bytes 786440 | tf_op jit(solution)/shard_map/ppermute | solution.py:415
  2.4 2.6 %collective-permute-start.1 = (f32[32,1024]{1,0:T(8,128)S(1)}, f32[32,1024]{1,0:T(8,128)S(1)}, u32[]{:S(2)}, u32[]{:S(2)}) collective-permute-start(f32[32,1024]{1,0:T(8,128)S(1)} %get-tuple-element.16), channel_id=1, source_target_pairs={{1,2},{2,1},{3,0},{0,3},{5,6},{6,5},{7,4},{4,7},{9,10},{10,9},{11,... | collective-permute-start | bytes 393224 | tf_op jit(solution)/shard_map/ppermute | solution.py:415
  5.0 0.0 copy-done.2
  5.0 0.0 copy-done.3
  5.1 1.6 %collective-permute-start.2 = (f32[9,2,1024]{2,1,0:T(2,128)S(1)}, f32[9,2,1024]{2,1,0:T(2,128)S(1)}, u32[]{:S(2)}, u32[]{:S(2)}) collective-permute-start(f32[9,2,1024]{2,1,0:T(2,128)S(1)} %tail_rows.1), channel_id=1, source_target_pairs={{0,4},{4,8},{8,12},{12,16},{16,20},{20,24},{24,28},{28,0},{1,5},{5... | collective-permute-start | bytes 221192 | tf_op jit(solution)/shard_map/ppermute | solution.py:420
  6.6 1.4 %interior.1 = (f32[16,128]{1,0:T(8,128)S(1)}, f32[8,32,1024]{2,1,0:T(8,128)S(1)}, f32[2,8,1024]{2,1,0:T(8,128)S(1)}) custom-call(f32[8,32,1024]{2,1,0:T(8,128)S(1)} %copy-done), custom_call_target="tpu_custom_call" | custom-call | flops 5242880 | bytes 2097152 | tf_op jit(solution)/shard_map/interior/pallas_call | solution.py:148
  8.0 4.2 %collective-permute-done.2.strip_ref = f32[9,2,1024]{2,1,0:T(2,128)S(1)} collective-permute-done((f32[9,2,1024]{2,1,0:T(2,128)S(1)}, f32[9,2,1024]{2,1,0:T(2,128)S(1)}, u32[]{:S(2)}, u32[]{:S(2)}) %collective-permute-start.2) | collective-permute-done | bytes 73760 | tf_op jit(solution)/shard_map/ppermute | solution.py:420
  12.2 0.0 collective-permute-done.1.far_ref
  12.2 0.0 collective-permute-done.near_ref
  12.2 0.8 %chunks.1 = (f32[32,1,128]{2,1,0:T(1,128)}, f32[1,1024]{1,0:T(1,128)S(1)}, f32[40,1024]{1,0:T(8,128)S(1)}, f32[2,8,1024]{2,1,0:T(8,128)S(1)}, f32[9,2,1024]{2,1,0:T(2,128)S(1)}) custom-call(f32[8,32,1024]{2,1,0:T(8,128)S(1)} %copy-done, f32[16,128]{1,0:T(8,128)S(1)} %get-tuple-element.13.part_ref, f32[2,8,1024]{2,1,0:T(8,128)S(1)} %get-tuple-element.14.rim_ref, ...), custom_call_target="tpu_custom_call" | custom-call | tf_op jit(solution)/shard_map/chunks/pallas_call | solution.py:214
  13.0 0.1 collective-permute-start.4
  13.1 3.4 %all-to-all-start = ((f32[32,1,128]{2,1,0:T(1,128)}), f32[32,1,128]{2,1,0:T(1,128)S(1)}, u32[]{:S(2)}, u32[]{:S(2)}) async-start(f32[32,1,128]{2,1,0:T(1,128)} %get-tuple-element.17), calls=%async_computation | async-start | bytes 32768 | tf_op jit(solution)/shard_map/all_to_all | solution.py:431
  16.5 0.3 %collective-permute-start.3 = (f32[1,1024]{1,0:T(1,128)S(1)}, f32[1,1024]{1,0:T(1,128)S(1)}, u32[]{:S(2)}, u32[]{:S(2)}) collective-permute-start(f32[1,1024]{1,0:T(1,128)S(1)} %get-tuple-element.18), channel_id=1, source_target_pairs={{0,1},{1,0},{2,3},{3,2},{4,5},{5,4},{6,7},{7,6},{8,9},{9,8},{10,11... | collective-permute-start | bytes 12296 | tf_op jit(solution)/shard_map/ppermute | solution.py:415
  16.8 0.0 copy-start.1
  16.8 4.5 %collective-permute-start.5 = (f32[9,2,1024]{2,1,0:T(2,128)S(1)}, f32[9,2,1024]{2,1,0:T(2,128)S(1)}, u32[]{:S(2)}, u32[]{:S(2)}) collective-permute-start(f32[9,2,1024]{2,1,0:T(2,128)S(1)} %get-tuple-element.22), channel_id=1, source_target_pairs={{0,28},{4,0},{8,4},{12,8},{16,12},{20,16},{24,20},{28,24},{1,29},{... | collective-permute-start | bytes 221192 | tf_op jit(solution)/shard_map/ppermute | solution.py:420
  21.2 2.3 %all-to-all-done.got_ref = f32[32,1,128]{2,1,0:T(1,128)S(1)} async-done(((f32[32,1,128]{2,1,0:T(1,128)}), f32[32,1,128]{2,1,0:T(1,128)S(1)}, u32[]{:S(2)}, u32[]{:S(2)}) %all-to-all-start) | async-done | bytes 16416 | tf_op jit(solution)/shard_map/all_to_all | solution.py:431
  23.5 0.2 speed_ratios.1.scale_ref
  23.8 0.0 collective-permute-done.3.near_corner_ref
  23.8 0.0 collective-permute-done.5.lead_ref
  23.8 0.0 collective-permute-done.4.rest_ref
  23.8 0.0 copy-done.1
  23.8 2.0 %final.1 = (f32[8]{0:T(128)}, f32[8,32,1024]{2,1,0:T(8,128)}, f32[8,32,1024]{2,1,0:T(8,128)}) custom-call(f32[12,8,128]{2,1,0:T(8,128)S(1)} %speed_ratios.1.scale_ref, f32[1,1024]{1,0:T(1,128)S(1)} %collective-permute-done.3.near_corner_ref, f32[40,1024]{1,0:T(8,128)S(1)} %collective-permute-done.4.rest_ref, f32[8,32,1024]{2,1,0:T(8,128)S(1)} %copy-done.1, ...), custom_call_target="tpu_custom_call" | custom-call | tf_op jit(solution)/shard_map/final/pallas_call | solution.py:394
  (2 shorter events, 0.0 us)
Async XLA Ops:
  0.6 1.2 %copy-start = (f32[8,32,1024]{2,1,0:T(8,128)S(1)}, f32[8,32,1024]{2,1,0:T(8,128)}, u32[]{:S(2)}) copy-start(f32[8,32,1024]{2,1,0:T(8,128)} %f_ref.9) | copy-start | bytes 3145732
  1.9 3.2 %copy-start.2 = (f32[32,1024]{1,0:T(8,128)S(1)}, f32[32,1024]{1,0:T(8,128)}, u32[]{:S(2)}) copy-start(f32[32,1024]{1,0:T(8,128)} %start_ref.5) | copy-start | bytes 393220
  1.9 3.2 %copy-start.3 = (f32[32,1024]{1,0:T(8,128)S(1)}, f32[32,1024]{1,0:T(8,128)}, u32[]{:S(2)}) copy-start(f32[32,1024]{1,0:T(8,128)} %end_ref.5) | copy-start | bytes 393220
  1.9 10.3 %collective-permute-start = (f32[2,32,1024]{2,1,0:T(8,128)S(1)}, f32[2,32,1024]{2,1,0:T(8,128)S(1)}, u32[]{:S(2)}, u32[]{:S(2)}) collective-permute-start(f32[2,32,1024]{2,1,0:T(8,128)S(1)} %get-tuple-element.15), channel_id=1, source_target_pairs={{0,1},{1,0},{2,3},{3,2},{4,5},{5,4},{6,7},{7,6},{8,9},{9,8},{10,11... | collective-permute-start | bytes 786440 | tf_op jit(solution)/shard_map/ppermute | solution.py:415
  2.4 9.8 %collective-permute-start.1 = (f32[32,1024]{1,0:T(8,128)S(1)}, f32[32,1024]{1,0:T(8,128)S(1)}, u32[]{:S(2)}, u32[]{:S(2)}) collective-permute-start(f32[32,1024]{1,0:T(8,128)S(1)} %get-tuple-element.16), channel_id=1, source_target_pairs={{1,2},{2,1},{3,0},{0,3},{5,6},{6,5},{7,4},{4,7},{9,10},{10,9},{11,... | collective-permute-start | bytes 393224 | tf_op jit(solution)/shard_map/ppermute | solution.py:415
  5.1 7.1 %collective-permute-start.2 = (f32[9,2,1024]{2,1,0:T(2,128)S(1)}, f32[9,2,1024]{2,1,0:T(2,128)S(1)}, u32[]{:S(2)}, u32[]{:S(2)}) collective-permute-start(f32[9,2,1024]{2,1,0:T(2,128)S(1)} %tail_rows.1), channel_id=1, source_target_pairs={{0,4},{4,8},{8,12},{12,16},{16,20},{20,24},{24,28},{28,0},{1,5},{5... | collective-permute-start | bytes 221192 | tf_op jit(solution)/shard_map/ppermute | solution.py:420
  13.0 10.8 %collective-permute-start.4 = (f32[40,1024]{1,0:T(8,128)S(1)}, f32[40,1024]{1,0:T(8,128)S(1)}, u32[]{:S(2)}, u32[]{:S(2)}) collective-permute-start(f32[40,1024]{1,0:T(8,128)S(1)} %get-tuple-element.19), channel_id=1, source_target_pairs={{1,2},{2,1},{3,0},{0,3},{5,6},{6,5},{7,4},{4,7},{9,10},{10,9},{11,... | collective-permute-start | bytes 491528 | tf_op jit(solution)/shard_map/ppermute | solution.py:415
  13.1 10.5 %all-to-all-start = ((f32[32,1,128]{2,1,0:T(1,128)}), f32[32,1,128]{2,1,0:T(1,128)S(1)}, u32[]{:S(2)}, u32[]{:S(2)}) async-start(f32[32,1,128]{2,1,0:T(1,128)} %get-tuple-element.17), calls=%async_computation | async-start | bytes 32768 | tf_op jit(solution)/shard_map/all_to_all | solution.py:431
  16.5 7.3 %collective-permute-start.3 = (f32[1,1024]{1,0:T(1,128)S(1)}, f32[1,1024]{1,0:T(1,128)S(1)}, u32[]{:S(2)}, u32[]{:S(2)}) collective-permute-start(f32[1,1024]{1,0:T(1,128)S(1)} %get-tuple-element.18), channel_id=1, source_target_pairs={{0,1},{1,0},{2,3},{3,2},{4,5},{5,4},{6,7},{7,6},{8,9},{9,8},{10,11... | collective-permute-start | bytes 12296 | tf_op jit(solution)/shard_map/ppermute | solution.py:415
  16.8 7.0 %copy-start.1 = (f32[8,32,1024]{2,1,0:T(8,128)S(1)}, f32[8,32,1024]{2,1,0:T(8,128)}, u32[]{:S(2)}) copy-start(f32[8,32,1024]{2,1,0:T(8,128)} %f_ref.9) | copy-start | bytes 3145732
  16.8 7.0 %collective-permute-start.5 = (f32[9,2,1024]{2,1,0:T(2,128)S(1)}, f32[9,2,1024]{2,1,0:T(2,128)S(1)}, u32[]{:S(2)}, u32[]{:S(2)}) collective-permute-start(f32[9,2,1024]{2,1,0:T(2,128)S(1)} %get-tuple-element.22), channel_id=1, source_target_pairs={{0,28},{4,0},{8,4},{12,8},{16,12},{20,16},{24,20},{28,24},{1,29},{... | collective-permute-start | bytes 221192 | tf_op jit(solution)/shard_map/ppermute | solution.py:420

commit v16 on v15

--- a/solution.py
+++ b/solution.py
@@ -160,8 +160,31 @@
     )(f)
 
 
+def ends_kernel(m, f_ref, near_ref, far_ref, start_ref, end_ref, ends_ref):
+    halo = Halo(m, near_ref, far_ref, start_ref, end_ref)
+    count, rows, _ = f_ref.shape
+    totals = [jnp.zeros((TILE, LANES), F32) for _ in range(2)]
+    for k in range(rows // TILE):
+        at = pl.ds(TILE * k, TILE)
+        tangents = (f_ref[1, at, :] - halo.below(at), halo.above(at) - f_ref[count - 2, at, :])
+        totals = [a + lanes_sum(t * t) for a, t in zip(totals, tangents)]
+    for i, total in enumerate(totals):
+        ends_ref[i : i + 1, :] = jnp.sum(total, axis=0, keepdims=True)
+
+
+def ends(m, f, near, far, start, end):
+    return pl.pallas_call(
+        functools.partial(ends_kernel, m),
+        out_shape=jax.ShapeDtypeStruct((2, LANES), F32),
+        in_specs=[VMEM] * 5,
+        out_specs=VMEM,
+        compiler_params=PARAMS,
+        name="ends",
+    )(f, near, far, start, end)
+
+
 def chunk_kernel(
-    m, n, f_ref, part_ref, rim_ref, near_ref, far_ref, start_ref, end_ref, strip_ref,
+    m, n, f_ref, part_ref, ends_ref, rim_ref, near_ref, far_ref, start_ref, end_ref, strip_ref,
     out_ref, near_corner_ref, rest_ref, tail_ref, head_ref, lines, sem,
 ):
     halo = Halo(m, near_ref, far_ref, start_ref, end_ref)
@@ -177,15 +200,9 @@
     drift_b = rim_ref[0] + r1
     drift = part_ref[0:count, :] + lanes_sum(drift_a * drift_a) + lanes_sum(drift_b * drift_b)
 
-    totals = [jnp.zeros((TILE, LANES), F32) for _ in range(2)]
-    for k in range(tiles):
-        at = pl.ds(TILE * k, TILE)
-        tangents = (f_ref[1, at, :] - halo.below(at), halo.above(at) - f_ref[count - 2, at, :])
-        totals = [a + lanes_sum(t * t) for a, t in zip(totals, tangents)]
-    head_sum, tail_sum = [jnp.sum(a, axis=0, keepdims=True) for a in totals]
     sub = iota((TILE, LANES), 0)
     tangent = part_ref[count : 2 * count, :]
-    tangent = jnp.where(sub == 0, head_sum, jnp.where(sub == count - 1, tail_sum, tangent))
+    tangent = jnp.where(sub == 0, ends_ref[0:1, :], jnp.where(sub == count - 1, ends_ref[1:2, :], tangent))
 
     lane = iota((TILE, LANES), 1)
     spread = jnp.where(lane == sub, jnp.sum(drift, axis=1, keepdims=True), 0.0)
@@ -209,7 +226,7 @@
     copy.wait()
 
 
-def chunks(m, n, f, part, rim, near, far, start, end, strip):
+def chunks(m, n, f, part, sums, rim, near, far, start, end, strip):
     count, rows, cols = f.shape
     return pl.pallas_call(
         functools.partial(chunk_kernel, m, n),
@@ -220,12 +237,12 @@
             jax.ShapeDtypeStruct((2, count, cols), F32),
             jax.ShapeDtypeStruct((count + 1, 2, cols), F32),
         ),
-        in_specs=[VMEM] * 8,
+        in_specs=[VMEM] * 9,
         out_specs=[ANY] + [VMEM] * 4,
         scratch_shapes=[pltpu.VMEM((m * n, 1, WIDTH), F32), pltpu.SemaphoreType.DMA],
         compiler_params=PARAMS,
         name="chunks",
-    )(f, part, rim, near, far, start, end, strip)
+    )(f, part, sums, rim, near, far, start, end, strip)
 
 
 def ratio_kernel(m, n, got_ref, scale_ref):
@@ -427,7 +444,7 @@
     near = swap(near, 0)
     part, drift, rim = interior(f)
     slabs = near, far, start, end
-    send, near_corner, rest, tail, head = chunks(m, n, f, part, rim, *slabs, strip)
+    send, near_corner, rest, tail, head = chunks(m, n, f, part, ends(m, f, *slabs), rim, *slabs, strip)
     got = lax.all_to_all(send, ("space", "path"), 0, 0, tiled=True)
     lead = ring(head, -1)
     late = swap(near_corner, 0), swap(rest, 1)

time: 26 us -> 26 us (level)
    ppermute x2, waiting for transfers between devices: 4.15 us -> 3.29 us  [ring(): lax.ppermute(x, 'space', [(i, (i + step) % size) for i in range(size)])]
    ppermute x4, waiting for transfers between devices: 0.01 us -> 0.8 us  [swap(): lax.ppermute(x, 'path', [((i + kind) % size, ((i ^ 1) + kind) % size) for...]
  transfers between devices with their start and end apart: 7 -> 7, of which waited for: 2 -> 3; matrix products, arithmetic and copies ran while one was open for 0% -> 0% of each run, Pallas kernels for 6% -> 7%
where the time goes in v16:
time: 26 us; the launch traced here: 25.8 us
  starting transfers between devices  12.9 us (50%)
  waiting for transfers between devices  6.38 us (25%)
  Pallas kernels  4.55 us (18%)
  local copies, waits for them, and re-layouts  1.23 us (5%)
  between operations  0.72 us (3%)
    ppermute x2, starting transfers between devices, ring(): lax.ppermute(x, 'space', [(i, (i + step) % size) for i in range(size)])  6.04 us
    ppermute x4, starting transfers between devices, swap(): lax.ppermute(x, 'path', [((i + kind) % size, ((i ^ 1) + kind) % size) for...  3.52 us
    all_to_all x1, starting transfers between devices, body(): got = lax.all_to_all(send, ('space', 'path'), 0, 0, tiled=True)  3.39 us
    ppermute x2, waiting for transfers between devices, ring(): lax.ppermute(x, 'space', [(i, (i + step) % size) for i in range(size)])  3.29 us
    all_to_all x1, waiting for transfers between devices, body(): got = lax.all_to_all(send, ('space', 'path'), 0, 0, tiled=True)  2.29 us
    pallas_call x1, Pallas kernels, final(): pl.pallas_call(functools.partial(final_kernel, m), out_shape=(jax.ShapeDt...  2.01 us
    pallas_call x1, Pallas kernels, interior(): pl.pallas_call(interior_kernel, out_shape=(jax.ShapeDtypeStruct((2 * coun...  1.38 us
    unnamed x8, local copies, waits for them, and re-layouts  1.23 us
  transfers between devices with their start and end apart: 7, of which 3 were waited for; matrix products, arithmetic and copies ran while one was open for 0% of the time, Pallas kernels for 7%

profile of v16, /device:TPU:0, one launch (start us, length us, event | category | flops | bytes accessed | tf_op | source)
XLA Modules:
  0.0 25.8 jit_solution(2759831397158102754)
XLA Ops:
  0.6 0.0 copy-start
  0.6 1.2 %copy-done = f32[8,32,1024]{2,1,0:T(8,128)S(1)} copy-done((f32[8,32,1024]{2,1,0:T(8,128)S(1)}, f32[8,32,1024]{2,1,0:T(8,128)}, u32[]{:S(2)}) %copy-start) | copy-done | bytes 1048600
  1.9 0.0 copy-start.2
  1.9 0.0 copy-start.3
  1.9 0.5 %collective-permute-start = (f32[2,32,1024]{2,1,0:T(8,128)S(1)}, f32[2,32,1024]{2,1,0:T(8,128)S(1)}, u32[]{:S(2)}, u32[]{:S(2)}) collective-permute-start(f32[2,32,1024]{2,1,0:T(8,128)S(1)} %get-tuple-element.14), channel_id=1, source_target_pairs={{0,1},{1,0},{2,3},{3,2},{4,5},{5,4},{6,7},{7,6},{8,9},{9,8},{10,11... | collective-permute-start | bytes 786440 | tf_op jit(solution)/shard_map/ppermute | solution.py:432
  2.4 2.6 %collective-permute-start.1 = (f32[32,1024]{1,0:T(8,128)S(1)}, f32[32,1024]{1,0:T(8,128)S(1)}, u32[]{:S(2)}, u32[]{:S(2)}) collective-permute-start(f32[32,1024]{1,0:T(8,128)S(1)} %get-tuple-element.15), channel_id=1, source_target_pairs={{1,2},{2,1},{3,0},{0,3},{5,6},{6,5},{7,4},{4,7},{9,10},{10,9},{11,... | collective-permute-start | bytes 393224 | tf_op jit(solution)/shard_map/ppermute | solution.py:432
  5.0 0.0 copy-done.2
  5.0 0.0 copy-done.3
  5.1 1.6 %collective-permute-start.2 = (f32[9,2,1024]{2,1,0:T(2,128)S(1)}, f32[9,2,1024]{2,1,0:T(2,128)S(1)}, u32[]{:S(2)}, u32[]{:S(2)}) collective-permute-start(f32[9,2,1024]{2,1,0:T(2,128)S(1)} %tail_rows.1), channel_id=1, source_target_pairs={{0,4},{4,8},{8,12},{12,16},{16,20},{20,24},{24,28},{28,0},{1,5},{5... | collective-permute-start | bytes 221192 | tf_op jit(solution)/shard_map/ppermute | solution.py:437
  6.6 1.4 %interior.1 = (f32[16,128]{1,0:T(8,128)S(1)}, f32[8,32,1024]{2,1,0:T(8,128)S(1)}, f32[2,8,1024]{2,1,0:T(8,128)S(1)}) custom-call(f32[8,32,1024]{2,1,0:T(8,128)S(1)} %copy-done), custom_call_target="tpu_custom_call" | custom-call | flops 5242880 | bytes 2097152 | tf_op jit(solution)/shard_map/interior/pallas_call | solution.py:148
  8.0 0.8 %collective-permute-done.1.far_ref = f32[32,1024]{1,0:T(8,128)S(1)} collective-permute-done((f32[32,1024]{1,0:T(8,128)S(1)}, f32[32,1024]{1,0:T(8,128)S(1)}, u32[]{:S(2)}, u32[]{:S(2)}) %collective-permute-start.1) | collective-permute-done | bytes 131104 | tf_op jit(solution)/shard_map/ppermute | solution.py:432
  8.8 0.0 collective-permute-done.near_ref
  8.8 0.1 ends.1.ends_ref
  8.9 3.3 %collective-permute-done.2.strip_ref = f32[9,2,1024]{2,1,0:T(2,128)S(1)} collective-permute-done((f32[9,2,1024]{2,1,0:T(2,128)S(1)}, f32[9,2,1024]{2,1,0:T(2,128)S(1)}, u32[]{:S(2)}, u32[]{:S(2)}) %collective-permute-start.2) | collective-permute-done | bytes 73760 | tf_op jit(solution)/shard_map/ppermute | solution.py:437
  12.2 0.8 %chunks.1 = (f32[32,1,128]{2,1,0:T(1,128)}, f32[1,1024]{1,0:T(1,128)S(1)}, f32[40,1024]{1,0:T(8,128)S(1)}, f32[2,8,1024]{2,1,0:T(8,128)S(1)}, f32[9,2,1024]{2,1,0:T(2,128)S(1)}) custom-call(f32[8,32,1024]{2,1,0:T(8,128)S(1)} %copy-done, f32[16,128]{1,0:T(8,128)S(1)} %get-tuple-element.13.part_ref, f32[2,128]{1,0:T(2,128)S(1)} %ends.1.ends_ref, ...), custom_call_target="tpu_custom_call" | custom-call | tf_op jit(solution)/shard_map/chunks/pallas_call | solution.py:231
  13.0 0.1 collective-permute-start.4
  13.1 3.4 %all-to-all-start = ((f32[32,1,128]{2,1,0:T(1,128)}), f32[32,1,128]{2,1,0:T(1,128)S(1)}, u32[]{:S(2)}, u32[]{:S(2)}) async-start(f32[32,1,128]{2,1,0:T(1,128)} %get-tuple-element.17), calls=%async_computation | async-start | bytes 32768 | tf_op jit(solution)/shard_map/all_to_all | solution.py:448
  16.5 0.3 %collective-permute-start.3 = (f32[1,1024]{1,0:T(1,128)S(1)}, f32[1,1024]{1,0:T(1,128)S(1)}, u32[]{:S(2)}, u32[]{:S(2)}) collective-permute-start(f32[1,1024]{1,0:T(1,128)S(1)} %get-tuple-element.18), channel_id=1, source_target_pairs={{0,1},{1,0},{2,3},{3,2},{4,5},{5,4},{6,7},{7,6},{8,9},{9,8},{10,11... | collective-permute-start | bytes 12296 | tf_op jit(solution)/shard_map/ppermute | solution.py:432
  16.8 0.0 copy-start.1
  16.8 4.5 %collective-permute-start.5 = (f32[9,2,1024]{2,1,0:T(2,128)S(1)}, f32[9,2,1024]{2,1,0:T(2,128)S(1)}, u32[]{:S(2)}, u32[]{:S(2)}) collective-permute-start(f32[9,2,1024]{2,1,0:T(2,128)S(1)} %get-tuple-element.22), channel_id=1, source_target_pairs={{0,28},{4,0},{8,4},{12,8},{16,12},{20,16},{24,20},{28,24},{1,29},{... | collective-permute-start | bytes 221192 | tf_op jit(solution)/shard_map/ppermute | solution.py:437
  21.2 2.3 %all-to-all-done.got_ref = f32[32,1,128]{2,1,0:T(1,128)S(1)} async-done(((f32[32,1,128]{2,1,0:T(1,128)}), f32[32,1,128]{2,1,0:T(1,128)S(1)}, u32[]{:S(2)}, u32[]{:S(2)}) %all-to-all-start) | async-done | bytes 16416 | tf_op jit(solution)/shard_map/all_to_all | solution.py:448
  23.5 0.2 speed_ratios.1.scale_ref
  23.8 0.0 collective-permute-done.3.near_corner_ref
  23.8 0.0 collective-permute-done.5.lead_ref
  23.8 0.0 collective-permute-done.4.rest_ref
  23.8 0.0 copy-done.1
  23.8 2.0 %final.1 = (f32[8]{0:T(128)}, f32[8,32,1024]{2,1,0:T(8,128)}, f32[8,32,1024]{2,1,0:T(8,128)}) custom-call(f32[12,8,128]{2,1,0:T(8,128)S(1)} %speed_ratios.1.scale_ref, f32[1,1024]{1,0:T(1,128)S(1)} %collective-permute-done.3.near_corner_ref, f32[40,1024]{1,0:T(8,128)S(1)} %collective-permute-done.4.rest_ref, f32[8,32,1024]{2,1,0:T(8,128)S(1)} %copy-done.1, ...), custom_call_target="tpu_custom_call" | custom-call | tf_op jit(solution)/shard_map/final/pallas_call | solution.py:411
  (2 shorter events, 0.0 us)
Async XLA Ops:
  0.6 1.2 %copy-start = (f32[8,32,1024]{2,1,0:T(8,128)S(1)}, f32[8,32,1024]{2,1,0:T(8,128)}, u32[]{:S(2)}) copy-start(f32[8,32,1024]{2,1,0:T(8,128)} %f_ref.11) | copy-start | bytes 3145732
  1.9 3.2 %copy-start.2 = (f32[32,1024]{1,0:T(8,128)S(1)}, f32[32,1024]{1,0:T(8,128)}, u32[]{:S(2)}) copy-start(f32[32,1024]{1,0:T(8,128)} %start_ref.7) | copy-start | bytes 393220
  1.9 3.2 %copy-start.3 = (f32[32,1024]{1,0:T(8,128)S(1)}, f32[32,1024]{1,0:T(8,128)}, u32[]{:S(2)}) copy-start(f32[32,1024]{1,0:T(8,128)} %end_ref.7) | copy-start | bytes 393220
  1.9 6.9 %collective-permute-start = (f32[2,32,1024]{2,1,0:T(8,128)S(1)}, f32[2,32,1024]{2,1,0:T(8,128)S(1)}, u32[]{:S(2)}, u32[]{:S(2)}) collective-permute-start(f32[2,32,1024]{2,1,0:T(8,128)S(1)} %get-tuple-element.14), channel_id=1, source_target_pairs={{0,1},{1,0},{2,3},{3,2},{4,5},{5,4},{6,7},{7,6},{8,9},{9,8},{10,11... | collective-permute-start | bytes 786440 | tf_op jit(solution)/shard_map/ppermute | solution.py:432
  2.4 6.4 %collective-permute-start.1 = (f32[32,1024]{1,0:T(8,128)S(1)}, f32[32,1024]{1,0:T(8,128)S(1)}, u32[]{:S(2)}, u32[]{:S(2)}) collective-permute-start(f32[32,1024]{1,0:T(8,128)S(1)} %get-tuple-element.15), channel_id=1, source_target_pairs={{1,2},{2,1},{3,0},{0,3},{5,6},{6,5},{7,4},{4,7},{9,10},{10,9},{11,... | collective-permute-start | bytes 393224 | tf_op jit(solution)/shard_map/ppermute | solution.py:432
  5.1 7.1 %collective-permute-start.2 = (f32[9,2,1024]{2,1,0:T(2,128)S(1)}, f32[9,2,1024]{2,1,0:T(2,128)S(1)}, u32[]{:S(2)}, u32[]{:S(2)}) collective-permute-start(f32[9,2,1024]{2,1,0:T(2,128)S(1)} %tail_rows.1), channel_id=1, source_target_pairs={{0,4},{4,8},{8,12},{12,16},{16,20},{20,24},{24,28},{28,0},{1,5},{5... | collective-permute-start | bytes 221192 | tf_op jit(solution)/shard_map/ppermute | solution.py:437
  13.0 10.8 %collective-permute-start.4 = (f32[40,1024]{1,0:T(8,128)S(1)}, f32[40,1024]{1,0:T(8,128)S(1)}, u32[]{:S(2)}, u32[]{:S(2)}) collective-permute-start(f32[40,1024]{1,0:T(8,128)S(1)} %get-tuple-element.19), channel_id=1, source_target_pairs={{1,2},{2,1},{3,0},{0,3},{5,6},{6,5},{7,4},{4,7},{9,10},{10,9},{11,... | collective-permute-start | bytes 491528 | tf_op jit(solution)/shard_map/ppermute | solution.py:432
  13.1 10.5 %all-to-all-start = ((f32[32,1,128]{2,1,0:T(1,128)}), f32[32,1,128]{2,1,0:T(1,128)S(1)}, u32[]{:S(2)}, u32[]{:S(2)}) async-start(f32[32,1,128]{2,1,0:T(1,128)} %get-tuple-element.17), calls=%async_computation | async-start | bytes 32768 | tf_op jit(solution)/shard_map/all_to_all | solution.py:448
  16.5 7.3 %collective-permute-start.3 = (f32[1,1024]{1,0:T(1,128)S(1)}, f32[1,1024]{1,0:T(1,128)S(1)}, u32[]{:S(2)}, u32[]{:S(2)}) collective-permute-start(f32[1,1024]{1,0:T(1,128)S(1)} %get-tuple-element.18), channel_id=1, source_target_pairs={{0,1},{1,0},{2,3},{3,2},{4,5},{5,4},{6,7},{7,6},{8,9},{9,8},{10,11... | collective-permute-start | bytes 12296 | tf_op jit(solution)/shard_map/ppermute | solution.py:432
  16.8 7.0 %copy-start.1 = (f32[8,32,1024]{2,1,0:T(8,128)S(1)}, f32[8,32,1024]{2,1,0:T(8,128)}, u32[]{:S(2)}) copy-start(f32[8,32,1024]{2,1,0:T(8,128)} %f_ref.11) | copy-start | bytes 3145732
  16.8 7.0 %collective-permute-start.5 = (f32[9,2,1024]{2,1,0:T(2,128)S(1)}, f32[9,2,1024]{2,1,0:T(2,128)S(1)}, u32[]{:S(2)}, u32[]{:S(2)}) collective-permute-start(f32[9,2,1024]{2,1,0:T(2,128)S(1)} %get-tuple-element.22), channel_id=1, source_target_pairs={{0,28},{4,0},{8,4},{12,8},{16,12},{20,16},{24,20},{28,24},{1,29},{... | collective-permute-start | bytes 221192 | tf_op jit(solution)/shard_map/ppermute | solution.py:437

commit v17 on v15

--- a/solution.py
+++ b/solution.py
@@ -340,13 +340,14 @@
         copy.start()
         copies.append(copy)
 
-    pieces = PIECES if count % PIECES == 0 else 1
-    step = count // pieces
-    for i in range(pieces):
-        for s in range(i * step, (i + 1) * step):
+    half = count // 2
+    res_cuts = (0, half, count)
+    grad_cuts = (0, half, count - 2, count - 1, count)
+    for i, (lo, hi) in enumerate(zip(res_cuts, res_cuts[1:])):
+        for s in range(lo, hi):
             residual_of(s)
-        span = pl.ds(i * step, step)
-        send(resid.at[pl.ds(i * step + 1, step), pl.ds(TILE, rows)], res_out.at[span], sem.at[0, i])
+        span = pl.ds(lo, hi - lo)
+        send(resid.at[pl.ds(lo + 1, hi - lo), pl.ds(TILE, rows)], res_out.at[span], sem.at[0, i])
 
     for k in range(tiles):
         outer[0, at(k), :] = halo.below(at(k))
@@ -379,10 +380,10 @@
             out = scale[s] * resid[s, at(k + 1), :] - scale[s + 2] * resid[s + 2, at(k + 1), :]
             grad[s, at(k), :] = out - (around - (3.0 + 3.0 * c * c) * r[k])
 
-    for i in range(pieces):
-        for s in range(i * step, (i + 1) * step):
+    for i, (lo, hi) in enumerate(zip(grad_cuts, grad_cuts[1:])):
+        for s in range(lo, hi):
             gradient_of(s)
-        span = pl.ds(i * step, step)
+        span = pl.ds(lo, hi - lo)
         send(grad.at[span], grad_out.at[span], sem.at[1, i])
     for copy in copies:
         copy.wait()

time: 26 us -> 26 us (level)
  no operation moved by 1% of the time
where the time goes in v17:
time: 26 us; the launch traced here: 25.8 us
  starting transfers between devices  12.9 us (50%)
  waiting for transfers between devices  6.45 us (25%)
  Pallas kernels  4.45 us (17%)
  local copies, waits for them, and re-layouts  1.23 us (5%)
  between operations  0.71 us (3%)
    ppermute x2, starting transfers between devices, ring(): lax.ppermute(x, 'space', [(i, (i + step) % size) for i in range(size)])  6.04 us
    ppermute x2, waiting for transfers between devices, ring(): lax.ppermute(x, 'space', [(i, (i + step) % size) for i in range(size)])  4.15 us
    ppermute x4, starting transfers between devices, swap(): lax.ppermute(x, 'path', [((i + kind) % size, ((i ^ 1) + kind) % size) for...  3.52 us
    all_to_all x1, starting transfers between devices, body(): got = lax.all_to_all(send, ('space', 'path'), 0, 0, tiled=True)  3.39 us
    all_to_all x1, waiting for transfers between devices, body(): got = lax.all_to_all(send, ('space', 'path'), 0, 0, tiled=True)  2.29 us
    pallas_call x1, Pallas kernels, final(): pl.pallas_call(functools.partial(final_kernel, m), out_shape=(jax.ShapeDt...  1.97 us
    pallas_call x1, Pallas kernels, interior(): pl.pallas_call(interior_kernel, out_shape=(jax.ShapeDtypeStruct((2 * coun...  1.38 us
    unnamed x8, local copies, waits for them, and re-layouts  1.23 us
  transfers between devices with their start and end apart: 7, of which 2 were waited for; matrix products, arithmetic and copies ran while one was open for 0% of the time, Pallas kernels for 6%

profile of v17, /device:TPU:0, one launch (start us, length us, event | category | flops | bytes accessed | tf_op | source)
XLA Modules:
  0.0 25.8 jit_solution(12918387132360668016)
XLA Ops:
  0.6 0.0 copy-start
  0.6 1.2 %copy-done = f32[8,32,1024]{2,1,0:T(8,128)S(1)} copy-done((f32[8,32,1024]{2,1,0:T(8,128)S(1)}, f32[8,32,1024]{2,1,0:T(8,128)}, u32[]{:S(2)}) %copy-start) | copy-done | bytes 1048600
  1.9 0.0 copy-start.2
  1.9 0.0 copy-start.3
  1.9 0.5 %collective-permute-start = (f32[2,32,1024]{2,1,0:T(8,128)S(1)}, f32[2,32,1024]{2,1,0:T(8,128)S(1)}, u32[]{:S(2)}, u32[]{:S(2)}) collective-permute-start(f32[2,32,1024]{2,1,0:T(8,128)S(1)} %get-tuple-element.15), channel_id=1, source_target_pairs={{0,1},{1,0},{2,3},{3,2},{4,5},{5,4},{6,7},{7,6},{8,9},{9,8},{10,11... | collective-permute-start | bytes 786440 | tf_op jit(solution)/shard_map/ppermute | solution.py:416
  2.4 2.6 %collective-permute-start.1 = (f32[32,1024]{1,0:T(8,128)S(1)}, f32[32,1024]{1,0:T(8,128)S(1)}, u32[]{:S(2)}, u32[]{:S(2)}) collective-permute-start(f32[32,1024]{1,0:T(8,128)S(1)} %get-tuple-element.16), channel_id=1, source_target_pairs={{1,2},{2,1},{3,0},{0,3},{5,6},{6,5},{7,4},{4,7},{9,10},{10,9},{11,... | collective-permute-start | bytes 393224 | tf_op jit(solution)/shard_map/ppermute | solution.py:416
  5.0 0.0 copy-done.2
  5.0 0.0 copy-done.3
  5.1 1.6 %collective-permute-start.2 = (f32[9,2,1024]{2,1,0:T(2,128)S(1)}, f32[9,2,1024]{2,1,0:T(2,128)S(1)}, u32[]{:S(2)}, u32[]{:S(2)}) collective-permute-start(f32[9,2,1024]{2,1,0:T(2,128)S(1)} %tail_rows.1), channel_id=1, source_target_pairs={{0,4},{4,8},{8,12},{12,16},{16,20},{20,24},{24,28},{28,0},{1,5},{5... | collective-permute-start | bytes 221192 | tf_op jit(solution)/shard_map/ppermute | solution.py:421
  6.6 1.4 %interior.1 = (f32[16,128]{1,0:T(8,128)S(1)}, f32[8,32,1024]{2,1,0:T(8,128)S(1)}, f32[2,8,1024]{2,1,0:T(8,128)S(1)}) custom-call(f32[8,32,1024]{2,1,0:T(8,128)S(1)} %copy-done), custom_call_target="tpu_custom_call" | custom-call | flops 5242880 | bytes 2097152 | tf_op jit(solution)/shard_map/interior/pallas_call | solution.py:148
  8.0 4.2 %collective-permute-done.2.strip_ref = f32[9,2,1024]{2,1,0:T(2,128)S(1)} collective-permute-done((f32[9,2,1024]{2,1,0:T(2,128)S(1)}, f32[9,2,1024]{2,1,0:T(2,128)S(1)}, u32[]{:S(2)}, u32[]{:S(2)}) %collective-permute-start.2) | collective-permute-done | bytes 73760 | tf_op jit(solution)/shard_map/ppermute | solution.py:421
  12.2 0.0 collective-permute-done.1.far_ref
  12.2 0.0 collective-permute-done.near_ref
  12.2 0.8 %chunks.1 = (f32[32,1,128]{2,1,0:T(1,128)}, f32[1,1024]{1,0:T(1,128)S(1)}, f32[40,1024]{1,0:T(8,128)S(1)}, f32[2,8,1024]{2,1,0:T(8,128)S(1)}, f32[9,2,1024]{2,1,0:T(2,128)S(1)}) custom-call(f32[8,32,1024]{2,1,0:T(8,128)S(1)} %copy-done, f32[16,128]{1,0:T(8,128)S(1)} %get-tuple-element.13.part_ref, f32[2,8,1024]{2,1,0:T(8,128)S(1)} %get-tuple-element.14.rim_ref, ...), custom_call_target="tpu_custom_call" | custom-call | tf_op jit(solution)/shard_map/chunks/pallas_call | solution.py:214
  13.0 0.1 collective-permute-start.4
  13.1 3.4 %all-to-all-start = ((f32[32,1,128]{2,1,0:T(1,128)}), f32[32,1,128]{2,1,0:T(1,128)S(1)}, u32[]{:S(2)}, u32[]{:S(2)}) async-start(f32[32,1,128]{2,1,0:T(1,128)} %get-tuple-element.17), calls=%async_computation | async-start | bytes 32768 | tf_op jit(solution)/shard_map/all_to_all | solution.py:432
  16.5 0.3 %collective-permute-start.3 = (f32[1,1024]{1,0:T(1,128)S(1)}, f32[1,1024]{1,0:T(1,128)S(1)}, u32[]{:S(2)}, u32[]{:S(2)}) collective-permute-start(f32[1,1024]{1,0:T(1,128)S(1)} %get-tuple-element.18), channel_id=1, source_target_pairs={{0,1},{1,0},{2,3},{3,2},{4,5},{5,4},{6,7},{7,6},{8,9},{9,8},{10,11... | collective-permute-start | bytes 12296 | tf_op jit(solution)/shard_map/ppermute | solution.py:416
  16.8 0.0 copy-start.1
  16.8 4.5 %collective-permute-start.5 = (f32[9,2,1024]{2,1,0:T(2,128)S(1)}, f32[9,2,1024]{2,1,0:T(2,128)S(1)}, u32[]{:S(2)}, u32[]{:S(2)}) collective-permute-start(f32[9,2,1024]{2,1,0:T(2,128)S(1)} %get-tuple-element.22), channel_id=1, source_target_pairs={{0,28},{4,0},{8,4},{12,8},{16,12},{20,16},{24,20},{28,24},{1,29},{... | collective-permute-start | bytes 221192 | tf_op jit(solution)/shard_map/ppermute | solution.py:421
  21.2 2.3 %all-to-all-done.got_ref = f32[32,1,128]{2,1,0:T(1,128)S(1)} async-done(((f32[32,1,128]{2,1,0:T(1,128)}), f32[32,1,128]{2,1,0:T(1,128)S(1)}, u32[]{:S(2)}, u32[]{:S(2)}) %all-to-all-start) | async-done | bytes 16416 | tf_op jit(solution)/shard_map/all_to_all | solution.py:432
  23.5 0.2 speed_ratios.1.scale_ref
  23.8 0.0 collective-permute-done.3.near_corner_ref
  23.8 0.0 collective-permute-done.5.lead_ref
  23.8 0.0 collective-permute-done.4.rest_ref
  23.8 0.0 copy-done.1
  23.8 2.0 %final.1 = (f32[8]{0:T(128)}, f32[8,32,1024]{2,1,0:T(8,128)}, f32[8,32,1024]{2,1,0:T(8,128)}) custom-call(f32[12,8,128]{2,1,0:T(8,128)S(1)} %speed_ratios.1.scale_ref, f32[1,1024]{1,0:T(1,128)S(1)} %collective-permute-done.3.near_corner_ref, f32[40,1024]{1,0:T(8,128)S(1)} %collective-permute-done.4.rest_ref, f32[8,32,1024]{2,1,0:T(8,128)S(1)} %copy-done.1, ...), custom_call_target="tpu_custom_call" | custom-call | tf_op jit(solution)/shard_map/final/pallas_call | solution.py:395
  (2 shorter events, 0.0 us)
Async XLA Ops:
  0.6 1.2 %copy-start = (f32[8,32,1024]{2,1,0:T(8,128)S(1)}, f32[8,32,1024]{2,1,0:T(8,128)}, u32[]{:S(2)}) copy-start(f32[8,32,1024]{2,1,0:T(8,128)} %f_ref.9) | copy-start | bytes 3145732
  1.9 3.2 %copy-start.2 = (f32[32,1024]{1,0:T(8,128)S(1)}, f32[32,1024]{1,0:T(8,128)}, u32[]{:S(2)}) copy-start(f32[32,1024]{1,0:T(8,128)} %start_ref.5) | copy-start | bytes 393220
  1.9 3.2 %copy-start.3 = (f32[32,1024]{1,0:T(8,128)S(1)}, f32[32,1024]{1,0:T(8,128)}, u32[]{:S(2)}) copy-start(f32[32,1024]{1,0:T(8,128)} %end_ref.5) | copy-start | bytes 393220
  1.9 10.3 %collective-permute-start = (f32[2,32,1024]{2,1,0:T(8,128)S(1)}, f32[2,32,1024]{2,1,0:T(8,128)S(1)}, u32[]{:S(2)}, u32[]{:S(2)}) collective-permute-start(f32[2,32,1024]{2,1,0:T(8,128)S(1)} %get-tuple-element.15), channel_id=1, source_target_pairs={{0,1},{1,0},{2,3},{3,2},{4,5},{5,4},{6,7},{7,6},{8,9},{9,8},{10,11... | collective-permute-start | bytes 786440 | tf_op jit(solution)/shard_map/ppermute | solution.py:416
  2.4 9.8 %collective-permute-start.1 = (f32[32,1024]{1,0:T(8,128)S(1)}, f32[32,1024]{1,0:T(8,128)S(1)}, u32[]{:S(2)}, u32[]{:S(2)}) collective-permute-start(f32[32,1024]{1,0:T(8,128)S(1)} %get-tuple-element.16), channel_id=1, source_target_pairs={{1,2},{2,1},{3,0},{0,3},{5,6},{6,5},{7,4},{4,7},{9,10},{10,9},{11,... | collective-permute-start | bytes 393224 | tf_op jit(solution)/shard_map/ppermute | solution.py:416
  5.1 7.1 %collective-permute-start.2 = (f32[9,2,1024]{2,1,0:T(2,128)S(1)}, f32[9,2,1024]{2,1,0:T(2,128)S(1)}, u32[]{:S(2)}, u32[]{:S(2)}) collective-permute-start(f32[9,2,1024]{2,1,0:T(2,128)S(1)} %tail_rows.1), channel_id=1, source_target_pairs={{0,4},{4,8},{8,12},{12,16},{16,20},{20,24},{24,28},{28,0},{1,5},{5... | collective-permute-start | bytes 221192 | tf_op jit(solution)/shard_map/ppermute | solution.py:421
  13.0 10.8 %collective-permute-start.4 = (f32[40,1024]{1,0:T(8,128)S(1)}, f32[40,1024]{1,0:T(8,128)S(1)}, u32[]{:S(2)}, u32[]{:S(2)}) collective-permute-start(f32[40,1024]{1,0:T(8,128)S(1)} %get-tuple-element.19), channel_id=1, source_target_pairs={{1,2},{2,1},{3,0},{0,3},{5,6},{6,5},{7,4},{4,7},{9,10},{10,9},{11,... | collective-permute-start | bytes 491528 | tf_op jit(solution)/shard_map/ppermute | solution.py:416
  13.1 10.5 %all-to-all-start = ((f32[32,1,128]{2,1,0:T(1,128)}), f32[32,1,128]{2,1,0:T(1,128)S(1)}, u32[]{:S(2)}, u32[]{:S(2)}) async-start(f32[32,1,128]{2,1,0:T(1,128)} %get-tuple-element.17), calls=%async_computation | async-start | bytes 32768 | tf_op jit(solution)/shard_map/all_to_all | solution.py:432
  16.5 7.3 %collective-permute-start.3 = (f32[1,1024]{1,0:T(1,128)S(1)}, f32[1,1024]{1,0:T(1,128)S(1)}, u32[]{:S(2)}, u32[]{:S(2)}) collective-permute-start(f32[1,1024]{1,0:T(1,128)S(1)} %get-tuple-element.18), channel_id=1, source_target_pairs={{0,1},{1,0},{2,3},{3,2},{4,5},{5,4},{6,7},{7,6},{8,9},{9,8},{10,11... | collective-permute-start | bytes 12296 | tf_op jit(solution)/shard_map/ppermute | solution.py:416
  16.8 7.0 %copy-start.1 = (f32[8,32,1024]{2,1,0:T(8,128)S(1)}, f32[8,32,1024]{2,1,0:T(8,128)}, u32[]{:S(2)}) copy-start(f32[8,32,1024]{2,1,0:T(8,128)} %f_ref.9) | copy-start | bytes 3145732
  16.8 7.0 %collective-permute-start.5 = (f32[9,2,1024]{2,1,0:T(2,128)S(1)}, f32[9,2,1024]{2,1,0:T(2,128)S(1)}, u32[]{:S(2)}, u32[]{:S(2)}) collective-permute-start(f32[9,2,1024]{2,1,0:T(2,128)S(1)} %get-tuple-element.22), channel_id=1, source_target_pairs={{0,28},{4,0},{8,4},{12,8},{16,12},{20,16},{24,20},{28,24},{1,29},{... | collective-permute-start | bytes 221192 | tf_op jit(solution)/shard_map/ppermute | solution.py:421
